TPU v7x, 32 devices: a whole 2x2x4 slice. The times are simulated.
32 devices in a mesh: dp: 16 (over z, x, core), mp: 2 (over y).
Axes of the slice: x: 2, y: 2, z: 4, core: 2. Of those that a mesh axis runs over, the one named last changes fastest.
Arguments:
- tokens: bfloat16 [31360, 768], P(('dp', 'mp')), may hold values from -6 to 6
- frame_counts: int32 [16, 2], P('dp'), may hold values from 1 to 8, 10 in all within a row
- norm_gains: float32 [3, 768], replicated, may hold values from 0.1 to 1.9
- norm_shifts: float32 [3, 768], replicated, may hold values from -2 to 2
- attend_weight: bfloat16 [768, 3, 768], P(None, None, 'mp'), may hold values from -0.21875 to 0.21875
- attend_offset: float32 [2, 768], P(None, 'mp'), may hold values from -3 to 3
- output_weight: bfloat16 [768, 768], P('mp'), may hold values from -0.875 to 0.875
- output_offset: float32 [768], replicated, may hold values from -2 to 2
- expand_weight: bfloat16 [768, 3072], P(None, 'mp'), may hold values from -0.21875 to 0.21875
- expand_offset: float32 [3072], P('mp'), may hold values from -3 to 3
- contract_weight: bfloat16 [3072, 768], P('mp'), may hold values from -0.109375 to 0.109375
- contract_offset: float32 [768], replicated, may hold values from -2 to 2
- learner_weight: bfloat16 [768, 8], replicated, may hold values from -0.4375 to 0.4375
- learner_offset: float32 [8], replicated, may hold values from -3 to 3
- pooled_cotangent: bfloat16 [160, 8, 768], P(('dp', 'mp')), may hold values from -6 to 6
Outputs:
- pooled: float32 [160, 8, 768], P(('dp', 'mp'))
- tokens_gradient: float32 [31360, 768], P(('dp', 'mp'))
- gains_gradient: float32 [3, 768], replicated
- shifts_gradient: float32 [3, 768], replicated
- attend_weight_gradient: float32 [768, 3, 768], P(None, None, 'mp')
- attend_offset_gradient: float32 [2, 768], P(None, 'mp')
- output_weight_gradient: float32 [768, 768], P('mp')
- output_offset_gradient: float32 [768], replicated
- expand_weight_gradient: float32 [768, 3072], P(None, 'mp')
- expand_offset_gradient: float32 [3072], P('mp')
- contract_weight_gradient: float32 [3072, 768], P('mp')
- contract_offset_gradient: float32 [768], replicated
- learner_weight_gradient: float32 [768, 8], replicated
- learner_offset_gradient: float32 [8], replicated
Inputs may be any that keep to these rules, and one draw needn't show every extreme that they name: `frame_counts`: each row holds the frame counts of one group's 2 clips in order; they sum to 10, and none exceeds 8.
All inputs are finite; a program needn't handle non-finite values.
Results may differ from a plain program's by a relative error of at most 0.0085.
Values may be sent and summed in bfloat16 or wider, within the bound.
No kernel may reach another device: no remote copies, remote signals or barrier semaphores. Data moves between devices by JAX's collectives and lax.ppermute only.
A program may use at most 192 MiB of HBM per device.

v0:
```python
import functools

import jax
import jax.numpy as jnp
from jax import lax
from jax.experimental import pallas as pl
from jax.experimental.pallas import tpu as pltpu
from jax.sharding import Mesh, PartitionSpec as P

HEAD_DIM = 64
MAPS = 8
FRAME_TOK = 196
EPS = 1e-06
BLK = 256
COST = 20.0
FAR = 1e30
GELU_C = 0.7978845608028654
GELU_A = 0.044715

F32 = jnp.float32
BF16 = jnp.bfloat16


def nn(a, b):
    return lax.dot_general(a, b, (((1,), (0,)), ((), ())), preferred_element_type=F32)


def nt(a, b):
    return lax.dot_general(a, b, (((1,), (1,)), ((), ())), preferred_element_type=F32)


def tn(a, b):
    return lax.dot_general(a, b, (((0,), (0,)), ((), ())), preferred_element_type=F32)


def fold8(values):
    rows, width = values.shape
    return jnp.sum(values.reshape(rows // 8, 8, width), axis=0)


def centre(values):
    average = jnp.mean(values, axis=-1, keepdims=True)
    centred = values - average
    spread = jnp.mean(centred * centred, axis=-1, keepdims=True)
    scale = lax.rsqrt(spread + EPS)
    return centred * scale, scale


def norm_back(xhat, scale, gain, grad):
    scaled = grad * gain
    along = jnp.mean(scaled * xhat, axis=-1, keepdims=True)
    return scale * (scaled - jnp.mean(scaled, axis=-1, keepdims=True) - xhat * along)


def cost(flops, nbytes):
    return pl.CostEstimate(
        flops=int(flops * COST), bytes_accessed=int(nbytes * COST), transcendentals=0
    )


def params(n):
    return pltpu.CompilerParams(
        dimension_semantics=("arbitrary",) * n, vmem_limit_bytes=60 * 1024 * 1024
    )


def whole(shape):
    return pl.BlockSpec(shape, lambda *_: (0,) * len(shape), pipeline_mode=pl.Buffered(1))


def after(value, *others):
    return lax.optimization_barrier((value, others))[0]


def pack_kernel(tokens, cot, out):
    here = tokens.shape[0]
    rows = out.shape[0] - cot.shape[0]
    edge = here // 16 * 16
    out[edge:, :] = jnp.zeros_like(out[edge:, :])
    out[:here, :] = tokens[...]
    out[rows:, :] = cot[...]


def pack(tokens, cot, half_rows):
    rows, width = half_rows + cot.shape[0], tokens.shape[1]
    return pl.pallas_call(
        pack_kernel,
        in_specs=[pl.BlockSpec(tokens.shape), pl.BlockSpec(cot.shape)],
        out_specs=pl.BlockSpec((rows, width)),
        out_shape=jax.ShapeDtypeStruct((rows, width), BF16),
        compiler_params=pltpu.CompilerParams(vmem_limit_bytes=16 * 1024 * 1024),
        cost_estimate=cost(0, 4 * rows * width),
        name="pack",
    )(tokens, cot)


def project_kernel(
    frames_here, scal, oth, own, gain, shift, weight, offset, first, qkv, qfeat, kfeat
):
    step = pl.program_id(0)
    half_blocks = pl.num_programs(0) // 2
    half_rows = half_blocks * BLK
    within = lax.rem(step, half_blocks) * BLK
    rows = pl.ds(pl.multiple_of(within, BLK), BLK)
    values = jnp.where(step < half_blocks, oth[rows, :], own[rows, :]).astype(F32)
    xhat, _ = centre(values)
    low = (xhat * gain[...] + shift[...]).astype(BF16)
    first[...] = low
    out = (nn(low, weight[...]) + offset[...]).astype(BF16)
    for pair in range(out.shape[1] // 384):
        at = pair * 384
        qkv[:, at : at + 128] = out[:, at : at + 128] * jnp.asarray(HEAD_DIM**-0.5, BF16)
        qkv[:, at + 128 : at + 384] = out[:, at + 128 : at + 384]
    core, count = scal[0], scal[2]
    half = jnp.where(step < half_blocks, 1 - core, core)
    edge = clip_edge(count, frames_here, half_rows)
    token = within + lax.broadcasted_iota(jnp.int32, (BLK, 128), 0)
    lane = lax.broadcasted_iota(jnp.int32, (BLK, 128), 1)
    clip = jnp.where(half * half_rows + token >= edge, 1, 0)
    clip = jnp.where(token >= frames_here * FRAME_TOK, 2, clip)
    hit = lane == clip
    qfeat[...] = jnp.where(hit, 1.0, 0.0).astype(BF16)
    kfeat[...] = jnp.where(hit, 0.0, jnp.where(lane < 3, -FAR, 0.0)).astype(BF16)


def clip_edge(count, frames_here, half_rows):
    return jnp.where(
        count <= frames_here,
        count * FRAME_TOK,
        half_rows + (count - frames_here) * FRAME_TOK,
    )


def clip_span(block, edge, blocks):
    low = jnp.where(block * BLK >= edge, edge // BLK, 0)
    high = jnp.where(block * BLK + BLK - 1 < edge, (edge + BLK - 1) // BLK, blocks)
    return low, high


def project(scal, oth, own, gain, shift, weight, offset, frames_here, half_rows):
    width, cols = weight.shape
    steps = 2 * half_rows // BLK
    rows = 2 * half_rows
    return pl.pallas_call(
        functools.partial(project_kernel, frames_here),
        grid_spec=pltpu.PrefetchScalarGridSpec(
            num_scalar_prefetch=1,
            grid=(steps,),
            in_specs=[
                whole(oth.shape),
                whole(own.shape),
                whole((1, width)),
                whole((1, width)),
                whole((width, cols)),
                whole((1, cols)),
            ],
            out_specs=[
                pl.BlockSpec((BLK, width), lambda i, *_: (i, 0)),
                pl.BlockSpec((BLK, cols), lambda i, *_: (i, 0)),
                pl.BlockSpec((BLK, 128), lambda i, *_: (i, 0)),
                pl.BlockSpec((BLK, 128), lambda i, *_: (i, 0)),
            ],
        ),
        out_shape=[
            jax.ShapeDtypeStruct((rows, width), BF16),
            jax.ShapeDtypeStruct((rows, cols), BF16),
            jax.ShapeDtypeStruct((rows, 128), BF16),
            jax.ShapeDtypeStruct((rows, 128), BF16),
        ],
        compiler_params=params(1),
        cost_estimate=cost(2 * rows * width * cols, 4 * rows * width + 2 * rows * cols),
        name="project",
    )(scal, oth, own, gain, shift, weight, offset)


def attend_kernel(
    frames_here,
    bk,
    shift,
    scal,
    q,
    qfeat,
    qkv,
    kfeat,
    mixed,
    wide,
    log_total,
    scores,
    tops,
    acc,
    keys_all,
    values_all,
):
    step = pl.program_id(0)
    half = pl.num_programs(0)
    blocks = 2 * half
    pairs = q.shape[1] // 384
    flip = half * (1 - scal[0])
    edge = clip_edge(scal[2], frames_here, half * BLK)
    low, high = clip_span((step + shift) ^ flip, edge, blocks)
    per = bk // BLK
    low, high = low // per, (high + per - 1) // per
    kflip = flip // per
    lane = lax.broadcasted_iota(jnp.int32, (BLK, 128), 1)
    left = lane < HEAD_DIM
    none = jnp.zeros((BLK, 128), BF16)
    queries = []
    for pair in range(pairs):
        both = q[:, pair * 384 : pair * 384 + 128]
        queries.append(jnp.concatenate([jnp.where(left, both, none), qfeat[...]], axis=1))
        queries.append(jnp.concatenate([jnp.where(left, none, both), qfeat[...]], axis=1))
    @pl.when(step == 0)
    def _():
        def prepare(block, carry):
            rows = pl.ds(pl.multiple_of(block * BLK, BLK), BLK)
            for pair in range(pairs):
                at = pair * 384
                keys_all[pair, rows, :128] = qkv[rows, at + 128 : at + 256]
                keys_all[pair, rows, 128:] = kfeat[rows, :]
                both = qkv[rows, at + 256 : at + 384]
                values_all[2 * pair, rows, :128] = jnp.where(left, both, none)
                values_all[2 * pair, rows, 128:] = jnp.where(lane == 0, 1.0, 0.0).astype(BF16)
                values_all[2 * pair + 1, rows, :128] = jnp.where(left, none, both)
                values_all[2 * pair + 1, rows, 128:] = jnp.where(lane == 1, 1.0, 0.0).astype(BF16)
            return carry

        lax.fori_loop(0, blocks, prepare, 0)

    for head in range(2 * pairs):
        tops[head] = jnp.full((BLK, 128), -3e38, F32)

    def score(block, carry):
        rows = pl.ds(pl.multiple_of((block ^ kflip) * bk, bk), bk)
        for pair in range(pairs):
            keys = keys_all[pair, rows, :]
            for head in (2 * pair, 2 * pair + 1):
                values = nt(queries[head], keys)
                scores[head, block] = values
                top = tops[head]
                for part in range(bk // 128):
                    top = jnp.maximum(top, values[:, part * 128 : (part + 1) * 128])
                tops[head] = top
        return carry

    lax.fori_loop(low, high, score, 0)
    peaks = []
    for head in range(2 * pairs):
        peaks.append(jnp.max(tops[head], axis=1, keepdims=True))
        tops[head] = jnp.broadcast_to(peaks[-1], (BLK, 128))
    acc[...] = jnp.zeros_like(acc)
    def mix(block, carry):
        rows = pl.ds(pl.multiple_of((block ^ kflip) * bk, bk), bk)
        for pair in range(pairs):
            soft = []
            for head in (2 * pair, 2 * pair + 1):
                top = tops[head]
                for part in range(bk // 128):
                    piece = scores[head, block, :, part * 128 : (part + 1) * 128]
                    soft.append(jnp.exp(piece - top).astype(BF16))
            values = jnp.concatenate(
                [values_all[2 * pair, rows, :], values_all[2 * pair + 1, rows, :]], axis=0
            )
            acc[pair] += nn(jnp.concatenate(soft, axis=1), values)
        return carry

    lax.fori_loop(low, high, mix, 0)
    for pair in range(pairs):
        cols = slice(pair * 128, (pair + 1) * 128)
        total_a, total_b = acc[pair, :, 128:129], acc[pair, :, 129:130]
        out = acc[pair, :, :128] / jnp.where(left, total_a, total_b)
        wide[:, cols] = out
        mixed[:, cols] = out.astype(BF16)

        logs = jnp.where(
            lane == 0,
            peaks[2 * pair] + jnp.log(total_a),
            jnp.where(lane == 1, peaks[2 * pair + 1] + jnp.log(total_b), 0.0),
        )
        log_total[pair, 0] = logs.T[:8]


def attend(scal, qkv, qfeat, kfeat, frames_here, own):
    rows, cols = qkv.shape
    width = cols // 3
    pairs = width // 128
    half = rows // BLK // 2
    bk = rows // 2
    shift = half if own else 0
    return pl.pallas_call(
        functools.partial(attend_kernel, frames_here, bk, shift),
        grid_spec=pltpu.PrefetchScalarGridSpec(
            num_scalar_prefetch=1,
            grid=(half,),
            in_specs=[
                pl.BlockSpec((BLK, cols), lambda i, *_: (i + shift, 0)),
                pl.BlockSpec((BLK, 128), lambda i, *_: (i + shift, 0)),
                whole((rows, cols)),
                whole((rows, 128)),
            ],
            out_specs=[
                pl.BlockSpec((BLK, width), lambda i, *_: (i, 0)),
                pl.BlockSpec((BLK, width), lambda i, *_: (i, 0)),
                pl.BlockSpec((pairs, 1, 8, BLK), lambda i, *_: (0, i, 0, 0)),
            ],
            scratch_shapes=[
                pltpu.VMEM((2 * pairs, rows // bk, BLK, bk), F32),
                pltpu.VMEM((2 * pairs, BLK, 128), F32),
                pltpu.VMEM((pairs, BLK, 256), F32),
                pltpu.VMEM((pairs, rows, 256), BF16),
                pltpu.VMEM((2 * pairs, rows, 256), BF16),
            ],
        ),
        out_shape=[
            jax.ShapeDtypeStruct((rows // 2, width), BF16),
            jax.ShapeDtypeStruct((rows // 2, width), F32),
            jax.ShapeDtypeStruct((pairs, half, 8, BLK), F32),
        ],
        compiler_params=params(1),
        cost_estimate=cost(8 * rows * rows * width, 16 * rows * width),
        name="attend",
    )(scal, qkv, qfeat, qkv, kfeat)


def gather_out_weight(scal, own_out, got_a, got_b, out_weight, hid):
    core, plane = scal[0], scal[1]
    share = own_out.shape[0]
    quarter = share // 2
    out_weight[pl.ds(pl.multiple_of(plane * share, 64), share), :] = own_out[...]
    base = (1 - plane) * share
    out_weight[pl.ds(pl.multiple_of(base + core * quarter, 64), quarter), :] = got_a[
        2 * hid : 2 * hid + quarter, :
    ]
    out_weight[pl.ds(pl.multiple_of(base + (1 - core) * quarter, 64), quarter), :] = got_b[
        2 * hid : 2 * hid + quarter, :
    ]


def up_weight(core, own_up, got_a, got_b, chunk):
    hid = got_a.shape[1]
    if chunk < 2:
        return (got_b, got_a)[chunk][hid : 2 * hid, :]
    pick = (1 - core) if chunk == 2 else core
    return own_up[:, pl.ds(pl.multiple_of(pick * hid, 128), hid)]


def down_weight(core, own_down, got_a, got_b, chunk):
    hid = got_a.shape[1]
    if chunk < 2:
        return (got_b, got_a)[chunk][:hid, :]
    pick = (1 - core) if chunk == 2 else core
    return own_down[pl.ds(pl.multiple_of(pick * hid, 128), hid), :]


def ahead_kernel(
    frames_here,
    scal,
    mixed_own,
    mixed_oth,
    tokens,
    cot,
    own_out,
    own_up,
    own_down,
    got_a,
    got_b,
    up_offset,
    gains,
    shifts,
    out_offset,
    down_offset,
    learner,
    learner_offset,
    out_grad_out,
    xhat_out,
    scale_out,
    hidden_out,
    slope_out,
    second_out,
    out_low_out,
    sums,
    pooled,
    learner_sums,
    learner_offset_sums,
    out_weight,
):
    step = pl.program_id(0)
    core, plane = scal[0], scal[1]
    hid = got_a.shape[1]
    share = own_out.shape[0]

    @pl.when(step == 0)
    def _():
        gather_out_weight(scal, own_out, got_a, got_b, out_weight, hid)
        for ref in (sums, pooled, learner_sums, learner_offset_sums):
            ref[...] = jnp.zeros_like(ref)

    def up_bias(chunk):
        side = (1 - plane) if chunk < 2 else plane
        pick = (1 - core) if chunk % 2 == 0 else core
        return up_offset[pl.ds(2 * side + pick, 1), :]

    mine = pl.ds(pl.multiple_of(core * share, 64), share)
    theirs = pl.ds(pl.multiple_of((1 - core) * share, 64), share)
    attended = nn(mixed_own[...], out_weight[mine, :]) + nn(mixed_oth[...], out_weight[theirs, :])
    residual = tokens[...].astype(F32) + attended + out_offset[...]
    xhat_two, scale_two = centre(residual)
    xhat_out[...] = xhat_two
    scale_out[...] = jnp.broadcast_to(scale_two, scale_out.shape)
    second = (xhat_two * gains[1:2, :] + shifts[1:2, :]).astype(BF16)
    second_out[...] = second
    block_out = residual + down_offset[...]
    for chunk in range(4):
        cols = slice(chunk * hid, (chunk + 1) * hid)
        pre = nn(second, up_weight(core, own_up, got_a, got_b, chunk)) + up_bias(chunk)
        square = pre * pre
        bend = jnp.tanh(GELU_C * (pre + GELU_A * (square * pre)))
        half_up = 0.5 * (1.0 + bend)
        hidden = (pre * half_up).astype(BF16)
        slope_out[:, cols] = half_up + (0.5 * pre) * (1.0 - bend * bend) * (
            GELU_C + (3.0 * GELU_A * GELU_C) * square
        )
        hidden_out[:, cols] = hidden
        block_out = block_out + nn(hidden, down_weight(core, own_down, got_a, got_b, chunk))
    xhat_three, scale_three = centre(block_out)
    third = (xhat_three * gains[2:3, :] + shifts[2:3, :]).astype(BF16)
    logits = nt(third, learner[...]) + learner_offset[...]
    sig = 1.0 / (1.0 + jnp.exp(-logits))
    token = step * BLK + lax.broadcasted_iota(jnp.int32, (BLK, 128), 0)
    first_token = (lax.broadcasted_iota(jnp.int32, (BLK, 128), 1) >> 3) * FRAME_TOK
    inside = (token >= first_token) & (token < first_token + FRAME_TOK)
    inside = inside & (first_token < frames_here * FRAME_TOK)
    maps = jnp.where(inside, sig, 0.0).astype(BF16)
    feature = block_out.astype(BF16)
    pooled[...] += tn(maps, feature)
    maps_grad = nt(feature, cot[...])
    pool_grad = nn(maps, cot[...])
    logits_grad = jnp.where(inside, maps_grad * sig * (1.0 - sig), 0.0).astype(BF16)
    learner_sums[...] += tn(logits_grad, third)
    learner_offset_sums[...] += fold8(logits_grad.astype(F32))
    third_grad = nn(logits_grad, learner[...])
    sums[0:8, :] += fold8(third_grad * xhat_three)
    sums[8:16, :] += fold8(third_grad)
    out_grad = pool_grad + norm_back(xhat_three, scale_three, gains[2:3, :], third_grad)
    sums[16:24, :] += fold8(out_grad)
    out_grad_out[...] = out_grad
    out_low_out[...] = out_grad.astype(BF16)


def behind_kernel(
    pooled_rows,
    scal,
    out_grad,
    out_low,
    xhat_two,
    scale_two,
    slope,
    own_out,
    own_up,
    own_down,
    got_a,
    got_b,
    gains,
    pooled,
    residual_grad_out,
    grad_own,
    grad_oth,
    pre_grad_out,
    residual_low_out,
    sums,
    up_sums,
    out_weight,
):
    core = scal[0]
    hid = got_a.shape[1]
    share = own_out.shape[0]

    @pl.when(pl.program_id(0) == 0)
    def _():
        gather_out_weight(scal, own_out, got_a, got_b, out_weight, hid)
        for ref in (sums, up_sums):
            ref[...] = jnp.zeros_like(ref)

    mine = pl.ds(pl.multiple_of(core * share, 64), share)
    theirs = pl.ds(pl.multiple_of((1 - core) * share, 64), share)
    low = out_low[...]
    second_grad = None
    for chunk in range(4):
        cols = slice(chunk * hid, (chunk + 1) * hid)
        hidden_grad = nt(low, down_weight(core, own_down, got_a, got_b, chunk))
        pre_grad = (hidden_grad * slope[:, cols]).astype(BF16)
        pre_grad_out[:, cols] = pre_grad
        up_sums[:, cols] += fold8(pre_grad.astype(F32))
        term = nt(pre_grad, up_weight(core, own_up, got_a, got_b, chunk))
        second_grad = term if second_grad is None else second_grad + term
    xhat = xhat_two[...]
    sums[0:8, :] += fold8(second_grad * xhat)
    sums[8:16, :] += fold8(second_grad)
    residual_grad = out_grad[...] + norm_back(
        xhat, scale_two[:, :1], gains[1:2, :], second_grad
    )
    sums[16:24, :] += fold8(residual_grad)
    residual_grad_out[...] = residual_grad

    @pl.when(pl.program_id(0) == pl.num_programs(0) - 1)
    def _():
        residual_grad_out[BLK - pooled_rows :, :] = pooled[:pooled_rows, :]

    residual_low = residual_grad.astype(BF16)
    residual_low_out[...] = residual_low
    grad_own[...] = nt(residual_low, out_weight[mine, :]).astype(BF16)
    grad_oth[...] = nt(residual_low, out_weight[theirs, :]).astype(BF16)


def row_block(cols):
    return pl.BlockSpec((BLK, cols), lambda i, *_: (i, 0))


def held(shape):
    return pl.BlockSpec(shape, lambda *_: (0,) * len(shape))


def row_call(kernel, name, scal, rowed, wholes, row_outs, held_outs, scratch, flops):
    rows = rowed[0].shape[0]
    nbytes = sum(x.size * x.dtype.itemsize for x in wholes)
    nbytes += rows * sum(c * (2 if t == BF16 else 4) for c, t in row_outs)
    return pl.pallas_call(
        kernel,
        grid_spec=pltpu.PrefetchScalarGridSpec(
            num_scalar_prefetch=1,
            grid=(rows // BLK,),
            in_specs=[row_block(x.shape[1]) for x in rowed] + [whole(x.shape) for x in wholes],
            out_specs=[row_block(cols) for cols, _ in row_outs] + [held(s) for s in held_outs],
            scratch_shapes=scratch,
        ),
        out_shape=[jax.ShapeDtypeStruct((rows, cols), t) for cols, t in row_outs]
        + [jax.ShapeDtypeStruct(s, F32) for s in held_outs],
        compiler_params=params(1),
        cost_estimate=cost(flops, nbytes),
        name=name,
    )(scal, *rowed, *wholes)


def ahead(scal, mixed_own, mixed_oth, packed, cot, weights, up_offset, small, frames_here):
    rows, share = mixed_own.shape
    width = packed.shape[1]
    hidden = up_offset.size
    return row_call(
        functools.partial(ahead_kernel, frames_here),
        "ahead",
        scal,
        [mixed_own, mixed_oth, packed],
        [cot, *weights, up_offset, *small],
        [
            (width, F32),
            (width, F32),
            (128, F32),
            (hidden, BF16),
            (hidden, F32),
            (width, BF16),
            (width, BF16),
        ],
        [(24, width), (128, width), (128, width), (8, 128)],
        [pltpu.VMEM((2 * share, width), BF16)],
        2 * rows * width * (2 * hidden + width),
    )


def behind(scal, out_grad, out_low, xhat_two, scale_two, slope, weights, gains, pooled, maps_all):
    rows, width = out_grad.shape
    share = weights[0].shape[0]
    hidden = slope.shape[1]
    return row_call(
        functools.partial(behind_kernel, maps_all),
        "behind",
        scal,
        [out_grad, out_low, xhat_two, scale_two, slope],
        [*weights, gains, pooled],
        [(width, F32), (share, BF16), (share, BF16), (hidden, BF16), (width, BF16)],
        [(24, width), (8, hidden)],
        [pltpu.VMEM((2 * share, width), BF16)],
        2 * rows * width * (2 * hidden + width),
    )


def down_grad_kernel(hidden, out_low, out):
    out[0] = tn(hidden[...], out_low[...]).astype(BF16)


def down_grad(hidden, out_low, odd):
    rows, width = out_low.shape
    hid = hidden.shape[1] // 4
    return pl.pallas_call(
        down_grad_kernel,
        grid=(2,),
        in_specs=[
            pl.BlockSpec((rows, hid), lambda n: (0, 2 * n + odd)),
            whole((rows, width)),
        ],
        out_specs=pl.BlockSpec((1, hid, width), lambda n: (n, 0, 0)),
        out_shape=jax.ShapeDtypeStruct((2, hid, width), BF16),
        compiler_params=params(1),
        cost_estimate=cost(4 * rows * hid * width, 8 * rows * hid),
        name="down_grad",
    )(hidden, out_low)


def up_grad_kernel(odd, scal, second, pre_grad, mixed_own, mixed_oth, residual_low, out):
    step = pl.program_id(0)
    core, plane = scal[0], scal[1]
    width, hid = second.shape[1], pre_grad.shape[1]
    share = mixed_own.shape[1]
    out[0, :width, :] = tn(second[...], pre_grad[...]).astype(BF16)
    side = jnp.where(step == 0, 1 - plane, plane)
    column = core if odd else 1 - core
    lhs = jnp.where(side == core, mixed_own[...], mixed_oth[...])
    rhs = residual_low[:, pl.ds(pl.multiple_of(column * (width // 2), 128), width // 2)]
    grad = tn(lhs, rhs).astype(BF16)
    out[0, width:, : width // 2] = grad[: share // 2]
    out[0, width:, width // 2 :] = grad[share // 2 :]


def up_grad(scal, second, pre_grad, mixed_own, mixed_oth, residual_low, odd):
    rows, width = second.shape
    hid = pre_grad.shape[1] // 4
    share = mixed_own.shape[1]
    return pl.pallas_call(
        functools.partial(up_grad_kernel, odd),
        grid_spec=pltpu.PrefetchScalarGridSpec(
            num_scalar_prefetch=1,
            grid=(2,),
            in_specs=[
                whole((rows, width)),
                pl.BlockSpec((rows, hid), lambda n, *_: (0, 2 * n + odd)),
                whole((rows, share)),
                whole((rows, share)),
                whole((rows, width)),
            ],
            out_specs=pl.BlockSpec((1, width + share // 2, hid), lambda n, *_: (n, 0, 0)),
        ),
        out_shape=jax.ShapeDtypeStruct((2, width + share // 2, hid), BF16),
        compiler_params=params(1),
        cost_estimate=cost(4 * rows * hid * width * 1.25, 10 * rows * hid),
        name="up_grad",
    )(scal, second, pre_grad, mixed_own, mixed_oth, residual_low)


def attend_back_kernel(
    frames_here,
    scal,
    k,
    v,
    kfeat,
    q,
    qfeat,
    grad_oth,
    grad_own,
    wide_oth,
    wide_own,
    log_oth,
    log_own,
    out_oth,
    out_own,
    queries,
    grads,
    inner,
    logs,
    dq,
    dkv,
):
    step = pl.program_id(0)
    half = grad_oth.shape[0] // BLK
    blocks = 2 * half
    flip = half * (1 - scal[0])
    edge = clip_edge(scal[2], frames_here, half * BLK)
    low, high = clip_span(step ^ flip, edge, blocks)
    bq = half * BLK
    low, high = low // half, (high + half - 1) // half
    qflip = 1 - scal[0]
    lane = lax.broadcasted_iota(jnp.int32, (BLK, 128), 1)
    left = lane < HEAD_DIM
    none = jnp.zeros((BLK, 128), BF16)

    @pl.when(step == 0)
    def _():
        dq[...] = jnp.zeros_like(dq)
        for side, (grad, wide, log_total) in enumerate(
            ((grad_oth, wide_oth, log_oth), (grad_own, wide_own, log_own))
        ):
            for block in range(bq // BLK):
                here = slice(block * BLK, (block + 1) * BLK)
                rows = slice(side * bq + block * BLK, side * bq + (block + 1) * BLK)
                grads[rows, :] = grad[here, :]
                queries[rows, :128] = q[rows, :]
                queries[rows, 128:] = qfeat[rows, :]
                product = (grad[here, :].astype(F32) * wide[here, :]).T
                inner[side, 0:1, here] = jnp.sum(product[:HEAD_DIM], axis=0, keepdims=True)
                inner[side, 1:2, here] = jnp.sum(product[HEAD_DIM:], axis=0, keepdims=True)
                logs[side, :, here] = log_total[0, block]

    ka = jnp.where(left, k[...], none)
    kb = jnp.where(left, none, k[...])
    key_a = jnp.concatenate([ka, kfeat[...]], axis=1)
    key_b = jnp.concatenate([kb, kfeat[...]], axis=1)
    keys = jnp.concatenate([ka, kb], axis=0)
    va = jnp.where(left, v[...], none)
    vb = jnp.where(left, none, v[...])
    dkv[...] = jnp.zeros_like(dkv)

    def pair(block, carry):
        local = block ^ qflip
        rows = pl.ds(pl.multiple_of(local * bq, bq), bq)
        query = queries[rows, :]
        grad = grads[rows, :]
        soft_a = jnp.exp(nt(key_a, query) - logs[local, 0:1])
        soft_b = jnp.exp(nt(key_b, query) - logs[local, 1:2])
        score_a = (soft_a * (nt(va, grad) - inner[local, 0:1])).astype(BF16)
        score_b = (soft_b * (nt(vb, grad) - inner[local, 1:2])).astype(BF16)
        dkv[0] += nn(soft_a.astype(BF16), grad)
        dkv[1] += nn(soft_b.astype(BF16), grad)
        dkv[2] += nn(score_a, query[:, :128])
        dkv[3] += nn(score_b, query[:, :128])
        dq[rows, :] += tn(jnp.concatenate([score_a, score_b], axis=0), keys)
        return carry

    lax.fori_loop(low, high, pair, 0)
    dk = jnp.where(left, dkv[2], dkv[3]).astype(BF16)
    dv = jnp.where(left, dkv[0], dkv[1]).astype(BF16)
    within = pl.ds(pl.multiple_of(lax.rem(step, half) * BLK, BLK), BLK)

    @pl.when(step < half)
    def _():
        out_oth[within, 128:256] = dk
        out_oth[within, 256:] = dv

    @pl.when(step >= half)
    def _():
        out_own[within, 128:256] = dk
        out_own[within, 256:] = dv

    @pl.when(step == blocks - 1)
    def _():
        half_rows = out_oth.shape[0]
        out_oth[:, :128] = (dq[:half_rows, :] * HEAD_DIM**-0.5).astype(BF16)
        out_own[:, :128] = (dq[half_rows:, :] * HEAD_DIM**-0.5).astype(BF16)

def attend_back(scal, qkv, qfeat, kfeat, grad_oth, grad_own, wide, logs, frames_here, pair):
    rows = qkv.shape[0]
    blocks = rows // BLK
    one = pl.Buffered(1)
    half_rows = pl.BlockSpec((rows // 2, 128), lambda j, *_: (0, pair), pipeline_mode=one)
    half_logs = pl.BlockSpec(
        (1, blocks // 2, 8, BLK), lambda j, *_: (pair, 0, 0, 0), pipeline_mode=one
    )
    return pl.pallas_call(
        functools.partial(attend_back_kernel, frames_here),
        grid_spec=pltpu.PrefetchScalarGridSpec(
            num_scalar_prefetch=1,
            grid=(blocks,),
            in_specs=[
                pl.BlockSpec((BLK, 128), lambda j, *_: (j, 3 * pair + 1)),
                pl.BlockSpec((BLK, 128), lambda j, *_: (j, 3 * pair + 2)),
                pl.BlockSpec((BLK, 128), lambda j, *_: (j, 0)),
                pl.BlockSpec((rows, 128), lambda j, *_: (0, 3 * pair), pipeline_mode=one),
                whole((rows, 128)),
                half_rows,
                half_rows,
                half_rows,
                half_rows,
                half_logs,
                half_logs,
            ],
            out_specs=[pl.BlockSpec((rows // 2, 384), lambda j, *_: (0, 0))] * 2,
            scratch_shapes=[
                pltpu.VMEM((rows, 256), BF16),
                pltpu.VMEM((rows, 128), BF16),
                pltpu.VMEM((2, 8, rows // 2), F32),
                pltpu.VMEM((2, 8, rows // 2), F32),
                pltpu.VMEM((rows, 128), F32),
                pltpu.VMEM((4, BLK, 128), F32),
            ],
        ),
        out_shape=[jax.ShapeDtypeStruct((rows // 2, 384), BF16)] * 2,
        compiler_params=params(1),
        cost_estimate=cost(40 * rows * rows * 128, 30 * rows * 128),
        name="attend_back",
    )(scal, qkv, qkv, kfeat, qkv, qfeat, grad_oth, grad_own, *wide, *logs)


def project_grad_kernel(pairs, scal, first, *refs):
    oth, own = refs[:pairs], refs[pairs : 2 * pairs]
    theirs, mine, offsets = refs[2 * pairs :]
    step = pl.program_id(0)
    half = oth[0].shape[0]
    one = jnp.concatenate([x[...] for x in oth], axis=1)
    two = jnp.concatenate([x[...] for x in own], axis=1)
    out = (tn(first[:half, :], one) + tn(first[half:, :], two)).astype(BF16)

    @pl.when(step == 0)
    def _():
        theirs[...] = out
        offsets[...] = fold8(one.astype(F32)) + fold8(two.astype(F32))

    @pl.when(step == 1)
    def _():
        mine[...] = out


def project_grad(scal, first, oth, own):
    pairs = len(oth)
    rows, width = first.shape
    cols = 384 * pairs
    return pl.pallas_call(
        functools.partial(project_grad_kernel, pairs),
        grid_spec=pltpu.PrefetchScalarGridSpec(
            num_scalar_prefetch=1,
            grid=(2,),
            in_specs=[
                pl.BlockSpec((rows, width // 2), lambda n, scal: (0, (1 - scal[0]) ^ n)),
            ]
            + [whole((rows // 2, 384))] * (2 * pairs),
            out_specs=[held((width // 2, cols)), held((width // 2, cols)), held((8, cols))],
        ),
        out_shape=[
            jax.ShapeDtypeStruct((width // 2, cols), BF16),
            jax.ShapeDtypeStruct((width // 2, cols), BF16),
            jax.ShapeDtypeStruct((8, cols), F32),
        ],
        compiler_params=params(1),
        cost_estimate=cost(2 * rows * width * cols, 2 * rows * (width + cols)),
        name="project_grad",
    )(scal, first, *oth, *own)


def first_grad_kernel(pairs, *refs):
    own, got = refs[:pairs], refs[pairs : 2 * pairs]
    mine, theirs, tokens, out, sums = refs[2 * pairs :]
    total = nt(jnp.concatenate([x[...] for x in own], axis=1), mine[...])
    total = total + nt(jnp.concatenate([x[...] for x in got], axis=1), theirs[...])
    out[...] = total.astype(BF16)

    @pl.when(pl.program_id(0) == 0)
    def _():
        sums[...] = jnp.zeros_like(sums)

    xhat, _ = centre(tokens[...].astype(F32))
    sums[0:8, :] += fold8(total * xhat)
    sums[8:16, :] += fold8(total)


def first_grad(own, got, mine, theirs, packed):
    pairs = len(own)
    rows, cols = own[0].shape
    width = mine.shape[0]
    return pl.pallas_call(
        functools.partial(first_grad_kernel, pairs),
        grid=(rows // BLK,),
        in_specs=[pl.BlockSpec((BLK, cols), lambda i: (i, 0))] * (2 * pairs)
        + [whole(mine.shape), whole(theirs.shape), pl.BlockSpec((BLK, width), lambda i: (i, 0))],
        out_specs=[
            pl.BlockSpec((BLK, width), lambda i: (i, 0)),
            pl.BlockSpec((16, width), lambda i: (0, 0)),
        ],
        out_shape=[
            jax.ShapeDtypeStruct((rows, width), BF16),
            jax.ShapeDtypeStruct((16, width), F32),
        ],
        compiler_params=params(1),
        cost_estimate=cost(
            4 * pairs * rows * width * cols, 4 * pairs * rows * cols + 4 * width * cols * pairs
        ),
        name="first_grad",
    )(*own, *got, mine, theirs, packed)


def last_kernel(scal, tokens, grad, grad_got, residual, residual_got, gain, out):
    xhat, scale = centre(tokens[...].astype(F32))
    straight = scal[0] == scal[1]
    wide = jnp.where(straight, grad[...], grad_got[...]).astype(F32)
    base = jnp.where(straight, residual[...], residual_got[...])
    out[...] = base + norm_back(xhat, scale, gain[...], wide)


def last(scal, packed, grad, grad_got, residual, residual_got, gain, tokens_here):
    rows, width = grad.shape
    return pl.pallas_call(
        last_kernel,
        grid_spec=pltpu.PrefetchScalarGridSpec(
            num_scalar_prefetch=1,
            grid=(rows // BLK,),
            in_specs=[row_block(width)] * 5 + [whole((1, width))],
            out_specs=row_block(width),
        ),
        out_shape=jax.ShapeDtypeStruct((tokens_here, width), F32),
        compiler_params=params(1),
        cost_estimate=cost(20 * rows * width, 12 * rows * width),
        name="last",
    )(scal, packed, grad, grad_got, residual, residual_got, gain)


def table_kernel(
    frames_here, scal, ahead_sums, behind_sums, first_sums, learner, learner_offset, up, *refs
):
    offsets, out = refs[:-1], refs[-1]
    core, plane = scal[0], scal[1]
    width = out.shape[1]
    hid = up.shape[1] // 4

    def total(ref, at):
        return jnp.sum(ref[at : at + 8, :], axis=0, keepdims=True)

    out[...] = jnp.zeros_like(out)
    for row, (ref, at) in enumerate(
        (
            (first_sums, 0),
            (behind_sums, 0),
            (ahead_sums, 0),
            (first_sums, 8),
            (behind_sums, 8),
            (ahead_sums, 8),
            (behind_sums, 16),
            (ahead_sums, 16),
        )
    ):
        out[row : row + 1, :] = total(ref, at)
    out[8:16, :] = sum(learner[MAPS * i : MAPS * (i + 1), :] for i in range(frames_here))
    row = total(learner_offset, 0)
    lane = lax.broadcasted_iota(jnp.int32, (1, 128), 1)
    kept = row
    for i in range(1, frames_here):
        kept = kept + pltpu.roll(row, 128 - MAPS * i, 1)
    out[16:17, :128] = jnp.where(lane < MAPS, kept, 0.0)
    for chunk in range(4):
        side = (1 - plane) if chunk < 2 else plane
        pick = (1 - core) if chunk % 2 == 0 else core
        out[pl.ds(17 + 2 * side + pick, 1), :] = jnp.sum(
            up[:, chunk * hid : (chunk + 1) * hid], axis=0, keepdims=True
        )
    pair = 0
    for ref in offsets:
        for at in range(0, ref.shape[1], 384):
            to = pl.ds(pl.multiple_of(core * (width // 2) + pair * 128, 128), 128)
            out[21:22, to] = jnp.sum(ref[:, at : at + 128], axis=0, keepdims=True)
            out[22:23, to] = jnp.sum(ref[:, at + 256 : at + 384], axis=0, keepdims=True)
            pair += 1


def small_table(scal, frames_here, *parts):
    width = parts[0].shape[1]
    return pl.pallas_call(
        functools.partial(table_kernel, frames_here),
        grid_spec=pltpu.PrefetchScalarGridSpec(
            num_scalar_prefetch=1,
            grid=(1,),
            in_specs=[held(x.shape) for x in parts],
            out_specs=held((24, width)),
        ),
        out_shape=jax.ShapeDtypeStruct((24, width), F32),
        compiler_params=pltpu.CompilerParams(vmem_limit_bytes=16 * 1024 * 1024),
        cost_estimate=cost(0, 1 << 20),
        name="small_table",
    )(scal, *parts)


def body(
    tokens,
    frame_counts,
    norm_gains,
    norm_shifts,
    attend_weight,
    attend_offset,
    output_weight,
    output_offset,
    expand_weight,
    expand_offset,
    contract_weight,
    contract_offset,
    learner_weight,
    learner_offset,
    pooled_cotangent,
):
    tokens_here, width = tokens.shape
    frames_here = tokens_here // FRAME_TOK
    half_rows = -(-tokens_here // BLK) * BLK
    share = attend_weight.shape[2]
    hid = contract_weight.shape[0] // 2
    chips = lax.axis_size("chip")
    core, plane = lax.axis_index("core"), lax.axis_index("mp")
    straight = core == plane
    flip2 = [(0, 1), (1, 0)]

    def turn(x):
        return lax.ppermute(x, ("core", "mp"), [(1, 2), (2, 1)])

    def to_core(x):
        return lax.ppermute(x, "core", flip2)

    def to_plane(x):
        return lax.ppermute(x, "mp", flip2)

    chip = lax.axis_index("chip")
    side = chip % 2
    hops = []
    while (2 << len(hops)) < chips:
        hops.append(2 << len(hops))

    def hop(x, step):
        return lax.ppermute(x, "chip", [(i, i ^ step) for i in range(chips)])

    def low(x):
        return x.astype(BF16)

    def plus(a, b):
        return a.astype(F32) + b.astype(F32)

    def pick(x, index):
        return lax.dynamic_index_in_dim(x, index, 0, keepdims=False)

    def halves_of(x):
        rows = x.shape[-2] // 2
        return x.reshape(*x.shape[:-2], 2, rows, x.shape[-1])

    def join(x, other, index, axis):
        return jnp.concatenate(
            [jnp.where(index == 0, x, other), jnp.where(index == 0, other, x)], axis=axis
        )

    pairs = share // 128

    weight_mine = (
        attend_weight.reshape(width, 3, pairs, 128).transpose(0, 2, 1, 3).reshape(width, 3 * share)
    )
    weight_part = turn(lax.dynamic_slice_in_dim(weight_mine, side * (width // 2), width // 2, 0))
    packed = pack(tokens, pooled_cotangent.reshape(frames_here * MAPS, width), half_rows)
    got_packed = turn(after(packed, weight_mine))
    small = jnp.concatenate(
        [
            attend_offset,
            jnp.broadcast_to(frame_counts[0, 0].astype(F32), (2, 128)),
        ],
        axis=1,
    )
    small = jnp.where(straight, small, turn(small))
    expand_got = to_plane(expand_offset)
    weight_rest = lax.ppermute(
        weight_part,
        ("chip", "core", "mp"),
        [(4 * i + j, 4 * (i ^ 1) + j) for i in range(chips) for j in (1, 2)],
    )
    weight_here = jnp.where(straight, weight_mine, join(weight_part, weight_rest, side, 0))
    own = jnp.where(straight, packed, got_packed)
    oth = to_core(own)
    count = small[0, share].astype(jnp.int32)
    scal = jnp.stack([core.astype(jnp.int32), plane.astype(jnp.int32), count])
    offset = jnp.stack([small[0, :share], jnp.zeros((share,), F32), small[1, :share]])
    offset = offset.reshape(3, pairs, 128).transpose(1, 0, 2).reshape(1, 3 * share)

    quarter = jnp.concatenate(
        [
            lax.dynamic_slice_in_dim(contract_weight, core * hid, hid, 0),
            lax.dynamic_slice_in_dim(expand_weight, core * hid, hid, 1),
            lax.dynamic_slice_in_dim(output_weight, core * (share // 2), share // 2, 0),
        ],
        axis=0,
    )
    got_a = to_plane(after(quarter, own, weight_here, small, expand_got))
    up_offset = jnp.where(
        plane == 0,
        jnp.concatenate([expand_offset, expand_got]),
        jnp.concatenate([expand_got, expand_offset]),
    ).reshape(4, hid)

    first, qkv, qfeat, kfeat = project(
        scal,
        oth,
        own,
        norm_gains[0:1],
        norm_shifts[0:1],
        weight_here,
        offset,
        frames_here,
        half_rows,
    )
    mixed_send, wide_oth, logs_oth = attend(scal, qkv, qfeat, kfeat, frames_here, False)
    mixed_oth = to_core(mixed_send)
    weight_there = to_core(after(weight_here, mixed_send))
    mixed_own, wide_own, logs_own = attend(
        after(scal, mixed_send), qkv, qfeat, kfeat, frames_here, True
    )
    got_b = to_core(after(got_a, mixed_own))

    maps_all = frames_here * MAPS
    cot = jnp.pad(own[half_rows:], ((0, 128 - maps_all), (0, 0)))
    learner = jnp.pad(jnp.tile(learner_weight.T, (frames_here, 1)), ((0, 128 - maps_all), (0, 0)))
    learner_bias = jnp.pad(jnp.tile(learner_offset, frames_here), (0, 128 - maps_all))[None]
    weights = (output_weight, expand_weight, contract_weight, got_a, got_b)
    (
        out_grad,
        xhat_two,
        scale_two,
        hidden,
        slope,
        second,
        out_low,
        sums_ahead,
        pooled,
        learner_sums,
        learner_offset_sums,
    ) = ahead(
        scal,
        mixed_own,
        mixed_oth,
        own,
        cot,
        weights,
        up_offset,
        (
            norm_gains,
            norm_shifts,
            output_offset[None],
            contract_offset[None],
            learner,
            learner_bias,
        ),
        frames_here,
    )

    down_theirs = down_grad(hidden, out_low, 0)
    down_got = to_core(down_theirs)
    down_mine = down_grad(hidden, after(out_low, down_theirs), 1)
    down_send = low(plus(down_got[0], down_mine[0]))
    down_keep = plus(down_got[1], down_mine[1])
    down_plane = to_plane(down_send)

    (
        residual_grad,
        grad_own,
        grad_send,
        pre_grad,
        residual_low,
        sums_behind,
        up_sums,
    ) = behind(
        after(scal, down_send),
        out_grad,
        out_low,
        xhat_two,
        scale_two,
        slope,
        weights,
        norm_gains,
        pooled,
        maps_all,
    )
    grad_oth = to_core(grad_send)
    down_half = halves_of(plus(down_keep, after(down_plane, residual_low)))
    down_x_send = low(pick(down_half, 1 - side))
    down_x_keep = pick(down_half, side)
    down_x = hop(down_x_send, 1)
    up_theirs = up_grad(
        after(scal, down_x_send), second, pre_grad, mixed_own, mixed_oth, residual_low, 0
    )
    up_got = to_core(up_theirs)
    up_mine = up_grad(
        after(scal, up_theirs),
        second,
        pre_grad,
        mixed_own,
        mixed_oth,
        residual_low,
        1,
    )
    up_half = halves_of(plus(up_got, up_mine))
    up_x_send = low(lax.dynamic_index_in_dim(up_half, 1 - side, 1, keepdims=False))
    up_x_keep = lax.dynamic_index_in_dim(up_half, side, 1, keepdims=False)
    up_x = hop(up_x_send, 1)

    def back(pair, *gate):
        return attend_back(
            after(scal, *gate),
            qkv,
            qfeat,
            kfeat,
            grad_oth,
            grad_own,
            (wide_oth, wide_own),
            (logs_oth, logs_own),
            frames_here,
            pair,
        )

    def project_fold(their, mine):
        got = to_core(their)
        return jnp.where(straight, got, mine), jnp.where(straight, mine, got)

    bit = (chip // 2) % 2

    def split(x):
        parts = halves_of(x)
        return low(pick(parts, 1 - bit)), pick(parts, bit)

    residual_got = turn(after(residual_grad, up_mine))
    oth_0, own_0 = back(0, up_x_send)
    got_0 = to_core(oth_0)
    down_send, down_keep = split(plus(down_x_keep, after(down_x, oth_0)))
    down_z = hop(down_send, hops[0])
    up_y = plus(up_x_keep, after(up_x, oth_0))
    up_y_send = low(up_y[0])
    up_y_got = to_plane(up_y_send)

    residual_got = after(residual_got, oth_0)
    oth_1, own_1 = back(1, down_send, up_y_send, residual_got)
    got_1 = to_core(oth_1)
    down_sum = plus(down_keep, after(down_z, oth_1))
    down_low = low(down_sum)
    down_z = hop(down_low, hops[1])
    up_send, up_keep = split(plus(up_y[1], after(up_y_got, oth_1)))
    up_z = hop(up_send, hops[0])
    their_0, mine_0, offsets_0 = project_grad(
        after(scal, down_low, up_send), first, (oth_0, oth_1), (own_0, own_1)
    )
    early_send, early_keep = project_fold(their_0, mine_0)
    early_got = to_plane(early_send)
    up_sum = plus(up_keep, after(up_z, mine_0))
    up_low = low(up_sum)
    up_z = hop(up_low, hops[1])

    oth_2, own_2 = back(2, early_send, up_low)
    got_2 = to_core(oth_2)

    def rest(total, got, steps):
        total = plus(total, got)
        for step in steps:
            total = plus(total, hop(low(total), step))
        return low(total)

    down_sum = rest(down_sum, after(down_z, oth_2), hops[2:])
    down_z = hop(down_sum, hops[0])
    up_sum = rest(up_sum, after(up_z, oth_2), hops[2:])
    up_z = hop(up_sum, hops[0])
    early_half = halves_of(plus(early_keep, after(early_got, oth_2)))
    early_send = low(pick(early_half, 1 - side))
    early_keep = pick(early_half, side)
    early_x = hop(early_send, 1)
    their_2, mine_2, offsets_2 = project_grad(
        after(scal, down_sum, up_sum, early_send), first, (oth_2,), (own_2,)
    )
    late_send, late_keep = project_fold(their_2, mine_2)
    late_got = to_plane(late_send)
    down_sum = join(down_sum, after(down_z, mine_2), bit, 0)
    down_x = hop(down_sum, 1)
    up_sum = join(up_sum, after(up_z, mine_2), bit, 0)
    up_x = hop(up_sum, 1)
    early_sum = plus(early_keep, after(early_x, mine_2))
    early_low = low(early_sum)
    early_z = hop(early_low, hops[0])
    first_low, first_sums = first_grad(
        (own_0, own_1, own_2),
        (got_0, got_1, got_2),
        weight_here,
        weight_there,
        after(own, late_send, down_sum, up_sum, early_low),
    )
    first_got = turn(first_low)
    table = small_table(
        scal,
        frames_here,
        sums_ahead,
        sums_behind,
        first_sums,
        learner_sums,
        learner_offset_sums,
        up_sums,
        offsets_0,
        offsets_2,
    )
    table = table + to_core(table)
    table = table + to_plane(table)
    for step in [1, *hops]:
        table = table + hop(table, step)

    def around(x):
        return join(x, hop(x, 1), side, 0)

    late_half = halves_of(plus(late_keep, after(late_got, first_low)))
    late_x_send = low(pick(late_half, 1 - side))
    late_sum = around(rest(pick(late_half, side), hop(late_x_send, 1), hops))
    early_sum = around(rest(early_sum, after(early_z, first_low), hops[1:]))
    up_sum = join(up_sum, after(up_x, first_low), side, 0)
    down_sum = join(down_sum, after(down_x, first_low), side, 0)

    tokens_gradient = last(
        scal, packed, first_low, first_got, residual_grad, residual_got, norm_gains[0:1], tokens_here
    )

    def two(x):
        other = to_core(x)
        return jnp.where(core == 0, x, other), jnp.where(core == 0, other, x)

    def out_block(x):
        return jnp.concatenate([x[width:, : width // 2], x[width:, width // 2 :]], axis=0)

    down_first, down_second = two(down_sum)
    up_first, up_second = two(up_sum)
    contract_gradient = jnp.concatenate([down_first, down_second], axis=0).astype(F32)
    expand_gradient = jnp.concatenate([up_first[:width], up_second[:width]], axis=1).astype(F32)
    output_gradient = jnp.concatenate([out_block(up_first), out_block(up_second)], axis=1).astype(F32)

    attend_gradient = jnp.concatenate(
        [jnp.concatenate(two(early_sum), axis=0), jnp.concatenate(two(late_sum), axis=0)], axis=1
    )
    attend_gradient = (
        attend_gradient.reshape(width, pairs, 3, 128).transpose(0, 2, 1, 3).astype(F32)
    )
    return (
        jnp.where(straight, pooled[:maps_all], residual_got[half_rows - maps_all :]).reshape(
            frames_here, MAPS, width
        ),
        tokens_gradient,
        table[0:3],
        table[3:6],
        attend_gradient.reshape(width, 3, share),
        lax.dynamic_slice_in_dim(table[21:23], plane * share, share, 1),
        output_gradient,
        table[6],
        expand_gradient,
        lax.dynamic_slice_in_dim(table[17:21], 2 * plane, 2, 0).reshape(2 * hid),
        contract_gradient,
        table[7],
        table[8:16].T,
        table[16, :MAPS],
    )


def solution(mesh):
    groups, sides = mesh.devices.shape
    fine = Mesh(mesh.devices.reshape(groups // 2, 2, sides), ("chip", "core", "mp"))
    dp = ("chip", "core")
    every = ("chip", "core", "mp")
    return jax.shard_map(
        body,
        mesh=fine,
        in_specs=(
            P(every, None),
            P(dp, None),
            P(),
            P(),
            P(None, None, "mp"),
            P(None, "mp"),
            P("mp", None),
            P(),
            P(None, "mp"),
            P("mp"),
            P("mp", None),
            P(),
            P(),
            P(),
            P(every, None, None),
        ),
        out_specs=(
            P(every, None, None),
            P(every, None),
            P(),
            P(),
            P(None, None, "mp"),
            P(None, "mp"),
            P("mp", None),
            P(),
            P(None, "mp"),
            P("mp"),
            P("mp", None),
            P(),
            P(),
            P(),
        ),
        check_vma=False,
    )
```

profile of v0, /device:TPU:0, one launch (start us, length us, event | category | flops | bytes accessed | tf_op | source)
XLA Modules:
  0.0 511.8 jit_solution(13001972510370339985)
XLA Ops:
  0.7 2.6 copy.32
  7.3 2.7 copy.35
  13.4 6.5 %collective-permute-start.6 = (f32[1536]{0:T(1024)S(1)}, f32[1536]{0:T(1024)S(1)}, u32[]{:S(2)}, u32[]{:S(2)}) collective-permute-start(f32[1536]{0:T(1024)S(1)} %copy-done.40), channel_id=1, source_target_pairs={{0,1},{1,0},{2,3},{3,2},{4,5},{5,4},{6,7},{7,6},{8,9},{9,8},{10,11... | collective-permute-start | bytes 18440 | tf_op jit(solution)/shard_map/ppermute | solution.py:998
  30.0 14.9 %collective-permute-start.2 = (bf16[1064,768]{1,0:T(8,128)(2,1)}, bf16[1064,768]{1,0:T(8,128)(2,1)}, u32[]{:S(2)}, u32[]{:S(2)}) collective-permute-start(bf16[1064,768]{1,0:T(8,128)(2,1)} %broadcast_select_fusion.own.tokens.refs_8_), channel_id=1, source_target_pairs={{0,2},{2,0},{1,3},{3,1},{4,6},{6,4},{5,7},{7,5},{8,10},{10,8},{9,1... | collective-permute-start | bytes 4902920 | tf_op jit(solution)/shard_map/ppermute | solution.py:995
  50.6 8.4 %collective-permute-start.7 = (bf16[1728,768]{1,0:T(8,128)(2,1)}, bf16[1728,768]{1,0:T(8,128)(2,1)}, u32[]{:S(2)}, u32[]{:S(2)}) collective-permute-start(bf16[1728,768]{1,0:T(8,128)(2,1)} %pad_maximum_fusion), channel_id=1, source_target_pairs={{0,1},{1,0},{2,3},{3,2},{4,5},{5,4},{6,7},{7,6},{8,9},{9,8},{10,11... | collective-permute-start | bytes 7962632 | tf_op jit(solution)/shard_map/ppermute | solution.py:998
  59.0 11.5 %project.1 = (bf16[2048,768]{1,0:T(8,128)(2,1)}, bf16[2048,1152]{1,0:T(8,128)(2,1)}, bf16[2048,128]{1,0:T(8,128)(2,1)}, bf16[2048,128]{1,0:T(8,128)(2,1)}) custom-call(s32[3]{0:T(128)} %pad_add_fusion.scal, bf16[1064,768]{1,0:T(8,128)(2,1)} %collective-permute-done.2.oth, bf16[1064,768]{1,0:T(8,128)(2,1)} %broadcast_select_fusion.own.tokens.refs_8_, ...), custom_call_target="tpu_custom_call" | custom-call | flops 72477573120 | bytes 220200960 | tf_op jit(solution)/shard_map/project/pallas_call | solution.py:144
  70.6 22.6 %attend.2 = (bf16[1024,384]{1,0:T(8,128)(2,1)}, f32[1024,384]{1,0:T(8,128)}, f32[3,4,8,256]{3,2,1,0:T(8,128)}) custom-call(s32[3]{0:T(128)} %pad_add_fusion.scal, bf16[2048,1152]{1,0:T(8,128)(2,1)} %get-tuple-element.90.q.qkv.k.v, bf16[2048,128]{1,0:T(8,128)(2,1)} %get-tuple-element.91.qfeat, bf16[2048,1152]{1,0:T(8,128)(2,1)} %get-tuple-element.90.q.qkv.k.v, ...), custom_call_target="tpu_custom_call" | custom-call | flops 257698037760 | bytes 251658240 | tf_op jit(solution)/shard_map/attend/pallas_call | solution.py:289
  93.2 27.1 %attend.3 = (bf16[1024,384]{1,0:T(8,128)(2,1)}, f32[1024,384]{1,0:T(8,128)}, f32[3,4,8,256]{3,2,1,0:T(8,128)}) custom-call(s32[3]{0:T(128)} %pad_add_fusion.scal, bf16[2048,1152]{1,0:T(8,128)(2,1)} %get-tuple-element.90.q.qkv.k.v, bf16[2048,128]{1,0:T(8,128)(2,1)} %get-tuple-element.91.qfeat, bf16[2048,1152]{1,0:T(8,128)(2,1)} %get-tuple-element.90.q.qkv.k.v, ...), custom_call_target="tpu_custom_call" | custom-call | flops 257698037760 | bytes 251658240 | tf_op jit(solution)/shard_map/attend/pallas_call | solution.py:289
  129.1 32.1 %ahead.1 = (f32[1024,768]{1,0:T(8,128)}, f32[1024,768]{1,0:T(8,128)}, f32[1024,128]{1,0:T(8,128)}, bf16[1024,3072]{1,0:T(8,128)(2,1)}, f32[1024,3072]{1,0:T(8,12...) custom-call(s32[3]{0:T(128)} %pad_add_fusion.scal, ...), custom_call_target="tpu_custom_call" | custom-call | flops 217432719360 | bytes 797665280 | tf_op jit(solution)/shard_map/ahead/pallas_call | solution.py:526
  161.2 5.8 %down_grad.2 = bf16[2,768,768]{2,1,0:T(8,128)(2,1)} custom-call(bf16[1024,3072]{1,0:T(8,128)(2,1)} %get-tuple-element.99.hidden, bf16[1024,768]{1,0:T(8,128)(2,1)} %get-tuple-element.101.out_low), custom_call_target="tpu_custom_call" | custom-call | flops 48318382080 | bytes 125829120 | tf_op jit(solution)/shard_map/down_grad/pallas_call | solution.py:592
  167.2 5.8 %down_grad.3 = bf16[2,768,768]{2,1,0:T(8,128)(2,1)} custom-call(bf16[1024,3072]{1,0:T(8,128)(2,1)} %get-tuple-element.99.hidden, bf16[1024,768]{1,0:T(8,128)(2,1)} %get-tuple-element.101.out_low), custom_call_target="tpu_custom_call" | custom-call | flops 48318382080 | bytes 125829120 | tf_op jit(solution)/shard_map/down_grad/pallas_call | solution.py:592
  173.0 3.4 fusion.2
  176.4 24.0 %behind.1 = (f32[1024,768]{1,0:T(8,128)}, bf16[1024,384]{1,0:T(8,128)(2,1)}, bf16[1024,384]{1,0:T(8,128)(2,1)}, bf16[1024,3072]{1,0:T(8,128)(2,1)}, bf16[1024,76...) custom-call(s32[3]{0:T(128)} %pad_add_fusion.scal, f32[1024,768]{1,0:T(8,128)} %get-tuple-element.103.out_grad, ...), custom_call_target="tpu_custom_call" | custom-call | flops 217432719360 | bytes 472043520 | tf_op jit(solution)/shard_map/behind/pallas_call | solution.py:526
  200.8 4.2 collective-permute-done.10
  204.9 2.0 bitcast_add_fusion.1
  209.3 19.2 %up_grad.2 = bf16[2,960,768]{2,1,0:T(8,128)(2,1)} custom-call(s32[3]{0:T(128)} %pad_add_fusion.scal, bf16[1024,768]{1,0:T(8,128)(2,1)} %get-tuple-element.111.second, bf16[1024,3072]{1,0:T(8,128)(2,1)} %get-tuple-element.112.pre_grad, bf16[1024,384]{1,0:T(8,128)(2,1)} %get-tuple-element.95.mixed_own, bf16[1024,384]{1,0:T(8,128)(2,1)} %copy-done.48, ...), custom_call_target="tpu_custom_call" | custom-call | flops 60397977600 | bytes 157286400 | tf_op jit(solution)/shard_map/up_grad/pallas_call | solution.py:626
  228.6 3.7 collective-permute-start.14
  232.3 8.3 %up_grad.3 = bf16[2,960,768]{2,1,0:T(8,128)(2,1)} custom-call(s32[3]{0:T(128)} %pad_add_fusion.scal, bf16[1024,768]{1,0:T(8,128)(2,1)} %get-tuple-element.111.second, bf16[1024,3072]{1,0:T(8,128)(2,1)} %get-tuple-element.112.pre_grad, bf16[1024,384]{1,0:T(8,128)(2,1)} %get-tuple-element.95.mixed_own, bf16[1024,384]{1,0:T(8,128)(2,1)} %copy-done.48, ...), custom_call_target="tpu_custom_call" | custom-call | flops 60397977600 | bytes 157286400 | tf_op jit(solution)/shard_map/up_grad/pallas_call | solution.py:626
  240.6 2.4 collective-permute-start.11
  243.0 2.5 convert_add_fusion
  245.5 2.5 copy-done.14
  250.1 29.0 %attend_back.3 = (bf16[1024,384]{1,0:T(8,128)(2,1)}, bf16[1024,384]{1,0:T(8,128)(2,1)}) custom-call(s32[3]{0:T(128)} %pad_add_fusion.scal, bf16[2048,1152]{1,0:T(8,128)(2,1)} %get-tuple-element.90.q.qkv.k.v, bf16[2048,1152]{1,0:T(8,128)(2,1)} %get-tuple-element.90.q.qkv.k.v, bf16[2048,128]{1,0:T(8,128)(2,1)} %get-tuple-element.92.kfeat, ...), custom_call_target="tpu_custom_call" | custom-call | flops 429496729600 | bytes 157286400 | tf_op jit(solution)/shard_map/attend_back/pallas_call | solution.py:754
  281.5 2.1 collective-permute-done.15
  283.6 2.6 bitcast_add_fusion
  288.7 2.4 collective-permute-start.17
  291.2 29.0 %attend_back.4 = (bf16[1024,384]{1,0:T(8,128)(2,1)}, bf16[1024,384]{1,0:T(8,128)(2,1)}) custom-call(s32[3]{0:T(128)} %pad_add_fusion.scal, bf16[2048,1152]{1,0:T(8,128)(2,1)} %get-tuple-element.90.q.qkv.k.v, bf16[2048,1152]{1,0:T(8,128)(2,1)} %get-tuple-element.90.q.qkv.k.v, bf16[2048,128]{1,0:T(8,128)(2,1)} %get-tuple-element.92.kfeat, ...), custom_call_target="tpu_custom_call" | custom-call | flops 429496729600 | bytes 157286400 | tf_op jit(solution)/shard_map/attend_back/pallas_call | solution.py:754
  323.8 7.5 %project_grad.2 = (bf16[384,768]{1,0:T(8,128)(2,1)}, bf16[384,768]{1,0:T(8,128)(2,1)}, f32[8,768]{1,0:T(8,128)}) custom-call(s32[3]{0:T(128)} %pad_add_fusion.scal, bf16[2048,768]{1,0:T(8,128)(2,1)} %get-tuple-element.133.first, bf16[1024,384]{1,0:T(8,128)(2,1)} %get-tuple-element.122.refs_0_, bf16[1024,384]{1,0:T(8,128)(2,1)} %get-tuple-element.129.refs_1_, ...), custom_call_target="tpu_custom_call" | custom-call | flops 48318382080 | bytes 125829120 | tf_op jit(solution)/shard_map/project_grad/pallas_call | solution.py:812
  331.9 3.9 collective-permute-start.24
  339.4 29.0 %attend_back.5 = (bf16[1024,384]{1,0:T(8,128)(2,1)}, bf16[1024,384]{1,0:T(8,128)(2,1)}) custom-call(s32[3]{0:T(128)} %pad_add_fusion.scal, bf16[2048,1152]{1,0:T(8,128)(2,1)} %get-tuple-element.90.q.qkv.k.v, bf16[2048,1152]{1,0:T(8,128)(2,1)} %get-tuple-element.90.q.qkv.k.v, bf16[2048,128]{1,0:T(8,128)(2,1)} %get-tuple-element.92.kfeat, ...), custom_call_target="tpu_custom_call" | custom-call | flops 429496729600 | bytes 157286400 | tf_op jit(solution)/shard_map/attend_back/pallas_call | solution.py:754
  371.2 2.1 collective-permute-start.29
  375.5 5.9 %project_grad.3 = (bf16[384,384]{1,0:T(8,128)(2,1)}, bf16[384,384]{1,0:T(8,128)(2,1)}, f32[8,384]{1,0:T(8,128)}) custom-call(s32[3]{0:T(128)} %pad_add_fusion.scal, bf16[2048,768]{1,0:T(8,128)(2,1)} %get-tuple-element.133.first, bf16[1024,384]{1,0:T(8,128)(2,1)} %get-tuple-element.139.refs_0_, bf16[1024,384]{1,0:T(8,128)(2,1)} %get-tuple-element.138.refs_1_.refs_2_), custom_call_target="tpu_custom_call" | custom-call | flops 24159191040 | bytes 94371840 | tf_op jit(solution)/shard_map/project_grad/pallas_call | solution.py:812
  383.9 3.2 collective-permute-done.29
  388.9 3.6 collective-permute-done.30
  398.8 9.7 %first_grad.1 = (bf16[1024,768]{1,0:T(8,128)(2,1)}, f32[16,768]{1,0:T(8,128)}) custom-call(bf16[1024,384]{1,0:T(8,128)(2,1)} %get-tuple-element.124.refs_2_.refs_0_, bf16[1024,384]{1,0:T(8,128)(2,1)} %get-tuple-element.128.refs_3_.refs_1_, bf16[1024,384]{1,0:T(8,128)(2,1)} %get-tuple-element.138.refs_1_.refs_2_, ...), custom_call_target="tpu_custom_call" | custom-call | flops 72477573120 | bytes 165150720 | tf_op jit(solution)/shard_map/first_grad/pallas_call | solution.py:854
  411.7 4.0 collective-permute-done.33
  426.4 3.5 collective-permute-done.37
  434.0 1.9 collective-permute-start.36
  436.0 19.2 %collective-permute-done.36 = f32[24,768]{1,0:T(8,128)} collective-permute-done((f32[24,768]{1,0:T(8,128)S(1)}, f32[24,768]{1,0:T(8,128)}, u32[]{:S(2)}, u32[]{:S(2)}) %collective-permute-start.36) | collective-permute-done | bytes 73760 | tf_op jit(solution)/shard_map/ppermute | solution.py:1007
  459.1 2.6 collective-permute-done.42
  462.5 5.0 collective-permute-done.43
  473.0 5.2 %collective-permute-done.44 = bf16[192,384]{0,1:T(8,128)(2,1)} collective-permute-done((bf16[192,384]{0,1:T(8,128)(2,1)}, bf16[192,384]{0,1:T(8,128)(2,1)}, u32[]{:S(2)}, u32[]{:S(2)}) %collective-permute-start.44) | collective-permute-done | bytes 147488 | tf_op jit(solution)/shard_map/ppermute | solution.py:1007
  480.9 4.2 collective-permute-done.45
  489.9 2.9 copy.42
  492.9 2.0 broadcast_select_fusion.4
  494.9 2.5 maximum_convert_fusion.1
  497.5 7.8 %last.1 = f32[980,768]{1,0:T(8,128)} custom-call(s32[3]{0:T(128)} %pad_add_fusion.scal, bf16[1064,768]{1,0:T(8,128)(2,1)} %copy-done.2, bf16[1024,768]{1,0:T(8,128)(2,1)} %get-tuple-element.151.grad, bf16[1024,768]{1,0:T(8,128)(2,1)} %collective-permute-done.31.grad_got, f32[1024,768]{1,0:T(8,128)} %get-tuple-element.114.residual, ...), custom_call_target="tpu_custom_call" | custom-call | flops 314572800 | bytes 188743680 | tf_op jit(solution)/shard_map/last/pallas_call | solution.py:885
  505.2 2.0 broadcast_select_fusion.2
  507.5 2.8 maximum_convert_fusion
  (281 shorter events, 101.0 us)
Async XLA Ops:
  5.4 23.2 %collective-permute-start.1 = (bf16[1064,768]{1,0:T(8,128)(2,1)S(1)}, bf16[1064,768]{1,0:T(8,128)(2,1)}, u32[]{:S(2)}, u32[]{:S(2)}) collective-permute-start(bf16[1064,768]{1,0:T(8,128)(2,1)S(1)} %pack.1.tokens), channel_id=1, source_target_pairs={{1,2},{2,1},{5,6},{6,5},{9,10},{10,9},{13,14},{14,13},{17,18},{18,... | collective-permute-start | bytes 4902920 | tf_op jit(solution)/shard_map/ppermute | solution.py:992
  11.1 15.9 %collective-permute-start.3 = (bf16[384,1152]{1,0:T(8,128)(2,1)}, bf16[384,1152]{1,0:T(8,128)(2,1)}, u32[]{:S(2)}, u32[]{:S(2)}) collective-permute-start(bf16[384,1152]{1,0:T(8,128)(2,1)} %constant_dynamic-slice_fusion.9), channel_id=1, source_target_pairs={{1,2},{2,1},{5,6},{6,5},{9,10},{10,9},{13,14},{14,13},{17,18},{18,... | collective-permute-start | bytes 2654216 | tf_op jit(solution)/shard_map/ppermute | solution.py:992
  12.7 14.3 %collective-permute-start = (f32[2,512]{1,0:T(2,128)S(1)}, f32[2,512]{1,0:T(2,128)S(1)}, u32[]{:S(2)}, u32[]{:S(2)}) collective-permute-start(f32[2,512]{1,0:T(2,128)S(1)} %concatenate.63), channel_id=1, source_target_pairs={{1,2},{2,1},{5,6},{6,5},{9,10},{10,9},{13,14},{14,13},{17,18},{18,... | collective-permute-start | bytes 12296 | tf_op jit(solution)/shard_map/ppermute | solution.py:992
  13.4 37.2 %collective-permute-start.6 = (f32[1536]{0:T(1024)S(1)}, f32[1536]{0:T(1024)S(1)}, u32[]{:S(2)}, u32[]{:S(2)}) collective-permute-start(f32[1536]{0:T(1024)S(1)} %copy-done.40), channel_id=1, source_target_pairs={{0,1},{1,0},{2,3},{3,2},{4,5},{5,4},{6,7},{7,6},{8,9},{9,8},{10,11... | collective-permute-start | bytes 18440 | tf_op jit(solution)/shard_map/ppermute | solution.py:998
  27.0 20.3 %collective-permute-start.4 = (bf16[384,1152]{1,0:T(8,128)(2,1)}, bf16[384,1152]{1,0:T(8,128)(2,1)}, u32[]{:S(2)}, u32[]{:S(2)}) collective-permute-start(bf16[384,1152]{1,0:T(8,128)(2,1)} %collective-permute-done.3), channel_id=1, source_target_pairs={{1,5},{2,6},{5,1},{6,2},{9,13},{10,14},{13,9},{14,10},{17,21},{18,... | collective-permute-start | bytes 2654216 | tf_op jit(solution)/shard_map/ppermute | solution.py:1044
  30.0 29.0 %collective-permute-start.2 = (bf16[1064,768]{1,0:T(8,128)(2,1)}, bf16[1064,768]{1,0:T(8,128)(2,1)}, u32[]{:S(2)}, u32[]{:S(2)}) collective-permute-start(bf16[1064,768]{1,0:T(8,128)(2,1)} %broadcast_select_fusion.own.tokens.refs_8_), channel_id=1, source_target_pairs={{0,2},{2,0},{1,3},{3,1},{4,6},{6,4},{5,7},{7,5},{8,10},{10,8},{9,1... | collective-permute-start | bytes 4902920 | tf_op jit(solution)/shard_map/ppermute | solution.py:995
  50.6 69.8 %collective-permute-start.7 = (bf16[1728,768]{1,0:T(8,128)(2,1)}, bf16[1728,768]{1,0:T(8,128)(2,1)}, u32[]{:S(2)}, u32[]{:S(2)}) collective-permute-start(bf16[1728,768]{1,0:T(8,128)(2,1)} %pad_maximum_fusion), channel_id=1, source_target_pairs={{0,1},{1,0},{2,3},{3,2},{4,5},{5,4},{6,7},{7,6},{8,9},{9,8},{10,11... | collective-permute-start | bytes 7962632 | tf_op jit(solution)/shard_map/ppermute | solution.py:998
  120.4 6.4 %collective-permute-start.8 = (bf16[1728,768]{1,0:T(8,128)(2,1)}, bf16[1728,768]{1,0:T(8,128)(2,1)S(1)}, u32[]{:S(2)}, u32[]{:S(2)}) collective-permute-start(bf16[1728,768]{1,0:T(8,128)(2,1)} %collective-permute-done.7.got_a), channel_id=1, source_target_pairs={{0,2},{2,0},{1,3},{3,1},{4,6},{6,4},{5,7},{7,5},{8,10},{10,8},{9,1... | collective-permute-start | bytes 7962632 | tf_op jit(solution)/shard_map/ppermute | solution.py:995
  120.4 6.3 %collective-permute-start.5 = (bf16[1024,384]{1,0:T(8,128)(2,1)}, bf16[1024,384]{1,0:T(8,128)(2,1)S(1)}, u32[]{:S(2)}, u32[]{:S(2)}) collective-permute-start(bf16[1024,384]{1,0:T(8,128)(2,1)} %get-tuple-element.93), channel_id=1, source_target_pairs={{0,2},{2,0},{1,3},{3,1},{4,6},{6,4},{5,7},{7,5},{8,10},{10,8},{9,1... | collective-permute-start | bytes 2359304 | tf_op jit(solution)/shard_map/ppermute | solution.py:995
  167.0 5.9 %collective-permute-start.9 = (bf16[2,768,768]{2,1,0:T(8,128)(2,1)}, bf16[2,768,768]{2,1,0:T(8,128)(2,1)S(1)}, u32[]{:S(2)}, u32[]{:S(2)}) collective-permute-start(bf16[2,768,768]{2,1,0:T(8,128)(2,1)} %down_grad.2), channel_id=1, source_target_pairs={{0,2},{2,0},{1,3},{3,1},{4,6},{6,4},{5,7},{7,5},{8,10},{10,8},{9,1... | collective-permute-start | bytes 7077896 | tf_op jit(solution)/shard_map/ppermute | solution.py:995
  176.4 28.6 %collective-permute-start.10 = (bf16[768,768]{1,0:T(8,128)(2,1)}, bf16[768,768]{1,0:T(8,128)(2,1)}, u32[]{:S(2)}, u32[]{:S(2)}) collective-permute-start(bf16[768,768]{1,0:T(8,128)(2,1)} %fusion.2), channel_id=1, source_target_pairs={{0,1},{1,0},{2,3},{3,2},{4,5},{5,4},{6,7},{7,6},{8,9},{9,8},{10,11... | collective-permute-start | bytes 3538952 | tf_op jit(solution)/shard_map/ppermute | solution.py:998
  200.4 48.9 %collective-permute-start.13 = (bf16[1024,384]{1,0:T(8,128)(2,1)}, bf16[1024,384]{1,0:T(8,128)(2,1)S(1)}, u32[]{:S(2)}, u32[]{:S(2)}) collective-permute-start(bf16[1024,384]{1,0:T(8,128)(2,1)} %get-tuple-element.116), channel_id=1, source_target_pairs={{0,2},{2,0},{1,3},{3,1},{4,6},{6,4},{5,7},{7,5},{8,10},{10,8},{9,1... | collective-permute-start | bytes 2359304 | tf_op jit(solution)/shard_map/ppermute | solution.py:995
  228.6 14.5 %collective-permute-start.12 = (bf16[2,960,768]{2,1,0:T(8,128)(2,1)}, bf16[2,960,768]{2,1,0:T(8,128)(2,1)S(1)}, u32[]{:S(2)}, u32[]{:S(2)}) collective-permute-start(bf16[2,960,768]{2,1,0:T(8,128)(2,1)} %up_grad.2), channel_id=1, source_target_pairs={{0,2},{2,0},{1,3},{3,1},{4,6},{6,4},{5,7},{7,5},{8,10},{10,8},{9,1... | collective-permute-start | bytes 8847368 | tf_op jit(solution)/shard_map/ppermute | solution.py:995
  228.6 50.6 %collective-permute-start.14 = (bf16[384,768]{1,0:T(8,128)(2,1)}, bf16[384,768]{1,0:T(8,128)(2,1)}, u32[]{:S(2)}, u32[]{:S(2)}) collective-permute-start(bf16[384,768]{1,0:T(8,128)(2,1)} %fusion.4), channel_id=1, source_target_pairs={{0,4},{4,0},{8,12},{12,8},{16,20},{20,16},{24,28},{28,24},{1,5},{5... | collective-permute-start | bytes 1769480 | tf_op jit(solution)/shard_map/ppermute | solution.py:1007
  240.6 40.6 %collective-permute-start.11 = (f32[1024,768]{1,0:T(8,128)}, f32[1024,768]{1,0:T(8,128)}, u32[]{:S(2)}, u32[]{:S(2)}) collective-permute-start(f32[1024,768]{1,0:T(8,128)} %get-tuple-element.114.residual), channel_id=1, source_target_pairs={{1,2},{2,1},{5,6},{6,5},{9,10},{10,9},{13,14},{14,13},{17,18},{18,... | collective-permute-start | bytes 9437192 | tf_op jit(solution)/shard_map/ppermute | solution.py:992
  249.2 34.4 %collective-permute-start.15 = (bf16[2,480,768]{2,1,0:T(8,128)(2,1)}, bf16[2,480,768]{2,1,0:T(8,128)(2,1)}, u32[]{:S(2)}, u32[]{:S(2)}) collective-permute-start(bf16[2,480,768]{2,1,0:T(8,128)(2,1)} %fusion), channel_id=1, source_target_pairs={{0,4},{4,0},{8,12},{12,8},{16,20},{20,16},{24,28},{28,24},{1,5},{5... | collective-permute-start | bytes 4423688 | tf_op jit(solution)/shard_map/ppermute | solution.py:1007
  281.2 38.9 %collective-permute-start.16 = (bf16[192,768]{1,0:T(8,128)(2,1)}, bf16[192,768]{1,0:T(8,128)(2,1)}, u32[]{:S(2)}, u32[]{:S(2)}) collective-permute-start(bf16[192,768]{1,0:T(8,128)(2,1)} %fusion.10), channel_id=1, source_target_pairs={{0,8},{4,12},{8,0},{12,4},{16,24},{20,28},{24,16},{28,20},{1,9},{5... | collective-permute-start | bytes 884744 | tf_op jit(solution)/shard_map/ppermute | solution.py:1007
  288.7 33.2 %collective-permute-start.17 = (bf16[480,768]{1,0:T(8,128)(2,1)}, bf16[480,768]{1,0:T(8,128)(2,1)}, u32[]{:S(2)}, u32[]{:S(2)}) collective-permute-start(bf16[480,768]{1,0:T(8,128)(2,1)} %fusion.3), channel_id=1, source_target_pairs={{0,1},{1,0},{2,3},{3,2},{4,5},{5,4},{6,7},{7,6},{8,9},{9,8},{10,11... | collective-permute-start | bytes 2211848 | tf_op jit(solution)/shard_map/ppermute | solution.py:998
  323.7 12.1 %collective-permute-start.19 = (bf16[240,768]{1,0:T(8,128)(2,1)S(1)}, bf16[240,768]{1,0:T(8,128)(2,1)S(1)}, u32[]{:S(2)}, u32[]{:S(2)}) collective-permute-start(bf16[240,768]{1,0:T(8,128)(2,1)S(1)} %fusion.8), channel_id=1, source_target_pairs={{0,8},{4,12},{8,0},{12,4},{16,24},{20,28},{24,16},{28,20},{1,9},{5... | collective-permute-start | bytes 1105928 | tf_op jit(solution)/shard_map/ppermute | solution.py:1007
  331.3 5.4 %collective-permute-start.18 = (bf16[384,768]{1,0:T(8,128)(2,1)}, bf16[384,768]{1,0:T(8,128)(2,1)S(1)}, u32[]{:S(2)}, u32[]{:S(2)}) collective-permute-start(bf16[384,768]{1,0:T(8,128)(2,1)} %get-tuple-element.134), channel_id=1, source_target_pairs={{0,2},{2,0},{1,3},{3,1},{4,6},{6,4},{5,7},{7,5},{8,10},{10,8},{9,1... | collective-permute-start | bytes 1769480 | tf_op jit(solution)/shard_map/ppermute | solution.py:995
  331.3 67.4 %collective-permute-start.23 = (bf16[768,1152]{1,0:T(8,128)(2,1)}, bf16[768,1152]{1,0:T(8,128)(2,1)}, u32[]{:S(2)}, u32[]{:S(2)}) collective-permute-start(bf16[768,1152]{1,0:T(8,128)(2,1)} %maximum_select_fusion.weight.refs_6_), channel_id=1, source_target_pairs={{0,2},{2,0},{1,3},{3,1},{4,6},{6,4},{5,7},{7,5},{8,10},{10,8},{9,1... | collective-permute-start | bytes 5308424 | tf_op jit(solution)/shard_map/ppermute | solution.py:995
  331.8 66.9 %collective-permute-start.20 = (bf16[1024,384]{1,0:T(8,128)(2,1)}, bf16[1024,384]{1,0:T(8,128)(2,1)}, u32[]{:S(2)}, u32[]{:S(2)}) collective-permute-start(bf16[1024,384]{1,0:T(8,128)(2,1)} %get-tuple-element.122.refs_0_), channel_id=1, source_target_pairs={{0,2},{2,0},{1,3},{3,1},{4,6},{6,4},{5,7},{7,5},{8,10},{10,8},{9,1... | collective-permute-start | bytes 2359304 | tf_op jit(solution)/shard_map/ppermute | solution.py:995
  331.9 36.6 %collective-permute-start.24 = (bf16[192,768]{1,0:T(8,128)(2,1)}, bf16[192,768]{1,0:T(8,128)(2,1)}, u32[]{:S(2)}, u32[]{:S(2)}) collective-permute-start(bf16[192,768]{1,0:T(8,128)(2,1)} %fusion.7), channel_id=1, source_target_pairs={{0,16},{4,20},{8,24},{12,28},{16,0},{20,4},{24,8},{28,12},{1,17},{... | collective-permute-start | bytes 884744 | tf_op jit(solution)/shard_map/ppermute | solution.py:1007
  336.7 33.2 %collective-permute-start.25 = (bf16[240,768]{1,0:T(8,128)(2,1)}, bf16[240,768]{1,0:T(8,128)(2,1)}, u32[]{:S(2)}, u32[]{:S(2)}) collective-permute-start(bf16[240,768]{1,0:T(8,128)(2,1)} %fusion.6), channel_id=1, source_target_pairs={{0,16},{4,20},{8,24},{12,28},{16,0},{20,4},{24,8},{28,12},{1,17},{... | collective-permute-start | bytes 1105928 | tf_op jit(solution)/shard_map/ppermute | solution.py:1007
  337.7 33.5 %collective-permute-start.26 = (bf16[384,768]{1,0:T(8,128)(2,1)}, bf16[384,768]{1,0:T(8,128)(2,1)}, u32[]{:S(2)}, u32[]{:S(2)}) collective-permute-start(bf16[384,768]{1,0:T(8,128)(2,1)} %broadcast_select_fusion.13), channel_id=1, source_target_pairs={{0,1},{1,0},{2,3},{3,2},{4,5},{5,4},{6,7},{7,6},{8,9},{9,8},{10,11... | collective-permute-start | bytes 1769480 | tf_op jit(solution)/shard_map/ppermute | solution.py:998
  368.5 30.3 %collective-permute-start.21 = (bf16[1024,384]{1,0:T(8,128)(2,1)}, bf16[1024,384]{1,0:T(8,128)(2,1)}, u32[]{:S(2)}, u32[]{:S(2)}) collective-permute-start(bf16[1024,384]{1,0:T(8,128)(2,1)} %get-tuple-element.129.refs_1_), channel_id=1, source_target_pairs={{0,2},{2,0},{1,3},{3,1},{4,6},{6,4},{5,7},{7,5},{8,10},{10,8},{9,1... | collective-permute-start | bytes 2359304 | tf_op jit(solution)/shard_map/ppermute | solution.py:995
  369.9 11.6 %collective-permute-start.28 = (bf16[192,768]{1,0:T(8,128)(2,1)S(1)}, bf16[192,768]{1,0:T(8,128)(2,1)S(1)}, u32[]{:S(2)}, u32[]{:S(2)}) collective-permute-start(bf16[192,768]{1,0:T(8,128)(2,1)S(1)} %add_convert_fusion.3), channel_id=1, source_target_pairs={{0,8},{4,12},{8,0},{12,4},{16,24},{20,28},{24,16},{28,20},{1,9},{5... | collective-permute-start | bytes 884744 | tf_op jit(solution)/shard_map/ppermute | solution.py:1007
  371.2 15.9 %collective-permute-start.29 = (bf16[240,768]{1,0:T(8,128)(2,1)S(1)}, bf16[240,768]{1,0:T(8,128)(2,1)S(1)}, u32[]{:S(2)}, u32[]{:S(2)}) collective-permute-start(bf16[240,768]{1,0:T(8,128)(2,1)S(1)} %add_convert_fusion.2), channel_id=1, source_target_pairs={{0,8},{4,12},{8,0},{12,4},{16,24},{20,28},{24,16},{28,20},{1,9},{5... | collective-permute-start | bytes 1105928 | tf_op jit(solution)/shard_map/ppermute | solution.py:1007
  381.5 11.1 %collective-permute-start.30 = (bf16[192,768]{0,1:T(8,128)(2,1)}, bf16[192,768]{0,1:T(8,128)(2,1)S(1)}, u32[]{:S(2)}, u32[]{:S(2)}) collective-permute-start(bf16[192,768]{0,1:T(8,128)(2,1)} %bitcast.90), channel_id=1, source_target_pairs={{0,4},{4,0},{8,12},{12,8},{16,20},{20,16},{24,28},{28,24},{1,5},{5... | collective-permute-start | bytes 884744 | tf_op jit(solution)/shard_map/ppermute | solution.py:1007
  387.8 10.9 %collective-permute-start.22 = (bf16[1024,384]{1,0:T(8,128)(2,1)}, bf16[1024,384]{1,0:T(8,128)(2,1)}, u32[]{:S(2)}, u32[]{:S(2)}) collective-permute-start(bf16[1024,384]{1,0:T(8,128)(2,1)} %get-tuple-element.139.refs_0_), channel_id=1, source_target_pairs={{0,2},{2,0},{1,3},{3,1},{4,6},{6,4},{5,7},{7,5},{8,10},{10,8},{9,1... | collective-permute-start | bytes 2359304 | tf_op jit(solution)/shard_map/ppermute | solution.py:995
  394.6 28.9 %collective-permute-start.49 = (bf16[384,768]{1,0:T(8,128)(2,1)}, bf16[384,768]{1,0:T(8,128)(2,1)}, u32[]{:S(2)}, u32[]{:S(2)}) collective-permute-start(bf16[384,768]{1,0:T(8,128)(2,1)} %pad_maximum_fusion.4), channel_id=1, source_target_pairs={{0,4},{4,0},{8,12},{12,8},{16,20},{20,16},{24,28},{28,24},{1,5},{5... | collective-permute-start | bytes 1769480 | tf_op jit(solution)/shard_map/ppermute | solution.py:1007
  411.3 4.4 collective-permute-start.33
  415.7 6.0 %collective-permute-start.34 = (f32[24,768]{1,0:T(8,128)S(1)}, f32[24,768]{1,0:T(8,128)S(1)}, u32[]{:S(2)}, u32[]{:S(2)}) collective-permute-start(f32[24,768]{1,0:T(8,128)S(1)} %add.159), channel_id=1, source_target_pairs={{0,4},{4,0},{8,12},{12,8},{16,20},{20,16},{24,28},{28,24},{1,5},{5... | collective-permute-start | bytes 221192 | tf_op jit(solution)/shard_map/ppermute | solution.py:1007
  418.0 55.0 %collective-permute-start.47 = (bf16[480,768]{1,0:T(8,128)(2,1)}, bf16[480,768]{1,0:T(8,128)(2,1)}, u32[]{:S(2)}, u32[]{:S(2)}) collective-permute-start(bf16[480,768]{1,0:T(8,128)(2,1)} %pad_maximum_fusion.3), channel_id=1, source_target_pairs={{0,4},{4,0},{8,12},{12,8},{16,20},{20,16},{24,28},{28,24},{1,5},{5... | collective-permute-start | bytes 2211848 | tf_op jit(solution)/shard_map/ppermute | solution.py:1007
  419.4 10.5 %collective-permute-start.37 = (bf16[192,768]{0,1:T(8,128)(2,1)}, bf16[192,768]{0,1:T(8,128)(2,1)S(1)}, u32[]{:S(2)}, u32[]{:S(2)}) collective-permute-start(bf16[192,768]{0,1:T(8,128)(2,1)} %fusion.9), channel_id=1, source_target_pairs={{0,8},{4,12},{8,0},{12,4},{16,24},{20,28},{24,16},{28,20},{1,9},{5... | collective-permute-start | bytes 884744 | tf_op jit(solution)/shard_map/ppermute | solution.py:1007
  421.0 9.8 %collective-permute-start.41 = (bf16[384,384]{1,0:T(8,128)(2,1)}, bf16[384,384]{1,0:T(8,128)(2,1)S(1)}, u32[]{:S(2)}, u32[]{:S(2)}) collective-permute-start(bf16[384,384]{1,0:T(8,128)(2,1)} %broadcast_select_fusion.22), channel_id=1, source_target_pairs={{0,1},{1,0},{2,3},{3,2},{4,5},{5,4},{6,7},{7,6},{8,9},{9,8},{10,11... | collective-permute-start | bytes 884744 | tf_op jit(solution)/shard_map/ppermute | solution.py:998
  421.7 75.8 %collective-permute-start.31 = (bf16[1024,768]{1,0:T(8,128)(2,1)}, bf16[1024,768]{1,0:T(8,128)(2,1)}, u32[]{:S(2)}, u32[]{:S(2)}) collective-permute-start(bf16[1024,768]{1,0:T(8,128)(2,1)} %get-tuple-element.151.grad), channel_id=1, source_target_pairs={{1,2},{2,1},{5,6},{6,5},{9,10},{10,9},{13,14},{14,13},{17,18},{18,... | collective-permute-start | bytes 4718600 | tf_op jit(solution)/shard_map/ppermute | solution.py:992
  423.5 10.5 %collective-permute-start.35 = (f32[24,768]{1,0:T(8,128)S(1)}, f32[24,768]{1,0:T(8,128)S(1)}, u32[]{:S(2)}, u32[]{:S(2)}) collective-permute-start(f32[24,768]{1,0:T(8,128)S(1)} %add.160), channel_id=1, source_target_pairs={{0,8},{4,12},{8,0},{12,4},{16,24},{20,28},{24,16},{28,20},{1,9},{5... | collective-permute-start | bytes 221192 | tf_op jit(solution)/shard_map/ppermute | solution.py:1007
  429.9 63.0 %collective-permute-start.50 = (bf16[768,768]{1,0:T(8,128)(2,1)}, bf16[768,768]{1,0:T(8,128)(2,1)}, u32[]{:S(2)}, u32[]{:S(2)}) collective-permute-start(bf16[768,768]{1,0:T(8,128)(2,1)} %pad_maximum_fusion.2), channel_id=1, source_target_pairs={{0,2},{2,0},{1,3},{3,1},{4,6},{6,4},{5,7},{7,5},{8,10},{10,8},{9,1... | collective-permute-start | bytes 3538952 | tf_op jit(solution)/shard_map/ppermute | solution.py:995
  430.8 39.0 %collective-permute-start.38 = (bf16[192,768]{0,1:T(8,128)(2,1)}, bf16[192,768]{0,1:T(8,128)(2,1)}, u32[]{:S(2)}, u32[]{:S(2)}) collective-permute-start(bf16[192,768]{0,1:T(8,128)(2,1)} %fusion.5), channel_id=1, source_target_pairs={{0,16},{4,20},{8,24},{12,28},{16,0},{20,4},{24,8},{28,12},{1,17},{... | collective-permute-start | bytes 884744 | tf_op jit(solution)/shard_map/ppermute | solution.py:1007
  434.0 21.2 %collective-permute-start.36 = (f32[24,768]{1,0:T(8,128)S(1)}, f32[24,768]{1,0:T(8,128)}, u32[]{:S(2)}, u32[]{:S(2)}) collective-permute-start(f32[24,768]{1,0:T(8,128)S(1)} %add.161), channel_id=1, source_target_pairs={{0,16},{4,20},{8,24},{12,28},{16,0},{20,4},{24,8},{28,12},{1,17},{... | collective-permute-start | bytes 221192 | tf_op jit(solution)/shard_map/ppermute | solution.py:1007
  455.2 6.5 %collective-permute-start.42 = (bf16[192,384]{0,1:T(8,128)(2,1)S(1)}, bf16[192,384]{0,1:T(8,128)(2,1)S(1)}, u32[]{:S(2)}, u32[]{:S(2)}) collective-permute-start(bf16[192,384]{0,1:T(8,128)(2,1)S(1)} %bitcast.113), channel_id=1, source_target_pairs={{0,4},{4,0},{8,12},{12,8},{16,20},{20,16},{24,28},{28,24},{1,5},{5... | collective-permute-start | bytes 442376 | tf_op jit(solution)/shard_map/ppermute | solution.py:1007
  461.8 5.7 %collective-permute-start.43 = (bf16[192,384]{0,1:T(8,128)(2,1)S(1)}, bf16[192,384]{0,1:T(8,128)(2,1)S(1)}, u32[]{:S(2)}, u32[]{:S(2)}) collective-permute-start(bf16[192,384]{0,1:T(8,128)(2,1)S(1)} %fusion.12), channel_id=1, source_target_pairs={{0,8},{4,12},{8,0},{12,4},{16,24},{20,28},{24,16},{28,20},{1,9},{5... | collective-permute-start | bytes 442376 | tf_op jit(solution)/shard_map/ppermute | solution.py:1007
  468.2 9.9 %collective-permute-start.44 = (bf16[192,384]{0,1:T(8,128)(2,1)}, bf16[192,384]{0,1:T(8,128)(2,1)}, u32[]{:S(2)}, u32[]{:S(2)}) collective-permute-start(bf16[192,384]{0,1:T(8,128)(2,1)} %fusion.11), channel_id=1, source_target_pairs={{0,16},{4,20},{8,24},{12,28},{16,0},{20,4},{24,8},{28,12},{1,17},{... | collective-permute-start | bytes 442376 | tf_op jit(solution)/shard_map/ppermute | solution.py:1007
  471.0 9.5 %collective-permute-start.39 = (bf16[192,768]{0,1:T(8,128)(2,1)S(1)}, bf16[192,768]{0,1:T(8,128)(2,1)S(1)}, u32[]{:S(2)}, u32[]{:S(2)}) collective-permute-start(bf16[192,768]{0,1:T(8,128)(2,1)S(1)} %add_convert_fusion.1), channel_id=1, source_target_pairs={{0,4},{4,0},{8,12},{12,8},{16,20},{20,16},{24,28},{28,24},{1,5},{5... | collective-permute-start | bytes 884744 | tf_op jit(solution)/shard_map/ppermute | solution.py:1007
  479.2 5.9 %collective-permute-start.45 = (bf16[192,384]{0,1:T(8,128)(2,1)S(1)}, bf16[192,384]{0,1:T(8,128)(2,1)S(1)}, u32[]{:S(2)}, u32[]{:S(2)}) collective-permute-start(bf16[192,384]{0,1:T(8,128)(2,1)S(1)} %add_convert_fusion.4), channel_id=1, source_target_pairs={{0,4},{4,0},{8,12},{12,8},{16,20},{20,16},{24,28},{28,24},{1,5},{5... | collective-permute-start | bytes 442376 | tf_op jit(solution)/shard_map/ppermute | solution.py:1007
  480.8 8.0 %collective-permute-start.40 = (bf16[384,768]{0,1:T(8,128)(2,1)S(1)}, bf16[384,768]{0,1:T(8,128)(2,1)S(1)}, u32[]{:S(2)}, u32[]{:S(2)}) collective-permute-start(bf16[384,768]{0,1:T(8,128)(2,1)S(1)} %pad_maximum_fusion.5), channel_id=1, source_target_pairs={{0,2},{2,0},{1,3},{3,1},{4,6},{6,4},{5,7},{7,5},{8,10},{10,8},{9,1... | collective-permute-start | bytes 1769480 | tf_op jit(solution)/shard_map/ppermute | solution.py:995
  488.1 17.1 %collective-permute-start.48 = (bf16[960,768]{1,0:T(8,128)(2,1)}, bf16[960,768]{1,0:T(8,128)(2,1)}, u32[]{:S(2)}, u32[]{:S(2)}) collective-permute-start(bf16[960,768]{1,0:T(8,128)(2,1)} %pad_maximum_fusion.1), channel_id=1, source_target_pairs={{0,2},{2,0},{1,3},{3,1},{4,6},{6,4},{5,7},{7,5},{8,10},{10,8},{9,1... | collective-permute-start | bytes 4423688 | tf_op jit(solution)/shard_map/ppermute | solution.py:995
  (54 other events, 667.9 us)
where the time goes:
time: 519 us; the launch traced here: 512 us
  Pallas kernels  275 us (53%)
  starting transfers between devices  72.2 us (14%)
  waiting for transfers between devices  59.4 us (11%)
  other arithmetic  58.4 us (11%)
  local copies, waits for them, and re-layouts  43.9 us (8%)
    pallas_call x3, Pallas kernels, attend_back(): pl.pallas_call(functools.partial(attend_back_kernel, frames_here), grid_s...  87 us
    pallas_call x2, Pallas kernels, row_call(): pl.pallas_call(kernel, grid_spec=pltpu.PrefetchScalarGridSpec(num_scalar_...  56.1 us
    pallas_call x2, Pallas kernels, attend(): pl.pallas_call(functools.partial(attend_kernel, frames_here, bk, shift),...  49.7 us
    ppermute x21, waiting for transfers between devices, hop(): return lax.ppermute(x, 'chip', [(i, i ^ step) for i in range(chips)])  48.8 us
    pallas_call x2, Pallas kernels, up_grad(): pl.pallas_call(functools.partial(up_grad_kernel, odd), grid_spec=pltpu.Pr...  27.6 us
    ppermute x21, starting transfers between devices, hop(): return lax.ppermute(x, 'chip', [(i, i ^ step) for i in range(chips)])  24.8 us
    ppermute x7, starting transfers between devices, to_plane(): return lax.ppermute(x, 'mp', flip2)  20.2 us
    unnamed x106, local copies, waits for them, and re-layouts  18.1 us
  transfers between devices with their start and end apart: 51, of which 13 were waited for; matrix products, arithmetic and copies ran while one was open for 15% of the time, Pallas kernels for 46%

commit v1 on v0

--- a/solution.py
+++ b/solution.py
@@ -58,9 +58,9 @@
     )
 
 
-def params(n):
+def params(n, mib=60):
     return pltpu.CompilerParams(
-        dimension_semantics=("arbitrary",) * n, vmem_limit_bytes=60 * 1024 * 1024
+        dimension_semantics=("arbitrary",) * n, vmem_limit_bytes=mib * 1024 * 1024
     )
 
 
@@ -72,36 +72,99 @@
     return lax.optimization_barrier((value, others))[0]
 
 
-def pack_kernel(tokens, cot, out):
+NOTE = 4
+
+
+def pack_kernel(tokens, cot, offset, count, out):
     here = tokens.shape[0]
     rows = out.shape[0] - cot.shape[0]
     edge = here // 16 * 16
-    out[edge:, :] = jnp.zeros_like(out[edge:, :])
+    width = out.shape[1]
     out[:here, :] = tokens[...]
+    left = offset[...]
+    lines = []
+    for _ in range(3):
+        line = left.astype(BF16)
+        lines.append(line.astype(F32))
+        left = left - lines[-1]
+    lines.append(jnp.broadcast_to(count[...], (1, width)))
+    tail = rows - here
+    row = lax.broadcasted_iota(jnp.int32, (tail, width), 0)
+    block = jnp.zeros((tail, width), F32)
+    for i, line in enumerate(lines):
+        block = jnp.where(row == NOTE + i, line, block)
+    out[here:rows, :] = block.astype(BF16)
     out[rows:, :] = cot[...]
 
 
-def pack(tokens, cot, half_rows):
+def pack(tokens, cot, offset, count, half_rows):
     rows, width = half_rows + cot.shape[0], tokens.shape[1]
     return pl.pallas_call(
         pack_kernel,
-        in_specs=[pl.BlockSpec(tokens.shape), pl.BlockSpec(cot.shape)],
+        in_specs=[pl.BlockSpec(x.shape) for x in (tokens, cot, offset, count)],
         out_specs=pl.BlockSpec((rows, width)),
         out_shape=jax.ShapeDtypeStruct((rows, width), BF16),
         compiler_params=pltpu.CompilerParams(vmem_limit_bytes=16 * 1024 * 1024),
         cost_estimate=cost(0, 4 * rows * width),
         name="pack",
-    )(tokens, cot)
+    )(tokens, cot, offset, count)
+
+
+def relay_kernel(scal, mine, first, second, out):
+    straight = scal[0] == scal[1]
+    rows = first.shape[0]
+    swap = scal[2] == 1
+    for half in range(2):
+        here = slice(half * rows, (half + 1) * rows)
+        one, two = (first, second) if half == 0 else (second, first)
+        got = jnp.where(swap, two[...], one[...])
+        kept = jnp.where(straight, mine[here, :], got)
+        share = kept.shape[1] // 3
+        for pair in range(share // 128):
+            for item in range(3):
+                to = pair * 384 + item * 128
+                at = item * share + pair * 128
+                out[here, to : to + 128] = kept[:, at : at + 128]
+
+
+def relay(scal, mine, first, second):
+    return pl.pallas_call(
+        relay_kernel,
+        grid_spec=pltpu.PrefetchScalarGridSpec(
+            num_scalar_prefetch=1,
+            grid=(1,),
+            in_specs=[held(mine.shape), held(first.shape), held(first.shape)],
+            out_specs=held(mine.shape),
+        ),
+        out_shape=jax.ShapeDtypeStruct(mine.shape, BF16),
+        compiler_params=params(1, 24),
+        cost_estimate=cost(0, 0),
+        name="relay",
+    )(scal, mine, first, second)
 
 
 def project_kernel(
-    frames_here, scal, oth, own, gain, shift, weight, offset, first, qkv, qfeat, kfeat
+    frames_here, scal, oth, own, gain, shift, weight, first, qkv, qfeat, kfeat, offset
 ):
     step = pl.program_id(0)
     half_blocks = pl.num_programs(0) // 2
     half_rows = half_blocks * BLK
     within = lax.rem(step, half_blocks) * BLK
     rows = pl.ds(pl.multiple_of(within, BLK), BLK)
+
+    @pl.when(step == 0)
+    def _():
+        start = frames_here * FRAME_TOK // 16 * 16
+        at = frames_here * FRAME_TOK + NOTE - start
+        block = own[start : start + 32, :].astype(F32)
+        note = block[at : at + 1, :] + block[at + 1 : at + 2, :] + block[at + 2 : at + 3, :]
+        share = weight.shape[1] // 3
+        offset[...] = jnp.zeros_like(offset)
+        for pair in range(share // 128):
+            here = pair * 128
+            offset[:, 3 * here : 3 * here + 128] = note[:, here : here + 128]
+            offset[:, 3 * here + 256 : 3 * here + 384] = note[:, share + here : share + here + 128]
+
     values = jnp.where(step < half_blocks, oth[rows, :], own[rows, :]).astype(F32)
     xhat, _ = centre(values)
     low = (xhat * gain[...] + shift[...]).astype(BF16)
@@ -137,7 +200,7 @@
     return low, high
 
 
-def project(scal, oth, own, gain, shift, weight, offset, frames_here, half_rows):
+def project(scal, oth, own, gain, shift, weight, frames_here, half_rows):
     width, cols = weight.shape
     steps = 2 * half_rows // BLK
     rows = 2 * half_rows
@@ -152,7 +215,6 @@
                 whole((1, width)),
                 whole((1, width)),
                 whole((width, cols)),
-                whole((1, cols)),
             ],
             out_specs=[
                 pl.BlockSpec((BLK, width), lambda i, *_: (i, 0)),
@@ -160,6 +222,7 @@
                 pl.BlockSpec((BLK, 128), lambda i, *_: (i, 0)),
                 pl.BlockSpec((BLK, 128), lambda i, *_: (i, 0)),
             ],
+            scratch_shapes=[pltpu.VMEM((1, cols), F32)],
         ),
         out_shape=[
             jax.ShapeDtypeStruct((rows, width), BF16),
@@ -167,16 +230,15 @@
             jax.ShapeDtypeStruct((rows, 128), BF16),
             jax.ShapeDtypeStruct((rows, 128), BF16),
         ],
-        compiler_params=params(1),
+        compiler_params=params(1, 22),
         cost_estimate=cost(2 * rows * width * cols, 4 * rows * width + 2 * rows * cols),
         name="project",
-    )(scal, oth, own, gain, shift, weight, offset)
+    )(scal, oth, own, gain, shift, weight)
 
 
 def attend_kernel(
     frames_here,
     bk,
-    shift,
     scal,
     q,
     qfeat,
@@ -197,7 +259,7 @@
     pairs = q.shape[1] // 384
     flip = half * (1 - scal[0])
     edge = clip_edge(scal[2], frames_here, half * BLK)
-    low, high = clip_span((step + shift) ^ flip, edge, blocks)
+    low, high = clip_span((step + half * scal[3]) ^ flip, edge, blocks)
     per = bk // BLK
     low, high = low // per, (high + per - 1) // per
     kflip = flip // per
@@ -219,9 +281,9 @@
                 keys_all[pair, rows, 128:] = kfeat[rows, :]
                 both = qkv[rows, at + 256 : at + 384]
                 values_all[2 * pair, rows, :128] = jnp.where(left, both, none)
-                values_all[2 * pair, rows, 128:] = jnp.where(lane == 0, 1.0, 0.0).astype(BF16)
+                values_all[2 * pair, rows, 128:] = jnp.where(left, 1.0, 0.0).astype(BF16)
                 values_all[2 * pair + 1, rows, :128] = jnp.where(left, none, both)
-                values_all[2 * pair + 1, rows, 128:] = jnp.where(lane == 1, 1.0, 0.0).astype(BF16)
+                values_all[2 * pair + 1, rows, 128:] = jnp.where(left, 0.0, 1.0).astype(BF16)
             return carry
 
         lax.fori_loop(0, blocks, prepare, 0)
@@ -243,10 +305,8 @@
         return carry
 
     lax.fori_loop(low, high, score, 0)
-    peaks = []
     for head in range(2 * pairs):
-        peaks.append(jnp.max(tops[head], axis=1, keepdims=True))
-        tops[head] = jnp.broadcast_to(peaks[-1], (BLK, 128))
+        tops[head] = jnp.broadcast_to(jnp.max(tops[head], axis=1, keepdims=True), (BLK, 128))
     acc[...] = jnp.zeros_like(acc)
     def mix(block, carry):
         rows = pl.ds(pl.multiple_of((block ^ kflip) * bk, bk), bk)
@@ -266,34 +326,29 @@
     lax.fori_loop(low, high, mix, 0)
     for pair in range(pairs):
         cols = slice(pair * 128, (pair + 1) * 128)
-        total_a, total_b = acc[pair, :, 128:129], acc[pair, :, 129:130]
-        out = acc[pair, :, :128] / jnp.where(left, total_a, total_b)
+        totals = acc[pair, :, 128:]
+        out = acc[pair, :, :128] / totals
         wide[:, cols] = out
         mixed[:, cols] = out.astype(BF16)
-
-        logs = jnp.where(
-            lane == 0,
-            peaks[2 * pair] + jnp.log(total_a),
-            jnp.where(lane == 1, peaks[2 * pair + 1] + jnp.log(total_b), 0.0),
-        )
-        log_total[pair, 0] = logs.T[:8]
-
-
-def attend(scal, qkv, qfeat, kfeat, frames_here, own):
+        logs = (jnp.where(left, tops[2 * pair], tops[2 * pair + 1]) + jnp.log(totals)).T
+        log_total[pair, 0, 0:1] = logs[0:1]
+        log_total[pair, 0, 1:2] = logs[HEAD_DIM : HEAD_DIM + 1]
+
+
+def attend(scal, qkv, qfeat, kfeat, frames_here):
     rows, cols = qkv.shape
     width = cols // 3
     pairs = width // 128
     half = rows // BLK // 2
     bk = rows // 2
-    shift = half if own else 0
     return pl.pallas_call(
-        functools.partial(attend_kernel, frames_here, bk, shift),
+        functools.partial(attend_kernel, frames_here, bk),
         grid_spec=pltpu.PrefetchScalarGridSpec(
             num_scalar_prefetch=1,
             grid=(half,),
             in_specs=[
-                pl.BlockSpec((BLK, cols), lambda i, *_: (i + shift, 0)),
-                pl.BlockSpec((BLK, 128), lambda i, *_: (i + shift, 0)),
+                pl.BlockSpec((BLK, cols), lambda i, scal: (i + half * scal[3], 0)),
+                pl.BlockSpec((BLK, 128), lambda i, scal: (i + half * scal[3], 0)),
                 whole((rows, cols)),
                 whole((rows, 128)),
             ],
@@ -315,7 +370,7 @@
             jax.ShapeDtypeStruct((rows // 2, width), F32),
             jax.ShapeDtypeStruct((pairs, half, 8, BLK), F32),
         ],
-        compiler_params=params(1),
+        compiler_params=params(1, 40),
         cost_estimate=cost(8 * rows * rows * width, 16 * rows * width),
         name="attend",
     )(scal, qkv, qfeat, qkv, kfeat)
@@ -413,12 +468,11 @@
         cols = slice(chunk * hid, (chunk + 1) * hid)
         pre = nn(second, up_weight(core, own_up, got_a, got_b, chunk)) + up_bias(chunk)
         square = pre * pre
-        bend = jnp.tanh(GELU_C * (pre + GELU_A * (square * pre)))
-        half_up = 0.5 * (1.0 + bend)
-        hidden = (pre * half_up).astype(BF16)
-        slope_out[:, cols] = half_up + (0.5 * pre) * (1.0 - bend * bend) * (
-            GELU_C + (3.0 * GELU_A * GELU_C) * square
-        )
+        gate = 0.5 + 0.5 * jnp.tanh(pre * (GELU_C + (GELU_A * GELU_C) * square))
+        product = pre * gate
+        hidden = product.astype(BF16)
+        bend = (1.0 - gate) * (2.0 * GELU_C + (6.0 * GELU_A * GELU_C) * square)
+        slope_out[:, cols] = (gate + product * bend).astype(BF16)
         hidden_out[:, cols] = hidden
         block_out = block_out + nn(hidden, down_weight(core, own_down, got_a, got_b, chunk))
     xhat_three, scale_three = centre(block_out)
@@ -487,7 +541,7 @@
     for chunk in range(4):
         cols = slice(chunk * hid, (chunk + 1) * hid)
         hidden_grad = nt(low, down_weight(core, own_down, got_a, got_b, chunk))
-        pre_grad = (hidden_grad * slope[:, cols]).astype(BF16)
+        pre_grad = (hidden_grad * slope[:, cols].astype(F32)).astype(BF16)
         pre_grad_out[:, cols] = pre_grad
         up_sums[:, cols] += fold8(pre_grad.astype(F32))
         term = nt(pre_grad, up_weight(core, own_up, got_a, got_b, chunk))
@@ -519,7 +573,7 @@
     return pl.BlockSpec(shape, lambda *_: (0,) * len(shape))
 
 
-def row_call(kernel, name, scal, rowed, wholes, row_outs, held_outs, scratch, flops):
+def row_call(kernel, name, scal, rowed, wholes, row_outs, held_outs, scratch, flops, mib):
     rows = rowed[0].shape[0]
     nbytes = sum(x.size * x.dtype.itemsize for x in wholes)
     nbytes += rows * sum(c * (2 if t == BF16 else 4) for c, t in row_outs)
@@ -534,7 +588,7 @@
         ),
         out_shape=[jax.ShapeDtypeStruct((rows, cols), t) for cols, t in row_outs]
         + [jax.ShapeDtypeStruct(s, F32) for s in held_outs],
-        compiler_params=params(1),
+        compiler_params=params(1, mib),
         cost_estimate=cost(flops, nbytes),
         name=name,
     )(scal, *rowed, *wholes)
@@ -555,13 +609,14 @@
             (width, F32),
             (128, F32),
             (hidden, BF16),
-            (hidden, F32),
+            (hidden, BF16),
             (width, BF16),
             (width, BF16),
         ],
         [(24, width), (128, width), (128, width), (8, 128)],
         [pltpu.VMEM((2 * share, width), BF16)],
         2 * rows * width * (2 * hidden + width),
+        40,
     )
 
 
@@ -579,39 +634,43 @@
         [(24, width), (8, hidden)],
         [pltpu.VMEM((2 * share, width), BF16)],
         2 * rows * width * (2 * hidden + width),
-    )
-
-
-def down_grad_kernel(hidden, out_low, out):
+        40,
+    )
+
+
+def down_grad_kernel(scal, hidden, out_low, out):
     out[0] = tn(hidden[...], out_low[...]).astype(BF16)
 
 
-def down_grad(hidden, out_low, odd):
+def down_grad(scal, hidden, out_low):
     rows, width = out_low.shape
     hid = hidden.shape[1] // 4
     return pl.pallas_call(
         down_grad_kernel,
-        grid=(2,),
-        in_specs=[
-            pl.BlockSpec((rows, hid), lambda n: (0, 2 * n + odd)),
-            whole((rows, width)),
-        ],
-        out_specs=pl.BlockSpec((1, hid, width), lambda n: (n, 0, 0)),
+        grid_spec=pltpu.PrefetchScalarGridSpec(
+            num_scalar_prefetch=1,
+            grid=(2,),
+            in_specs=[
+                pl.BlockSpec((rows, hid), lambda n, scal: (0, 2 * n + scal[3])),
+                whole((rows, width)),
+            ],
+            out_specs=pl.BlockSpec((1, hid, width), lambda n, *_: (n, 0, 0)),
+        ),
         out_shape=jax.ShapeDtypeStruct((2, hid, width), BF16),
-        compiler_params=params(1),
+        compiler_params=params(1, 14),
         cost_estimate=cost(4 * rows * hid * width, 8 * rows * hid),
         name="down_grad",
-    )(hidden, out_low)
-
-
-def up_grad_kernel(odd, scal, second, pre_grad, mixed_own, mixed_oth, residual_low, out):
+    )(scal, hidden, out_low)
+
+
+def up_grad_kernel(scal, second, pre_grad, mixed_own, mixed_oth, residual_low, out):
     step = pl.program_id(0)
     core, plane = scal[0], scal[1]
     width, hid = second.shape[1], pre_grad.shape[1]
     share = mixed_own.shape[1]
     out[0, :width, :] = tn(second[...], pre_grad[...]).astype(BF16)
     side = jnp.where(step == 0, 1 - plane, plane)
-    column = core if odd else 1 - core
+    column = jnp.where(scal[3] == 1, core, 1 - core)
     lhs = jnp.where(side == core, mixed_own[...], mixed_oth[...])
     rhs = residual_low[:, pl.ds(pl.multiple_of(column * (width // 2), 128), width // 2)]
     grad = tn(lhs, rhs).astype(BF16)
@@ -619,18 +678,18 @@
     out[0, width:, width // 2 :] = grad[share // 2 :]
 
 
-def up_grad(scal, second, pre_grad, mixed_own, mixed_oth, residual_low, odd):
+def up_grad(scal, second, pre_grad, mixed_own, mixed_oth, residual_low):
     rows, width = second.shape
     hid = pre_grad.shape[1] // 4
     share = mixed_own.shape[1]
     return pl.pallas_call(
-        functools.partial(up_grad_kernel, odd),
+        up_grad_kernel,
         grid_spec=pltpu.PrefetchScalarGridSpec(
             num_scalar_prefetch=1,
             grid=(2,),
             in_specs=[
                 whole((rows, width)),
-                pl.BlockSpec((rows, hid), lambda n, *_: (0, 2 * n + odd)),
+                pl.BlockSpec((rows, hid), lambda n, scal: (0, 2 * n + scal[3])),
                 whole((rows, share)),
                 whole((rows, share)),
                 whole((rows, width)),
@@ -638,7 +697,7 @@
             out_specs=pl.BlockSpec((1, width + share // 2, hid), lambda n, *_: (n, 0, 0)),
         ),
         out_shape=jax.ShapeDtypeStruct((2, width + share // 2, hid), BF16),
-        compiler_params=params(1),
+        compiler_params=params(1, 18),
         cost_estimate=cost(4 * rows * hid * width * 1.25, 10 * rows * hid),
         name="up_grad",
     )(scal, second, pre_grad, mixed_own, mixed_oth, residual_low)
@@ -743,13 +802,13 @@
         out_oth[:, :128] = (dq[:half_rows, :] * HEAD_DIM**-0.5).astype(BF16)
         out_own[:, :128] = (dq[half_rows:, :] * HEAD_DIM**-0.5).astype(BF16)
 
-def attend_back(scal, qkv, qfeat, kfeat, grad_oth, grad_own, wide, logs, frames_here, pair):
+def attend_back(scal, qkv, qfeat, kfeat, grad_oth, grad_own, wide, logs, frames_here):
     rows = qkv.shape[0]
     blocks = rows // BLK
     one = pl.Buffered(1)
-    half_rows = pl.BlockSpec((rows // 2, 128), lambda j, *_: (0, pair), pipeline_mode=one)
+    half_rows = pl.BlockSpec((rows // 2, 128), lambda j, scal: (0, scal[3]), pipeline_mode=one)
     half_logs = pl.BlockSpec(
-        (1, blocks // 2, 8, BLK), lambda j, *_: (pair, 0, 0, 0), pipeline_mode=one
+        (1, blocks // 2, 8, BLK), lambda j, scal: (scal[3], 0, 0, 0), pipeline_mode=one
     )
     return pl.pallas_call(
         functools.partial(attend_back_kernel, frames_here),
@@ -757,10 +816,10 @@
             num_scalar_prefetch=1,
             grid=(blocks,),
             in_specs=[
-                pl.BlockSpec((BLK, 128), lambda j, *_: (j, 3 * pair + 1)),
-                pl.BlockSpec((BLK, 128), lambda j, *_: (j, 3 * pair + 2)),
+                pl.BlockSpec((BLK, 128), lambda j, scal: (j, 3 * scal[3] + 1)),
+                pl.BlockSpec((BLK, 128), lambda j, scal: (j, 3 * scal[3] + 2)),
                 pl.BlockSpec((BLK, 128), lambda j, *_: (j, 0)),
-                pl.BlockSpec((rows, 128), lambda j, *_: (0, 3 * pair), pipeline_mode=one),
+                pl.BlockSpec((rows, 128), lambda j, scal: (0, 3 * scal[3]), pipeline_mode=one),
                 whole((rows, 128)),
                 half_rows,
                 half_rows,
@@ -780,7 +839,7 @@
             ],
         ),
         out_shape=[jax.ShapeDtypeStruct((rows // 2, 384), BF16)] * 2,
-        compiler_params=params(1),
+        compiler_params=params(1, 20),
         cost_estimate=cost(40 * rows * rows * 128, 30 * rows * 128),
         name="attend_back",
     )(scal, qkv, qkv, kfeat, qkv, qfeat, grad_oth, grad_own, *wide, *logs)
@@ -825,7 +884,7 @@
             jax.ShapeDtypeStruct((width // 2, cols), BF16),
             jax.ShapeDtypeStruct((8, cols), F32),
         ],
-        compiler_params=params(1),
+        compiler_params=params(1, 18),
         cost_estimate=cost(2 * rows * width * cols, 2 * rows * (width + cols)),
         name="project_grad",
     )(scal, first, *oth, *own)
@@ -864,7 +923,7 @@
             jax.ShapeDtypeStruct((rows, width), BF16),
             jax.ShapeDtypeStruct((16, width), F32),
         ],
-        compiler_params=params(1),
+        compiler_params=params(1, 18),
         cost_estimate=cost(
             4 * pairs * rows * width * cols, 4 * pairs * rows * cols + 4 * width * cols * pairs
         ),
@@ -891,7 +950,7 @@
             out_specs=row_block(width),
         ),
         out_shape=jax.ShapeDtypeStruct((tokens_here, width), F32),
-        compiler_params=params(1),
+        compiler_params=params(1, 20),
         cost_estimate=cost(20 * rows * width, 12 * rows * width),
         name="last",
     )(scal, packed, grad, grad_got, residual, residual_got, gain)
@@ -1026,33 +1085,34 @@
 
     pairs = share // 128
 
-    weight_mine = (
-        attend_weight.reshape(width, 3, pairs, 128).transpose(0, 2, 1, 3).reshape(width, 3 * share)
-    )
-    weight_part = turn(lax.dynamic_slice_in_dim(weight_mine, side * (width // 2), width // 2, 0))
-    packed = pack(tokens, pooled_cotangent.reshape(frames_here * MAPS, width), half_rows)
-    got_packed = turn(after(packed, weight_mine))
-    small = jnp.concatenate(
-        [
-            attend_offset,
-            jnp.broadcast_to(frame_counts[0, 0].astype(F32), (2, 128)),
-        ],
-        axis=1,
-    )
-    small = jnp.where(straight, small, turn(small))
-    expand_got = to_plane(expand_offset)
+    weight_mine = attend_weight.reshape(width, 3 * share)
+    weight_part = lax.dynamic_slice_in_dim(weight_mine, side * (width // 2), width // 2, 0)
+    weight_got = turn(weight_part)
+    packed = pack(
+        after(tokens, weight_part),
+        pooled_cotangent.reshape(frames_here * MAPS, width),
+        attend_offset.reshape(1, 2 * share),
+        frame_counts[:, :1].astype(F32),
+        half_rows,
+    )
+    got_packed = turn(packed)
+    expand_got = to_plane(after(expand_offset, packed))
     weight_rest = lax.ppermute(
-        weight_part,
+        weight_got,
         ("chip", "core", "mp"),
         [(4 * i + j, 4 * (i ^ 1) + j) for i in range(chips) for j in (1, 2)],
     )
-    weight_here = jnp.where(straight, weight_mine, join(weight_part, weight_rest, side, 0))
-    own = jnp.where(straight, packed, got_packed)
+    weight_here = relay(
+        jnp.stack([core, plane, side]).astype(jnp.int32), weight_mine, weight_got, weight_rest
+    )
+    own = jnp.where(straight, packed, after(got_packed, weight_here))
     oth = to_core(own)
-    count = small[0, share].astype(jnp.int32)
-    scal = jnp.stack([core.astype(jnp.int32), plane.astype(jnp.int32), count])
-    offset = jnp.stack([small[0, :share], jnp.zeros((share,), F32), small[1, :share]])
-    offset = offset.reshape(3, pairs, 128).transpose(1, 0, 2).reshape(1, 3 * share)
+    count = own[tokens_here + NOTE + 3, 0].astype(jnp.int32)
+    numbered = [
+        jnp.stack([core.astype(jnp.int32), plane.astype(jnp.int32), count, jnp.int32(i)])
+        for i in range(pairs)
+    ]
+    scal = numbered[0]
 
     quarter = jnp.concatenate(
         [
@@ -1062,7 +1122,7 @@
         ],
         axis=0,
     )
-    got_a = to_plane(after(quarter, own, weight_here, small, expand_got))
+    got_a = to_plane(after(quarter, own, weight_here))
     up_offset = jnp.where(
         plane == 0,
         jnp.concatenate([expand_offset, expand_got]),
@@ -1076,15 +1136,14 @@
         norm_gains[0:1],
         norm_shifts[0:1],
         weight_here,
-        offset,
         frames_here,
         half_rows,
     )
-    mixed_send, wide_oth, logs_oth = attend(scal, qkv, qfeat, kfeat, frames_here, False)
+    mixed_send, wide_oth, logs_oth = attend(numbered[0], qkv, qfeat, kfeat, frames_here)
     mixed_oth = to_core(mixed_send)
     weight_there = to_core(after(weight_here, mixed_send))
     mixed_own, wide_own, logs_own = attend(
-        after(scal, mixed_send), qkv, qfeat, kfeat, frames_here, True
+        after(numbered[1], mixed_send), qkv, qfeat, kfeat, frames_here
     )
     got_b = to_core(after(got_a, mixed_own))
 
@@ -1106,7 +1165,7 @@
         learner_sums,
         learner_offset_sums,
     ) = ahead(
-        scal,
+        after(scal, weight_there),
         mixed_own,
         mixed_oth,
         own,
@@ -1124,9 +1183,9 @@
         frames_here,
     )
 
-    down_theirs = down_grad(hidden, out_low, 0)
+    down_theirs = down_grad(numbered[0], hidden, out_low)
     down_got = to_core(down_theirs)
-    down_mine = down_grad(hidden, after(out_low, down_theirs), 1)
+    down_mine = down_grad(after(numbered[1], down_theirs), hidden, out_low)
     down_send = low(plus(down_got[0], down_mine[0]))
     down_keep = plus(down_got[1], down_mine[1])
     down_plane = to_plane(down_send)
@@ -1157,17 +1216,11 @@
     down_x_keep = pick(down_half, side)
     down_x = hop(down_x_send, 1)
     up_theirs = up_grad(
-        after(scal, down_x_send), second, pre_grad, mixed_own, mixed_oth, residual_low, 0
+        after(numbered[0], down_x_send), second, pre_grad, mixed_own, mixed_oth, residual_low
     )
     up_got = to_core(up_theirs)
     up_mine = up_grad(
-        after(scal, up_theirs),
-        second,
-        pre_grad,
-        mixed_own,
-        mixed_oth,
-        residual_low,
-        1,
+        after(numbered[1], up_theirs), second, pre_grad, mixed_own, mixed_oth, residual_low
     )
     up_half = halves_of(plus(up_got, up_mine))
     up_x_send = low(lax.dynamic_index_in_dim(up_half, 1 - side, 1, keepdims=False))
@@ -1176,7 +1229,7 @@
 
     def back(pair, *gate):
         return attend_back(
-            after(scal, *gate),
+            after(numbered[pair], *gate),
             qkv,
             qfeat,
             kfeat,
@@ -1185,7 +1238,6 @@
             (wide_oth, wide_own),
             (logs_oth, logs_own),
             frames_here,
-            pair,
         )
 
     def project_fold(their, mine):
@@ -1199,24 +1251,33 @@
         return low(pick(parts, 1 - bit)), pick(parts, bit)
 
     residual_got = turn(after(residual_grad, up_mine))
-    oth_0, own_0 = back(0, up_x_send)
+    down_send, down_keep = split(plus(down_x_keep, after(down_x, up_x_send)))
+    down_z = hop(down_send, hops[0])
+    oth_0, own_0 = back(0, down_send)
     got_0 = to_core(oth_0)
-    down_send, down_keep = split(plus(down_x_keep, after(down_x, oth_0)))
-    down_z = hop(down_send, hops[0])
+    down_sum = plus(down_keep, after(down_z, oth_0))
+    down_low = low(down_sum)
+    down_z = hop(down_low, hops[1])
     up_y = plus(up_x_keep, after(up_x, oth_0))
     up_y_send = low(up_y[0])
     up_y_got = to_plane(up_y_send)
 
     residual_got = after(residual_got, oth_0)
-    oth_1, own_1 = back(1, down_send, up_y_send, residual_got)
+    oth_1, own_1 = back(1, down_low, up_y_send, residual_got, got_0)
     got_1 = to_core(oth_1)
-    down_sum = plus(down_keep, after(down_z, oth_1))
-    down_low = low(down_sum)
-    down_z = hop(down_low, hops[1])
+
+    def rest(total, got, steps):
+        total = plus(total, got)
+        for step in steps:
+            total = plus(total, hop(low(total), step))
+        return low(total)
+
+    down_sum = rest(down_sum, after(down_z, oth_1), hops[2:])
+    down_z = hop(down_sum, hops[0])
     up_send, up_keep = split(plus(up_y[1], after(up_y_got, oth_1)))
     up_z = hop(up_send, hops[0])
     their_0, mine_0, offsets_0 = project_grad(
-        after(scal, down_low, up_send), first, (oth_0, oth_1), (own_0, own_1)
+        after(scal, down_sum, up_send), first, (oth_0, oth_1), (own_0, own_1)
     )
     early_send, early_keep = project_fold(their_0, mine_0)
     early_got = to_plane(early_send)
@@ -1224,17 +1285,11 @@
     up_low = low(up_sum)
     up_z = hop(up_low, hops[1])
 
-    oth_2, own_2 = back(2, early_send, up_low)
+    down_sum = join(down_sum, after(down_z, mine_0), bit, 0)
+    down_x = hop(down_sum, 1)
+
+    oth_2, own_2 = back(2, early_send, up_low, down_sum, got_1)
     got_2 = to_core(oth_2)
-
-    def rest(total, got, steps):
-        total = plus(total, got)
-        for step in steps:
-            total = plus(total, hop(low(total), step))
-        return low(total)
-
-    down_sum = rest(down_sum, after(down_z, oth_2), hops[2:])
-    down_z = hop(down_sum, hops[0])
     up_sum = rest(up_sum, after(up_z, oth_2), hops[2:])
     up_z = hop(up_sum, hops[0])
     early_half = halves_of(plus(early_keep, after(early_got, oth_2)))
@@ -1242,14 +1297,13 @@
     early_keep = pick(early_half, side)
     early_x = hop(early_send, 1)
     their_2, mine_2, offsets_2 = project_grad(
-        after(scal, down_sum, up_sum, early_send), first, (oth_2,), (own_2,)
+        after(scal, up_sum, early_send), first, (oth_2,), (own_2,)
     )
     late_send, late_keep = project_fold(their_2, mine_2)
     late_got = to_plane(late_send)
-    down_sum = join(down_sum, after(down_z, mine_2), bit, 0)
-    down_x = hop(down_sum, 1)
     up_sum = join(up_sum, after(up_z, mine_2), bit, 0)
-    up_x = hop(up_sum, 1)
+    down_sum = join(down_sum, after(down_x, mine_2), side, 0)
+    down_got = to_core(down_sum)
     early_sum = plus(early_keep, after(early_x, mine_2))
     early_low = low(early_sum)
     early_z = hop(early_low, hops[0])
@@ -1258,7 +1312,7 @@
         (got_0, got_1, got_2),
         weight_here,
         weight_there,
-        after(own, late_send, down_sum, up_sum, early_low),
+        after(own, late_send, up_sum, early_low),
     )
     first_got = turn(first_low)
     table = small_table(
@@ -1273,44 +1327,77 @@
         offsets_0,
         offsets_2,
     )
-    table = table + to_core(table)
-    table = table + to_plane(table)
-    for step in [1, *hops]:
+
+    late_half = halves_of(plus(late_keep, after(late_got, table)))
+    late_send = low(pick(late_half, 1 - side))
+    late_keep = pick(late_half, side)
+    late_x = hop(late_send, 1)
+    early_sum = plus(early_sum, after(early_z, late_send))
+    early_low = low(early_sum)
+    early_z = hop(early_low, hops[1])
+    up_x = hop(after(up_sum, early_low), 1)
+    table = table + after(to_core(table), early_low)
+    table_got = to_plane(table)
+    late_sum = plus(late_keep, after(late_x, table))
+    late_low = low(late_sum)
+    late_z = hop(late_low, hops[0])
+    table = table + after(table_got, late_low)
+    table_got = hop(table, hops[0])
+    late_sum = plus(late_sum, after(late_z, table))
+    late_low = low(late_sum)
+    late_z = hop(late_low, hops[1])
+    table = table + after(table_got, late_low)
+    table_got = hop(table, hops[1])
+    up_sum = join(up_sum, after(up_x, table), side, 0)
+    up_got = to_core(up_sum)
+    early_sum = rest(early_sum, after(early_z, up_sum), hops[2:])
+    early_x = hop(early_sum, 1)
+    tokens_gradient = last(
+        after(scal, early_sum),
+        packed,
+        first_low,
+        first_got,
+        residual_grad,
+        residual_got,
+        norm_gains[0:1],
+        tokens_here,
+    )
+    late_sum = rest(late_sum, after(late_z, tokens_gradient), hops[2:])
+    late_x = hop(late_sum, 1)
+    table = table + after(table_got, late_sum)
+    for step in [*hops[2:], 1]:
         table = table + hop(table, step)
-
-    def around(x):
-        return join(x, hop(x, 1), side, 0)
-
-    late_half = halves_of(plus(late_keep, after(late_got, first_low)))
-    late_x_send = low(pick(late_half, 1 - side))
-    late_sum = around(rest(pick(late_half, side), hop(late_x_send, 1), hops))
-    early_sum = around(rest(early_sum, after(early_z, first_low), hops[1:]))
-    up_sum = join(up_sum, after(up_x, first_low), side, 0)
-    down_sum = join(down_sum, after(down_x, first_low), side, 0)
-
-    tokens_gradient = last(
-        scal, packed, first_low, first_got, residual_grad, residual_got, norm_gains[0:1], tokens_here
-    )
-
-    def two(x):
-        other = to_core(x)
+    early_sum = join(early_sum, after(early_x, late_sum), side, 0)
+    early_got = to_core(early_sum)
+    late_sum = join(late_sum, after(late_x, early_sum), side, 0)
+    late_got = to_core(late_sum)
+
+    def two(x, other):
         return jnp.where(core == 0, x, other), jnp.where(core == 0, other, x)
 
     def out_block(x):
         return jnp.concatenate([x[width:, : width // 2], x[width:, width // 2 :]], axis=0)
 
-    down_first, down_second = two(down_sum)
-    up_first, up_second = two(up_sum)
+    down_first, down_second = two(down_sum, down_got)
+    up_first, up_second = two(up_sum, up_got)
     contract_gradient = jnp.concatenate([down_first, down_second], axis=0).astype(F32)
     expand_gradient = jnp.concatenate([up_first[:width], up_second[:width]], axis=1).astype(F32)
     output_gradient = jnp.concatenate([out_block(up_first), out_block(up_second)], axis=1).astype(F32)
 
-    attend_gradient = jnp.concatenate(
-        [jnp.concatenate(two(early_sum), axis=0), jnp.concatenate(two(late_sum), axis=0)], axis=1
-    )
-    attend_gradient = (
-        attend_gradient.reshape(width, pairs, 3, 128).transpose(0, 2, 1, 3).astype(F32)
-    )
+    early_two, late_two = two(early_sum, early_got), two(late_sum, late_got)
+
+    def column(pair, part):
+        halves, at = (early_two, pair) if pair < pairs - 1 else (late_two, 0)
+        at = at * 384 + part * 128
+        return jnp.concatenate([x[:, at : at + 128] for x in halves], axis=0)
+
+    attend_gradient = jnp.stack(
+        [
+            jnp.concatenate([column(pair, part) for pair in range(pairs)], axis=1)
+            for part in range(3)
+        ],
+        axis=1,
+    ).astype(F32)
     return (
         jnp.where(straight, pooled[:maps_all], residual_got[half_rows - maps_all :]).reshape(
             frames_here, MAPS, width
@@ -1318,7 +1405,7 @@
         tokens_gradient,
         table[0:3],
         table[3:6],
-        attend_gradient.reshape(width, 3, share),
+        attend_gradient,
         lax.dynamic_slice_in_dim(table[21:23], plane * share, share, 1),
         output_gradient,
         table[6],

time: 519 us -> 436 us (0.84)
  Pallas kernels: 275 us -> 230 us
  other arithmetic: 58.4 us -> 39.7 us
  waiting for transfers between devices: 59.4 us -> 44.1 us
    pallas_call x7 -> x8, Pallas kernels: 89 us -> 63.6 us  [the longest x2 42.4 us: attend(): pl.pallas_call(functools.partial(attend_kernel, frames_here, bk), grid_sp...]
    ppermute x21, waiting for transfers between devices: 48.8 us -> 31.4 us  [hop(): return lax.ppermute(x, 'chip', [(i, i ^ step) for i in range(chips)])]
    ppermute x7, starting transfers between devices: 20.2 us -> 7.37 us  [to_plane(): return lax.ppermute(x, 'mp', flip2)]
    ppermute x17, starting transfers between devices: 17.3 us -> 28.6 us  [to_core(): return lax.ppermute(x, 'core', flip2)]
    unnamed x106 -> x170, local copies, waits for them, and re-layouts: 18.1 us -> 26.7 us
    convert_element_type x11, other arithmetic: 13.3 us -> 7.01 us  [low(): return x.astype(BF16)]
    pallas_call x2, Pallas kernels: 56.1 us -> 50 us  [row_call(): pl.pallas_call(kernel, grid_spec=pltpu.PrefetchScalarGridSpec(num_scalar_...]
    pallas_call x2, Pallas kernels: 13.4 us -> 7.72 us  [project_grad(): pl.pallas_call(functools.partial(project_grad_kernel, pairs), grid_spec=p...]
  transfers between devices with their start and end apart: 51 -> 50, of which waited for: 13 -> 16; matrix products, arithmetic and copies ran while one was open for 15% -> 11% of each run, Pallas kernels for 46% -> 46%
where the time goes in v1:
time: 436 us; the launch traced here: 433 us
  Pallas kernels  230 us (53%)
  starting transfers between devices  72.6 us (17%)
  waiting for transfers between devices  44.1 us (10%)
  local copies, waits for them, and re-layouts  43.2 us (10%)
  other arithmetic  39.7 us (9%)
    pallas_call x3, Pallas kernels, attend_back(): pl.pallas_call(functools.partial(attend_back_kernel, frames_here), grid_s...  83.9 us
    pallas_call x2, Pallas kernels, row_call(): pl.pallas_call(kernel, grid_spec=pltpu.PrefetchScalarGridSpec(num_scalar_...  50 us
    pallas_call x2, Pallas kernels, attend(): pl.pallas_call(functools.partial(attend_kernel, frames_here, bk), grid_sp...  42.4 us
    ppermute x21, waiting for transfers between devices, hop(): return lax.ppermute(x, 'chip', [(i, i ^ step) for i in range(chips)])  31.4 us
    ppermute x17, starting transfers between devices, to_core(): return lax.ppermute(x, 'core', flip2)  28.6 us
    ppermute x21, starting transfers between devices, hop(): return lax.ppermute(x, 'chip', [(i, i ^ step) for i in range(chips)])  28.3 us
    unnamed x170, local copies, waits for them, and re-layouts  26.7 us
    pallas_call x2, Pallas kernels, up_grad(): pl.pallas_call(up_grad_kernel, grid_spec=pltpu.PrefetchScalarGridSpec(num...  11.1 us
  transfers between devices with their start and end apart: 50, of which 16 were waited for; matrix products, arithmetic and copies ran while one was open for 11% of the time, Pallas kernels for 46%

profile of v1, /device:TPU:0, one launch (start us, length us, event | category | flops | bytes accessed | tf_op | source)
XLA Modules:
  0.0 432.8 jit_solution(9900109267008449364)
XLA Ops:
  0.7 3.8 copy.30
  4.5 2.7 copy.31.mine
  9.3 1.8 collective-permute-start
  12.8 2.6 relay.1.weight.refs_6_
  16.6 25.9 %collective-permute-start.3 = (bf16[1064,768]{1,0:T(8,128)(2,1)S(1)}, bf16[1064,768]{1,0:T(8,128)(2,1)}, u32[]{:S(2)}, u32[]{:S(2)}) collective-permute-start(bf16[1064,768]{1,0:T(8,128)(2,1)S(1)} %broadcast_select_fusion.own.tokens.refs_8_), channel_id=1, source_target_pairs={{0,2},{2,0},{1,3},{3,1},{4,6},{6,4},{5,7},{7,5},{8,10},{10,8},{9,1... | collective-permute-start | bytes 4902920 | tf_op jit(solution)/shard_map/ppermute | solution.py:1054
  44.9 1.8 constant_dynamic-slice_fusion.3
  48.9 2.6 collective-permute-start.6
  52.4 10.1 %project.1 = (bf16[2048,768]{1,0:T(8,128)(2,1)S(1)}, bf16[2048,1152]{1,0:T(8,128)(2,1)S(1)}, bf16[2048,128]{1,0:T(8,128)(2,1)S(1)}, bf16[2048,128]{1,0:T(8,128)(2,1)S(1)}) custom-call(s32[4]{0:T(128)S(1)} %get-tuple-element.187.scal, bf16[1064,768]{1,0:T(8,128)(2,1)} %collective-permute-done.3.oth, ...), custom_call_target="tpu_custom_call" | custom-call | flops 72477573120 | bytes 220200960 | tf_op jit(solution)/shard_map/project/pallas_call | solution.py:207
  64.2 22.6 %attend.2 = (bf16[1024,384]{1,0:T(8,128)(2,1)}, f32[1024,384]{1,0:T(8,128)S(1)}, f32[3,4,8,256]{3,2,1,0:T(8,128)S(1)}) custom-call(s32[4]{0:T(128)S(1)} %get-tuple-element.187.scal, bf16[2048,1152]{1,0:T(8,128)(2,1)S(1)} %get-tuple-element.106.q.qkv.k.v, bf16[2048,128]{1,0:T(8,128)(2,1)S(1)} %get-tuple-element.107.qfeat, ...), custom_call_target="tpu_custom_call" | custom-call | flops 257698037760 | bytes 251658240 | tf_op jit(solution)/shard_map/attend/pallas_call | solution.py:344
  87.0 19.8 %attend.3 = (bf16[1024,384]{1,0:T(8,128)(2,1)S(1)}, f32[1024,384]{1,0:T(8,128)S(1)}, f32[3,4,8,256]{3,2,1,0:T(8,128)S(1)}) custom-call(s32[4]{0:T(128)S(1)} %get-tuple-element.146.scal, bf16[2048,1152]{1,0:T(8,128)(2,1)S(1)} %get-tuple-element.106.q.qkv.k.v, bf16[2048,128]{1,0:T(8,128)(2,1)S(1)} %get-tuple-element.107.qfeat, ...), custom_call_target="tpu_custom_call" | custom-call | flops 257698037760 | bytes 251658240 | tf_op jit(solution)/shard_map/attend/pallas_call | solution.py:344
  115.1 3.3 collective-permute-done.4.refs_7_
  126.9 28.7 %ahead.1 = (f32[1024,768]{1,0:T(8,128)}, f32[1024,768]{1,0:T(8,128)}, f32[1024,128]{1,0:T(8,128)S(1)}, bf16[1024,3072]{1,0:T(8,128)(2,1)}, bf16[1024,3072]{1,0:T...) custom-call(s32[4]{0:T(128)S(1)} %copy-done.24, ...), custom_call_target="tpu_custom_call" | custom-call | flops 217432719360 | bytes 671836160 | tf_op jit(solution)/shard_map/ahead/pallas_call | solution.py:580
  156.8 2.8 copy-done.36
  159.6 3.7 down_grad.2
  163.5 3.7 down_grad.3
  171.1 21.3 %behind.1 = (f32[1024,768]{1,0:T(8,128)}, bf16[1024,384]{1,0:T(8,128)(2,1)S(1)}, bf16[1024,384]{1,0:T(8,128)(2,1)S(1)}, bf16[1024,3072]{1,0:T(8,128)(2,1)}, bf16...) custom-call(s32[4]{0:T(128)S(1)} %copy-done.24, f32[1024,768]{1,0:T(8,128)} %get-tuple-element.122.out_grad, ...), custom_call_target="tpu_custom_call" | custom-call | flops 217432719360 | bytes 472043520 | tf_op jit(solution)/shard_map/behind/pallas_call | solution.py:580
  192.9 4.7 %collective-permute-done.10 = bf16[768,768]{1,0:T(8,128)(2,1)} collective-permute-done((bf16[768,768]{1,0:T(8,128)(2,1)}, bf16[768,768]{1,0:T(8,128)(2,1)}, u32[]{:S(2)}, u32[]{:S(2)}) %collective-permute-start.10) | collective-permute-done | bytes 1179680 | tf_op jit(solution)/shard_map/ppermute | solution.py:1057
  197.6 1.9 bitcast_add_fusion.1
  202.3 5.6 %up_grad.2 = bf16[2,960,768]{2,1,0:T(8,128)(2,1)S(1)} custom-call(s32[4]{0:T(128)S(1)} %copy-done.24, bf16[1024,768]{1,0:T(8,128)(2,1)S(1)} %copy-done.41, bf16[1024,3072]{1,0:T(8,128)(2,1)S(1)} %copy-done.38, bf16[1024,384]{1,0:T(8,128)(2,1)S(1)} %copy-done.47, bf16[1024,384]{1,0:T(8,128)(2,1)} %collective-permute-done.5.mixed_oth, ...), custom_call_target="tpu_custom_call" | custom-call | flops 60397977600 | bytes 157286400 | tf_op jit(solution)/shard_map/up_grad/pallas_call | solution.py:685
  209.5 5.5 %up_grad.3 = bf16[2,960,768]{2,1,0:T(8,128)(2,1)S(1)} custom-call(s32[4]{0:T(128)S(1)} %copy-done.28, bf16[1024,768]{1,0:T(8,128)(2,1)S(1)} %copy-done.42, bf16[1024,3072]{1,0:T(8,128)(2,1)S(1)} %copy-done.38, bf16[1024,384]{1,0:T(8,128)(2,1)S(1)} %copy-done.47, bf16[1024,384]{1,0:T(8,128)(2,1)} %collective-permute-done.5.mixed_oth, ...), custom_call_target="tpu_custom_call" | custom-call | flops 60397977600 | bytes 157286400 | tf_op jit(solution)/shard_map/up_grad/pallas_call | solution.py:685
  215.1 2.4 collective-permute-start.11
  217.5 2.4 convert_add_fusion
  219.9 2.5 copy-done.60
  226.8 28.0 %attend_back.3 = (bf16[1024,384]{1,0:T(8,128)(2,1)S(1)}, bf16[1024,384]{1,0:T(8,128)(2,1)S(1)}) custom-call(s32[4]{0:T(128)S(1)} %copy-done.24, bf16[2048,1152]{1,0:T(8,128)(2,1)S(1)} %bitcast.92, bf16[2048,1152]{1,0:T(8,128)(2,1)S(1)} %bitcast.92, bf16[2048,128]{1,0:T(8,128)(2,1)S(1)} %copy-done.51, bf16[2048,1152]{1,0:T(8,128)(2,1)S(1)} %bitcast.92, ...), custom_call_target="tpu_custom_call" | custom-call | flops 429496729600 | bytes 157286400 | tf_op jit(solution)/shard_map/attend_back/pallas_call | solution.py:813
  255.8 1.9 fusion.7
  257.7 2.6 collective-permute-start.16
  260.3 2.6 bitcast_add_fusion
  263.9 27.8 %attend_back.4 = (bf16[1024,384]{1,0:T(8,128)(2,1)S(1)}, bf16[1024,384]{1,0:T(8,128)(2,1)S(1)}) custom-call(s32[4]{0:T(128)S(1)} %copy-done.28, bf16[2048,1152]{1,0:T(8,128)(2,1)S(1)} %bitcast.92, bf16[2048,1152]{1,0:T(8,128)(2,1)S(1)} %bitcast.92, bf16[2048,128]{1,0:T(8,128)(2,1)S(1)} %copy-done.51, bf16[2048,1152]{1,0:T(8,128)(2,1)S(1)} %bitcast.92, ...), custom_call_target="tpu_custom_call" | custom-call | flops 429496729600 | bytes 157286400 | tf_op jit(solution)/shard_map/attend_back/pallas_call | solution.py:813
  293.3 1.9 fusion.1
  295.2 1.9 collective-permute-start.22
  297.2 4.4 %project_grad.2 = (bf16[384,768]{1,0:T(8,128)(2,1)S(1)}, bf16[384,768]{1,0:T(8,128)(2,1)S(1)}, f32[8,768]{1,0:T(8,128)S(1)}) custom-call(s32[4]{0:T(128)S(1)} %copy-done.24, bf16[2048,768]{1,0:T(8,128)(2,1)S(1)} %copy-done.34, bf16[1024,384]{1,0:T(8,128)(2,1)S(1)} %copy-done.32, bf16[1024,384]{1,0:T(8,128)(2,1)S(1)} %get-tuple-element.147.refs_1_, ...), custom_call_target="tpu_custom_call" | custom-call | flops 48318382080 | bytes 125829120 | tf_op jit(solution)/shard_map/project_grad/pallas_call | solution.py:871
  304.1 6.3 %collective-permute-done.22 = bf16[240,768]{1,0:T(8,128)(2,1)S(1)} collective-permute-done((bf16[240,768]{1,0:T(8,128)(2,1)S(1)}, bf16[240,768]{1,0:T(8,128)(2,1)S(1)}, u32[]{:S(2)}, u32[]{:S(2)}) %collective-permute-start.22) | collective-permute-done | bytes 368672 | tf_op jit(solution)/shard_map/ppermute | solution.py:1066
  311.3 2.4 collective-permute-start.26
  314.8 28.1 %attend_back.5 = (bf16[1024,384]{1,0:T(8,128)(2,1)S(1)}, bf16[1024,384]{1,0:T(8,128)(2,1)S(1)}) custom-call(s32[4]{0:T(128)S(1)} %get-tuple-element.158.scal, bf16[2048,1152]{1,0:T(8,128)(2,1)S(1)} %bitcast.92, bf16[2048,1152]{1,0:T(8,128)(2,1)S(1)} %bitcast.92, bf16[2048,128]{1,0:T(8,128)(2,1)S(1)} %copy-done.51, bf16[2048,1152]{1,0:T(8,128)(2,1)S(1)} %bitcast.92, ...), custom_call_target="tpu_custom_call" | custom-call | flops 429496729600 | bytes 157286400 | tf_op jit(solution)/shard_map/attend_back/pallas_call | solution.py:813
  347.2 3.3 project_grad.3
  352.0 3.2 collective-permute-done.31
  358.6 7.7 %first_grad.1 = (bf16[1024,768]{1,0:T(8,128)(2,1)S(1)}, f32[16,768]{1,0:T(8,128)S(1)}) custom-call(bf16[1024,384]{1,0:T(8,128)(2,1)S(1)} %copy-done.44, bf16[1024,384]{1,0:T(8,128)(2,1)S(1)} %get-tuple-element.153.refs_3_.refs_1_, bf16[1024,384]{1,0:T(8,128)(2,1)S(1)} %get-tuple-element.163.refs_1_.refs_2_, bf16[1024,384]{1,0:T(8,128)(2,1)S(1)} %copy-done.30, ...), custom_call_target="tpu_custom_call" | custom-call | flops 72477573120 | bytes 165150720 | tf_op jit(solution)/shard_map/first_grad/pallas_call | solution.py:913
  370.3 3.6 collective-permute-done.36
  380.5 4.8 %collective-permute-done.37 = f32[24,768]{1,0:T(8,128)S(1)} collective-permute-done((f32[24,768]{1,0:T(8,128)S(1)}, f32[24,768]{1,0:T(8,128)S(1)}, u32[]{:S(2)}, u32[]{:S(2)}) %collective-permute-start.37) | collective-permute-done | bytes 73760 | tf_op jit(solution)/shard_map/ppermute | solution.py:1066
  385.3 4.3 collective-permute-start.41
  391.7 6.9 %collective-permute-done.32 = bf16[192,768]{1,0:T(8,128)(2,1)S(1)} collective-permute-done((bf16[192,768]{1,0:T(8,128)(2,1)S(1)}, bf16[192,768]{1,0:T(8,128)(2,1)S(1)}, u32[]{:S(2)}, u32[]{:S(2)}) %collective-permute-start.32) | collective-permute-done | bytes 294944 | tf_op jit(solution)/shard_map/ppermute | solution.py:1066
  398.8 2.2 collective-permute-start.43
  401.1 2.5 maximum_convert_fusion.1
  403.6 6.4 %last.1 = f32[980,768]{1,0:T(8,128)} custom-call(s32[4]{0:T(128)S(1)} %copy-done.24, bf16[1064,768]{1,0:T(8,128)(2,1)S(1)} %pack.1.tokens, bf16[1024,768]{1,0:T(8,128)(2,1)S(1)} %get-tuple-element.188.grad, bf16[1024,768]{1,0:T(8,128)(2,1)S(1)} %collective-permute-done.39.grad_got, f32[1024,768]{1,0:T(8,128)} %get-tuple-element.133.residual, ...), custom_call_target="tpu_custom_call" | custom-call | flops 314572800 | bytes 188743680 | tf_op jit(solution)/shard_map/last/pallas_call | solution.py:944
  413.2 4.8 %collective-permute-done.42 = f32[24,768]{1,0:T(8,128)S(1)} collective-permute-done((f32[24,768]{1,0:T(8,128)S(1)}, f32[24,768]{1,0:T(8,128)S(1)}, u32[]{:S(2)}, u32[]{:S(2)}) %collective-permute-start.42) | collective-permute-done | bytes 73760 | tf_op jit(solution)/shard_map/ppermute | solution.py:1066
  424.1 2.1 maximum_convert_fusion.2
  426.2 2.0 broadcast_select_fusion.2
  428.5 2.8 maximum_convert_fusion
  (339 shorter events, 82.8 us)
Async XLA Ops:
  7.4 3.8 collective-permute-start.1
  9.3 6.1 %collective-permute-start = (bf16[1064,768]{1,0:T(8,128)(2,1)S(1)}, bf16[1064,768]{1,0:T(8,128)(2,1)}, u32[]{:S(2)}, u32[]{:S(2)}) collective-permute-start(bf16[1064,768]{1,0:T(8,128)(2,1)S(1)} %pack.1.tokens), channel_id=1, source_target_pairs={{1,2},{2,1},{5,6},{6,5},{9,10},{10,9},{13,14},{14,13},{17,18},{18,... | collective-permute-start | bytes 4902920 | tf_op jit(solution)/shard_map/ppermute | solution.py:1051
  11.1 1.7 collective-permute-start.2
  16.6 35.8 %collective-permute-start.3 = (bf16[1064,768]{1,0:T(8,128)(2,1)S(1)}, bf16[1064,768]{1,0:T(8,128)(2,1)}, u32[]{:S(2)}, u32[]{:S(2)}) collective-permute-start(bf16[1064,768]{1,0:T(8,128)(2,1)S(1)} %broadcast_select_fusion.own.tokens.refs_8_), channel_id=1, source_target_pairs={{0,2},{2,0},{1,3},{3,1},{4,6},{6,4},{5,7},{7,5},{8,10},{10,8},{9,1... | collective-permute-start | bytes 4902920 | tf_op jit(solution)/shard_map/ppermute | solution.py:1054
  48.9 61.1 %collective-permute-start.6 = (bf16[1728,768]{1,0:T(8,128)(2,1)}, bf16[1728,768]{1,0:T(8,128)(2,1)}, u32[]{:S(2)}, u32[]{:S(2)}) collective-permute-start(bf16[1728,768]{1,0:T(8,128)(2,1)} %pad_maximum_fusion), channel_id=1, source_target_pairs={{0,1},{1,0},{2,3},{3,2},{4,5},{5,4},{6,7},{7,6},{8,9},{9,8},{10,11... | collective-permute-start | bytes 7962632 | tf_op jit(solution)/shard_map/ppermute | solution.py:1057
  110.1 9.0 %collective-permute-start.7 = (bf16[1728,768]{1,0:T(8,128)(2,1)}, bf16[1728,768]{1,0:T(8,128)(2,1)}, u32[]{:S(2)}, u32[]{:S(2)}) collective-permute-start(bf16[1728,768]{1,0:T(8,128)(2,1)} %collective-permute-done.6.got_a), channel_id=1, source_target_pairs={{0,2},{2,0},{1,3},{3,1},{4,6},{6,4},{5,7},{7,5},{8,10},{10,8},{9,1... | collective-permute-start | bytes 7962632 | tf_op jit(solution)/shard_map/ppermute | solution.py:1054
  110.1 8.4 %collective-permute-start.4 = (bf16[768,1152]{1,0:T(8,128)(2,1)S(1)}, bf16[768,1152]{1,0:T(8,128)(2,1)}, u32[]{:S(2)}, u32[]{:S(2)}) collective-permute-start(bf16[768,1152]{1,0:T(8,128)(2,1)S(1)} %copy-done.8), channel_id=1, source_target_pairs={{0,2},{2,0},{1,3},{3,1},{4,6},{6,4},{5,7},{7,5},{8,10},{10,8},{9,1... | collective-permute-start | bytes 5308424 | tf_op jit(solution)/shard_map/ppermute | solution.py:1054
  110.6 8.4 %collective-permute-start.5 = (bf16[1024,384]{1,0:T(8,128)(2,1)}, bf16[1024,384]{1,0:T(8,128)(2,1)}, u32[]{:S(2)}, u32[]{:S(2)}) collective-permute-start(bf16[1024,384]{1,0:T(8,128)(2,1)} %get-tuple-element.109), channel_id=1, source_target_pairs={{0,2},{2,0},{1,3},{3,1},{4,6},{6,4},{5,7},{7,5},{8,10},{10,8},{9,1... | collective-permute-start | bytes 2359304 | tf_op jit(solution)/shard_map/ppermute | solution.py:1054
  110.6 3.7 collective-permute-start.8
  163.3 4.6 %collective-permute-start.9 = (bf16[2,768,768]{2,1,0:T(8,128)(2,1)S(1)}, bf16[2,768,768]{2,1,0:T(8,128)(2,1)S(1)}, u32[]{:S(2)}, u32[]{:S(2)}) collective-permute-start(bf16[2,768,768]{2,1,0:T(8,128)(2,1)S(1)} %down_grad.2), channel_id=1, source_target_pairs={{0,2},{2,0},{1,3},{3,1},{4,6},{6,4},{5,7},{7,5},{8,10},{10,8},{9,1... | collective-permute-start | bytes 7077896 | tf_op jit(solution)/shard_map/ppermute | solution.py:1054
  169.2 28.3 %collective-permute-start.10 = (bf16[768,768]{1,0:T(8,128)(2,1)}, bf16[768,768]{1,0:T(8,128)(2,1)}, u32[]{:S(2)}, u32[]{:S(2)}) collective-permute-start(bf16[768,768]{1,0:T(8,128)(2,1)} %fusion.2), channel_id=1, source_target_pairs={{0,1},{1,0},{2,3},{3,2},{4,5},{5,4},{6,7},{7,6},{8,9},{9,8},{10,11... | collective-permute-start | bytes 3538952 | tf_op jit(solution)/shard_map/ppermute | solution.py:1057
  192.4 34.3 %collective-permute-start.14 = (bf16[1024,384]{1,0:T(8,128)(2,1)S(1)}, bf16[1024,384]{1,0:T(8,128)(2,1)S(1)}, u32[]{:S(2)}, u32[]{:S(2)}) collective-permute-start(bf16[1024,384]{1,0:T(8,128)(2,1)S(1)} %get-tuple-element.136), channel_id=1, source_target_pairs={{0,2},{2,0},{1,3},{3,1},{4,6},{6,4},{5,7},{7,5},{8,10},{10,8},{9,1... | collective-permute-start | bytes 2359304 | tf_op jit(solution)/shard_map/ppermute | solution.py:1054
  207.9 9.6 %collective-permute-start.13 = (bf16[2,960,768]{2,1,0:T(8,128)(2,1)S(1)}, bf16[2,960,768]{2,1,0:T(8,128)(2,1)}, u32[]{:S(2)}, u32[]{:S(2)}) collective-permute-start(bf16[2,960,768]{2,1,0:T(8,128)(2,1)S(1)} %up_grad.2), channel_id=1, source_target_pairs={{0,2},{2,0},{1,3},{3,1},{4,6},{6,4},{5,7},{7,5},{8,10},{10,8},{9,1... | collective-permute-start | bytes 8847368 | tf_op jit(solution)/shard_map/ppermute | solution.py:1054
  207.9 16.3 %collective-permute-start.12 = (bf16[384,768]{1,0:T(8,128)(2,1)S(1)}, bf16[384,768]{1,0:T(8,128)(2,1)S(1)}, u32[]{:S(2)}, u32[]{:S(2)}) collective-permute-start(bf16[384,768]{1,0:T(8,128)(2,1)S(1)} %fusion.4), channel_id=1, source_target_pairs={{0,4},{4,0},{8,12},{12,8},{16,20},{20,16},{24,28},{28,24},{1,5},{5... | collective-permute-start | bytes 1769480 | tf_op jit(solution)/shard_map/ppermute | solution.py:1066
  215.1 40.7 %collective-permute-start.11 = (f32[1024,768]{1,0:T(8,128)}, f32[1024,768]{1,0:T(8,128)}, u32[]{:S(2)}, u32[]{:S(2)}) collective-permute-start(f32[1024,768]{1,0:T(8,128)} %get-tuple-element.133.residual), channel_id=1, source_target_pairs={{1,2},{2,1},{5,6},{6,5},{9,10},{10,9},{13,14},{14,13},{17,18},{18,... | collective-permute-start | bytes 9437192 | tf_op jit(solution)/shard_map/ppermute | solution.py:1051
  223.6 36.7 %collective-permute-start.17 = (bf16[2,480,768]{2,1,0:T(8,128)(2,1)}, bf16[2,480,768]{2,1,0:T(8,128)(2,1)}, u32[]{:S(2)}, u32[]{:S(2)}) collective-permute-start(bf16[2,480,768]{2,1,0:T(8,128)(2,1)} %fusion), channel_id=1, source_target_pairs={{0,4},{4,0},{8,12},{12,8},{16,20},{20,16},{24,28},{28,24},{1,5},{5... | collective-permute-start | bytes 4423688 | tf_op jit(solution)/shard_map/ppermute | solution.py:1066
  225.1 30.6 %collective-permute-start.15 = (bf16[192,768]{1,0:T(8,128)(2,1)}, bf16[192,768]{1,0:T(8,128)(2,1)}, u32[]{:S(2)}, u32[]{:S(2)}) collective-permute-start(bf16[192,768]{1,0:T(8,128)(2,1)} %fusion.9), channel_id=1, source_target_pairs={{0,8},{4,12},{8,0},{12,4},{16,24},{20,28},{24,16},{28,20},{1,9},{5... | collective-permute-start | bytes 884744 | tf_op jit(solution)/shard_map/ppermute | solution.py:1066
  254.9 9.0 %collective-permute-start.18 = (bf16[1024,384]{1,0:T(8,128)(2,1)S(1)}, bf16[1024,384]{1,0:T(8,128)(2,1)S(1)}, u32[]{:S(2)}, u32[]{:S(2)}) collective-permute-start(bf16[1024,384]{1,0:T(8,128)(2,1)S(1)} %get-tuple-element.142.refs_0_), channel_id=1, source_target_pairs={{0,2},{2,0},{1,3},{3,1},{4,6},{6,4},{5,7},{7,5},{8,10},{10,8},{9,1... | collective-permute-start | bytes 2359304 | tf_op jit(solution)/shard_map/ppermute | solution.py:1054
  257.7 34.3 %collective-permute-start.16 = (bf16[192,768]{1,0:T(8,128)(2,1)}, bf16[192,768]{1,0:T(8,128)(2,1)}, u32[]{:S(2)}, u32[]{:S(2)}) collective-permute-start(bf16[192,768]{1,0:T(8,128)(2,1)} %fusion.7), channel_id=1, source_target_pairs={{0,16},{4,20},{8,24},{12,28},{16,0},{20,4},{24,8},{28,12},{1,17},{... | collective-permute-start | bytes 884744 | tf_op jit(solution)/shard_map/ppermute | solution.py:1066
  263.9 29.4 %collective-permute-start.19 = (bf16[480,768]{1,0:T(8,128)(2,1)}, bf16[480,768]{1,0:T(8,128)(2,1)}, u32[]{:S(2)}, u32[]{:S(2)}) collective-permute-start(bf16[480,768]{1,0:T(8,128)(2,1)} %fusion.3), channel_id=1, source_target_pairs={{0,1},{1,0},{2,3},{3,2},{4,5},{5,4},{6,7},{7,6},{8,9},{9,8},{10,11... | collective-permute-start | bytes 2211848 | tf_op jit(solution)/shard_map/ppermute | solution.py:1057
  291.8 23.0 %collective-permute-start.24 = (bf16[1024,384]{1,0:T(8,128)(2,1)S(1)}, bf16[1024,384]{1,0:T(8,128)(2,1)S(1)}, u32[]{:S(2)}, u32[]{:S(2)}) collective-permute-start(bf16[1024,384]{1,0:T(8,128)(2,1)S(1)} %get-tuple-element.147.refs_1_), channel_id=1, source_target_pairs={{0,2},{2,0},{1,3},{3,1},{4,6},{6,4},{5,7},{7,5},{8,10},{10,8},{9,1... | collective-permute-start | bytes 2359304 | tf_op jit(solution)/shard_map/ppermute | solution.py:1054
  293.2 9.9 %collective-permute-start.23 = (bf16[192,768]{1,0:T(8,128)(2,1)S(1)}, bf16[192,768]{1,0:T(8,128)(2,1)S(1)}, u32[]{:S(2)}, u32[]{:S(2)}) collective-permute-start(bf16[192,768]{1,0:T(8,128)(2,1)S(1)} %add_convert_fusion.3), channel_id=1, source_target_pairs={{0,8},{4,12},{8,0},{12,4},{16,24},{20,28},{24,16},{28,20},{1,9},{5... | collective-permute-start | bytes 884744 | tf_op jit(solution)/shard_map/ppermute | solution.py:1066
  295.2 15.2 %collective-permute-start.22 = (bf16[240,768]{1,0:T(8,128)(2,1)S(1)}, bf16[240,768]{1,0:T(8,128)(2,1)S(1)}, u32[]{:S(2)}, u32[]{:S(2)}) collective-permute-start(bf16[240,768]{1,0:T(8,128)(2,1)S(1)} %fusion.8), channel_id=1, source_target_pairs={{0,8},{4,12},{8,0},{12,4},{16,24},{20,28},{24,16},{28,20},{1,9},{5... | collective-permute-start | bytes 1105928 | tf_op jit(solution)/shard_map/ppermute | solution.py:1066
  303.1 10.6 %collective-permute-start.20 = (bf16[384,768]{1,0:T(8,128)(2,1)S(1)}, bf16[384,768]{1,0:T(8,128)(2,1)S(1)}, u32[]{:S(2)}, u32[]{:S(2)}) collective-permute-start(bf16[384,768]{1,0:T(8,128)(2,1)S(1)} %get-tuple-element.155), channel_id=1, source_target_pairs={{0,2},{2,0},{1,3},{3,1},{4,6},{6,4},{5,7},{7,5},{8,10},{10,8},{9,1... | collective-permute-start | bytes 1769480 | tf_op jit(solution)/shard_map/ppermute | solution.py:1054
  304.1 46.4 %collective-permute-start.48 = (bf16[384,768]{1,0:T(8,128)(2,1)}, bf16[384,768]{1,0:T(8,128)(2,1)}, u32[]{:S(2)}, u32[]{:S(2)}) collective-permute-start(bf16[384,768]{1,0:T(8,128)(2,1)} %pad_maximum_fusion.4), channel_id=1, source_target_pairs={{0,4},{4,0},{8,12},{12,8},{16,20},{20,16},{24,28},{28,24},{1,5},{5... | collective-permute-start | bytes 1769480 | tf_op jit(solution)/shard_map/ppermute | solution.py:1066
  311.3 31.7 %collective-permute-start.26 = (bf16[240,768]{1,0:T(8,128)(2,1)}, bf16[240,768]{1,0:T(8,128)(2,1)}, u32[]{:S(2)}, u32[]{:S(2)}) collective-permute-start(bf16[240,768]{1,0:T(8,128)(2,1)} %fusion.5), channel_id=1, source_target_pairs={{0,16},{4,20},{8,24},{12,28},{16,0},{20,4},{24,8},{28,12},{1,17},{... | collective-permute-start | bytes 1105928 | tf_op jit(solution)/shard_map/ppermute | solution.py:1066
  314.7 29.6 %collective-permute-start.21 = (bf16[384,768]{1,0:T(8,128)(2,1)}, bf16[384,768]{1,0:T(8,128)(2,1)}, u32[]{:S(2)}, u32[]{:S(2)}) collective-permute-start(bf16[384,768]{1,0:T(8,128)(2,1)} %broadcast_select_fusion.11), channel_id=1, source_target_pairs={{0,1},{1,0},{2,3},{3,2},{4,5},{5,4},{6,7},{7,6},{8,9},{9,8},{10,11... | collective-permute-start | bytes 1769480 | tf_op jit(solution)/shard_map/ppermute | solution.py:1057
  342.9 15.7 %collective-permute-start.30 = (bf16[1024,384]{1,0:T(8,128)(2,1)S(1)}, bf16[1024,384]{1,0:T(8,128)(2,1)S(1)}, u32[]{:S(2)}, u32[]{:S(2)}) collective-permute-start(bf16[1024,384]{1,0:T(8,128)(2,1)S(1)} %get-tuple-element.159.refs_0_), channel_id=1, source_target_pairs={{0,2},{2,0},{1,3},{3,1},{4,6},{6,4},{5,7},{7,5},{8,10},{10,8},{9,1... | collective-permute-start | bytes 2359304 | tf_op jit(solution)/shard_map/ppermute | solution.py:1054
  344.2 11.0 %collective-permute-start.31 = (bf16[240,768]{1,0:T(8,128)(2,1)S(1)}, bf16[240,768]{1,0:T(8,128)(2,1)S(1)}, u32[]{:S(2)}, u32[]{:S(2)}) collective-permute-start(bf16[240,768]{1,0:T(8,128)(2,1)S(1)} %add_convert_fusion.1), channel_id=1, source_target_pairs={{0,8},{4,12},{8,0},{12,4},{16,24},{20,28},{24,16},{28,20},{1,9},{5... | collective-permute-start | bytes 1105928 | tf_op jit(solution)/shard_map/ppermute | solution.py:1066
  345.9 9.5 %collective-permute-start.25 = (bf16[192,768]{1,0:T(8,128)(2,1)S(1)}, bf16[192,768]{1,0:T(8,128)(2,1)S(1)}, u32[]{:S(2)}, u32[]{:S(2)}) collective-permute-start(bf16[192,768]{1,0:T(8,128)(2,1)S(1)} %fusion.10), channel_id=1, source_target_pairs={{0,4},{4,0},{8,12},{12,8},{16,20},{20,16},{24,28},{28,24},{1,5},{5... | collective-permute-start | bytes 884744 | tf_op jit(solution)/shard_map/ppermute | solution.py:1066
  352.0 37.7 %collective-permute-start.49 = (bf16[768,768]{1,0:T(8,128)(2,1)S(1)}, bf16[768,768]{1,0:T(8,128)(2,1)S(1)}, u32[]{:S(2)}, u32[]{:S(2)}) collective-permute-start(bf16[768,768]{1,0:T(8,128)(2,1)S(1)} %pad_maximum_fusion.2), channel_id=1, source_target_pairs={{0,2},{2,0},{1,3},{3,1},{4,6},{6,4},{5,7},{7,5},{8,10},{10,8},{9,1... | collective-permute-start | bytes 3538952 | tf_op jit(solution)/shard_map/ppermute | solution.py:1054
  356.8 10.2 %collective-permute-start.29 = (bf16[384,384]{1,0:T(8,128)(2,1)S(1)}, bf16[384,384]{1,0:T(8,128)(2,1)S(1)}, u32[]{:S(2)}, u32[]{:S(2)}) collective-permute-start(bf16[384,384]{1,0:T(8,128)(2,1)S(1)} %broadcast_select_fusion.18), channel_id=1, source_target_pairs={{0,1},{1,0},{2,3},{3,2},{4,5},{5,4},{6,7},{7,6},{8,9},{9,8},{10,11... | collective-permute-start | bytes 884744 | tf_op jit(solution)/shard_map/ppermute | solution.py:1057
  357.3 11.2 %collective-permute-start.27 = (bf16[192,768]{1,0:T(8,128)(2,1)S(1)}, bf16[192,768]{1,0:T(8,128)(2,1)S(1)}, u32[]{:S(2)}, u32[]{:S(2)}) collective-permute-start(bf16[192,768]{1,0:T(8,128)(2,1)S(1)} %fusion.12), channel_id=1, source_target_pairs={{0,8},{4,12},{8,0},{12,4},{16,24},{20,28},{24,16},{28,20},{1,9},{5... | collective-permute-start | bytes 884744 | tf_op jit(solution)/shard_map/ppermute | solution.py:1066
  366.9 1.7 collective-permute-start.34
  367.2 6.7 %collective-permute-start.36 = (bf16[192,384]{1,0:T(8,128)(2,1)S(1)}, bf16[192,384]{1,0:T(8,128)(2,1)S(1)}, u32[]{:S(2)}, u32[]{:S(2)}) collective-permute-start(bf16[192,384]{1,0:T(8,128)(2,1)S(1)} %fusion.13), channel_id=1, source_target_pairs={{0,4},{4,0},{8,12},{12,8},{16,20},{20,16},{24,28},{28,24},{1,5},{5... | collective-permute-start | bytes 442376 | tf_op jit(solution)/shard_map/ppermute | solution.py:1066
  368.6 8.7 %collective-permute-start.35 = (f32[24,768]{1,0:T(8,128)S(1)}, f32[24,768]{1,0:T(8,128)S(1)}, u32[]{:S(2)}, u32[]{:S(2)}) collective-permute-start(f32[24,768]{1,0:T(8,128)S(1)} %add.158), channel_id=1, source_target_pairs={{0,1},{1,0},{2,3},{3,2},{4,5},{5,4},{6,7},{7,6},{8,9},{9,8},{10,11... | collective-permute-start | bytes 221192 | tf_op jit(solution)/shard_map/ppermute | solution.py:1057
  369.4 20.8 %collective-permute-start.33 = (bf16[480,768]{1,0:T(8,128)(2,1)S(1)}, bf16[480,768]{1,0:T(8,128)(2,1)S(1)}, u32[]{:S(2)}, u32[]{:S(2)}) collective-permute-start(bf16[480,768]{1,0:T(8,128)(2,1)S(1)} %pad_maximum_fusion.3), channel_id=1, source_target_pairs={{0,4},{4,0},{8,12},{12,8},{16,20},{20,16},{24,28},{28,24},{1,5},{5... | collective-permute-start | bytes 2211848 | tf_op jit(solution)/shard_map/ppermute | solution.py:1066
  373.9 5.2 %collective-permute-start.38 = (bf16[192,384]{1,0:T(8,128)(2,1)S(1)}, bf16[192,384]{1,0:T(8,128)(2,1)S(1)}, u32[]{:S(2)}, u32[]{:S(2)}) collective-permute-start(bf16[192,384]{1,0:T(8,128)(2,1)S(1)} %fusion.14), channel_id=1, source_target_pairs={{0,8},{4,12},{8,0},{12,4},{16,24},{20,28},{24,16},{28,20},{1,9},{5... | collective-permute-start | bytes 442376 | tf_op jit(solution)/shard_map/ppermute | solution.py:1066
  376.6 27.1 %collective-permute-start.39 = (bf16[1024,768]{1,0:T(8,128)(2,1)S(1)}, bf16[1024,768]{1,0:T(8,128)(2,1)S(1)}, u32[]{:S(2)}, u32[]{:S(2)}) collective-permute-start(bf16[1024,768]{1,0:T(8,128)(2,1)S(1)} %get-tuple-element.188.grad), channel_id=1, source_target_pairs={{1,2},{2,1},{5,6},{6,5},{9,10},{10,9},{13,14},{14,13},{17,18},{18,... | collective-permute-start | bytes 4718600 | tf_op jit(solution)/shard_map/ppermute | solution.py:1051
  377.3 21.3 %collective-permute-start.32 = (bf16[192,768]{1,0:T(8,128)(2,1)S(1)}, bf16[192,768]{1,0:T(8,128)(2,1)S(1)}, u32[]{:S(2)}, u32[]{:S(2)}) collective-permute-start(bf16[192,768]{1,0:T(8,128)(2,1)S(1)} %fusion.6), channel_id=1, source_target_pairs={{0,16},{4,20},{8,24},{12,28},{16,0},{20,4},{24,8},{28,12},{1,17},{... | collective-permute-start | bytes 884744 | tf_op jit(solution)/shard_map/ppermute | solution.py:1066
  379.1 6.2 %collective-permute-start.37 = (f32[24,768]{1,0:T(8,128)S(1)}, f32[24,768]{1,0:T(8,128)S(1)}, u32[]{:S(2)}, u32[]{:S(2)}) collective-permute-start(f32[24,768]{1,0:T(8,128)S(1)} %add.160), channel_id=1, source_target_pairs={{0,8},{4,12},{8,0},{12,4},{16,24},{20,28},{24,16},{28,20},{1,9},{5... | collective-permute-start | bytes 221192 | tf_op jit(solution)/shard_map/ppermute | solution.py:1066
  385.3 24.8 %collective-permute-start.41 = (bf16[192,384]{1,0:T(8,128)(2,1)S(1)}, bf16[192,384]{1,0:T(8,128)(2,1)S(1)}, u32[]{:S(2)}, u32[]{:S(2)}) collective-permute-start(bf16[192,384]{1,0:T(8,128)(2,1)S(1)} %fusion.11), channel_id=1, source_target_pairs={{0,16},{4,20},{8,24},{12,28},{16,0},{20,4},{24,8},{28,12},{1,17},{... | collective-permute-start | bytes 442376 | tf_op jit(solution)/shard_map/ppermute | solution.py:1066
  389.6 21.5 %collective-permute-start.40 = (f32[24,768]{1,0:T(8,128)S(1)}, f32[24,768]{1,0:T(8,128)S(1)}, u32[]{:S(2)}, u32[]{:S(2)}) collective-permute-start(f32[24,768]{1,0:T(8,128)S(1)} %add.162), channel_id=1, source_target_pairs={{0,16},{4,20},{8,24},{12,28},{16,0},{20,4},{24,8},{28,12},{1,17},{... | collective-permute-start | bytes 221192 | tf_op jit(solution)/shard_map/ppermute | solution.py:1066
  398.8 12.2 %collective-permute-start.43 = (bf16[192,768]{1,0:T(8,128)(2,1)S(1)}, bf16[192,768]{1,0:T(8,128)(2,1)S(1)}, u32[]{:S(2)}, u32[]{:S(2)}) collective-permute-start(bf16[192,768]{1,0:T(8,128)(2,1)S(1)} %add_convert_fusion.2), channel_id=1, source_target_pairs={{0,4},{4,0},{8,12},{12,8},{16,20},{20,16},{24,28},{28,24},{1,5},{5... | collective-permute-start | bytes 884744 | tf_op jit(solution)/shard_map/ppermute | solution.py:1066
  403.6 22.6 %collective-permute-start.47 = (bf16[960,768]{1,0:T(8,128)(2,1)}, bf16[960,768]{1,0:T(8,128)(2,1)}, u32[]{:S(2)}, u32[]{:S(2)}) collective-permute-start(bf16[960,768]{1,0:T(8,128)(2,1)} %pad_maximum_fusion.1), channel_id=1, source_target_pairs={{0,2},{2,0},{1,3},{3,1},{4,6},{6,4},{5,7},{7,5},{8,10},{10,8},{9,1... | collective-permute-start | bytes 4423688 | tf_op jit(solution)/shard_map/ppermute | solution.py:1054
  410.1 10.3 %collective-permute-start.45 = (bf16[192,384]{1,0:T(8,128)(2,1)S(1)}, bf16[192,384]{1,0:T(8,128)(2,1)S(1)}, u32[]{:S(2)}, u32[]{:S(2)}) collective-permute-start(bf16[192,384]{1,0:T(8,128)(2,1)S(1)} %add_convert_fusion.4), channel_id=1, source_target_pairs={{0,4},{4,0},{8,12},{12,8},{16,20},{20,16},{24,28},{28,24},{1,5},{5... | collective-permute-start | bytes 442376 | tf_op jit(solution)/shard_map/ppermute | solution.py:1066
  411.1 6.9 %collective-permute-start.42 = (f32[24,768]{1,0:T(8,128)S(1)}, f32[24,768]{1,0:T(8,128)S(1)}, u32[]{:S(2)}, u32[]{:S(2)}) collective-permute-start(f32[24,768]{1,0:T(8,128)S(1)} %add.165), channel_id=1, source_target_pairs={{0,4},{4,0},{8,12},{12,8},{16,20},{20,16},{24,28},{28,24},{1,5},{5... | collective-permute-start | bytes 221192 | tf_op jit(solution)/shard_map/ppermute | solution.py:1066
  413.2 9.1 %collective-permute-start.44 = (bf16[384,768]{1,0:T(8,128)(2,1)}, bf16[384,768]{1,0:T(8,128)(2,1)}, u32[]{:S(2)}, u32[]{:S(2)}) collective-permute-start(bf16[384,768]{1,0:T(8,128)(2,1)} %pad_maximum_fusion.5), channel_id=1, source_target_pairs={{0,2},{2,0},{1,3},{3,1},{4,6},{6,4},{5,7},{7,5},{8,10},{10,8},{9,1... | collective-permute-start | bytes 1769480 | tf_op jit(solution)/shard_map/ppermute | solution.py:1054
  (86 other events, 1041.1 us)

commit v2 on v1

--- a/solution.py
+++ b/solution.py
@@ -104,7 +104,7 @@
         in_specs=[pl.BlockSpec(x.shape) for x in (tokens, cot, offset, count)],
         out_specs=pl.BlockSpec((rows, width)),
         out_shape=jax.ShapeDtypeStruct((rows, width), BF16),
-        compiler_params=pltpu.CompilerParams(vmem_limit_bytes=16 * 1024 * 1024),
+        compiler_params=pltpu.CompilerParams(vmem_limit_bytes=8 * 1024 * 1024),
         cost_estimate=cost(0, 4 * rows * width),
         name="pack",
     )(tokens, cot, offset, count)
@@ -137,7 +137,7 @@
             out_specs=held(mine.shape),
         ),
         out_shape=jax.ShapeDtypeStruct(mine.shape, BF16),
-        compiler_params=params(1, 24),
+        compiler_params=params(1, 10),
         cost_estimate=cost(0, 0),
         name="relay",
     )(scal, mine, first, second)
@@ -188,7 +188,7 @@
 
 def clip_edge(count, frames_here, half_rows):
     return jnp.where(
-        count <= frames_here,
+        count < frames_here,
         count * FRAME_TOK,
         half_rows + (count - frames_here) * FRAME_TOK,
     )
@@ -230,7 +230,7 @@
             jax.ShapeDtypeStruct((rows, 128), BF16),
             jax.ShapeDtypeStruct((rows, 128), BF16),
         ],
-        compiler_params=params(1, 22),
+        compiler_params=params(1, 10),
         cost_estimate=cost(2 * rows * width * cols, 4 * rows * width + 2 * rows * cols),
         name="project",
     )(scal, oth, own, gain, shift, weight)
@@ -370,38 +370,38 @@
             jax.ShapeDtypeStruct((rows // 2, width), F32),
             jax.ShapeDtypeStruct((pairs, half, 8, BLK), F32),
         ],
-        compiler_params=params(1, 40),
+        compiler_params=params(1, 28),
         cost_estimate=cost(8 * rows * rows * width, 16 * rows * width),
         name="attend",
     )(scal, qkv, qfeat, qkv, kfeat)
 
 
-def gather_out_weight(scal, own_out, got_a, got_b, out_weight, hid):
+def gather_out_weight(scal, own_out, got_up, more_up, out_weight, hid):
     core, plane = scal[0], scal[1]
     share = own_out.shape[0]
     quarter = share // 2
     out_weight[pl.ds(pl.multiple_of(plane * share, 64), share), :] = own_out[...]
     base = (1 - plane) * share
-    out_weight[pl.ds(pl.multiple_of(base + core * quarter, 64), quarter), :] = got_a[
-        2 * hid : 2 * hid + quarter, :
+    out_weight[pl.ds(pl.multiple_of(base + core * quarter, 64), quarter), :] = got_up[
+        hid : hid + quarter, :
     ]
-    out_weight[pl.ds(pl.multiple_of(base + (1 - core) * quarter, 64), quarter), :] = got_b[
-        2 * hid : 2 * hid + quarter, :
+    out_weight[pl.ds(pl.multiple_of(base + (1 - core) * quarter, 64), quarter), :] = more_up[
+        hid : hid + quarter, :
     ]
 
 
-def up_weight(core, own_up, got_a, got_b, chunk):
-    hid = got_a.shape[1]
+def up_weight(core, own_up, got_up, more_up, chunk):
+    hid = got_up.shape[1]
     if chunk < 2:
-        return (got_b, got_a)[chunk][hid : 2 * hid, :]
+        return (more_up, got_up)[chunk][:hid, :]
     pick = (1 - core) if chunk == 2 else core
     return own_up[:, pl.ds(pl.multiple_of(pick * hid, 128), hid)]
 
 
-def down_weight(core, own_down, got_a, got_b, chunk):
-    hid = got_a.shape[1]
+def down_weight(core, own_down, got_down, more_down, chunk):
+    hid = got_down.shape[1]
     if chunk < 2:
-        return (got_b, got_a)[chunk][:hid, :]
+        return (more_down, got_down)[chunk][...]
     pick = (1 - core) if chunk == 2 else core
     return own_down[pl.ds(pl.multiple_of(pick * hid, 128), hid), :]
 
@@ -416,8 +416,10 @@
     own_out,
     own_up,
     own_down,
-    got_a,
-    got_b,
+    got_up,
+    got_down,
+    more_up,
+    more_down,
     up_offset,
     gains,
     shifts,
@@ -428,7 +430,6 @@
     out_grad_out,
     xhat_out,
     scale_out,
-    hidden_out,
     slope_out,
     second_out,
     out_low_out,
@@ -436,23 +437,33 @@
     pooled,
     learner_sums,
     learner_offset_sums,
+    theirs_out,
+    mine_out,
     out_weight,
+    hidden_kept,
+    down_total,
 ):
     step = pl.program_id(0)
     core, plane = scal[0], scal[1]
-    hid = got_a.shape[1]
+    hid = got_up.shape[1]
     share = own_out.shape[0]
 
     @pl.when(step == 0)
     def _():
-        gather_out_weight(scal, own_out, got_a, got_b, out_weight, hid)
-        for ref in (sums, pooled, learner_sums, learner_offset_sums):
+        gather_out_weight(scal, own_out, got_up, more_up, out_weight, hid)
+        for ref in (sums, pooled, learner_sums, learner_offset_sums, down_total):
             ref[...] = jnp.zeros_like(ref)
 
     def up_bias(chunk):
-        side = (1 - plane) if chunk < 2 else plane
         pick = (1 - core) if chunk % 2 == 0 else core
-        return up_offset[pl.ds(2 * side + pick, 1), :]
+        if chunk >= 2:
+            return up_offset[pl.ds(pick, 1), :]
+        note = got_up[hid + share // 2 :, :].astype(F32)
+        sums = [
+            note[3 * i : 3 * i + 1] + note[3 * i + 1 : 3 * i + 2] + note[3 * i + 2 : 3 * i + 3]
+            for i in range(2)
+        ]
+        return jnp.where(pick == 0, sums[0], sums[1])
 
     mine = pl.ds(pl.multiple_of(core * share, 64), share)
     theirs = pl.ds(pl.multiple_of((1 - core) * share, 64), share)
@@ -466,15 +477,15 @@
     block_out = residual + down_offset[...]
     for chunk in range(4):
         cols = slice(chunk * hid, (chunk + 1) * hid)
-        pre = nn(second, up_weight(core, own_up, got_a, got_b, chunk)) + up_bias(chunk)
+        pre = nn(second, up_weight(core, own_up, got_up, more_up, chunk)) + up_bias(chunk)
         square = pre * pre
         gate = 0.5 + 0.5 * jnp.tanh(pre * (GELU_C + (GELU_A * GELU_C) * square))
         product = pre * gate
         hidden = product.astype(BF16)
         bend = (1.0 - gate) * (2.0 * GELU_C + (6.0 * GELU_A * GELU_C) * square)
         slope_out[:, cols] = (gate + product * bend).astype(BF16)
-        hidden_out[:, cols] = hidden
-        block_out = block_out + nn(hidden, down_weight(core, own_down, got_a, got_b, chunk))
+        hidden_kept[:, cols] = hidden
+        block_out = block_out + nn(hidden, down_weight(core, own_down, got_down, more_down, chunk))
     xhat_three, scale_three = centre(block_out)
     third = (xhat_three * gains[2:3, :] + shifts[2:3, :]).astype(BF16)
     logits = nt(third, learner[...]) + learner_offset[...]
@@ -497,7 +508,16 @@
     out_grad = pool_grad + norm_back(xhat_three, scale_three, gains[2:3, :], third_grad)
     sums[16:24, :] += fold8(out_grad)
     out_grad_out[...] = out_grad
-    out_low_out[...] = out_grad.astype(BF16)
+    out_low = out_grad.astype(BF16)
+    out_low_out[...] = out_low
+    for chunk in range(4):
+        down_total[chunk] += tn(hidden_kept[:, chunk * hid : (chunk + 1) * hid], out_low)
+
+    @pl.when(step == pl.num_programs(0) - 1)
+    def _():
+        for n in range(2):
+            theirs_out[n] = down_total[2 * n].astype(BF16)
+            mine_out[n] = down_total[2 * n + 1].astype(BF16)
 
 
 def behind_kernel(
@@ -508,43 +528,51 @@
     xhat_two,
     scale_two,
     slope,
+    second,
+    mixed_own,
+    mixed_oth,
     own_out,
     own_up,
     own_down,
-    got_a,
-    got_b,
+    got_up,
+    got_down,
+    more_up,
+    more_down,
     gains,
     pooled,
     residual_grad_out,
     grad_own,
     grad_oth,
-    pre_grad_out,
-    residual_low_out,
     sums,
     up_sums,
+    theirs_out,
+    mine_out,
     out_weight,
+    up_total,
+    out_total,
 ):
-    core = scal[0]
-    hid = got_a.shape[1]
+    core, plane = scal[0], scal[1]
+    hid = got_up.shape[1]
     share = own_out.shape[0]
 
     @pl.when(pl.program_id(0) == 0)
     def _():
-        gather_out_weight(scal, own_out, got_a, got_b, out_weight, hid)
-        for ref in (sums, up_sums):
+        gather_out_weight(scal, own_out, got_up, more_up, out_weight, hid)
+        for ref in (sums, up_sums, up_total, out_total):
             ref[...] = jnp.zeros_like(ref)
 
     mine = pl.ds(pl.multiple_of(core * share, 64), share)
     theirs = pl.ds(pl.multiple_of((1 - core) * share, 64), share)
     low = out_low[...]
+    second_turned = second[...].T
     second_grad = None
     for chunk in range(4):
         cols = slice(chunk * hid, (chunk + 1) * hid)
-        hidden_grad = nt(low, down_weight(core, own_down, got_a, got_b, chunk))
+        hidden_grad = nt(low, down_weight(core, own_down, got_down, more_down, chunk))
         pre_grad = (hidden_grad * slope[:, cols].astype(F32)).astype(BF16)
-        pre_grad_out[:, cols] = pre_grad
+        up_total[chunk] += nn(second_turned, pre_grad)
         up_sums[:, cols] += fold8(pre_grad.astype(F32))
-        term = nt(pre_grad, up_weight(core, own_up, got_a, got_b, chunk))
+        term = nt(pre_grad, up_weight(core, own_up, got_up, more_up, chunk))
         second_grad = term if second_grad is None else second_grad + term
     xhat = xhat_two[...]
     sums[0:8, :] += fold8(second_grad * xhat)
@@ -560,9 +588,23 @@
         residual_grad_out[BLK - pooled_rows :, :] = pooled[:pooled_rows, :]
 
     residual_low = residual_grad.astype(BF16)
-    residual_low_out[...] = residual_low
     grad_own[...] = nt(residual_low, out_weight[mine, :]).astype(BF16)
     grad_oth[...] = nt(residual_low, out_weight[theirs, :]).astype(BF16)
+    out_total[0] += tn(mixed_own[...], residual_low)
+    out_total[1] += tn(mixed_oth[...], residual_low)
+
+    @pl.when(pl.program_id(0) == pl.num_programs(0) - 1)
+    def _():
+        width = second.shape[1]
+        half = width // 2
+        for odd, (out, column) in enumerate(((theirs_out, 1 - core), (mine_out, core))):
+            for n in range(2):
+                out[n, :width, :] = up_total[2 * n + odd].astype(BF16)
+                side = (1 - plane) if n == 0 else plane
+                at = pl.ds(pl.multiple_of(column * half, 128), half)
+                grad = out_total[jnp.where(side == core, 0, 1), :, at].astype(BF16)
+                out[n, width:, :half] = grad[: share // 2]
+                out[n, width:, half:] = grad[share // 2 :]
 
 
 def row_block(cols):
@@ -573,7 +615,7 @@
     return pl.BlockSpec(shape, lambda *_: (0,) * len(shape))
 
 
-def row_call(kernel, name, scal, rowed, wholes, row_outs, held_outs, scratch, flops, mib):
+def row_call(kernel, name, scal, rowed, wholes, row_outs, held_outs, scratch, flops, mib, low_outs=()):
     rows = rowed[0].shape[0]
     nbytes = sum(x.size * x.dtype.itemsize for x in wholes)
     nbytes += rows * sum(c * (2 if t == BF16 else 4) for c, t in row_outs)
@@ -583,11 +625,14 @@
             num_scalar_prefetch=1,
             grid=(rows // BLK,),
             in_specs=[row_block(x.shape[1]) for x in rowed] + [whole(x.shape) for x in wholes],
-            out_specs=[row_block(cols) for cols, _ in row_outs] + [held(s) for s in held_outs],
+            out_specs=[row_block(cols) for cols, _ in row_outs]
+            + [held(s) for s in held_outs]
+            + [whole(s) for s in low_outs],
             scratch_shapes=scratch,
         ),
         out_shape=[jax.ShapeDtypeStruct((rows, cols), t) for cols, t in row_outs]
-        + [jax.ShapeDtypeStruct(s, F32) for s in held_outs],
+        + [jax.ShapeDtypeStruct(s, F32) for s in held_outs]
+        + [jax.ShapeDtypeStruct(s, BF16) for s in low_outs],
         compiler_params=params(1, mib),
         cost_estimate=cost(flops, nbytes),
         name=name,
@@ -597,7 +642,7 @@
 def ahead(scal, mixed_own, mixed_oth, packed, cot, weights, up_offset, small, frames_here):
     rows, share = mixed_own.shape
     width = packed.shape[1]
-    hidden = up_offset.size
+    hidden = 2 * up_offset.size
     return row_call(
         functools.partial(ahead_kernel, frames_here),
         "ahead",
@@ -609,98 +654,43 @@
             (width, F32),
             (128, F32),
             (hidden, BF16),
-            (hidden, BF16),
             (width, BF16),
             (width, BF16),
         ],
         [(24, width), (128, width), (128, width), (8, 128)],
-        [pltpu.VMEM((2 * share, width), BF16)],
-        2 * rows * width * (2 * hidden + width),
-        40,
-    )
-
-
-def behind(scal, out_grad, out_low, xhat_two, scale_two, slope, weights, gains, pooled, maps_all):
-    rows, width = out_grad.shape
+        [
+            pltpu.VMEM((2 * share, width), BF16),
+            pltpu.VMEM((BLK, hidden), BF16),
+            pltpu.VMEM((4, hidden // 4, width), F32),
+        ],
+        2 * rows * width * (3 * hidden + width),
+        42,
+        [(2, hidden // 4, width)] * 2,
+    )
+
+
+def behind(scal, rowed, weights, gains, pooled, maps_all):
+    rows, width = rowed[0].shape
     share = weights[0].shape[0]
-    hidden = slope.shape[1]
+    hidden = rowed[4].shape[1]
+    hid = hidden // 4
     return row_call(
         functools.partial(behind_kernel, maps_all),
         "behind",
         scal,
-        [out_grad, out_low, xhat_two, scale_two, slope],
+        rowed,
         [*weights, gains, pooled],
-        [(width, F32), (share, BF16), (share, BF16), (hidden, BF16), (width, BF16)],
+        [(width, F32), (share, BF16), (share, BF16)],
         [(24, width), (8, hidden)],
-        [pltpu.VMEM((2 * share, width), BF16)],
-        2 * rows * width * (2 * hidden + width),
-        40,
-    )
-
-
-def down_grad_kernel(scal, hidden, out_low, out):
-    out[0] = tn(hidden[...], out_low[...]).astype(BF16)
-
-
-def down_grad(scal, hidden, out_low):
-    rows, width = out_low.shape
-    hid = hidden.shape[1] // 4
-    return pl.pallas_call(
-        down_grad_kernel,
-        grid_spec=pltpu.PrefetchScalarGridSpec(
-            num_scalar_prefetch=1,
-            grid=(2,),
-            in_specs=[
-                pl.BlockSpec((rows, hid), lambda n, scal: (0, 2 * n + scal[3])),
-                whole((rows, width)),
-            ],
-            out_specs=pl.BlockSpec((1, hid, width), lambda n, *_: (n, 0, 0)),
-        ),
-        out_shape=jax.ShapeDtypeStruct((2, hid, width), BF16),
-        compiler_params=params(1, 14),
-        cost_estimate=cost(4 * rows * hid * width, 8 * rows * hid),
-        name="down_grad",
-    )(scal, hidden, out_low)
-
-
-def up_grad_kernel(scal, second, pre_grad, mixed_own, mixed_oth, residual_low, out):
-    step = pl.program_id(0)
-    core, plane = scal[0], scal[1]
-    width, hid = second.shape[1], pre_grad.shape[1]
-    share = mixed_own.shape[1]
-    out[0, :width, :] = tn(second[...], pre_grad[...]).astype(BF16)
-    side = jnp.where(step == 0, 1 - plane, plane)
-    column = jnp.where(scal[3] == 1, core, 1 - core)
-    lhs = jnp.where(side == core, mixed_own[...], mixed_oth[...])
-    rhs = residual_low[:, pl.ds(pl.multiple_of(column * (width // 2), 128), width // 2)]
-    grad = tn(lhs, rhs).astype(BF16)
-    out[0, width:, : width // 2] = grad[: share // 2]
-    out[0, width:, width // 2 :] = grad[share // 2 :]
-
-
-def up_grad(scal, second, pre_grad, mixed_own, mixed_oth, residual_low):
-    rows, width = second.shape
-    hid = pre_grad.shape[1] // 4
-    share = mixed_own.shape[1]
-    return pl.pallas_call(
-        up_grad_kernel,
-        grid_spec=pltpu.PrefetchScalarGridSpec(
-            num_scalar_prefetch=1,
-            grid=(2,),
-            in_specs=[
-                whole((rows, width)),
-                pl.BlockSpec((rows, hid), lambda n, scal: (0, 2 * n + scal[3])),
-                whole((rows, share)),
-                whole((rows, share)),
-                whole((rows, width)),
-            ],
-            out_specs=pl.BlockSpec((1, width + share // 2, hid), lambda n, *_: (n, 0, 0)),
-        ),
-        out_shape=jax.ShapeDtypeStruct((2, width + share // 2, hid), BF16),
-        compiler_params=params(1, 18),
-        cost_estimate=cost(4 * rows * hid * width * 1.25, 10 * rows * hid),
-        name="up_grad",
-    )(scal, second, pre_grad, mixed_own, mixed_oth, residual_low)
+        [
+            pltpu.VMEM((2 * share, width), BF16),
+            pltpu.VMEM((4, width, hid), F32),
+            pltpu.VMEM((2, share, width), F32),
+        ],
+        2 * rows * width * (3 * hidden + 2 * width),
+        44,
+        [(2, width + share // 2, hid)] * 2,
+    )
 
 
 def attend_back_kernel(
@@ -839,7 +829,7 @@
             ],
         ),
         out_shape=[jax.ShapeDtypeStruct((rows // 2, 384), BF16)] * 2,
-        compiler_params=params(1, 20),
+        compiler_params=params(1, 14),
         cost_estimate=cost(40 * rows * rows * 128, 30 * rows * 128),
         name="attend_back",
     )(scal, qkv, qkv, kfeat, qkv, qfeat, grad_oth, grad_own, *wide, *logs)
@@ -884,7 +874,7 @@
             jax.ShapeDtypeStruct((width // 2, cols), BF16),
             jax.ShapeDtypeStruct((8, cols), F32),
         ],
-        compiler_params=params(1, 18),
+        compiler_params=params(1, 12),
         cost_estimate=cost(2 * rows * width * cols, 2 * rows * (width + cols)),
         name="project_grad",
     )(scal, first, *oth, *own)
@@ -923,7 +913,7 @@
             jax.ShapeDtypeStruct((rows, width), BF16),
             jax.ShapeDtypeStruct((16, width), F32),
         ],
-        compiler_params=params(1, 18),
+        compiler_params=params(1, 12),
         cost_estimate=cost(
             4 * pairs * rows * width * cols, 4 * pairs * rows * cols + 4 * width * cols * pairs
         ),
@@ -950,7 +940,7 @@
             out_specs=row_block(width),
         ),
         out_shape=jax.ShapeDtypeStruct((tokens_here, width), F32),
-        compiler_params=params(1, 20),
+        compiler_params=params(1, 12),
         cost_estimate=cost(20 * rows * width, 12 * rows * width),
         name="last",
     )(scal, packed, grad, grad_got, residual, residual_got, gain)
@@ -1014,7 +1004,7 @@
             out_specs=held((24, width)),
         ),
         out_shape=jax.ShapeDtypeStruct((24, width), F32),
-        compiler_params=pltpu.CompilerParams(vmem_limit_bytes=16 * 1024 * 1024),
+        compiler_params=pltpu.CompilerParams(vmem_limit_bytes=6 * 1024 * 1024),
         cost_estimate=cost(0, 1 << 20),
         name="small_table",
     )(scal, *parts)
@@ -1086,7 +1076,8 @@
     pairs = share // 128
 
     weight_mine = attend_weight.reshape(width, 3 * share)
-    weight_part = lax.dynamic_slice_in_dim(weight_mine, side * (width // 2), width // 2, 0)
+    weight_part = lax.dynamic_slice_in_dim(attend_weight, side * (width // 2), width // 2, 0)
+    weight_part = weight_part.reshape(width // 2, 3 * share)
     weight_got = turn(weight_part)
     packed = pack(
         after(tokens, weight_part),
@@ -1096,7 +1087,6 @@
         half_rows,
     )
     got_packed = turn(packed)
-    expand_got = to_plane(after(expand_offset, packed))
     weight_rest = lax.ppermute(
         weight_got,
         ("chip", "core", "mp"),
@@ -1105,7 +1095,23 @@
     weight_here = relay(
         jnp.stack([core, plane, side]).astype(jnp.int32), weight_mine, weight_got, weight_rest
     )
-    own = jnp.where(straight, packed, after(got_packed, weight_here))
+    left, notes = expand_offset.reshape(2, hid), []
+    for _ in range(3):
+        notes.append(lax.reduce_precision(left, 8, 7))
+        left = left - notes[-1]
+    notes = jnp.stack(notes, axis=1).reshape(6, hid)
+    up_quarter = jnp.concatenate(
+        [
+            lax.dynamic_slice_in_dim(expand_weight, core * hid, hid, 1),
+            lax.dynamic_slice_in_dim(output_weight, core * (share // 2), share // 2, 0),
+            jnp.pad(notes, ((0, 10), (0, 0))).astype(BF16),
+        ],
+        axis=0,
+    )
+    down_quarter = lax.dynamic_slice_in_dim(contract_weight, core * hid, hid, 0)
+    own = jnp.where(
+        straight, packed, after(got_packed, weight_here, up_quarter, down_quarter)
+    )
     oth = to_core(own)
     count = own[tokens_here + NOTE + 3, 0].astype(jnp.int32)
     numbered = [
@@ -1114,20 +1120,8 @@
     ]
     scal = numbered[0]
 
-    quarter = jnp.concatenate(
-        [
-            lax.dynamic_slice_in_dim(contract_weight, core * hid, hid, 0),
-            lax.dynamic_slice_in_dim(expand_weight, core * hid, hid, 1),
-            lax.dynamic_slice_in_dim(output_weight, core * (share // 2), share // 2, 0),
-        ],
-        axis=0,
-    )
-    got_a = to_plane(after(quarter, own, weight_here))
-    up_offset = jnp.where(
-        plane == 0,
-        jnp.concatenate([expand_offset, expand_got]),
-        jnp.concatenate([expand_got, expand_offset]),
-    ).reshape(4, hid)
+    up_got_a = to_plane(after(up_quarter, own, weight_here))
+    down_got_a = to_plane(after(down_quarter, oth))
 
     first, qkv, qfeat, kfeat = project(
         scal,
@@ -1139,24 +1133,33 @@
         frames_here,
         half_rows,
     )
+    weight_there = to_core(after(weight_here, qkv))
     mixed_send, wide_oth, logs_oth = attend(numbered[0], qkv, qfeat, kfeat, frames_here)
     mixed_oth = to_core(mixed_send)
-    weight_there = to_core(after(weight_here, mixed_send))
+    up_got_b = to_core(after(up_got_a, mixed_send))
     mixed_own, wide_own, logs_own = attend(
-        after(numbered[1], mixed_send), qkv, qfeat, kfeat, frames_here
-    )
-    got_b = to_core(after(got_a, mixed_own))
+        after(numbered[1], mixed_send, weight_there), qkv, qfeat, kfeat, frames_here
+    )
+    down_got_b = to_core(after(down_got_a, mixed_own))
 
     maps_all = frames_here * MAPS
     cot = jnp.pad(own[half_rows:], ((0, 128 - maps_all), (0, 0)))
     learner = jnp.pad(jnp.tile(learner_weight.T, (frames_here, 1)), ((0, 128 - maps_all), (0, 0)))
     learner_bias = jnp.pad(jnp.tile(learner_offset, frames_here), (0, 128 - maps_all))[None]
-    weights = (output_weight, expand_weight, contract_weight, got_a, got_b)
+    weights = (
+        *(
+            pltpu.with_memory_space_constraint(x, pltpu.HBM)
+            for x in (output_weight, expand_weight, contract_weight)
+        ),
+        up_got_a,
+        down_got_a,
+        up_got_b,
+        down_got_b,
+    )
     (
         out_grad,
         xhat_two,
         scale_two,
-        hidden,
         slope,
         second,
         out_low,
@@ -1164,14 +1167,16 @@
         pooled,
         learner_sums,
         learner_offset_sums,
+        down_theirs,
+        down_mine,
     ) = ahead(
-        after(scal, weight_there),
+        scal,
         mixed_own,
         mixed_oth,
         own,
         cot,
         weights,
-        up_offset,
+        expand_offset.reshape(2, hid),
         (
             norm_gains,
             norm_shifts,
@@ -1183,9 +1188,7 @@
         frames_here,
     )
 
-    down_theirs = down_grad(numbered[0], hidden, out_low)
     down_got = to_core(down_theirs)
-    down_mine = down_grad(after(numbered[1], down_theirs), hidden, out_low)
     down_send = low(plus(down_got[0], down_mine[0]))
     down_keep = plus(down_got[1], down_mine[1])
     down_plane = to_plane(down_send)
@@ -1194,35 +1197,25 @@
         residual_grad,
         grad_own,
         grad_send,
-        pre_grad,
-        residual_low,
         sums_behind,
         up_sums,
+        up_theirs,
+        up_mine,
     ) = behind(
         after(scal, down_send),
-        out_grad,
-        out_low,
-        xhat_two,
-        scale_two,
-        slope,
+        [out_grad, out_low, xhat_two, scale_two, slope, second, mixed_own, mixed_oth],
         weights,
         norm_gains,
         pooled,
         maps_all,
     )
-    grad_oth = to_core(grad_send)
-    down_half = halves_of(plus(down_keep, after(down_plane, residual_low)))
+    down_half = halves_of(plus(down_keep, after(down_plane, residual_grad)))
     down_x_send = low(pick(down_half, 1 - side))
     down_x_keep = pick(down_half, side)
     down_x = hop(down_x_send, 1)
-    up_theirs = up_grad(
-        after(numbered[0], down_x_send), second, pre_grad, mixed_own, mixed_oth, residual_low
-    )
-    up_got = to_core(up_theirs)
-    up_mine = up_grad(
-        after(numbered[1], up_theirs), second, pre_grad, mixed_own, mixed_oth, residual_low
-    )
-    up_half = halves_of(plus(up_got, up_mine))
+    up_got = to_core(after(up_theirs, down_x_send))
+    grad_oth = to_core(after(grad_send, down_x_send))
+    up_half = halves_of(plus(up_got, after(up_mine, down_x_send)))
     up_x_send = low(lax.dynamic_index_in_dim(up_half, 1 - side, 1, keepdims=False))
     up_x_keep = lax.dynamic_index_in_dim(up_half, side, 1, keepdims=False)
     up_x = hop(up_x_send, 1)
@@ -1250,7 +1243,7 @@
         parts = halves_of(x)
         return low(pick(parts, 1 - bit)), pick(parts, bit)
 
-    residual_got = turn(after(residual_grad, up_mine))
+    residual_got = turn(after(residual_grad, up_x_send))
     down_send, down_keep = split(plus(down_x_keep, after(down_x, up_x_send)))
     down_z = hop(down_send, hops[0])
     oth_0, own_0 = back(0, down_send)
@@ -1328,32 +1321,38 @@
         offsets_2,
     )
 
-    late_half = halves_of(plus(late_keep, after(late_got, table)))
+    early_sum = plus(early_sum, after(early_z, table))
+    early_low = low(early_sum)
+    early_z = hop(early_low, hops[1])
+    late_half = halves_of(plus(late_keep, after(late_got, early_low)))
     late_send = low(pick(late_half, 1 - side))
     late_keep = pick(late_half, side)
     late_x = hop(late_send, 1)
-    early_sum = plus(early_sum, after(early_z, late_send))
-    early_low = low(early_sum)
-    early_z = hop(early_low, hops[1])
-    up_x = hop(after(up_sum, early_low), 1)
-    table = table + after(to_core(table), early_low)
+    table = table + after(to_core(table), late_send)
     table_got = to_plane(table)
+    up_x = hop(after(up_sum, table), 1)
     late_sum = plus(late_keep, after(late_x, table))
     late_low = low(late_sum)
     late_z = hop(late_low, hops[0])
     table = table + after(table_got, late_low)
-    table_got = hop(table, hops[0])
     late_sum = plus(late_sum, after(late_z, table))
     late_low = low(late_sum)
     late_z = hop(late_low, hops[1])
-    table = table + after(table_got, late_low)
+    table_got = hop(after(table, late_low), hops[0])
+    early_sum = rest(early_sum, after(early_z, late_low), hops[2:])
+    early_x = hop(early_sum, 1)
+    table = table + after(table_got, early_sum)
     table_got = hop(table, hops[1])
     up_sum = join(up_sum, after(up_x, table), side, 0)
     up_got = to_core(up_sum)
-    early_sum = rest(early_sum, after(early_z, up_sum), hops[2:])
-    early_x = hop(early_sum, 1)
+    late_sum = rest(late_sum, after(late_z, up_sum), hops[2:])
+    late_x = hop(late_sum, 1)
+    table = table + after(table_got, late_sum)
+    for step in hops[2:]:
+        table = table + hop(table, step)
+    table_got = hop(table, 1)
     tokens_gradient = last(
-        after(scal, early_sum),
+        after(scal, table),
         packed,
         first_low,
         first_got,
@@ -1362,12 +1361,8 @@
         norm_gains[0:1],
         tokens_here,
     )
-    late_sum = rest(late_sum, after(late_z, tokens_gradient), hops[2:])
-    late_x = hop(late_sum, 1)
-    table = table + after(table_got, late_sum)
-    for step in [*hops[2:], 1]:
-        table = table + hop(table, step)
-    early_sum = join(early_sum, after(early_x, late_sum), side, 0)
+    table = table + after(table_got, tokens_gradient)
+    early_sum = join(early_sum, after(early_x, tokens_gradient), side, 0)
     early_got = to_core(early_sum)
     late_sum = join(late_sum, after(late_x, early_sum), side, 0)
     late_got = to_core(late_sum)

time: 436 us -> 435 us (level)
  starting transfers between devices: 72.6 us -> 85.4 us
  waiting for transfers between devices: 44.1 us -> 32.9 us
  other arithmetic: 39.7 us -> 48.8 us
  Pallas kernels: 230 us -> 221 us
  local copies, waits for them, and re-layouts: 43.2 us -> 38.4 us
    pallas_call x2, Pallas kernels: 50 us -> 71.9 us  [row_call(): pl.pallas_call(kernel, grid_spec=pltpu.PrefetchScalarGridSpec(num_scalar_...]
    ppermute x21, starting transfers between devices: 28.3 us -> 48.3 us  [hop(): return lax.ppermute(x, 'chip', [(i, i ^ step) for i in range(chips)])]
    pallas_call x4 -> x0, Pallas kernels: 18.5 us -> none  [the longest x2 11.1 us: up_grad(): pl.pallas_call(up_grad_kernel, grid_spec=pltpu.PrefetchScalarGridSpec(num...]
    ppermute x21, waiting for transfers between devices: 31.4 us -> 16.4 us  [hop(): return lax.ppermute(x, 'chip', [(i, i ^ step) for i in range(chips)])]
    pallas_call x3, Pallas kernels: 83.9 us -> 74.1 us  [attend_back(): pl.pallas_call(functools.partial(attend_back_kernel, frames_here), grid_s...]
    unnamed x170 -> x206, local copies, waits for them, and re-layouts: 26.7 us -> 17.9 us
    ppermute x17 -> x18, starting transfers between devices: 28.6 us -> 22.6 us  [to_core(): return lax.ppermute(x, 'core', flip2)]
    convert_element_type x11, other arithmetic: 7.01 us -> 12.2 us  [low(): return x.astype(BF16)]
  transfers between devices with their start and end apart: 50 -> 51, of which waited for: 16 -> 9; matrix products, arithmetic and copies ran while one was open for 11% -> 12% of each run, Pallas kernels for 46% -> 42%
where the time goes in v2:
time: 435 us; the launch traced here: 430 us
  Pallas kernels  221 us (51%)
  starting transfers between devices  85.4 us (20%)
  other arithmetic  48.8 us (11%)
  local copies, waits for them, and re-layouts  38.4 us (9%)
  waiting for transfers between devices  32.9 us (8%)
    pallas_call x3, Pallas kernels, attend_back(): pl.pallas_call(functools.partial(attend_back_kernel, frames_here), grid_s...  74.1 us
    pallas_call x2, Pallas kernels, row_call(): pl.pallas_call(kernel, grid_spec=pltpu.PrefetchScalarGridSpec(num_scalar_...  71.9 us
    ppermute x21, starting transfers between devices, hop(): return lax.ppermute(x, 'chip', [(i, i ^ step) for i in range(chips)])  48.3 us
    pallas_call x2, Pallas kernels, attend(): pl.pallas_call(functools.partial(attend_kernel, frames_here, bk), grid_sp...  37.9 us
    ppermute x18, starting transfers between devices, to_core(): return lax.ppermute(x, 'core', flip2)  22.6 us
    unnamed x206, local copies, waits for them, and re-layouts  17.9 us
    ppermute x21, waiting for transfers between devices, hop(): return lax.ppermute(x, 'chip', [(i, i ^ step) for i in range(chips)])  16.4 us
    add x7, other arithmetic, plus(): return a.astype(F32) + b.astype(F32)  12.5 us
  transfers between devices with their start and end apart: 51, of which 9 were waited for; matrix products, arithmetic and copies ran while one was open for 12% of the time, Pallas kernels for 42%

profile of v2, /device:TPU:0, one launch (start us, length us, event | category | flops | bytes accessed | tf_op | source)
XLA Modules:
  0.0 429.6 jit_solution(13332501524999570634)
XLA Ops:
  0.7 3.8 copy.31
  11.0 2.7 copy.34.mine
  16.6 2.8 constant_dynamic-slice_fusion.2
  20.6 3.8 relay.1.weight.refs_6_
  24.6 18.4 %collective-permute-start.3 = (bf16[1064,768]{1,0:T(8,128)(2,1)S(1)}, bf16[1064,768]{1,0:T(8,128)(2,1)S(1)}, u32[]{:S(2)}, u32[]{:S(2)}) collective-permute-start(bf16[1064,768]{1,0:T(8,128)(2,1)S(1)} %broadcast_select_fusion.own.tokens.refs_8_), channel_id=1, source_target_pairs={{0,2},{2,0},{1,3},{3,1},{4,6},{6,4},{5,7},{7,5},{8,10},{10,8},{9,1... | collective-permute-start | bytes 4902920 | tf_op jit(solution)/shard_map/ppermute | solution.py:1044
  45.6 2.9 collective-permute-start.6
  48.6 9.7 %project.1 = (bf16[2048,768]{1,0:T(8,128)(2,1)S(1)}, bf16[2048,1152]{1,0:T(8,128)(2,1)S(1)}, bf16[2048,128]{1,0:T(8,128)(2,1)S(1)}, bf16[2048,128]{1,0:T(8,128)(2,1)S(1)}) custom-call(s32[4]{0:T(128)S(1)} %get-tuple-element.194.scal, bf16[1064,768]{1,0:T(8,128)(2,1)S(1)} %collective-permute-done.3.oth, ...), custom_call_target="tpu_custom_call" | custom-call | flops 72477573120 | bytes 220200960 | tf_op jit(solution)/shard_map/project/pallas_call | solution.py:207
  60.9 22.6 %attend.2 = (bf16[1024,384]{1,0:T(8,128)(2,1)}, f32[1024,384]{1,0:T(8,128)S(1)}, f32[3,4,8,256]{3,2,1,0:T(8,128)S(1)}) custom-call(s32[4]{0:T(128)S(1)} %get-tuple-element.194.scal, bf16[2048,1152]{1,0:T(8,128)(2,1)S(1)} %get-tuple-element.109.q.qkv.k.v, bf16[2048,128]{1,0:T(8,128)(2,1)S(1)} %get-tuple-element.110.qfeat, ...), custom_call_target="tpu_custom_call" | custom-call | flops 257698037760 | bytes 251658240 | tf_op jit(solution)/shard_map/attend/pallas_call | solution.py:344
  83.7 15.3 %attend.3 = (bf16[1024,384]{1,0:T(8,128)(2,1)S(1)}, f32[1024,384]{1,0:T(8,128)S(1)}, f32[3,4,8,256]{3,2,1,0:T(8,128)S(1)}) custom-call(s32[4]{0:T(128)S(1)} %get-tuple-element.153.scal, bf16[2048,1152]{1,0:T(8,128)(2,1)S(1)} %get-tuple-element.109.q.qkv.k.v, bf16[2048,128]{1,0:T(8,128)(2,1)S(1)} %get-tuple-element.110.qfeat, ...), custom_call_target="tpu_custom_call" | custom-call | flops 257698037760 | bytes 251658240 | tf_op jit(solution)/shard_map/attend/pallas_call | solution.py:344
  101.7 5.8 %collective-permute-done.7.got_down = bf16[768,768]{1,0:T(8,128)(2,1)} collective-permute-done((bf16[768,768]{1,0:T(8,128)(2,1)}, bf16[768,768]{1,0:T(8,128)(2,1)}, u32[]{:S(2)}, u32[]{:S(2)}) %collective-permute-start.7) | collective-permute-done | bytes 1179680 | tf_op jit(solution)/shard_map/ppermute | solution.py:1047
  109.9 2.8 collective-permute-done.5.mixed_oth
  113.8 39.0 %ahead.1 = (f32[1024,768]{1,0:T(8,128)}, f32[1024,768]{1,0:T(8,128)}, f32[1024,128]{1,0:T(8,128)S(1)}, bf16[1024,3072]{1,0:T(8,128)(2,1)}, bf16[1024,768]{1,0:T(...) custom-call(s32[4]{0:T(128)S(1)} %copy-done.14, ...), custom_call_target="tpu_custom_call" | custom-call | flops 314069483520 | bytes 546867200 | tf_op jit(solution)/shard_map/ahead/pallas_call | solution.py:622
  157.1 4.5 %collective-permute-done.10 = bf16[2,768,768]{2,1,0:T(8,128)(2,1)} collective-permute-done((bf16[2,768,768]{2,1,0:T(8,128)(2,1)}, bf16[2,768,768]{2,1,0:T(8,128)(2,1)}, u32[]{:S(2)}, u32[]{:S(2)}) %collective-permute-start.10) | collective-permute-done | bytes 2359328 | tf_op jit(solution)/shard_map/ppermute | solution.py:1044
  161.6 3.0 fusion.4
  165.4 32.9 %behind.1 = (f32[1024,768]{1,0:T(8,128)}, bf16[1024,384]{1,0:T(8,128)(2,1)S(1)}, bf16[1024,384]{1,0:T(8,128)(2,1)S(1)}, f32[24,768]{1,0:T(8,128)S(1)}, f32[8,307...) custom-call(s32[4]{0:T(128)S(1)} %copy-done.14, ...), custom_call_target="tpu_custom_call" | custom-call | flops 338228674560 | bytes 315740160 | tf_op jit(solution)/shard_map/behind/pallas_call | solution.py:622
  198.3 2.7 bitcast_add_fusion.1
  202.7 2.2 collective-permute-start.14
  204.9 3.4 collective-permute-done.12
  208.3 3.5 convert_add_fusion
  213.2 3.3 collective-permute-start.17
  216.4 2.6 collective-permute-done.14
  219.9 2.1 collective-permute-start.16
  222.0 2.3 collective-permute-start.13
  224.4 2.3 copy-done.31
  226.7 24.8 %attend_back.3 = (bf16[1024,384]{1,0:T(8,128)(2,1)S(1)}, bf16[1024,384]{1,0:T(8,128)(2,1)S(1)}) custom-call(s32[4]{0:T(128)S(1)} %copy-done.14, bf16[2048,1152]{1,0:T(8,128)(2,1)S(1)} %copy-done.31, bf16[2048,1152]{1,0:T(8,128)(2,1)S(1)} %copy-done.31, bf16[2048,128]{1,0:T(8,128)(2,1)S(1)} %copy-done.37, bf16[2048,1152]{1,0:T(8,128)(2,1)S(1)} %copy-done.31, ...), custom_call_target="tpu_custom_call" | custom-call | flops 429496729600 | bytes 157286400 | tf_op jit(solution)/shard_map/attend_back/pallas_call | solution.py:803
  253.6 4.5 %collective-permute-start.19 = (bf16[192,768]{1,0:T(8,128)(2,1)}, bf16[192,768]{1,0:T(8,128)(2,1)}, u32[]{:S(2)}, u32[]{:S(2)}) collective-permute-start(bf16[192,768]{1,0:T(8,128)(2,1)} %fusion.9), channel_id=1, source_target_pairs={{0,16},{4,20},{8,24},{12,28},{16,0},{20,4},{24,8},{28,12},{1,17},{... | collective-permute-start | bytes 884744 | tf_op jit(solution)/shard_map/ppermute | solution.py:1056
  258.0 2.6 bitcast_add_fusion
  261.8 24.6 %attend_back.4 = (bf16[1024,384]{1,0:T(8,128)(2,1)S(1)}, bf16[1024,384]{1,0:T(8,128)(2,1)S(1)}) custom-call(s32[4]{0:T(128)S(1)} %copy-done.19, bf16[2048,1152]{1,0:T(8,128)(2,1)S(1)} %bitcast.93, bf16[2048,1152]{1,0:T(8,128)(2,1)S(1)} %bitcast.93, bf16[2048,128]{1,0:T(8,128)(2,1)S(1)} %copy-done.37, bf16[2048,1152]{1,0:T(8,128)(2,1)S(1)} %bitcast.93, ...), custom_call_target="tpu_custom_call" | custom-call | flops 429496729600 | bytes 157286400 | tf_op jit(solution)/shard_map/attend_back/pallas_call | solution.py:803
  286.4 2.0 fusion.3
  290.6 2.0 collective-permute-start.22
  292.7 4.4 %project_grad.2 = (bf16[384,768]{1,0:T(8,128)(2,1)S(1)}, bf16[384,768]{1,0:T(8,128)(2,1)S(1)}, f32[8,768]{1,0:T(8,128)S(1)}) custom-call(s32[4]{0:T(128)S(1)} %copy-done.14, bf16[2048,768]{1,0:T(8,128)(2,1)S(1)} %copy-done.28, bf16[1024,384]{1,0:T(8,128)(2,1)S(1)} %copy-done.26, bf16[1024,384]{1,0:T(8,128)(2,1)S(1)} %get-tuple-element.155.refs_1_, ...), custom_call_target="tpu_custom_call" | custom-call | flops 48318382080 | bytes 125829120 | tf_op jit(solution)/shard_map/project_grad/pallas_call | solution.py:861
  297.7 2.9 collective-permute-done.23
  301.5 6.1 %collective-permute-start.49 = (bf16[384,768]{1,0:T(8,128)(2,1)}, bf16[384,768]{1,0:T(8,128)(2,1)}, u32[]{:S(2)}, u32[]{:S(2)}) collective-permute-start(bf16[384,768]{1,0:T(8,128)(2,1)} %pad_maximum_fusion.3), channel_id=1, source_target_pairs={{0,4},{4,0},{8,12},{12,8},{16,20},{20,16},{24,28},{28,24},{1,5},{5... | collective-permute-start | bytes 1769480 | tf_op jit(solution)/shard_map/ppermute | solution.py:1056
  308.6 3.6 collective-permute-start.26
  313.3 24.8 %attend_back.5 = (bf16[1024,384]{1,0:T(8,128)(2,1)S(1)}, bf16[1024,384]{1,0:T(8,128)(2,1)S(1)}) custom-call(s32[4]{0:T(128)S(1)} %get-tuple-element.164.scal, bf16[2048,1152]{1,0:T(8,128)(2,1)S(1)} %bitcast.93, bf16[2048,1152]{1,0:T(8,128)(2,1)S(1)} %bitcast.93, bf16[2048,128]{1,0:T(8,128)(2,1)S(1)} %copy-done.37, bf16[2048,1152]{1,0:T(8,128)(2,1)S(1)} %bitcast.93, ...), custom_call_target="tpu_custom_call" | custom-call | flops 429496729600 | bytes 157286400 | tf_op jit(solution)/shard_map/attend_back/pallas_call | solution.py:803
  341.1 7.5 %collective-permute-start.30 = (bf16[192,768]{1,0:T(8,128)(2,1)S(1)}, bf16[192,768]{1,0:T(8,128)(2,1)S(1)}, u32[]{:S(2)}, u32[]{:S(2)}) collective-permute-start(bf16[192,768]{1,0:T(8,128)(2,1)S(1)} %fusion.12), channel_id=1, source_target_pairs={{0,4},{4,0},{8,12},{12,8},{16,20},{20,16},{24,28},{28,24},{1,5},{5... | collective-permute-start | bytes 884744 | tf_op jit(solution)/shard_map/ppermute | solution.py:1056
  348.7 3.3 project_grad.3
  358.9 8.2 %first_grad.1 = (bf16[1024,768]{1,0:T(8,128)(2,1)S(1)}, f32[16,768]{1,0:T(8,128)S(1)}) custom-call(bf16[1024,384]{1,0:T(8,128)(2,1)S(1)} %get-tuple-element.150.refs_2_.refs_0_, bf16[1024,384]{1,0:T(8,128)(2,1)S(1)} %copy-done.33, bf16[1024,384]{1,0:T(8,128)(2,1)S(1)} %get-tuple-element.165.refs_1_.refs_2_, bf16[1024,384]{1,0:T(8,128)(2,1)S(1)} %copy-done.21, ...), custom_call_target="tpu_custom_call" | custom-call | flops 72477573120 | bytes 165150720 | tf_op jit(solution)/shard_map/first_grad/pallas_call | solution.py:903
  371.6 2.9 collective-permute-start.38
  382.3 6.6 %collective-permute-done.36 = bf16[192,384]{1,0:T(8,128)(2,1)S(1)} collective-permute-done((bf16[192,384]{1,0:T(8,128)(2,1)S(1)}, bf16[192,384]{1,0:T(8,128)(2,1)S(1)}, u32[]{:S(2)}, u32[]{:S(2)}) %collective-permute-start.36) | collective-permute-done | bytes 147488 | tf_op jit(solution)/shard_map/ppermute | solution.py:1056
  390.4 4.1 collective-permute-done.37
  394.5 3.7 collective-permute-start.44
  398.3 2.4 collective-permute-start.39
  404.5 2.5 maximum_convert_fusion.1
  407.1 2.0 collective-permute-start.46
  409.1 6.4 %last.1 = f32[980,768]{1,0:T(8,128)} custom-call(s32[4]{0:T(128)S(1)} %copy-done.15, bf16[1064,768]{1,0:T(8,128)(2,1)S(1)} %pack.1.tokens, bf16[1024,768]{1,0:T(8,128)(2,1)S(1)} %get-tuple-element.195.grad, bf16[1024,768]{1,0:T(8,128)(2,1)S(1)} %collective-permute-done.42.grad_got, f32[1024,768]{1,0:T(8,128)} %get-tuple-element.136.residual, ...), custom_call_target="tpu_custom_call" | custom-call | flops 314572800 | bytes 188743680 | tf_op jit(solution)/shard_map/last/pallas_call | solution.py:934
  420.9 2.1 maximum_convert_fusion.2
  425.2 2.8 maximum_convert_fusion
  (376 shorter events, 74.7 us)
Async XLA Ops:
  7.4 6.4 %collective-permute-start.1 = (bf16[384,1152]{1,0:T(8,128)(2,1)}, bf16[384,1152]{1,0:T(8,128)(2,1)}, u32[]{:S(2)}, u32[]{:S(2)}) collective-permute-start(bf16[384,1152]{1,0:T(8,128)(2,1)} %copy.33), channel_id=1, source_target_pairs={{1,2},{2,1},{5,6},{6,5},{9,10},{10,9},{13,14},{14,13},{17,18},{18,... | collective-permute-start | bytes 2654216 | tf_op jit(solution)/shard_map/ppermute | solution.py:1041
  9.2 15.2 %collective-permute-start = (bf16[1064,768]{1,0:T(8,128)(2,1)S(1)}, bf16[1064,768]{1,0:T(8,128)(2,1)}, u32[]{:S(2)}, u32[]{:S(2)}) collective-permute-start(bf16[1064,768]{1,0:T(8,128)(2,1)S(1)} %pack.1.tokens), channel_id=1, source_target_pairs={{1,2},{2,1},{5,6},{6,5},{9,10},{10,9},{13,14},{14,13},{17,18},{18,... | collective-permute-start | bytes 4902920 | tf_op jit(solution)/shard_map/ppermute | solution.py:1041
  13.8 6.8 %collective-permute-start.2 = (bf16[384,1152]{1,0:T(8,128)(2,1)}, bf16[384,1152]{1,0:T(8,128)(2,1)}, u32[]{:S(2)}, u32[]{:S(2)}) collective-permute-start(bf16[384,1152]{1,0:T(8,128)(2,1)} %collective-permute-done.1.first), channel_id=1, source_target_pairs={{1,5},{2,6},{5,1},{6,2},{9,13},{10,14},{13,9},{14,10},{17,21},{18,... | collective-permute-start | bytes 2654216 | tf_op jit(solution)/shard_map/ppermute | solution.py:1090
  24.6 24.1 %collective-permute-start.3 = (bf16[1064,768]{1,0:T(8,128)(2,1)S(1)}, bf16[1064,768]{1,0:T(8,128)(2,1)S(1)}, u32[]{:S(2)}, u32[]{:S(2)}) collective-permute-start(bf16[1064,768]{1,0:T(8,128)(2,1)S(1)} %broadcast_select_fusion.own.tokens.refs_8_), channel_id=1, source_target_pairs={{0,2},{2,0},{1,3},{3,1},{4,6},{6,4},{5,7},{7,5},{8,10},{10,8},{9,1... | collective-permute-start | bytes 4902920 | tf_op jit(solution)/shard_map/ppermute | solution.py:1044
  45.6 37.9 %collective-permute-start.6 = (bf16[976,768]{1,0:T(8,128)(2,1)}, bf16[976,768]{1,0:T(8,128)(2,1)}, u32[]{:S(2)}, u32[]{:S(2)}) collective-permute-start(bf16[976,768]{1,0:T(8,128)(2,1)} %fusion.1), channel_id=1, source_target_pairs={{0,1},{1,0},{2,3},{3,2},{4,5},{5,4},{6,7},{7,6},{8,9},{9,8},{10,11... | collective-permute-start | bytes 4497416 | tf_op jit(solution)/shard_map/ppermute | solution.py:1047
  60.1 23.5 %collective-permute-start.4 = (bf16[768,1152]{1,0:T(8,128)(2,1)}, bf16[768,1152]{1,0:T(8,128)(2,1)}, u32[]{:S(2)}, u32[]{:S(2)}) collective-permute-start(bf16[768,1152]{1,0:T(8,128)(2,1)} %relay.1.weight.refs_6_), channel_id=1, source_target_pairs={{0,2},{2,0},{1,3},{3,1},{4,6},{6,4},{5,7},{7,5},{8,10},{10,8},{9,1... | collective-permute-start | bytes 5308424 | tf_op jit(solution)/shard_map/ppermute | solution.py:1044
  60.3 47.2 %collective-permute-start.7 = (bf16[768,768]{1,0:T(8,128)(2,1)}, bf16[768,768]{1,0:T(8,128)(2,1)}, u32[]{:S(2)}, u32[]{:S(2)}) collective-permute-start(bf16[768,768]{1,0:T(8,128)(2,1)} %get-tuple-element.117), channel_id=1, source_target_pairs={{0,1},{1,0},{2,3},{3,2},{4,5},{5,4},{6,7},{7,6},{8,9},{9,8},{10,11... | collective-permute-start | bytes 3538952 | tf_op jit(solution)/shard_map/ppermute | solution.py:1047
  83.5 29.2 %collective-permute-start.8 = (bf16[976,768]{1,0:T(8,128)(2,1)}, bf16[976,768]{1,0:T(8,128)(2,1)}, u32[]{:S(2)}, u32[]{:S(2)}) collective-permute-start(bf16[976,768]{1,0:T(8,128)(2,1)} %collective-permute-done.6.got_up), channel_id=1, source_target_pairs={{0,2},{2,0},{1,3},{3,1},{4,6},{6,4},{5,7},{7,5},{8,10},{10,8},{9,1... | collective-permute-start | bytes 4497416 | tf_op jit(solution)/shard_map/ppermute | solution.py:1044
  107.5 5.2 %collective-permute-start.9 = (bf16[768,768]{1,0:T(8,128)(2,1)}, bf16[768,768]{1,0:T(8,128)(2,1)S(1)}, u32[]{:S(2)}, u32[]{:S(2)}) collective-permute-start(bf16[768,768]{1,0:T(8,128)(2,1)} %collective-permute-done.7.got_down), channel_id=1, source_target_pairs={{0,2},{2,0},{1,3},{3,1},{4,6},{6,4},{5,7},{7,5},{8,10},{10,8},{9,1... | collective-permute-start | bytes 3538952 | tf_op jit(solution)/shard_map/ppermute | solution.py:1044
  108.9 3.8 collective-permute-start.5
  156.7 4.9 %collective-permute-start.10 = (bf16[2,768,768]{2,1,0:T(8,128)(2,1)}, bf16[2,768,768]{2,1,0:T(8,128)(2,1)}, u32[]{:S(2)}, u32[]{:S(2)}) collective-permute-start(bf16[2,768,768]{2,1,0:T(8,128)(2,1)} %get-tuple-element.121), channel_id=1, source_target_pairs={{0,2},{2,0},{1,3},{3,1},{4,6},{6,4},{5,7},{7,5},{8,10},{10,8},{9,1... | collective-permute-start | bytes 7077896 | tf_op jit(solution)/shard_map/ppermute | solution.py:1044
  164.6 33.7 %collective-permute-start.11 = (bf16[768,768]{1,0:T(8,128)(2,1)}, bf16[768,768]{1,0:T(8,128)(2,1)}, u32[]{:S(2)}, u32[]{:S(2)}) collective-permute-start(bf16[768,768]{1,0:T(8,128)(2,1)} %fusion.4), channel_id=1, source_target_pairs={{0,1},{1,0},{2,3},{3,2},{4,5},{5,4},{6,7},{7,6},{8,9},{9,8},{10,11... | collective-permute-start | bytes 3538952 | tf_op jit(solution)/shard_map/ppermute | solution.py:1047
  202.5 5.8 %collective-permute-start.12 = (bf16[2,960,768]{2,1,0:T(8,128)(2,1)}, bf16[2,960,768]{2,1,0:T(8,128)(2,1)}, u32[]{:S(2)}, u32[]{:S(2)}) collective-permute-start(bf16[2,960,768]{2,1,0:T(8,128)(2,1)} %get-tuple-element.133), channel_id=1, source_target_pairs={{0,2},{2,0},{1,3},{3,1},{4,6},{6,4},{5,7},{7,5},{8,10},{10,8},{9,1... | collective-permute-start | bytes 8847368 | tf_op jit(solution)/shard_map/ppermute | solution.py:1044
  202.7 16.3 %collective-permute-start.14 = (bf16[384,768]{1,0:T(8,128)(2,1)S(1)}, bf16[384,768]{1,0:T(8,128)(2,1)S(1)}, u32[]{:S(2)}, u32[]{:S(2)}) collective-permute-start(bf16[384,768]{1,0:T(8,128)(2,1)S(1)} %fusion.6), channel_id=1, source_target_pairs={{0,4},{4,0},{8,12},{12,8},{16,20},{20,16},{24,28},{28,24},{1,5},{5... | collective-permute-start | bytes 1769480 | tf_op jit(solution)/shard_map/ppermute | solution.py:1056
  204.8 19.5 %collective-permute-start.15 = (bf16[1024,384]{1,0:T(8,128)(2,1)}, bf16[1024,384]{1,0:T(8,128)(2,1)S(1)}, u32[]{:S(2)}, u32[]{:S(2)}) collective-permute-start(bf16[1024,384]{1,0:T(8,128)(2,1)} %copy-done.24), channel_id=1, source_target_pairs={{0,2},{2,0},{1,3},{3,1},{4,6},{6,4},{5,7},{7,5},{8,10},{10,8},{9,1... | collective-permute-start | bytes 2359304 | tf_op jit(solution)/shard_map/ppermute | solution.py:1044
  213.2 44.9 %collective-permute-start.17 = (bf16[2,480,768]{2,1,0:T(8,128)(2,1)}, bf16[2,480,768]{2,1,0:T(8,128)(2,1)}, u32[]{:S(2)}, u32[]{:S(2)}) collective-permute-start(bf16[2,480,768]{2,1,0:T(8,128)(2,1)} %fusion.2), channel_id=1, source_target_pairs={{0,4},{4,0},{8,12},{12,8},{16,20},{20,16},{24,28},{28,24},{1,5},{5... | collective-permute-start | bytes 4423688 | tf_op jit(solution)/shard_map/ppermute | solution.py:1056
  219.9 31.6 %collective-permute-start.16 = (bf16[192,768]{1,0:T(8,128)(2,1)}, bf16[192,768]{1,0:T(8,128)(2,1)}, u32[]{:S(2)}, u32[]{:S(2)}) collective-permute-start(bf16[192,768]{1,0:T(8,128)(2,1)} %fusion.11), channel_id=1, source_target_pairs={{0,8},{4,12},{8,0},{12,4},{16,24},{20,28},{24,16},{28,20},{1,9},{5... | collective-permute-start | bytes 884744 | tf_op jit(solution)/shard_map/ppermute | solution.py:1056
  222.0 39.7 %collective-permute-start.13 = (f32[1024,768]{1,0:T(8,128)}, f32[1024,768]{1,0:T(8,128)}, u32[]{:S(2)}, u32[]{:S(2)}) collective-permute-start(f32[1024,768]{1,0:T(8,128)} %get-tuple-element.136.residual), channel_id=1, source_target_pairs={{1,2},{2,1},{5,6},{6,5},{9,10},{10,9},{13,14},{14,13},{17,18},{18,... | collective-permute-start | bytes 9437192 | tf_op jit(solution)/shard_map/ppermute | solution.py:1041
  251.5 10.2 %collective-permute-start.18 = (bf16[1024,384]{1,0:T(8,128)(2,1)S(1)}, bf16[1024,384]{1,0:T(8,128)(2,1)S(1)}, u32[]{:S(2)}, u32[]{:S(2)}) collective-permute-start(bf16[1024,384]{1,0:T(8,128)(2,1)S(1)} %get-tuple-element.146.refs_0_), channel_id=1, source_target_pairs={{0,2},{2,0},{1,3},{3,1},{4,6},{6,4},{5,7},{7,5},{8,10},{10,8},{9,1... | collective-permute-start | bytes 2359304 | tf_op jit(solution)/shard_map/ppermute | solution.py:1044
  253.6 34.9 %collective-permute-start.19 = (bf16[192,768]{1,0:T(8,128)(2,1)}, bf16[192,768]{1,0:T(8,128)(2,1)}, u32[]{:S(2)}, u32[]{:S(2)}) collective-permute-start(bf16[192,768]{1,0:T(8,128)(2,1)} %fusion.9), channel_id=1, source_target_pairs={{0,16},{4,20},{8,24},{12,28},{16,0},{20,4},{24,8},{28,12},{1,17},{... | collective-permute-start | bytes 884744 | tf_op jit(solution)/shard_map/ppermute | solution.py:1056
  261.7 24.7 %collective-permute-start.20 = (bf16[480,768]{1,0:T(8,128)(2,1)}, bf16[480,768]{1,0:T(8,128)(2,1)}, u32[]{:S(2)}, u32[]{:S(2)}) collective-permute-start(bf16[480,768]{1,0:T(8,128)(2,1)} %fusion.5), channel_id=1, source_target_pairs={{0,1},{1,0},{2,3},{3,2},{4,5},{5,4},{6,7},{7,6},{8,9},{9,8},{10,11... | collective-permute-start | bytes 2211848 | tf_op jit(solution)/shard_map/ppermute | solution.py:1047
  290.6 10.0 %collective-permute-start.23 = (bf16[192,768]{1,0:T(8,128)(2,1)S(1)}, bf16[192,768]{1,0:T(8,128)(2,1)S(1)}, u32[]{:S(2)}, u32[]{:S(2)}) collective-permute-start(bf16[192,768]{1,0:T(8,128)(2,1)S(1)} %add_convert_fusion.3), channel_id=1, source_target_pairs={{0,8},{4,12},{8,0},{12,4},{16,24},{20,28},{24,16},{28,20},{1,9},{5... | collective-permute-start | bytes 884744 | tf_op jit(solution)/shard_map/ppermute | solution.py:1056
  290.6 17.0 %collective-permute-start.22 = (bf16[240,768]{1,0:T(8,128)(2,1)S(1)}, bf16[240,768]{1,0:T(8,128)(2,1)S(1)}, u32[]{:S(2)}, u32[]{:S(2)}) collective-permute-start(bf16[240,768]{1,0:T(8,128)(2,1)S(1)} %fusion.10), channel_id=1, source_target_pairs={{0,8},{4,12},{8,0},{12,4},{16,24},{20,28},{24,16},{28,20},{1,9},{5... | collective-permute-start | bytes 1105928 | tf_op jit(solution)/shard_map/ppermute | solution.py:1056
  292.7 20.6 %collective-permute-start.24 = (bf16[1024,384]{1,0:T(8,128)(2,1)S(1)}, bf16[1024,384]{1,0:T(8,128)(2,1)S(1)}, u32[]{:S(2)}, u32[]{:S(2)}) collective-permute-start(bf16[1024,384]{1,0:T(8,128)(2,1)S(1)} %get-tuple-element.155.refs_1_), channel_id=1, source_target_pairs={{0,2},{2,0},{1,3},{3,1},{4,6},{6,4},{5,7},{7,5},{8,10},{10,8},{9,1... | collective-permute-start | bytes 2359304 | tf_op jit(solution)/shard_map/ppermute | solution.py:1044
  297.1 15.1 %collective-permute-start.21 = (bf16[384,768]{1,0:T(8,128)(2,1)S(1)}, bf16[384,768]{1,0:T(8,128)(2,1)S(1)}, u32[]{:S(2)}, u32[]{:S(2)}) collective-permute-start(bf16[384,768]{1,0:T(8,128)(2,1)S(1)} %get-tuple-element.160), channel_id=1, source_target_pairs={{0,2},{2,0},{1,3},{3,1},{4,6},{6,4},{5,7},{7,5},{8,10},{10,8},{9,1... | collective-permute-start | bytes 1769480 | tf_op jit(solution)/shard_map/ppermute | solution.py:1044
  301.5 50.5 %collective-permute-start.49 = (bf16[384,768]{1,0:T(8,128)(2,1)}, bf16[384,768]{1,0:T(8,128)(2,1)}, u32[]{:S(2)}, u32[]{:S(2)}) collective-permute-start(bf16[384,768]{1,0:T(8,128)(2,1)} %pad_maximum_fusion.3), channel_id=1, source_target_pairs={{0,4},{4,0},{8,12},{12,8},{16,20},{20,16},{24,28},{28,24},{1,5},{5... | collective-permute-start | bytes 1769480 | tf_op jit(solution)/shard_map/ppermute | solution.py:1056
  308.6 29.7 %collective-permute-start.26 = (bf16[240,768]{1,0:T(8,128)(2,1)}, bf16[240,768]{1,0:T(8,128)(2,1)}, u32[]{:S(2)}, u32[]{:S(2)}) collective-permute-start(bf16[240,768]{1,0:T(8,128)(2,1)} %fusion.7), channel_id=1, source_target_pairs={{0,16},{4,20},{8,24},{12,28},{16,0},{20,4},{24,8},{28,12},{1,17},{... | collective-permute-start | bytes 1105928 | tf_op jit(solution)/shard_map/ppermute | solution.py:1056
  313.2 26.4 %collective-permute-start.27 = (bf16[384,768]{1,0:T(8,128)(2,1)}, bf16[384,768]{1,0:T(8,128)(2,1)}, u32[]{:S(2)}, u32[]{:S(2)}) collective-permute-start(bf16[384,768]{1,0:T(8,128)(2,1)} %broadcast_select_fusion.11), channel_id=1, source_target_pairs={{0,1},{1,0},{2,3},{3,2},{4,5},{5,4},{6,7},{7,6},{8,9},{9,8},{10,11... | collective-permute-start | bytes 1769480 | tf_op jit(solution)/shard_map/ppermute | solution.py:1047
  338.1 20.8 %collective-permute-start.25 = (bf16[1024,384]{1,0:T(8,128)(2,1)S(1)}, bf16[1024,384]{1,0:T(8,128)(2,1)S(1)}, u32[]{:S(2)}, u32[]{:S(2)}) collective-permute-start(bf16[1024,384]{1,0:T(8,128)(2,1)S(1)} %get-tuple-element.166.refs_0_), channel_id=1, source_target_pairs={{0,2},{2,0},{1,3},{3,1},{4,6},{6,4},{5,7},{7,5},{8,10},{10,8},{9,1... | collective-permute-start | bytes 2359304 | tf_op jit(solution)/shard_map/ppermute | solution.py:1044
  339.5 15.2 %collective-permute-start.29 = (bf16[240,768]{1,0:T(8,128)(2,1)S(1)}, bf16[240,768]{1,0:T(8,128)(2,1)S(1)}, u32[]{:S(2)}, u32[]{:S(2)}) collective-permute-start(bf16[240,768]{1,0:T(8,128)(2,1)S(1)} %add_convert_fusion.1), channel_id=1, source_target_pairs={{0,8},{4,12},{8,0},{12,4},{16,24},{20,28},{24,16},{28,20},{1,9},{5... | collective-permute-start | bytes 1105928 | tf_op jit(solution)/shard_map/ppermute | solution.py:1056
  341.1 15.1 %collective-permute-start.30 = (bf16[192,768]{1,0:T(8,128)(2,1)S(1)}, bf16[192,768]{1,0:T(8,128)(2,1)S(1)}, u32[]{:S(2)}, u32[]{:S(2)}) collective-permute-start(bf16[192,768]{1,0:T(8,128)(2,1)S(1)} %fusion.12), channel_id=1, source_target_pairs={{0,4},{4,0},{8,12},{12,8},{16,20},{20,16},{24,28},{28,24},{1,5},{5... | collective-permute-start | bytes 884744 | tf_op jit(solution)/shard_map/ppermute | solution.py:1056
  354.5 43.8 %collective-permute-start.50 = (bf16[768,768]{1,0:T(8,128)(2,1)}, bf16[768,768]{1,0:T(8,128)(2,1)}, u32[]{:S(2)}, u32[]{:S(2)}) collective-permute-start(bf16[768,768]{1,0:T(8,128)(2,1)} %pad_maximum_fusion.1), channel_id=1, source_target_pairs={{0,2},{2,0},{1,3},{3,1},{4,6},{6,4},{5,7},{7,5},{8,10},{10,8},{9,1... | collective-permute-start | bytes 3538952 | tf_op jit(solution)/shard_map/ppermute | solution.py:1044
  354.7 3.4 collective-permute-start.28
  356.3 11.5 %collective-permute-start.33 = (bf16[192,768]{1,0:T(8,128)(2,1)S(1)}, bf16[192,768]{1,0:T(8,128)(2,1)S(1)}, u32[]{:S(2)}, u32[]{:S(2)}) collective-permute-start(bf16[192,768]{1,0:T(8,128)(2,1)S(1)} %fusion.14), channel_id=1, source_target_pairs={{0,8},{4,12},{8,0},{12,4},{16,24},{20,28},{24,16},{28,20},{1,9},{5... | collective-permute-start | bytes 884744 | tf_op jit(solution)/shard_map/ppermute | solution.py:1056
  358.1 10.5 %collective-permute-start.32 = (bf16[384,384]{1,0:T(8,128)(2,1)S(1)}, bf16[384,384]{1,0:T(8,128)(2,1)S(1)}, u32[]{:S(2)}, u32[]{:S(2)}) collective-permute-start(bf16[384,384]{1,0:T(8,128)(2,1)S(1)} %broadcast_select_fusion.18), channel_id=1, source_target_pairs={{0,1},{1,0},{2,3},{3,2},{4,5},{5,4},{6,7},{7,6},{8,9},{9,8},{10,11... | collective-permute-start | bytes 884744 | tf_op jit(solution)/shard_map/ppermute | solution.py:1047
  369.7 6.9 %collective-permute-start.35 = (bf16[192,384]{1,0:T(8,128)(2,1)}, bf16[192,384]{1,0:T(8,128)(2,1)S(1)}, u32[]{:S(2)}, u32[]{:S(2)}) collective-permute-start(bf16[192,384]{1,0:T(8,128)(2,1)} %fusion.15), channel_id=1, source_target_pairs={{0,4},{4,0},{8,12},{12,8},{16,20},{20,16},{24,28},{28,24},{1,5},{5... | collective-permute-start | bytes 442376 | tf_op jit(solution)/shard_map/ppermute | solution.py:1056
  371.6 18.5 %collective-permute-start.38 = (bf16[192,768]{1,0:T(8,128)(2,1)}, bf16[192,768]{1,0:T(8,128)(2,1)S(1)}, u32[]{:S(2)}, u32[]{:S(2)}) collective-permute-start(bf16[192,768]{1,0:T(8,128)(2,1)} %fusion.8), channel_id=1, source_target_pairs={{0,16},{4,20},{8,24},{12,28},{16,0},{20,4},{24,8},{28,12},{1,17},{... | collective-permute-start | bytes 884744 | tf_op jit(solution)/shard_map/ppermute | solution.py:1056
  375.4 6.2 %collective-permute-start.34 = (f32[24,768]{1,0:T(8,128)S(1)}, f32[24,768]{1,0:T(8,128)S(1)}, u32[]{:S(2)}, u32[]{:S(2)}) collective-permute-start(f32[24,768]{1,0:T(8,128)S(1)} %add.160), channel_id=1, source_target_pairs={{0,1},{1,0},{2,3},{3,2},{4,5},{5,4},{6,7},{7,6},{8,9},{9,8},{10,11... | collective-permute-start | bytes 221192 | tf_op jit(solution)/shard_map/ppermute | solution.py:1047
  377.6 11.4 %collective-permute-start.36 = (bf16[192,384]{1,0:T(8,128)(2,1)S(1)}, bf16[192,384]{1,0:T(8,128)(2,1)S(1)}, u32[]{:S(2)}, u32[]{:S(2)}) collective-permute-start(bf16[192,384]{1,0:T(8,128)(2,1)S(1)} %fusion.16), channel_id=1, source_target_pairs={{0,8},{4,12},{8,0},{12,4},{16,24},{20,28},{24,16},{28,20},{1,9},{5... | collective-permute-start | bytes 442376 | tf_op jit(solution)/shard_map/ppermute | solution.py:1056
  380.7 28.3 %collective-permute-start.42 = (bf16[1024,768]{1,0:T(8,128)(2,1)S(1)}, bf16[1024,768]{1,0:T(8,128)(2,1)S(1)}, u32[]{:S(2)}, u32[]{:S(2)}) collective-permute-start(bf16[1024,768]{1,0:T(8,128)(2,1)S(1)} %get-tuple-element.195.grad), channel_id=1, source_target_pairs={{1,2},{2,1},{5,6},{6,5},{9,10},{10,9},{13,14},{14,13},{17,18},{18,... | collective-permute-start | bytes 4718600 | tf_op jit(solution)/shard_map/ppermute | solution.py:1041
  381.6 20.8 %collective-permute-start.41 = (bf16[480,768]{1,0:T(8,128)(2,1)}, bf16[480,768]{1,0:T(8,128)(2,1)S(1)}, u32[]{:S(2)}, u32[]{:S(2)}) collective-permute-start(bf16[480,768]{1,0:T(8,128)(2,1)} %pad_maximum_fusion.2), channel_id=1, source_target_pairs={{0,4},{4,0},{8,12},{12,8},{16,20},{20,16},{24,28},{28,24},{1,5},{5... | collective-permute-start | bytes 2211848 | tf_op jit(solution)/shard_map/ppermute | solution.py:1056
  390.0 14.3 %collective-permute-start.40 = (bf16[192,384]{1,0:T(8,128)(2,1)S(1)}, bf16[192,384]{1,0:T(8,128)(2,1)S(1)}, u32[]{:S(2)}, u32[]{:S(2)}) collective-permute-start(bf16[192,384]{1,0:T(8,128)(2,1)S(1)} %fusion.13), channel_id=1, source_target_pairs={{0,16},{4,20},{8,24},{12,28},{16,0},{20,4},{24,8},{28,12},{1,17},{... | collective-permute-start | bytes 442376 | tf_op jit(solution)/shard_map/ppermute | solution.py:1056
  390.1 4.4 %collective-permute-start.37 = (f32[24,768]{1,0:T(8,128)S(1)}, f32[24,768]{1,0:T(8,128)S(1)}, u32[]{:S(2)}, u32[]{:S(2)}) collective-permute-start(f32[24,768]{1,0:T(8,128)S(1)} %add.162), channel_id=1, source_target_pairs={{0,8},{4,12},{8,0},{12,4},{16,24},{20,28},{24,16},{28,20},{1,9},{5... | collective-permute-start | bytes 221192 | tf_op jit(solution)/shard_map/ppermute | solution.py:1056
  394.5 22.1 %collective-permute-start.44 = (bf16[192,768]{1,0:T(8,128)(2,1)S(1)}, bf16[192,768]{1,0:T(8,128)(2,1)S(1)}, u32[]{:S(2)}, u32[]{:S(2)}) collective-permute-start(bf16[192,768]{1,0:T(8,128)(2,1)S(1)} %add_convert_fusion.2), channel_id=1, source_target_pairs={{0,4},{4,0},{8,12},{12,8},{16,20},{20,16},{24,28},{28,24},{1,5},{5... | collective-permute-start | bytes 884744 | tf_op jit(solution)/shard_map/ppermute | solution.py:1056
  398.3 6.1 %collective-permute-start.39 = (f32[24,768]{1,0:T(8,128)S(1)}, f32[24,768]{1,0:T(8,128)S(1)}, u32[]{:S(2)}, u32[]{:S(2)}) collective-permute-start(f32[24,768]{1,0:T(8,128)S(1)} %add.165), channel_id=1, source_target_pairs={{0,16},{4,20},{8,24},{12,28},{16,0},{20,4},{24,8},{28,12},{1,17},{... | collective-permute-start | bytes 221192 | tf_op jit(solution)/shard_map/ppermute | solution.py:1056
  404.4 11.1 %collective-permute-start.43 = (f32[24,768]{1,0:T(8,128)S(1)}, f32[24,768]{1,0:T(8,128)S(1)}, u32[]{:S(2)}, u32[]{:S(2)}) collective-permute-start(f32[24,768]{1,0:T(8,128)S(1)} %add.167), channel_id=1, source_target_pairs={{0,4},{4,0},{8,12},{12,8},{16,20},{20,16},{24,28},{28,24},{1,5},{5... | collective-permute-start | bytes 221192 | tf_op jit(solution)/shard_map/ppermute | solution.py:1056
  407.1 15.9 %collective-permute-start.48 = (bf16[960,768]{1,0:T(8,128)(2,1)}, bf16[960,768]{1,0:T(8,128)(2,1)}, u32[]{:S(2)}, u32[]{:S(2)}) collective-permute-start(bf16[960,768]{1,0:T(8,128)(2,1)} %pad_maximum_fusion), channel_id=1, source_target_pairs={{0,2},{2,0},{1,3},{3,1},{4,6},{6,4},{5,7},{7,5},{8,10},{10,8},{9,1... | collective-permute-start | bytes 4423688 | tf_op jit(solution)/shard_map/ppermute | solution.py:1044
  407.1 10.6 %collective-permute-start.46 = (bf16[192,384]{1,0:T(8,128)(2,1)S(1)}, bf16[192,384]{1,0:T(8,128)(2,1)S(1)}, u32[]{:S(2)}, u32[]{:S(2)}) collective-permute-start(bf16[192,384]{1,0:T(8,128)(2,1)S(1)} %add_convert_fusion.4), channel_id=1, source_target_pairs={{0,4},{4,0},{8,12},{12,8},{16,20},{20,16},{24,28},{28,24},{1,5},{5... | collective-permute-start | bytes 442376 | tf_op jit(solution)/shard_map/ppermute | solution.py:1056
  (105 other events, 1221.0 us)

commit v3 on v2

--- a/solution.py
+++ b/solution.py
@@ -50,6 +50,19 @@
     scaled = grad * gain
     along = jnp.mean(scaled * xhat, axis=-1, keepdims=True)
     return scale * (scaled - jnp.mean(scaled, axis=-1, keepdims=True) - xhat * along)
+
+
+STRIP = 96
+
+
+def clear(ref):
+    def strip(index, carry):
+        rows = pl.ds(pl.multiple_of(index * STRIP, 32), STRIP)
+        for part in range(ref.shape[0]):
+            ref[part, rows, :] = jnp.zeros((STRIP, ref.shape[2]), ref.dtype)
+        return carry
+
+    lax.fori_loop(0, ref.shape[1] // STRIP, strip, 0)
 
 
 def cost(flops, nbytes):
@@ -451,8 +464,9 @@
     @pl.when(step == 0)
     def _():
         gather_out_weight(scal, own_out, got_up, more_up, out_weight, hid)
-        for ref in (sums, pooled, learner_sums, learner_offset_sums, down_total):
+        for ref in (sums, pooled, learner_sums, learner_offset_sums):
             ref[...] = jnp.zeros_like(ref)
+        clear(down_total)
 
     def up_bias(chunk):
         pick = (1 - core) if chunk % 2 == 0 else core
@@ -515,9 +529,14 @@
 
     @pl.when(step == pl.num_programs(0) - 1)
     def _():
-        for n in range(2):
-            theirs_out[n] = down_total[2 * n].astype(BF16)
-            mine_out[n] = down_total[2 * n + 1].astype(BF16)
+        def strip(index, carry):
+            rows = pl.ds(pl.multiple_of(index * STRIP, 32), STRIP)
+            for n in range(2):
+                theirs_out[n, rows, :] = down_total[2 * n, rows, :].astype(BF16)
+                mine_out[n, rows, :] = down_total[2 * n + 1, rows, :].astype(BF16)
+            return carry
+
+        lax.fori_loop(0, hid // STRIP, strip, 0)
 
 
 def behind_kernel(
@@ -558,8 +577,10 @@
     @pl.when(pl.program_id(0) == 0)
     def _():
         gather_out_weight(scal, own_out, got_up, more_up, out_weight, hid)
-        for ref in (sums, up_sums, up_total, out_total):
+        for ref in (sums, up_sums):
             ref[...] = jnp.zeros_like(ref)
+        clear(up_total)
+        clear(out_total)
 
     mine = pl.ds(pl.multiple_of(core * share, 64), share)
     theirs = pl.ds(pl.multiple_of((1 - core) * share, 64), share)
@@ -597,9 +618,17 @@
     def _():
         width = second.shape[1]
         half = width // 2
-        for odd, (out, column) in enumerate(((theirs_out, 1 - core), (mine_out, core))):
+
+        def strip(index, carry):
+            rows = pl.ds(pl.multiple_of(index * STRIP, 32), STRIP)
             for n in range(2):
-                out[n, :width, :] = up_total[2 * n + odd].astype(BF16)
+                theirs_out[n, rows, :] = up_total[2 * n, rows, :].astype(BF16)
+                mine_out[n, rows, :] = up_total[2 * n + 1, rows, :].astype(BF16)
+            return carry
+
+        lax.fori_loop(0, width // STRIP, strip, 0)
+        for out, column in ((theirs_out, 1 - core), (mine_out, core)):
+            for n in range(2):
                 side = (1 - plane) if n == 0 else plane
                 at = pl.ds(pl.multiple_of(column * half, 128), half)
                 grad = out_total[jnp.where(side == core, 0, 1), :, at].astype(BF16)

time: 435 us -> 436 us (level)
  Pallas kernels: 221 us -> 185 us
  starting transfers between devices: 85.4 us -> 106 us
  waiting for transfers between devices: 32.9 us -> 47.6 us
    pallas_call x3, Pallas kernels: 74.1 us -> 49.4 us  [attend_back(): pl.pallas_call(functools.partial(attend_back_kernel, frames_here), grid_s...]
    ppermute x21, starting transfers between devices: 48.3 us -> 63.5 us  [hop(): return lax.ppermute(x, 'chip', [(i, i ^ step) for i in range(chips)])]
    ppermute x7, waiting for transfers between devices: 5.82 us -> 17.8 us  [to_plane(): return lax.ppermute(x, 'mp', flip2)]
    pallas_call x2, Pallas kernels: 37.9 us -> 26.8 us  [attend(): pl.pallas_call(functools.partial(attend_kernel, frames_here, bk), grid_sp...]
    ppermute x7, starting transfers between devices: 6.21 us -> 11.4 us  [to_plane(): return lax.ppermute(x, 'mp', flip2)]
  transfers between devices with their start and end apart: 51 -> 51, of which waited for: 9 -> 12; matrix products, arithmetic and copies ran while one was open for 12% -> 12% of each run, Pallas kernels for 42% -> 34%
where the time goes in v3:
time: 436 us; the launch traced here: 429 us
  Pallas kernels  185 us (42%)
  starting transfers between devices  106 us (24%)
  other arithmetic  48.3 us (11%)
  waiting for transfers between devices  47.6 us (11%)
  local copies, waits for them, and re-layouts  38.3 us (9%)
    pallas_call x2, Pallas kernels, row_call(): pl.pallas_call(kernel, grid_spec=pltpu.PrefetchScalarGridSpec(num_scalar_...  72.3 us
    ppermute x21, starting transfers between devices, hop(): return lax.ppermute(x, 'chip', [(i, i ^ step) for i in range(chips)])  63.5 us
    pallas_call x3, Pallas kernels, attend_back(): pl.pallas_call(functools.partial(attend_back_kernel, frames_here), grid_s...  49.4 us
    pallas_call x2, Pallas kernels, attend(): pl.pallas_call(functools.partial(attend_kernel, frames_here, bk), grid_sp...  26.8 us
    ppermute x18, starting transfers between devices, to_core(): return lax.ppermute(x, 'core', flip2)  22.9 us
    ppermute x21, waiting for transfers between devices, hop(): return lax.ppermute(x, 'chip', [(i, i ^ step) for i in range(chips)])  18.3 us
    ppermute x7, waiting for transfers between devices, to_plane(): return lax.ppermute(x, 'mp', flip2)  17.8 us
    unnamed x206, local copies, waits for them, and re-layouts  17.8 us
  transfers between devices with their start and end apart: 51, of which 12 were waited for; matrix products, arithmetic and copies ran while one was open for 12% of the time, Pallas kernels for 34%

profile of v3, /device:TPU:0, one launch (start us, length us, event | category | flops | bytes accessed | tf_op | source)
XLA Modules:
  0.0 428.6 jit_solution(8902476915814576827)
XLA Ops:
  0.7 3.8 copy.31
  11.0 2.7 copy.34.mine
  16.6 2.8 constant_dynamic-slice_fusion.2
  20.6 3.8 relay.1.weight.refs_6_
  24.6 18.4 %collective-permute-start.3 = (bf16[1064,768]{1,0:T(8,128)(2,1)S(1)}, bf16[1064,768]{1,0:T(8,128)(2,1)S(1)}, u32[]{:S(2)}, u32[]{:S(2)}) collective-permute-start(bf16[1064,768]{1,0:T(8,128)(2,1)S(1)} %broadcast_select_fusion.own.tokens.refs_8_), channel_id=1, source_target_pairs={{0,2},{2,0},{1,3},{3,1},{4,6},{6,4},{5,7},{7,5},{8,10},{10,8},{9,1... | collective-permute-start | bytes 4902920 | tf_op jit(solution)/shard_map/ppermute | solution.py:1073
  45.6 2.9 collective-permute-start.6
  48.6 9.7 %project.1 = (bf16[2048,768]{1,0:T(8,128)(2,1)S(1)}, bf16[2048,1152]{1,0:T(8,128)(2,1)S(1)}, bf16[2048,128]{1,0:T(8,128)(2,1)S(1)}, bf16[2048,128]{1,0:T(8,128)(2,1)S(1)}) custom-call(s32[4]{0:T(128)S(1)} %get-tuple-element.194.scal, bf16[1064,768]{1,0:T(8,128)(2,1)S(1)} %collective-permute-done.3.oth, ...), custom_call_target="tpu_custom_call" | custom-call | flops 72477573120 | bytes 220200960 | tf_op jit(solution)/shard_map/project/pallas_call | solution.py:220
  60.9 13.7 %attend.2 = (bf16[1024,384]{1,0:T(8,128)(2,1)}, f32[1024,384]{1,0:T(8,128)S(1)}, f32[3,4,8,256]{3,2,1,0:T(8,128)S(1)}) custom-call(s32[4]{0:T(128)S(1)} %get-tuple-element.194.scal, bf16[2048,1152]{1,0:T(8,128)(2,1)S(1)} %get-tuple-element.109.q.qkv.k.v, bf16[2048,128]{1,0:T(8,128)(2,1)S(1)} %get-tuple-element.110.qfeat, ...), custom_call_target="tpu_custom_call" | custom-call | flops 257698037760 | bytes 251658240 | tf_op jit(solution)/shard_map/attend/pallas_call | solution.py:357
  74.6 7.9 %collective-permute-done.6.got_up = bf16[976,768]{1,0:T(8,128)(2,1)} collective-permute-done((bf16[976,768]{1,0:T(8,128)(2,1)}, bf16[976,768]{1,0:T(8,128)(2,1)}, u32[]{:S(2)}, u32[]{:S(2)}) %collective-permute-start.6) | collective-permute-done | bytes 1499168 | tf_op jit(solution)/shard_map/ppermute | solution.py:1076
  82.6 13.1 %attend.3 = (bf16[1024,384]{1,0:T(8,128)(2,1)S(1)}, f32[1024,384]{1,0:T(8,128)S(1)}, f32[3,4,8,256]{3,2,1,0:T(8,128)S(1)}) custom-call(s32[4]{0:T(128)S(1)} %get-tuple-element.153.scal, bf16[2048,1152]{1,0:T(8,128)(2,1)S(1)} %get-tuple-element.109.q.qkv.k.v, bf16[2048,128]{1,0:T(8,128)(2,1)S(1)} %get-tuple-element.110.qfeat, ...), custom_call_target="tpu_custom_call" | custom-call | flops 257698037760 | bytes 251658240 | tf_op jit(solution)/shard_map/attend/pallas_call | solution.py:357
  98.4 9.1 %collective-permute-done.7.got_down = bf16[768,768]{1,0:T(8,128)(2,1)} collective-permute-done((bf16[768,768]{1,0:T(8,128)(2,1)}, bf16[768,768]{1,0:T(8,128)(2,1)}, u32[]{:S(2)}, u32[]{:S(2)}) %collective-permute-start.7) | collective-permute-done | bytes 1179680 | tf_op jit(solution)/shard_map/ppermute | solution.py:1076
  109.1 2.4 collective-permute-done.5.mixed_oth
  112.8 38.9 %ahead.1 = (f32[1024,768]{1,0:T(8,128)}, f32[1024,768]{1,0:T(8,128)}, f32[1024,128]{1,0:T(8,128)S(1)}, bf16[1024,3072]{1,0:T(8,128)(2,1)}, bf16[1024,768]{1,0:T(...) custom-call(s32[4]{0:T(128)S(1)} %copy-done.14, ...), custom_call_target="tpu_custom_call" | custom-call | flops 314069483520 | bytes 546867200 | tf_op jit(solution)/shard_map/ahead/pallas_call | solution.py:651
  155.8 4.7 %collective-permute-done.10 = bf16[2,768,768]{2,1,0:T(8,128)(2,1)} collective-permute-done((bf16[2,768,768]{2,1,0:T(8,128)(2,1)}, bf16[2,768,768]{2,1,0:T(8,128)(2,1)}, u32[]{:S(2)}, u32[]{:S(2)}) %collective-permute-start.10) | collective-permute-done | bytes 2359328 | tf_op jit(solution)/shard_map/ppermute | solution.py:1073
  160.5 3.0 fusion.4
  163.5 2.5 collective-permute-start.11
  166.0 33.4 %behind.1 = (f32[1024,768]{1,0:T(8,128)}, bf16[1024,384]{1,0:T(8,128)(2,1)S(1)}, bf16[1024,384]{1,0:T(8,128)(2,1)S(1)}, f32[24,768]{1,0:T(8,128)S(1)}, f32[8,307...) custom-call(s32[4]{0:T(128)S(1)} %copy-done.14, ...), custom_call_target="tpu_custom_call" | custom-call | flops 338228674560 | bytes 315740160 | tf_op jit(solution)/shard_map/behind/pallas_call | solution.py:651
  199.4 2.7 bitcast_add_fusion.1
  205.3 4.1 collective-permute-done.12
  209.4 3.5 convert_add_fusion
  215.7 4.3 %collective-permute-done.14 = bf16[384,768]{1,0:T(8,128)(2,1)S(1)} collective-permute-done((bf16[384,768]{1,0:T(8,128)(2,1)S(1)}, bf16[384,768]{1,0:T(8,128)(2,1)S(1)}, u32[]{:S(2)}, u32[]{:S(2)}) %collective-permute-start.14) | collective-permute-done | bytes 589856 | tf_op jit(solution)/shard_map/ppermute | solution.py:1085
  222.4 2.3 collective-permute-start.13
  224.7 2.3 copy-done.31
  227.1 16.5 %attend_back.3 = (bf16[1024,384]{1,0:T(8,128)(2,1)S(1)}, bf16[1024,384]{1,0:T(8,128)(2,1)S(1)}) custom-call(s32[4]{0:T(128)S(1)} %copy-done.14, bf16[2048,1152]{1,0:T(8,128)(2,1)S(1)} %copy-done.31, bf16[2048,1152]{1,0:T(8,128)(2,1)S(1)} %copy-done.31, bf16[2048,128]{1,0:T(8,128)(2,1)S(1)} %copy-done.37, bf16[2048,1152]{1,0:T(8,128)(2,1)S(1)} %copy-done.31, ...), custom_call_target="tpu_custom_call" | custom-call | flops 429496729600 | bytes 157286400 | tf_op jit(solution)/shard_map/attend_back/pallas_call | solution.py:832
  245.9 12.3 %collective-permute-start.19 = (bf16[192,768]{1,0:T(8,128)(2,1)}, bf16[192,768]{1,0:T(8,128)(2,1)}, u32[]{:S(2)}, u32[]{:S(2)}) collective-permute-start(bf16[192,768]{1,0:T(8,128)(2,1)} %fusion.9), channel_id=1, source_target_pairs={{0,16},{4,20},{8,24},{12,28},{16,0},{20,4},{24,8},{28,12},{1,17},{... | collective-permute-start | bytes 884744 | tf_op jit(solution)/shard_map/ppermute | solution.py:1085
  258.2 2.6 bitcast_add_fusion
  263.6 16.4 %attend_back.4 = (bf16[1024,384]{1,0:T(8,128)(2,1)S(1)}, bf16[1024,384]{1,0:T(8,128)(2,1)S(1)}) custom-call(s32[4]{0:T(128)S(1)} %copy-done.19, bf16[2048,1152]{1,0:T(8,128)(2,1)S(1)} %bitcast.93, bf16[2048,1152]{1,0:T(8,128)(2,1)S(1)} %bitcast.93, bf16[2048,128]{1,0:T(8,128)(2,1)S(1)} %copy-done.37, bf16[2048,1152]{1,0:T(8,128)(2,1)S(1)} %bitcast.93, ...), custom_call_target="tpu_custom_call" | custom-call | flops 429496729600 | bytes 157286400 | tf_op jit(solution)/shard_map/attend_back/pallas_call | solution.py:832
  284.6 6.9 %collective-permute-start.23 = (bf16[192,768]{1,0:T(8,128)(2,1)S(1)}, bf16[192,768]{1,0:T(8,128)(2,1)S(1)}, u32[]{:S(2)}, u32[]{:S(2)}) collective-permute-start(bf16[192,768]{1,0:T(8,128)(2,1)S(1)} %add_convert_fusion.3), channel_id=1, source_target_pairs={{0,8},{4,12},{8,0},{12,4},{16,24},{20,28},{24,16},{28,20},{1,9},{5... | collective-permute-start | bytes 884744 | tf_op jit(solution)/shard_map/ppermute | solution.py:1085
  291.6 4.4 %project_grad.2 = (bf16[384,768]{1,0:T(8,128)(2,1)S(1)}, bf16[384,768]{1,0:T(8,128)(2,1)S(1)}, f32[8,768]{1,0:T(8,128)S(1)}) custom-call(s32[4]{0:T(128)S(1)} %copy-done.14, bf16[2048,768]{1,0:T(8,128)(2,1)S(1)} %copy-done.28, bf16[1024,384]{1,0:T(8,128)(2,1)S(1)} %copy-done.26, bf16[1024,384]{1,0:T(8,128)(2,1)S(1)} %get-tuple-element.155.refs_1_, ...), custom_call_target="tpu_custom_call" | custom-call | flops 48318382080 | bytes 125829120 | tf_op jit(solution)/shard_map/project_grad/pallas_call | solution.py:890
  296.6 2.7 collective-permute-done.23
  300.3 7.9 %collective-permute-start.49 = (bf16[384,768]{1,0:T(8,128)(2,1)}, bf16[384,768]{1,0:T(8,128)(2,1)}, u32[]{:S(2)}, u32[]{:S(2)}) collective-permute-start(bf16[384,768]{1,0:T(8,128)(2,1)} %pad_maximum_fusion.3), channel_id=1, source_target_pairs={{0,4},{4,0},{8,12},{12,8},{16,20},{20,16},{24,28},{28,24},{1,5},{5... | collective-permute-start | bytes 1769480 | tf_op jit(solution)/shard_map/ppermute | solution.py:1085
  309.1 2.9 collective-permute-start.26
  313.0 2.1 collective-permute-start.27
  315.1 16.6 %attend_back.5 = (bf16[1024,384]{1,0:T(8,128)(2,1)S(1)}, bf16[1024,384]{1,0:T(8,128)(2,1)S(1)}) custom-call(s32[4]{0:T(128)S(1)} %get-tuple-element.164.scal, bf16[2048,1152]{1,0:T(8,128)(2,1)S(1)} %bitcast.93, bf16[2048,1152]{1,0:T(8,128)(2,1)S(1)} %bitcast.93, bf16[2048,128]{1,0:T(8,128)(2,1)S(1)} %copy-done.37, bf16[2048,1152]{1,0:T(8,128)(2,1)S(1)} %bitcast.93, ...), custom_call_target="tpu_custom_call" | custom-call | flops 429496729600 | bytes 157286400 | tf_op jit(solution)/shard_map/attend_back/pallas_call | solution.py:832
  333.0 8.5 %collective-permute-start.29 = (bf16[240,768]{1,0:T(8,128)(2,1)S(1)}, bf16[240,768]{1,0:T(8,128)(2,1)S(1)}, u32[]{:S(2)}, u32[]{:S(2)}) collective-permute-start(bf16[240,768]{1,0:T(8,128)(2,1)S(1)} %add_convert_fusion.1), channel_id=1, source_target_pairs={{0,8},{4,12},{8,0},{12,4},{16,24},{20,28},{24,16},{28,20},{1,9},{5... | collective-permute-start | bytes 1105928 | tf_op jit(solution)/shard_map/ppermute | solution.py:1085
  343.0 6.3 %collective-permute-start.30 = (bf16[192,768]{1,0:T(8,128)(2,1)S(1)}, bf16[192,768]{1,0:T(8,128)(2,1)S(1)}, u32[]{:S(2)}, u32[]{:S(2)}) collective-permute-start(bf16[192,768]{1,0:T(8,128)(2,1)S(1)} %fusion.12), channel_id=1, source_target_pairs={{0,4},{4,0},{8,12},{12,8},{16,20},{20,16},{24,28},{28,24},{1,5},{5... | collective-permute-start | bytes 884744 | tf_op jit(solution)/shard_map/ppermute | solution.py:1085
  349.3 3.3 project_grad.3
  358.9 8.2 %first_grad.1 = (bf16[1024,768]{1,0:T(8,128)(2,1)S(1)}, f32[16,768]{1,0:T(8,128)S(1)}) custom-call(bf16[1024,384]{1,0:T(8,128)(2,1)S(1)} %get-tuple-element.150.refs_2_.refs_0_, bf16[1024,384]{1,0:T(8,128)(2,1)S(1)} %copy-done.33, bf16[1024,384]{1,0:T(8,128)(2,1)S(1)} %get-tuple-element.165.refs_1_.refs_2_, bf16[1024,384]{1,0:T(8,128)(2,1)S(1)} %copy-done.21, ...), custom_call_target="tpu_custom_call" | custom-call | flops 72477573120 | bytes 165150720 | tf_op jit(solution)/shard_map/first_grad/pallas_call | solution.py:932
  369.6 2.4 collective-permute-start.35
  382.6 6.9 %collective-permute-done.36 = bf16[192,384]{1,0:T(8,128)(2,1)S(1)} collective-permute-done((bf16[192,384]{1,0:T(8,128)(2,1)S(1)}, bf16[192,384]{1,0:T(8,128)(2,1)S(1)}, u32[]{:S(2)}, u32[]{:S(2)}) %collective-permute-start.36) | collective-permute-done | bytes 147488 | tf_op jit(solution)/shard_map/ppermute | solution.py:1085
  390.8 4.1 collective-permute-done.37
  395.0 2.6 collective-permute-start.44
  397.6 1.9 collective-permute-start.39
  403.8 2.5 maximum_convert_fusion.1
  408.3 6.4 %last.1 = f32[980,768]{1,0:T(8,128)} custom-call(s32[4]{0:T(128)S(1)} %copy-done.15, bf16[1064,768]{1,0:T(8,128)(2,1)S(1)} %pack.1.tokens, bf16[1024,768]{1,0:T(8,128)(2,1)S(1)} %get-tuple-element.195.grad, bf16[1024,768]{1,0:T(8,128)(2,1)S(1)} %collective-permute-done.42.grad_got, f32[1024,768]{1,0:T(8,128)} %get-tuple-element.136.residual, ...), custom_call_target="tpu_custom_call" | custom-call | flops 314572800 | bytes 188743680 | tf_op jit(solution)/shard_map/last/pallas_call | solution.py:963
  420.1 2.1 maximum_convert_fusion.2
  422.2 2.0 broadcast_select_fusion.2
  424.5 2.8 maximum_convert_fusion
  (376 shorter events, 81.9 us)
Async XLA Ops:
  7.4 6.4 %collective-permute-start.1 = (bf16[384,1152]{1,0:T(8,128)(2,1)}, bf16[384,1152]{1,0:T(8,128)(2,1)}, u32[]{:S(2)}, u32[]{:S(2)}) collective-permute-start(bf16[384,1152]{1,0:T(8,128)(2,1)} %copy.33), channel_id=1, source_target_pairs={{1,2},{2,1},{5,6},{6,5},{9,10},{10,9},{13,14},{14,13},{17,18},{18,... | collective-permute-start | bytes 2654216 | tf_op jit(solution)/shard_map/ppermute | solution.py:1070
  9.2 15.2 %collective-permute-start = (bf16[1064,768]{1,0:T(8,128)(2,1)S(1)}, bf16[1064,768]{1,0:T(8,128)(2,1)}, u32[]{:S(2)}, u32[]{:S(2)}) collective-permute-start(bf16[1064,768]{1,0:T(8,128)(2,1)S(1)} %pack.1.tokens), channel_id=1, source_target_pairs={{1,2},{2,1},{5,6},{6,5},{9,10},{10,9},{13,14},{14,13},{17,18},{18,... | collective-permute-start | bytes 4902920 | tf_op jit(solution)/shard_map/ppermute | solution.py:1070
  13.8 6.8 %collective-permute-start.2 = (bf16[384,1152]{1,0:T(8,128)(2,1)}, bf16[384,1152]{1,0:T(8,128)(2,1)}, u32[]{:S(2)}, u32[]{:S(2)}) collective-permute-start(bf16[384,1152]{1,0:T(8,128)(2,1)} %collective-permute-done.1.first), channel_id=1, source_target_pairs={{1,5},{2,6},{5,1},{6,2},{9,13},{10,14},{13,9},{14,10},{17,21},{18,... | collective-permute-start | bytes 2654216 | tf_op jit(solution)/shard_map/ppermute | solution.py:1119
  24.6 24.1 %collective-permute-start.3 = (bf16[1064,768]{1,0:T(8,128)(2,1)S(1)}, bf16[1064,768]{1,0:T(8,128)(2,1)S(1)}, u32[]{:S(2)}, u32[]{:S(2)}) collective-permute-start(bf16[1064,768]{1,0:T(8,128)(2,1)S(1)} %broadcast_select_fusion.own.tokens.refs_8_), channel_id=1, source_target_pairs={{0,2},{2,0},{1,3},{3,1},{4,6},{6,4},{5,7},{7,5},{8,10},{10,8},{9,1... | collective-permute-start | bytes 4902920 | tf_op jit(solution)/shard_map/ppermute | solution.py:1073
  45.6 36.9 %collective-permute-start.6 = (bf16[976,768]{1,0:T(8,128)(2,1)}, bf16[976,768]{1,0:T(8,128)(2,1)}, u32[]{:S(2)}, u32[]{:S(2)}) collective-permute-start(bf16[976,768]{1,0:T(8,128)(2,1)} %fusion.1), channel_id=1, source_target_pairs={{0,1},{1,0},{2,3},{3,2},{4,5},{5,4},{6,7},{7,6},{8,9},{9,8},{10,11... | collective-permute-start | bytes 4497416 | tf_op jit(solution)/shard_map/ppermute | solution.py:1076
  60.1 22.4 %collective-permute-start.4 = (bf16[768,1152]{1,0:T(8,128)(2,1)}, bf16[768,1152]{1,0:T(8,128)(2,1)}, u32[]{:S(2)}, u32[]{:S(2)}) collective-permute-start(bf16[768,1152]{1,0:T(8,128)(2,1)} %relay.1.weight.refs_6_), channel_id=1, source_target_pairs={{0,2},{2,0},{1,3},{3,1},{4,6},{6,4},{5,7},{7,5},{8,10},{10,8},{9,1... | collective-permute-start | bytes 5308424 | tf_op jit(solution)/shard_map/ppermute | solution.py:1073
  60.3 47.2 %collective-permute-start.7 = (bf16[768,768]{1,0:T(8,128)(2,1)}, bf16[768,768]{1,0:T(8,128)(2,1)}, u32[]{:S(2)}, u32[]{:S(2)}) collective-permute-start(bf16[768,768]{1,0:T(8,128)(2,1)} %get-tuple-element.117), channel_id=1, source_target_pairs={{0,1},{1,0},{2,3},{3,2},{4,5},{5,4},{6,7},{7,6},{8,9},{9,8},{10,11... | collective-permute-start | bytes 3538952 | tf_op jit(solution)/shard_map/ppermute | solution.py:1076
  82.5 29.0 %collective-permute-start.8 = (bf16[976,768]{1,0:T(8,128)(2,1)}, bf16[976,768]{1,0:T(8,128)(2,1)}, u32[]{:S(2)}, u32[]{:S(2)}) collective-permute-start(bf16[976,768]{1,0:T(8,128)(2,1)} %collective-permute-done.6.got_up), channel_id=1, source_target_pairs={{0,2},{2,0},{1,3},{3,1},{4,6},{6,4},{5,7},{7,5},{8,10},{10,8},{9,1... | collective-permute-start | bytes 4497416 | tf_op jit(solution)/shard_map/ppermute | solution.py:1073
  107.5 4.2 collective-permute-start.9
  107.5 3.9 collective-permute-start.5
  155.6 4.9 %collective-permute-start.10 = (bf16[2,768,768]{2,1,0:T(8,128)(2,1)}, bf16[2,768,768]{2,1,0:T(8,128)(2,1)}, u32[]{:S(2)}, u32[]{:S(2)}) collective-permute-start(bf16[2,768,768]{2,1,0:T(8,128)(2,1)} %get-tuple-element.121), channel_id=1, source_target_pairs={{0,2},{2,0},{1,3},{3,1},{4,6},{6,4},{5,7},{7,5},{8,10},{10,8},{9,1... | collective-permute-start | bytes 7077896 | tf_op jit(solution)/shard_map/ppermute | solution.py:1073
  163.5 35.9 %collective-permute-start.11 = (bf16[768,768]{1,0:T(8,128)(2,1)}, bf16[768,768]{1,0:T(8,128)(2,1)}, u32[]{:S(2)}, u32[]{:S(2)}) collective-permute-start(bf16[768,768]{1,0:T(8,128)(2,1)} %fusion.4), channel_id=1, source_target_pairs={{0,1},{1,0},{2,3},{3,2},{4,5},{5,4},{6,7},{7,6},{8,9},{9,8},{10,11... | collective-permute-start | bytes 3538952 | tf_op jit(solution)/shard_map/ppermute | solution.py:1076
  203.6 5.8 %collective-permute-start.12 = (bf16[2,960,768]{2,1,0:T(8,128)(2,1)}, bf16[2,960,768]{2,1,0:T(8,128)(2,1)}, u32[]{:S(2)}, u32[]{:S(2)}) collective-permute-start(bf16[2,960,768]{2,1,0:T(8,128)(2,1)} %get-tuple-element.133), channel_id=1, source_target_pairs={{0,2},{2,0},{1,3},{3,1},{4,6},{6,4},{5,7},{7,5},{8,10},{10,8},{9,1... | collective-permute-start | bytes 8847368 | tf_op jit(solution)/shard_map/ppermute | solution.py:1073
  203.7 16.2 %collective-permute-start.14 = (bf16[384,768]{1,0:T(8,128)(2,1)S(1)}, bf16[384,768]{1,0:T(8,128)(2,1)S(1)}, u32[]{:S(2)}, u32[]{:S(2)}) collective-permute-start(bf16[384,768]{1,0:T(8,128)(2,1)S(1)} %fusion.6), channel_id=1, source_target_pairs={{0,4},{4,0},{8,12},{12,8},{16,20},{20,16},{24,28},{28,24},{1,5},{5... | collective-permute-start | bytes 1769480 | tf_op jit(solution)/shard_map/ppermute | solution.py:1085
  205.2 19.5 %collective-permute-start.15 = (bf16[1024,384]{1,0:T(8,128)(2,1)}, bf16[1024,384]{1,0:T(8,128)(2,1)S(1)}, u32[]{:S(2)}, u32[]{:S(2)}) collective-permute-start(bf16[1024,384]{1,0:T(8,128)(2,1)} %copy-done.24), channel_id=1, source_target_pairs={{0,2},{2,0},{1,3},{3,1},{4,6},{6,4},{5,7},{7,5},{8,10},{10,8},{9,1... | collective-permute-start | bytes 2359304 | tf_op jit(solution)/shard_map/ppermute | solution.py:1073
  214.2 44.0 %collective-permute-start.17 = (bf16[2,480,768]{2,1,0:T(8,128)(2,1)}, bf16[2,480,768]{2,1,0:T(8,128)(2,1)}, u32[]{:S(2)}, u32[]{:S(2)}) collective-permute-start(bf16[2,480,768]{2,1,0:T(8,128)(2,1)} %fusion.2), channel_id=1, source_target_pairs={{0,4},{4,0},{8,12},{12,8},{16,20},{20,16},{24,28},{28,24},{1,5},{5... | collective-permute-start | bytes 4423688 | tf_op jit(solution)/shard_map/ppermute | solution.py:1085
  220.9 23.1 %collective-permute-start.16 = (bf16[192,768]{1,0:T(8,128)(2,1)}, bf16[192,768]{1,0:T(8,128)(2,1)}, u32[]{:S(2)}, u32[]{:S(2)}) collective-permute-start(bf16[192,768]{1,0:T(8,128)(2,1)} %fusion.11), channel_id=1, source_target_pairs={{0,8},{4,12},{8,0},{12,4},{16,24},{20,28},{24,16},{28,20},{1,9},{5... | collective-permute-start | bytes 884744 | tf_op jit(solution)/shard_map/ppermute | solution.py:1085
  222.4 41.2 %collective-permute-start.13 = (f32[1024,768]{1,0:T(8,128)}, f32[1024,768]{1,0:T(8,128)}, u32[]{:S(2)}, u32[]{:S(2)}) collective-permute-start(f32[1024,768]{1,0:T(8,128)} %get-tuple-element.136.residual), channel_id=1, source_target_pairs={{1,2},{2,1},{5,6},{6,5},{9,10},{10,9},{13,14},{14,13},{17,18},{18,... | collective-permute-start | bytes 9437192 | tf_op jit(solution)/shard_map/ppermute | solution.py:1070
  243.6 19.9 %collective-permute-start.18 = (bf16[1024,384]{1,0:T(8,128)(2,1)S(1)}, bf16[1024,384]{1,0:T(8,128)(2,1)S(1)}, u32[]{:S(2)}, u32[]{:S(2)}) collective-permute-start(bf16[1024,384]{1,0:T(8,128)(2,1)S(1)} %get-tuple-element.146.refs_0_), channel_id=1, source_target_pairs={{0,2},{2,0},{1,3},{3,1},{4,6},{6,4},{5,7},{7,5},{8,10},{10,8},{9,1... | collective-permute-start | bytes 2359304 | tf_op jit(solution)/shard_map/ppermute | solution.py:1073
  245.9 36.8 %collective-permute-start.19 = (bf16[192,768]{1,0:T(8,128)(2,1)}, bf16[192,768]{1,0:T(8,128)(2,1)}, u32[]{:S(2)}, u32[]{:S(2)}) collective-permute-start(bf16[192,768]{1,0:T(8,128)(2,1)} %fusion.9), channel_id=1, source_target_pairs={{0,16},{4,20},{8,24},{12,28},{16,0},{20,4},{24,8},{28,12},{1,17},{... | collective-permute-start | bytes 884744 | tf_op jit(solution)/shard_map/ppermute | solution.py:1085
  261.9 18.9 %collective-permute-start.20 = (bf16[480,768]{1,0:T(8,128)(2,1)}, bf16[480,768]{1,0:T(8,128)(2,1)}, u32[]{:S(2)}, u32[]{:S(2)}) collective-permute-start(bf16[480,768]{1,0:T(8,128)(2,1)} %fusion.5), channel_id=1, source_target_pairs={{0,1},{1,0},{2,3},{3,2},{4,5},{5,4},{6,7},{7,6},{8,9},{9,8},{10,11... | collective-permute-start | bytes 2211848 | tf_op jit(solution)/shard_map/ppermute | solution.py:1076
  284.6 14.7 %collective-permute-start.23 = (bf16[192,768]{1,0:T(8,128)(2,1)S(1)}, bf16[192,768]{1,0:T(8,128)(2,1)S(1)}, u32[]{:S(2)}, u32[]{:S(2)}) collective-permute-start(bf16[192,768]{1,0:T(8,128)(2,1)S(1)} %add_convert_fusion.3), channel_id=1, source_target_pairs={{0,8},{4,12},{8,0},{12,4},{16,24},{20,28},{24,16},{28,20},{1,9},{5... | collective-permute-start | bytes 884744 | tf_op jit(solution)/shard_map/ppermute | solution.py:1085
  291.5 16.8 %collective-permute-start.22 = (bf16[240,768]{1,0:T(8,128)(2,1)S(1)}, bf16[240,768]{1,0:T(8,128)(2,1)S(1)}, u32[]{:S(2)}, u32[]{:S(2)}) collective-permute-start(bf16[240,768]{1,0:T(8,128)(2,1)S(1)} %fusion.10), channel_id=1, source_target_pairs={{0,8},{4,12},{8,0},{12,4},{16,24},{20,28},{24,16},{28,20},{1,9},{5... | collective-permute-start | bytes 1105928 | tf_op jit(solution)/shard_map/ppermute | solution.py:1085
  291.6 23.5 %collective-permute-start.24 = (bf16[1024,384]{1,0:T(8,128)(2,1)S(1)}, bf16[1024,384]{1,0:T(8,128)(2,1)S(1)}, u32[]{:S(2)}, u32[]{:S(2)}) collective-permute-start(bf16[1024,384]{1,0:T(8,128)(2,1)S(1)} %get-tuple-element.155.refs_1_), channel_id=1, source_target_pairs={{0,2},{2,0},{1,3},{3,1},{4,6},{6,4},{5,7},{7,5},{8,10},{10,8},{9,1... | collective-permute-start | bytes 2359304 | tf_op jit(solution)/shard_map/ppermute | solution.py:1073
  296.0 16.0 %collective-permute-start.21 = (bf16[384,768]{1,0:T(8,128)(2,1)S(1)}, bf16[384,768]{1,0:T(8,128)(2,1)S(1)}, u32[]{:S(2)}, u32[]{:S(2)}) collective-permute-start(bf16[384,768]{1,0:T(8,128)(2,1)S(1)} %get-tuple-element.160), channel_id=1, source_target_pairs={{0,2},{2,0},{1,3},{3,1},{4,6},{6,4},{5,7},{7,5},{8,10},{10,8},{9,1... | collective-permute-start | bytes 1769480 | tf_op jit(solution)/shard_map/ppermute | solution.py:1073
  300.3 52.3 %collective-permute-start.49 = (bf16[384,768]{1,0:T(8,128)(2,1)}, bf16[384,768]{1,0:T(8,128)(2,1)}, u32[]{:S(2)}, u32[]{:S(2)}) collective-permute-start(bf16[384,768]{1,0:T(8,128)(2,1)} %pad_maximum_fusion.3), channel_id=1, source_target_pairs={{0,4},{4,0},{8,12},{12,8},{16,20},{20,16},{24,28},{28,24},{1,5},{5... | collective-permute-start | bytes 1769480 | tf_op jit(solution)/shard_map/ppermute | solution.py:1085
  309.1 22.6 %collective-permute-start.26 = (bf16[240,768]{1,0:T(8,128)(2,1)}, bf16[240,768]{1,0:T(8,128)(2,1)}, u32[]{:S(2)}, u32[]{:S(2)}) collective-permute-start(bf16[240,768]{1,0:T(8,128)(2,1)} %fusion.7), channel_id=1, source_target_pairs={{0,16},{4,20},{8,24},{12,28},{16,0},{20,4},{24,8},{28,12},{1,17},{... | collective-permute-start | bytes 1105928 | tf_op jit(solution)/shard_map/ppermute | solution.py:1085
  313.0 28.6 %collective-permute-start.27 = (bf16[384,768]{1,0:T(8,128)(2,1)}, bf16[384,768]{1,0:T(8,128)(2,1)}, u32[]{:S(2)}, u32[]{:S(2)}) collective-permute-start(bf16[384,768]{1,0:T(8,128)(2,1)} %broadcast_select_fusion.11), channel_id=1, source_target_pairs={{0,1},{1,0},{2,3},{3,2},{4,5},{5,4},{6,7},{7,6},{8,9},{9,8},{10,11... | collective-permute-start | bytes 1769480 | tf_op jit(solution)/shard_map/ppermute | solution.py:1076
  331.7 27.1 %collective-permute-start.25 = (bf16[1024,384]{1,0:T(8,128)(2,1)S(1)}, bf16[1024,384]{1,0:T(8,128)(2,1)S(1)}, u32[]{:S(2)}, u32[]{:S(2)}) collective-permute-start(bf16[1024,384]{1,0:T(8,128)(2,1)S(1)} %get-tuple-element.166.refs_0_), channel_id=1, source_target_pairs={{0,2},{2,0},{1,3},{3,1},{4,6},{6,4},{5,7},{7,5},{8,10},{10,8},{9,1... | collective-permute-start | bytes 2359304 | tf_op jit(solution)/shard_map/ppermute | solution.py:1073
  333.0 22.2 %collective-permute-start.29 = (bf16[240,768]{1,0:T(8,128)(2,1)S(1)}, bf16[240,768]{1,0:T(8,128)(2,1)S(1)}, u32[]{:S(2)}, u32[]{:S(2)}) collective-permute-start(bf16[240,768]{1,0:T(8,128)(2,1)S(1)} %add_convert_fusion.1), channel_id=1, source_target_pairs={{0,8},{4,12},{8,0},{12,4},{16,24},{20,28},{24,16},{28,20},{1,9},{5... | collective-permute-start | bytes 1105928 | tf_op jit(solution)/shard_map/ppermute | solution.py:1085
  343.0 13.8 %collective-permute-start.30 = (bf16[192,768]{1,0:T(8,128)(2,1)S(1)}, bf16[192,768]{1,0:T(8,128)(2,1)S(1)}, u32[]{:S(2)}, u32[]{:S(2)}) collective-permute-start(bf16[192,768]{1,0:T(8,128)(2,1)S(1)} %fusion.12), channel_id=1, source_target_pairs={{0,4},{4,0},{8,12},{12,8},{16,20},{20,16},{24,28},{28,24},{1,5},{5... | collective-permute-start | bytes 884744 | tf_op jit(solution)/shard_map/ppermute | solution.py:1085
  355.1 42.5 %collective-permute-start.50 = (bf16[768,768]{1,0:T(8,128)(2,1)}, bf16[768,768]{1,0:T(8,128)(2,1)}, u32[]{:S(2)}, u32[]{:S(2)}) collective-permute-start(bf16[768,768]{1,0:T(8,128)(2,1)} %pad_maximum_fusion.1), channel_id=1, source_target_pairs={{0,2},{2,0},{1,3},{3,1},{4,6},{6,4},{5,7},{7,5},{8,10},{10,8},{9,1... | collective-permute-start | bytes 3538952 | tf_op jit(solution)/shard_map/ppermute | solution.py:1073
  355.3 3.4 collective-permute-start.28
  356.9 10.8 %collective-permute-start.33 = (bf16[192,768]{1,0:T(8,128)(2,1)S(1)}, bf16[192,768]{1,0:T(8,128)(2,1)S(1)}, u32[]{:S(2)}, u32[]{:S(2)}) collective-permute-start(bf16[192,768]{1,0:T(8,128)(2,1)S(1)} %fusion.14), channel_id=1, source_target_pairs={{0,8},{4,12},{8,0},{12,4},{16,24},{20,28},{24,16},{28,20},{1,9},{5... | collective-permute-start | bytes 884744 | tf_op jit(solution)/shard_map/ppermute | solution.py:1085
  358.7 9.9 %collective-permute-start.32 = (bf16[384,384]{1,0:T(8,128)(2,1)S(1)}, bf16[384,384]{1,0:T(8,128)(2,1)S(1)}, u32[]{:S(2)}, u32[]{:S(2)}) collective-permute-start(bf16[384,384]{1,0:T(8,128)(2,1)S(1)} %broadcast_select_fusion.18), channel_id=1, source_target_pairs={{0,1},{1,0},{2,3},{3,2},{4,5},{5,4},{6,7},{7,6},{8,9},{9,8},{10,11... | collective-permute-start | bytes 884744 | tf_op jit(solution)/shard_map/ppermute | solution.py:1076
  369.6 7.1 %collective-permute-start.35 = (bf16[192,384]{1,0:T(8,128)(2,1)}, bf16[192,384]{1,0:T(8,128)(2,1)S(1)}, u32[]{:S(2)}, u32[]{:S(2)}) collective-permute-start(bf16[192,384]{1,0:T(8,128)(2,1)} %fusion.15), channel_id=1, source_target_pairs={{0,4},{4,0},{8,12},{12,8},{16,20},{20,16},{24,28},{28,24},{1,5},{5... | collective-permute-start | bytes 442376 | tf_op jit(solution)/shard_map/ppermute | solution.py:1085
  372.2 18.3 %collective-permute-start.38 = (bf16[192,768]{1,0:T(8,128)(2,1)}, bf16[192,768]{1,0:T(8,128)(2,1)S(1)}, u32[]{:S(2)}, u32[]{:S(2)}) collective-permute-start(bf16[192,768]{1,0:T(8,128)(2,1)} %fusion.8), channel_id=1, source_target_pairs={{0,16},{4,20},{8,24},{12,28},{16,0},{20,4},{24,8},{28,12},{1,17},{... | collective-permute-start | bytes 884744 | tf_op jit(solution)/shard_map/ppermute | solution.py:1085
  375.0 5.9 %collective-permute-start.34 = (f32[24,768]{1,0:T(8,128)S(1)}, f32[24,768]{1,0:T(8,128)S(1)}, u32[]{:S(2)}, u32[]{:S(2)}) collective-permute-start(f32[24,768]{1,0:T(8,128)S(1)} %add.160), channel_id=1, source_target_pairs={{0,1},{1,0},{2,3},{3,2},{4,5},{5,4},{6,7},{7,6},{8,9},{9,8},{10,11... | collective-permute-start | bytes 221192 | tf_op jit(solution)/shard_map/ppermute | solution.py:1076
  377.7 11.7 %collective-permute-start.36 = (bf16[192,384]{1,0:T(8,128)(2,1)S(1)}, bf16[192,384]{1,0:T(8,128)(2,1)S(1)}, u32[]{:S(2)}, u32[]{:S(2)}) collective-permute-start(bf16[192,384]{1,0:T(8,128)(2,1)S(1)} %fusion.16), channel_id=1, source_target_pairs={{0,8},{4,12},{8,0},{12,4},{16,24},{20,28},{24,16},{28,20},{1,9},{5... | collective-permute-start | bytes 442376 | tf_op jit(solution)/shard_map/ppermute | solution.py:1085
  380.0 28.3 %collective-permute-start.42 = (bf16[1024,768]{1,0:T(8,128)(2,1)S(1)}, bf16[1024,768]{1,0:T(8,128)(2,1)S(1)}, u32[]{:S(2)}, u32[]{:S(2)}) collective-permute-start(bf16[1024,768]{1,0:T(8,128)(2,1)S(1)} %get-tuple-element.195.grad), channel_id=1, source_target_pairs={{1,2},{2,1},{5,6},{6,5},{9,10},{10,9},{13,14},{14,13},{17,18},{18,... | collective-permute-start | bytes 4718600 | tf_op jit(solution)/shard_map/ppermute | solution.py:1070
  380.9 20.4 %collective-permute-start.41 = (bf16[480,768]{1,0:T(8,128)(2,1)}, bf16[480,768]{1,0:T(8,128)(2,1)S(1)}, u32[]{:S(2)}, u32[]{:S(2)}) collective-permute-start(bf16[480,768]{1,0:T(8,128)(2,1)} %pad_maximum_fusion.2), channel_id=1, source_target_pairs={{0,4},{4,0},{8,12},{12,8},{16,20},{20,16},{24,28},{28,24},{1,5},{5... | collective-permute-start | bytes 2211848 | tf_op jit(solution)/shard_map/ppermute | solution.py:1085
  390.5 12.8 %collective-permute-start.40 = (bf16[192,384]{1,0:T(8,128)(2,1)S(1)}, bf16[192,384]{1,0:T(8,128)(2,1)S(1)}, u32[]{:S(2)}, u32[]{:S(2)}) collective-permute-start(bf16[192,384]{1,0:T(8,128)(2,1)S(1)} %fusion.13), channel_id=1, source_target_pairs={{0,16},{4,20},{8,24},{12,28},{16,0},{20,4},{24,8},{28,12},{1,17},{... | collective-permute-start | bytes 442376 | tf_op jit(solution)/shard_map/ppermute | solution.py:1085
  390.6 4.4 %collective-permute-start.37 = (f32[24,768]{1,0:T(8,128)S(1)}, f32[24,768]{1,0:T(8,128)S(1)}, u32[]{:S(2)}, u32[]{:S(2)}) collective-permute-start(f32[24,768]{1,0:T(8,128)S(1)} %add.162), channel_id=1, source_target_pairs={{0,8},{4,12},{8,0},{12,4},{16,24},{20,28},{24,16},{28,20},{1,9},{5... | collective-permute-start | bytes 221192 | tf_op jit(solution)/shard_map/ppermute | solution.py:1085
  395.0 20.9 %collective-permute-start.44 = (bf16[192,768]{1,0:T(8,128)(2,1)S(1)}, bf16[192,768]{1,0:T(8,128)(2,1)S(1)}, u32[]{:S(2)}, u32[]{:S(2)}) collective-permute-start(bf16[192,768]{1,0:T(8,128)(2,1)S(1)} %add_convert_fusion.2), channel_id=1, source_target_pairs={{0,4},{4,0},{8,12},{12,8},{16,20},{20,16},{24,28},{28,24},{1,5},{5... | collective-permute-start | bytes 884744 | tf_op jit(solution)/shard_map/ppermute | solution.py:1085
  397.6 5.7 %collective-permute-start.39 = (f32[24,768]{1,0:T(8,128)S(1)}, f32[24,768]{1,0:T(8,128)S(1)}, u32[]{:S(2)}, u32[]{:S(2)}) collective-permute-start(f32[24,768]{1,0:T(8,128)S(1)} %add.165), channel_id=1, source_target_pairs={{0,16},{4,20},{8,24},{12,28},{16,0},{20,4},{24,8},{28,12},{1,17},{... | collective-permute-start | bytes 221192 | tf_op jit(solution)/shard_map/ppermute | solution.py:1085
  403.3 11.4 %collective-permute-start.43 = (f32[24,768]{1,0:T(8,128)S(1)}, f32[24,768]{1,0:T(8,128)S(1)}, u32[]{:S(2)}, u32[]{:S(2)}) collective-permute-start(f32[24,768]{1,0:T(8,128)S(1)} %add.167), channel_id=1, source_target_pairs={{0,4},{4,0},{8,12},{12,8},{16,20},{20,16},{24,28},{28,24},{1,5},{5... | collective-permute-start | bytes 221192 | tf_op jit(solution)/shard_map/ppermute | solution.py:1085
  406.3 15.9 %collective-permute-start.48 = (bf16[960,768]{1,0:T(8,128)(2,1)}, bf16[960,768]{1,0:T(8,128)(2,1)}, u32[]{:S(2)}, u32[]{:S(2)}) collective-permute-start(bf16[960,768]{1,0:T(8,128)(2,1)} %pad_maximum_fusion), channel_id=1, source_target_pairs={{0,2},{2,0},{1,3},{3,1},{4,6},{6,4},{5,7},{7,5},{8,10},{10,8},{9,1... | collective-permute-start | bytes 4423688 | tf_op jit(solution)/shard_map/ppermute | solution.py:1073
  407.5 9.2 %collective-permute-start.46 = (bf16[192,384]{1,0:T(8,128)(2,1)S(1)}, bf16[192,384]{1,0:T(8,128)(2,1)S(1)}, u32[]{:S(2)}, u32[]{:S(2)}) collective-permute-start(bf16[192,384]{1,0:T(8,128)(2,1)S(1)} %add_convert_fusion.4), channel_id=1, source_target_pairs={{0,4},{4,0},{8,12},{12,8},{16,20},{20,16},{24,28},{28,24},{1,5},{5... | collective-permute-start | bytes 442376 | tf_op jit(solution)/shard_map/ppermute | solution.py:1085
  (105 other events, 1247.5 us)

commit v4 on v2

--- a/solution.py
+++ b/solution.py
@@ -835,9 +835,14 @@
     )(scal, qkv, qkv, kfeat, qkv, qfeat, grad_oth, grad_own, *wide, *logs)
 
 
-def project_grad_kernel(pairs, scal, first, *refs):
+def project_grad_kernel(pairs, more, scal, first, *refs):
     oth, own = refs[:pairs], refs[pairs : 2 * pairs]
-    theirs, mine, offsets = refs[2 * pairs :]
+    refs = refs[2 * pairs :]
+    if more:
+        got, weight_mine, weight_theirs = refs[:pairs], refs[pairs], refs[pairs + 1]
+        theirs, mine, offsets, part = refs[pairs + 2 :]
+    else:
+        theirs, mine, offsets = refs
     step = pl.program_id(0)
     half = oth[0].shape[0]
     one = jnp.concatenate([x[...] for x in oth], axis=1)
@@ -853,38 +858,51 @@
     def _():
         mine[...] = out
 
-
-def project_grad(scal, first, oth, own):
+    if more:
+        lines = half // 2
+        rows = pl.ds(pl.multiple_of(step * lines, BLK), lines)
+        total = nt(jnp.concatenate([x[rows, :] for x in own], axis=1), weight_mine[...])
+        part[...] = total + nt(
+            jnp.concatenate([x[rows, :] for x in got], axis=1), weight_theirs[...]
+        )
+
+
+def project_grad(scal, first, oth, own, *more):
     pairs = len(oth)
     rows, width = first.shape
     cols = 384 * pairs
+    got, weights = (more[0], more[1:]) if more else ((), ())
+    weight = pl.BlockSpec((width, cols), lambda *_: (0, 0), pipeline_mode=pl.Buffered(1))
+    shapes = [
+        jax.ShapeDtypeStruct((width // 2, cols), BF16),
+        jax.ShapeDtypeStruct((width // 2, cols), BF16),
+        jax.ShapeDtypeStruct((8, cols), F32),
+    ]
+    specs = [held((width // 2, cols)), held((width // 2, cols)), held((8, cols))]
+    if more:
+        shapes.append(jax.ShapeDtypeStruct((rows // 2, width), F32))
+        specs.append(pl.BlockSpec((rows // 4, width), lambda n, *_: (n, 0)))
     return pl.pallas_call(
-        functools.partial(project_grad_kernel, pairs),
+        functools.partial(project_grad_kernel, pairs, bool(more)),
         grid_spec=pltpu.PrefetchScalarGridSpec(
             num_scalar_prefetch=1,
             grid=(2,),
             in_specs=[
                 pl.BlockSpec((rows, width // 2), lambda n, scal: (0, (1 - scal[0]) ^ n)),
             ]
-            + [whole((rows // 2, 384))] * (2 * pairs),
-            out_specs=[held((width // 2, cols)), held((width // 2, cols)), held((8, cols))],
+            + [whole((rows // 2, 384))] * (2 * pairs + len(got))
+            + [weight] * len(weights),
+            out_specs=specs,
         ),
-        out_shape=[
-            jax.ShapeDtypeStruct((width // 2, cols), BF16),
-            jax.ShapeDtypeStruct((width // 2, cols), BF16),
-            jax.ShapeDtypeStruct((8, cols), F32),
-        ],
-        compiler_params=params(1, 12),
+        out_shape=shapes,
+        compiler_params=params(1, 24),
         cost_estimate=cost(2 * rows * width * cols, 2 * rows * (width + cols)),
         name="project_grad",
-    )(scal, first, *oth, *own)
-
-
-def first_grad_kernel(pairs, *refs):
-    own, got = refs[:pairs], refs[pairs : 2 * pairs]
-    mine, theirs, tokens, out, sums = refs[2 * pairs :]
-    total = nt(jnp.concatenate([x[...] for x in own], axis=1), mine[...])
-    total = total + nt(jnp.concatenate([x[...] for x in got], axis=1), theirs[...])
+    )(scal, first, *oth, *own, *got, *weights)
+
+
+def first_grad_kernel(own, got, mine, theirs, part, tokens, out, sums):
+    total = part[...] + nt(own[...], mine[...]) + nt(got[...], theirs[...])
     out[...] = total.astype(BF16)
 
     @pl.when(pl.program_id(0) == 0)
@@ -896,29 +914,27 @@
     sums[8:16, :] += fold8(total)
 
 
-def first_grad(own, got, mine, theirs, packed):
-    pairs = len(own)
-    rows, cols = own[0].shape
+def first_grad(own, got, mine, theirs, part, packed):
+    rows, cols = own.shape
     width = mine.shape[0]
+    last_pair = mine.shape[1] // cols - 1
+    weight = pl.BlockSpec(
+        (width, cols), lambda *_: (0, last_pair), pipeline_mode=pl.Buffered(1)
+    )
+    row = pl.BlockSpec((BLK, width), lambda i: (i, 0))
     return pl.pallas_call(
-        functools.partial(first_grad_kernel, pairs),
+        first_grad_kernel,
         grid=(rows // BLK,),
-        in_specs=[pl.BlockSpec((BLK, cols), lambda i: (i, 0))] * (2 * pairs)
-        + [whole(mine.shape), whole(theirs.shape), pl.BlockSpec((BLK, width), lambda i: (i, 0))],
-        out_specs=[
-            pl.BlockSpec((BLK, width), lambda i: (i, 0)),
-            pl.BlockSpec((16, width), lambda i: (0, 0)),
-        ],
+        in_specs=[pl.BlockSpec((BLK, cols), lambda i: (i, 0))] * 2 + [weight] * 2 + [row] * 2,
+        out_specs=[row, pl.BlockSpec((16, width), lambda i: (0, 0))],
         out_shape=[
             jax.ShapeDtypeStruct((rows, width), BF16),
             jax.ShapeDtypeStruct((16, width), F32),
         ],
-        compiler_params=params(1, 12),
-        cost_estimate=cost(
-            4 * pairs * rows * width * cols, 4 * pairs * rows * cols + 4 * width * cols * pairs
-        ),
+        compiler_params=params(1, 16),
+        cost_estimate=cost(4 * rows * width * cols, 12 * rows * width),
         name="first_grad",
-    )(*own, *got, mine, theirs, packed)
+    )(own, got, mine, theirs, part, packed)
 
 
 def last_kernel(scal, tokens, grad, grad_got, residual, residual_got, gain, out):
@@ -1269,16 +1285,22 @@
     down_z = hop(down_sum, hops[0])
     up_send, up_keep = split(plus(up_y[1], after(up_y_got, oth_1)))
     up_z = hop(up_send, hops[0])
-    their_0, mine_0, offsets_0 = project_grad(
-        after(scal, down_sum, up_send), first, (oth_0, oth_1), (own_0, own_1)
+    their_0, mine_0, offsets_0, part = project_grad(
+        after(scal, down_sum, up_send),
+        first,
+        (oth_0, oth_1),
+        (own_0, own_1),
+        (got_0, got_1),
+        weight_here,
+        weight_there,
     )
     early_send, early_keep = project_fold(their_0, mine_0)
     early_got = to_plane(early_send)
-    up_sum = plus(up_keep, after(up_z, mine_0))
+    up_sum = plus(up_keep, after(up_z, part))
     up_low = low(up_sum)
     up_z = hop(up_low, hops[1])
 
-    down_sum = join(down_sum, after(down_z, mine_0), bit, 0)
+    down_sum = join(down_sum, after(down_z, part), bit, 0)
     down_x = hop(down_sum, 1)
 
     oth_2, own_2 = back(2, early_send, up_low, down_sum, got_1)
@@ -1301,10 +1323,11 @@
     early_low = low(early_sum)
     early_z = hop(early_low, hops[0])
     first_low, first_sums = first_grad(
-        (own_0, own_1, own_2),
-        (got_0, got_1, got_2),
+        own_2,
+        got_2,
         weight_here,
         weight_there,
+        part,
         after(own, late_send, up_sum, early_low),
     )
     first_got = turn(first_low)

time: 435 us -> 435 us (level)
  starting transfers between devices: 85.4 us -> 75.3 us
  local copies, waits for them, and re-layouts: 38.4 us -> 44.1 us
    ppermute x21, starting transfers between devices: 48.3 us -> 37.1 us  [hop(): return lax.ppermute(x, 'chip', [(i, i ^ step) for i in range(chips)])]
    unnamed x206 -> x222, local copies, waits for them, and re-layouts: 17.9 us -> 23.7 us
  transfers between devices with their start and end apart: 51 -> 51, of which waited for: 9 -> 14; matrix products, arithmetic and copies ran while one was open for 12% -> 12% of each run, Pallas kernels for 42% -> 43%
where the time goes in v4:
time: 435 us; the launch traced here: 428 us
  Pallas kernels  224 us (51%)
  starting transfers between devices  75.3 us (17%)
  other arithmetic  46.9 us (11%)
  local copies, waits for them, and re-layouts  44.1 us (10%)
  waiting for transfers between devices  33.9 us (8%)
    pallas_call x3, Pallas kernels, attend_back(): pl.pallas_call(functools.partial(attend_back_kernel, frames_here), grid_s...  74.1 us
    pallas_call x2, Pallas kernels, row_call(): pl.pallas_call(kernel, grid_spec=pltpu.PrefetchScalarGridSpec(num_scalar_...  72 us
    pallas_call x2, Pallas kernels, attend(): pl.pallas_call(functools.partial(attend_kernel, frames_here, bk), grid_sp...  37.9 us
    ppermute x21, starting transfers between devices, hop(): return lax.ppermute(x, 'chip', [(i, i ^ step) for i in range(chips)])  37.1 us
    unnamed x222, local copies, waits for them, and re-layouts  23.7 us
    ppermute x18, starting transfers between devices, to_core(): return lax.ppermute(x, 'core', flip2)  21.7 us
    ppermute x21, waiting for transfers between devices, hop(): return lax.ppermute(x, 'chip', [(i, i ^ step) for i in range(chips)])  15.9 us
    pallas_call x2, Pallas kernels, project_grad(): pl.pallas_call(functools.partial(project_grad_kernel, pairs, bool(more)),...  13.8 us
  transfers between devices with their start and end apart: 51, of which 14 were waited for; matrix products, arithmetic and copies ran while one was open for 12% of the time, Pallas kernels for 43%

profile of v4, /device:TPU:0, one launch (start us, length us, event | category | flops | bytes accessed | tf_op | source)
XLA Modules:
  0.0 427.5 jit_solution(18303682644488000673)
XLA Ops:
  0.7 3.8 copy.31
  9.2 1.8 collective-permute-start
  11.0 2.7 copy.34.mine
  16.6 2.8 constant_dynamic-slice_fusion.2
  20.6 3.8 relay.1.weight.refs_6_.mine
  24.6 18.4 %collective-permute-start.3 = (bf16[1064,768]{1,0:T(8,128)(2,1)S(1)}, bf16[1064,768]{1,0:T(8,128)(2,1)S(1)}, u32[]{:S(2)}, u32[]{:S(2)}) collective-permute-start(bf16[1064,768]{1,0:T(8,128)(2,1)S(1)} %broadcast_select_fusion.own.tokens), channel_id=1, source_target_pairs={{0,2},{2,0},{1,3},{3,1},{4,6},{6,4},{5,7},{7,5},{8,10},{10,8},{9,1... | collective-permute-start | bytes 4902920 | tf_op jit(solution)/shard_map/ppermute | solution.py:1060
  45.6 2.9 collective-permute-start.6
  48.6 9.7 %project.1 = (bf16[2048,768]{1,0:T(8,128)(2,1)S(1)}, bf16[2048,1152]{1,0:T(8,128)(2,1)S(1)}, bf16[2048,128]{1,0:T(8,128)(2,1)S(1)}, bf16[2048,128]{1,0:T(8,128)(2,1)S(1)}) custom-call(s32[4]{0:T(128)S(1)} %get-tuple-element.196.scal, bf16[1064,768]{1,0:T(8,128)(2,1)S(1)} %collective-permute-done.3.oth, ...), custom_call_target="tpu_custom_call" | custom-call | flops 72477573120 | bytes 220200960 | tf_op jit(solution)/shard_map/project/pallas_call | solution.py:207
  60.9 22.6 %attend.2 = (bf16[1024,384]{1,0:T(8,128)(2,1)}, f32[1024,384]{1,0:T(8,128)S(1)}, f32[3,4,8,256]{3,2,1,0:T(8,128)S(1)}) custom-call(s32[4]{0:T(128)S(1)} %get-tuple-element.196.scal, bf16[2048,1152]{1,0:T(8,128)(2,1)S(1)} %get-tuple-element.110.q.qkv.k.v, bf16[2048,128]{1,0:T(8,128)(2,1)S(1)} %get-tuple-element.111.qfeat, ...), custom_call_target="tpu_custom_call" | custom-call | flops 257698037760 | bytes 251658240 | tf_op jit(solution)/shard_map/attend/pallas_call | solution.py:344
  83.7 15.3 %attend.3 = (bf16[1024,384]{1,0:T(8,128)(2,1)S(1)}, f32[1024,384]{1,0:T(8,128)S(1)}, f32[3,4,8,256]{3,2,1,0:T(8,128)S(1)}) custom-call(s32[4]{0:T(128)S(1)} %get-tuple-element.153.scal, bf16[2048,1152]{1,0:T(8,128)(2,1)S(1)} %get-tuple-element.110.q.qkv.k.v, bf16[2048,128]{1,0:T(8,128)(2,1)S(1)} %get-tuple-element.111.qfeat, ...), custom_call_target="tpu_custom_call" | custom-call | flops 257698037760 | bytes 251658240 | tf_op jit(solution)/shard_map/attend/pallas_call | solution.py:344
  101.7 5.8 %collective-permute-done.7.got_down = bf16[768,768]{1,0:T(8,128)(2,1)} collective-permute-done((bf16[768,768]{1,0:T(8,128)(2,1)}, bf16[768,768]{1,0:T(8,128)(2,1)}, u32[]{:S(2)}, u32[]{:S(2)}) %collective-permute-start.7) | collective-permute-done | bytes 1179680 | tf_op jit(solution)/shard_map/ppermute | solution.py:1063
  109.9 2.8 collective-permute-done.5.mixed_oth
  113.9 39.1 %ahead.1 = (f32[1024,768]{1,0:T(8,128)}, f32[1024,768]{1,0:T(8,128)}, f32[1024,128]{1,0:T(8,128)S(1)}, bf16[1024,3072]{1,0:T(8,128)(2,1)}, bf16[1024,768]{1,0:T(...) custom-call(s32[4]{0:T(128)S(1)} %copy-done.14, ...), custom_call_target="tpu_custom_call" | custom-call | flops 314069483520 | bytes 546867200 | tf_op jit(solution)/shard_map/ahead/pallas_call | solution.py:622
  157.2 4.5 %collective-permute-done.10 = bf16[2,768,768]{2,1,0:T(8,128)(2,1)} collective-permute-done((bf16[2,768,768]{2,1,0:T(8,128)(2,1)}, bf16[2,768,768]{2,1,0:T(8,128)(2,1)}, u32[]{:S(2)}, u32[]{:S(2)}) %collective-permute-start.10) | collective-permute-done | bytes 2359328 | tf_op jit(solution)/shard_map/ppermute | solution.py:1060
  161.7 3.0 fusion.4
  166.2 32.9 %behind.1 = (f32[1024,768]{1,0:T(8,128)}, bf16[1024,384]{1,0:T(8,128)(2,1)S(1)}, bf16[1024,384]{1,0:T(8,128)(2,1)S(1)}, f32[24,768]{1,0:T(8,128)S(1)}, f32[8,307...) custom-call(s32[4]{0:T(128)S(1)} %copy-done.14, ...), custom_call_target="tpu_custom_call" | custom-call | flops 338228674560 | bytes 315740160 | tf_op jit(solution)/shard_map/behind/pallas_call | solution.py:622
  199.2 2.7 bitcast_add_fusion.1
  205.0 4.1 collective-permute-done.12
  209.2 3.5 convert_add_fusion
  212.7 2.5 copy-done.62
  221.7 2.3 collective-permute-start.13
  224.1 2.3 copy-done.29
  226.4 24.7 %attend_back.3 = (bf16[1024,384]{1,0:T(8,128)(2,1)S(1)}, bf16[1024,384]{1,0:T(8,128)(2,1)S(1)}) custom-call(s32[4]{0:T(128)S(1)} %copy-done.14, bf16[2048,1152]{1,0:T(8,128)(2,1)S(1)} %copy-done.29, bf16[2048,1152]{1,0:T(8,128)(2,1)S(1)} %copy-done.29, bf16[2048,128]{1,0:T(8,128)(2,1)S(1)} %copy-done.38, bf16[2048,1152]{1,0:T(8,128)(2,1)S(1)} %copy-done.29, ...), custom_call_target="tpu_custom_call" | custom-call | flops 429496729600 | bytes 157286400 | tf_op jit(solution)/shard_map/attend_back/pallas_call | solution.py:803
  252.3 1.9 fusion.9
  254.2 2.6 collective-permute-start.17
  256.8 2.6 bitcast_add_fusion
  260.4 2.0 collective-permute-start.20
  262.5 24.5 %attend_back.4 = (bf16[1024,384]{1,0:T(8,128)(2,1)S(1)}, bf16[1024,384]{1,0:T(8,128)(2,1)S(1)}) custom-call(s32[4]{0:T(128)S(1)} %copy-done.19, bf16[2048,1152]{1,0:T(8,128)(2,1)S(1)} %bitcast.93, bf16[2048,1152]{1,0:T(8,128)(2,1)S(1)} %bitcast.93, bf16[2048,128]{1,0:T(8,128)(2,1)S(1)} %copy-done.38, bf16[2048,1152]{1,0:T(8,128)(2,1)S(1)} %bitcast.93, ...), custom_call_target="tpu_custom_call" | custom-call | flops 429496729600 | bytes 157286400 | tf_op jit(solution)/shard_map/attend_back/pallas_call | solution.py:803
  289.5 3.8 collective-permute-start.24
  293.3 1.8 fusion.3
  296.9 10.5 %project_grad.2 = (bf16[384,768]{1,0:T(8,128)(2,1)S(1)}, bf16[384,768]{1,0:T(8,128)(2,1)S(1)}, f32[8,768]{1,0:T(8,128)S(1)}, f32[1024,768]{1,0:T(8,128)S(1)}) custom-call(s32[4]{0:T(128)S(1)} %copy-done.14, bf16[2048,768]{1,0:T(8,128)(2,1)S(1)} %copy-done.26, bf16[1024,384]{1,0:T(8,128)(2,1)S(1)} %copy-done.22, ...), custom_call_target="tpu_custom_call" | custom-call | flops 48318382080 | bytes 125829120 | tf_op jit(solution)/shard_map/project_grad/pallas_call | solution.py:885
  310.8 4.9 %collective-permute-start.49 = (bf16[384,768]{1,0:T(8,128)(2,1)}, bf16[384,768]{1,0:T(8,128)(2,1)}, u32[]{:S(2)}, u32[]{:S(2)}) collective-permute-start(bf16[384,768]{1,0:T(8,128)(2,1)} %pad_maximum_fusion.3), channel_id=1, source_target_pairs={{0,4},{4,0},{8,12},{12,8},{16,20},{20,16},{24,28},{28,24},{1,5},{5... | collective-permute-start | bytes 1769480 | tf_op jit(solution)/shard_map/ppermute | solution.py:1072
  317.9 24.8 %attend_back.5 = (bf16[1024,384]{1,0:T(8,128)(2,1)S(1)}, bf16[1024,384]{1,0:T(8,128)(2,1)S(1)}) custom-call(s32[4]{0:T(128)S(1)} %get-tuple-element.166.scal, bf16[2048,1152]{1,0:T(8,128)(2,1)S(1)} %bitcast.95, bf16[2048,1152]{1,0:T(8,128)(2,1)S(1)} %bitcast.95, bf16[2048,128]{1,0:T(8,128)(2,1)S(1)} %copy-done.39, bf16[2048,1152]{1,0:T(8,128)(2,1)S(1)} %bitcast.95, ...), custom_call_target="tpu_custom_call" | custom-call | flops 429496729600 | bytes 157286400 | tf_op jit(solution)/shard_map/attend_back/pallas_call | solution.py:803
  344.0 3.6 collective-permute-start.29
  349.2 3.3 project_grad.3
  359.9 5.0 %first_grad.1 = (bf16[1024,768]{1,0:T(8,128)(2,1)S(1)}, f32[16,768]{1,0:T(8,128)S(1)}) custom-call(bf16[1024,384]{1,0:T(8,128)(2,1)S(1)} %get-tuple-element.167.refs_1_.own, bf16[1024,384]{1,0:T(8,128)(2,1)S(1)} %collective-permute-done.25.got, bf16[768,1152]{1,0:T(8,128)(2,1)} %relay.1.weight.refs_6_.mine, ...), custom_call_target="tpu_custom_call" | custom-call | flops 24159191040 | bytes 188743680 | tf_op jit(solution)/shard_map/first_grad/pallas_call | solution.py:925
  365.6 1.9 collective-permute-done.33
  370.4 3.3 collective-permute-start.38
  380.6 3.3 collective-permute-done.36
  385.0 1.9 collective-permute-start.40
  388.7 3.4 collective-permute-done.37
  392.2 4.3 collective-permute-start.44
  398.2 1.7 broadcast_select_fusion.4
  402.5 2.5 maximum_convert_fusion.1
  406.7 6.7 %last.1 = f32[980,768]{1,0:T(8,128)} custom-call(s32[4]{0:T(128)S(1)} %copy-done.15, bf16[1064,768]{1,0:T(8,128)(2,1)S(1)} %pack.1.tokens, bf16[1024,768]{1,0:T(8,128)(2,1)S(1)} %get-tuple-element.197.grad, bf16[1024,768]{1,0:T(8,128)(2,1)S(1)} %collective-permute-done.42.grad_got, f32[1024,768]{1,0:T(8,128)} %get-tuple-element.137.residual, ...), custom_call_target="tpu_custom_call" | custom-call | flops 314572800 | bytes 188743680 | tf_op jit(solution)/shard_map/last/pallas_call | solution.py:950
  418.8 2.1 maximum_convert_fusion.2
  420.9 1.9 broadcast_select_fusion.2
  423.1 2.8 maximum_convert_fusion
  (393 shorter events, 82.6 us)
Async XLA Ops:
  7.4 6.4 %collective-permute-start.1 = (bf16[384,1152]{1,0:T(8,128)(2,1)}, bf16[384,1152]{1,0:T(8,128)(2,1)}, u32[]{:S(2)}, u32[]{:S(2)}) collective-permute-start(bf16[384,1152]{1,0:T(8,128)(2,1)} %copy.33), channel_id=1, source_target_pairs={{1,2},{2,1},{5,6},{6,5},{9,10},{10,9},{13,14},{14,13},{17,18},{18,... | collective-permute-start | bytes 2654216 | tf_op jit(solution)/shard_map/ppermute | solution.py:1057
  9.2 15.2 %collective-permute-start = (bf16[1064,768]{1,0:T(8,128)(2,1)S(1)}, bf16[1064,768]{1,0:T(8,128)(2,1)}, u32[]{:S(2)}, u32[]{:S(2)}) collective-permute-start(bf16[1064,768]{1,0:T(8,128)(2,1)S(1)} %pack.1.tokens), channel_id=1, source_target_pairs={{1,2},{2,1},{5,6},{6,5},{9,10},{10,9},{13,14},{14,13},{17,18},{18,... | collective-permute-start | bytes 4902920 | tf_op jit(solution)/shard_map/ppermute | solution.py:1057
  13.8 6.8 %collective-permute-start.2 = (bf16[384,1152]{1,0:T(8,128)(2,1)}, bf16[384,1152]{1,0:T(8,128)(2,1)}, u32[]{:S(2)}, u32[]{:S(2)}) collective-permute-start(bf16[384,1152]{1,0:T(8,128)(2,1)} %collective-permute-done.1.first), channel_id=1, source_target_pairs={{1,5},{2,6},{5,1},{6,2},{9,13},{10,14},{13,9},{14,10},{17,21},{18,... | collective-permute-start | bytes 2654216 | tf_op jit(solution)/shard_map/ppermute | solution.py:1106
  24.6 24.1 %collective-permute-start.3 = (bf16[1064,768]{1,0:T(8,128)(2,1)S(1)}, bf16[1064,768]{1,0:T(8,128)(2,1)S(1)}, u32[]{:S(2)}, u32[]{:S(2)}) collective-permute-start(bf16[1064,768]{1,0:T(8,128)(2,1)S(1)} %broadcast_select_fusion.own.tokens), channel_id=1, source_target_pairs={{0,2},{2,0},{1,3},{3,1},{4,6},{6,4},{5,7},{7,5},{8,10},{10,8},{9,1... | collective-permute-start | bytes 4902920 | tf_op jit(solution)/shard_map/ppermute | solution.py:1060
  45.6 37.9 %collective-permute-start.6 = (bf16[976,768]{1,0:T(8,128)(2,1)}, bf16[976,768]{1,0:T(8,128)(2,1)}, u32[]{:S(2)}, u32[]{:S(2)}) collective-permute-start(bf16[976,768]{1,0:T(8,128)(2,1)} %fusion.1), channel_id=1, source_target_pairs={{0,1},{1,0},{2,3},{3,2},{4,5},{5,4},{6,7},{7,6},{8,9},{9,8},{10,11... | collective-permute-start | bytes 4497416 | tf_op jit(solution)/shard_map/ppermute | solution.py:1063
  60.1 23.5 %collective-permute-start.4 = (bf16[768,1152]{1,0:T(8,128)(2,1)}, bf16[768,1152]{1,0:T(8,128)(2,1)}, u32[]{:S(2)}, u32[]{:S(2)}) collective-permute-start(bf16[768,1152]{1,0:T(8,128)(2,1)} %relay.1.weight.refs_6_.mine), channel_id=1, source_target_pairs={{0,2},{2,0},{1,3},{3,1},{4,6},{6,4},{5,7},{7,5},{8,10},{10,8},{9,1... | collective-permute-start | bytes 5308424 | tf_op jit(solution)/shard_map/ppermute | solution.py:1060
  60.3 47.2 %collective-permute-start.7 = (bf16[768,768]{1,0:T(8,128)(2,1)}, bf16[768,768]{1,0:T(8,128)(2,1)}, u32[]{:S(2)}, u32[]{:S(2)}) collective-permute-start(bf16[768,768]{1,0:T(8,128)(2,1)} %get-tuple-element.118), channel_id=1, source_target_pairs={{0,1},{1,0},{2,3},{3,2},{4,5},{5,4},{6,7},{7,6},{8,9},{9,8},{10,11... | collective-permute-start | bytes 3538952 | tf_op jit(solution)/shard_map/ppermute | solution.py:1063
  83.5 29.2 %collective-permute-start.8 = (bf16[976,768]{1,0:T(8,128)(2,1)}, bf16[976,768]{1,0:T(8,128)(2,1)}, u32[]{:S(2)}, u32[]{:S(2)}) collective-permute-start(bf16[976,768]{1,0:T(8,128)(2,1)} %collective-permute-done.6.got_up), channel_id=1, source_target_pairs={{0,2},{2,0},{1,3},{3,1},{4,6},{6,4},{5,7},{7,5},{8,10},{10,8},{9,1... | collective-permute-start | bytes 4497416 | tf_op jit(solution)/shard_map/ppermute | solution.py:1060
  107.5 5.2 %collective-permute-start.9 = (bf16[768,768]{1,0:T(8,128)(2,1)}, bf16[768,768]{1,0:T(8,128)(2,1)S(1)}, u32[]{:S(2)}, u32[]{:S(2)}) collective-permute-start(bf16[768,768]{1,0:T(8,128)(2,1)} %collective-permute-done.7.got_down), channel_id=1, source_target_pairs={{0,2},{2,0},{1,3},{3,1},{4,6},{6,4},{5,7},{7,5},{8,10},{10,8},{9,1... | collective-permute-start | bytes 3538952 | tf_op jit(solution)/shard_map/ppermute | solution.py:1060
  108.9 3.8 collective-permute-start.5
  156.8 4.9 %collective-permute-start.10 = (bf16[2,768,768]{2,1,0:T(8,128)(2,1)}, bf16[2,768,768]{2,1,0:T(8,128)(2,1)}, u32[]{:S(2)}, u32[]{:S(2)}) collective-permute-start(bf16[2,768,768]{2,1,0:T(8,128)(2,1)} %get-tuple-element.122), channel_id=1, source_target_pairs={{0,2},{2,0},{1,3},{3,1},{4,6},{6,4},{5,7},{7,5},{8,10},{10,8},{9,1... | collective-permute-start | bytes 7077896 | tf_op jit(solution)/shard_map/ppermute | solution.py:1060
  164.7 34.4 %collective-permute-start.11 = (bf16[768,768]{1,0:T(8,128)(2,1)}, bf16[768,768]{1,0:T(8,128)(2,1)}, u32[]{:S(2)}, u32[]{:S(2)}) collective-permute-start(bf16[768,768]{1,0:T(8,128)(2,1)} %fusion.4), channel_id=1, source_target_pairs={{0,1},{1,0},{2,3},{3,2},{4,5},{5,4},{6,7},{7,6},{8,9},{9,8},{10,11... | collective-permute-start | bytes 3538952 | tf_op jit(solution)/shard_map/ppermute | solution.py:1063
  203.4 5.8 %collective-permute-start.12 = (bf16[2,960,768]{2,1,0:T(8,128)(2,1)}, bf16[2,960,768]{2,1,0:T(8,128)(2,1)}, u32[]{:S(2)}, u32[]{:S(2)}) collective-permute-start(bf16[2,960,768]{2,1,0:T(8,128)(2,1)} %get-tuple-element.134), channel_id=1, source_target_pairs={{0,2},{2,0},{1,3},{3,1},{4,6},{6,4},{5,7},{7,5},{8,10},{10,8},{9,1... | collective-permute-start | bytes 8847368 | tf_op jit(solution)/shard_map/ppermute | solution.py:1060
  203.5 15.7 %collective-permute-start.14 = (bf16[384,768]{1,0:T(8,128)(2,1)S(1)}, bf16[384,768]{1,0:T(8,128)(2,1)S(1)}, u32[]{:S(2)}, u32[]{:S(2)}) collective-permute-start(bf16[384,768]{1,0:T(8,128)(2,1)S(1)} %fusion.6), channel_id=1, source_target_pairs={{0,4},{4,0},{8,12},{12,8},{16,20},{20,16},{24,28},{28,24},{1,5},{5... | collective-permute-start | bytes 1769480 | tf_op jit(solution)/shard_map/ppermute | solution.py:1072
  205.0 19.1 %collective-permute-start.15 = (bf16[1024,384]{1,0:T(8,128)(2,1)}, bf16[1024,384]{1,0:T(8,128)(2,1)S(1)}, u32[]{:S(2)}, u32[]{:S(2)}) collective-permute-start(bf16[1024,384]{1,0:T(8,128)(2,1)} %copy-done.20), channel_id=1, source_target_pairs={{0,2},{2,0},{1,3},{3,1},{4,6},{6,4},{5,7},{7,5},{8,10},{10,8},{9,1... | collective-permute-start | bytes 2359304 | tf_op jit(solution)/shard_map/ppermute | solution.py:1060
  216.5 40.3 %collective-permute-start.18 = (bf16[2,480,768]{2,1,0:T(8,128)(2,1)}, bf16[2,480,768]{2,1,0:T(8,128)(2,1)}, u32[]{:S(2)}, u32[]{:S(2)}) collective-permute-start(bf16[2,480,768]{2,1,0:T(8,128)(2,1)} %fusion.2), channel_id=1, source_target_pairs={{0,4},{4,0},{8,12},{12,8},{16,20},{20,16},{24,28},{28,24},{1,5},{5... | collective-permute-start | bytes 4423688 | tf_op jit(solution)/shard_map/ppermute | solution.py:1072
  220.1 32.2 %collective-permute-start.16 = (bf16[192,768]{1,0:T(8,128)(2,1)}, bf16[192,768]{1,0:T(8,128)(2,1)}, u32[]{:S(2)}, u32[]{:S(2)}) collective-permute-start(bf16[192,768]{1,0:T(8,128)(2,1)} %fusion.11), channel_id=1, source_target_pairs={{0,8},{4,12},{8,0},{12,4},{16,24},{20,28},{24,16},{28,20},{1,9},{5... | collective-permute-start | bytes 884744 | tf_op jit(solution)/shard_map/ppermute | solution.py:1072
  221.7 40.7 %collective-permute-start.13 = (f32[1024,768]{1,0:T(8,128)}, f32[1024,768]{1,0:T(8,128)}, u32[]{:S(2)}, u32[]{:S(2)}) collective-permute-start(f32[1024,768]{1,0:T(8,128)} %get-tuple-element.137.residual), channel_id=1, source_target_pairs={{1,2},{2,1},{5,6},{6,5},{9,10},{10,9},{13,14},{14,13},{17,18},{18,... | collective-permute-start | bytes 9437192 | tf_op jit(solution)/shard_map/ppermute | solution.py:1057
  252.1 10.4 %collective-permute-start.19 = (bf16[1024,384]{1,0:T(8,128)(2,1)S(1)}, bf16[1024,384]{1,0:T(8,128)(2,1)S(1)}, u32[]{:S(2)}, u32[]{:S(2)}) collective-permute-start(bf16[1024,384]{1,0:T(8,128)(2,1)S(1)} %get-tuple-element.147.refs_0_), channel_id=1, source_target_pairs={{0,2},{2,0},{1,3},{3,1},{4,6},{6,4},{5,7},{7,5},{8,10},{10,8},{9,1... | collective-permute-start | bytes 2359304 | tf_op jit(solution)/shard_map/ppermute | solution.py:1060
  254.2 33.8 %collective-permute-start.17 = (bf16[192,768]{1,0:T(8,128)(2,1)}, bf16[192,768]{1,0:T(8,128)(2,1)}, u32[]{:S(2)}, u32[]{:S(2)}) collective-permute-start(bf16[192,768]{1,0:T(8,128)(2,1)} %fusion.9), channel_id=1, source_target_pairs={{0,16},{4,20},{8,24},{12,28},{16,0},{20,4},{24,8},{28,12},{1,17},{... | collective-permute-start | bytes 884744 | tf_op jit(solution)/shard_map/ppermute | solution.py:1072
  260.4 27.6 %collective-permute-start.20 = (bf16[480,768]{1,0:T(8,128)(2,1)}, bf16[480,768]{1,0:T(8,128)(2,1)}, u32[]{:S(2)}, u32[]{:S(2)}) collective-permute-start(bf16[480,768]{1,0:T(8,128)(2,1)} %fusion.5), channel_id=1, source_target_pairs={{0,1},{1,0},{2,3},{3,2},{4,5},{5,4},{6,7},{7,6},{8,9},{9,8},{10,11... | collective-permute-start | bytes 2211848 | tf_op jit(solution)/shard_map/ppermute | solution.py:1063
  288.0 7.4 %collective-permute-start.21 = (bf16[1024,384]{1,0:T(8,128)(2,1)S(1)}, bf16[1024,384]{1,0:T(8,128)(2,1)}, u32[]{:S(2)}, u32[]{:S(2)}) collective-permute-start(bf16[1024,384]{1,0:T(8,128)(2,1)S(1)} %get-tuple-element.154.refs_1_), channel_id=1, source_target_pairs={{0,2},{2,0},{1,3},{3,1},{4,6},{6,4},{5,7},{7,5},{8,10},{10,8},{9,1... | collective-permute-start | bytes 2359304 | tf_op jit(solution)/shard_map/ppermute | solution.py:1060
  289.5 17.9 %collective-permute-start.24 = (bf16[192,768]{1,0:T(8,128)(2,1)S(1)}, bf16[192,768]{1,0:T(8,128)(2,1)S(1)}, u32[]{:S(2)}, u32[]{:S(2)}) collective-permute-start(bf16[192,768]{1,0:T(8,128)(2,1)S(1)} %add_convert_fusion.3), channel_id=1, source_target_pairs={{0,8},{4,12},{8,0},{12,4},{16,24},{20,28},{24,16},{28,20},{1,9},{5... | collective-permute-start | bytes 884744 | tf_op jit(solution)/shard_map/ppermute | solution.py:1072
  295.2 13.7 %collective-permute-start.23 = (bf16[240,768]{1,0:T(8,128)(2,1)S(1)}, bf16[240,768]{1,0:T(8,128)(2,1)S(1)}, u32[]{:S(2)}, u32[]{:S(2)}) collective-permute-start(bf16[240,768]{1,0:T(8,128)(2,1)S(1)} %fusion.10), channel_id=1, source_target_pairs={{0,8},{4,12},{8,0},{12,4},{16,24},{20,28},{24,16},{28,20},{1,9},{5... | collective-permute-start | bytes 1105928 | tf_op jit(solution)/shard_map/ppermute | solution.py:1072
  308.9 6.7 %collective-permute-start.22 = (bf16[384,768]{1,0:T(8,128)(2,1)S(1)}, bf16[384,768]{1,0:T(8,128)(2,1)S(1)}, u32[]{:S(2)}, u32[]{:S(2)}) collective-permute-start(bf16[384,768]{1,0:T(8,128)(2,1)S(1)} %get-tuple-element.161), channel_id=1, source_target_pairs={{0,2},{2,0},{1,3},{3,1},{4,6},{6,4},{5,7},{7,5},{8,10},{10,8},{9,1... | collective-permute-start | bytes 1769480 | tf_op jit(solution)/shard_map/ppermute | solution.py:1060
  309.8 33.0 %collective-permute-start.26 = (bf16[240,768]{1,0:T(8,128)(2,1)}, bf16[240,768]{1,0:T(8,128)(2,1)}, u32[]{:S(2)}, u32[]{:S(2)}) collective-permute-start(bf16[240,768]{1,0:T(8,128)(2,1)} %fusion.7), channel_id=1, source_target_pairs={{0,16},{4,20},{8,24},{12,28},{16,0},{20,4},{24,8},{28,12},{1,17},{... | collective-permute-start | bytes 1105928 | tf_op jit(solution)/shard_map/ppermute | solution.py:1072
  310.8 41.7 %collective-permute-start.49 = (bf16[384,768]{1,0:T(8,128)(2,1)}, bf16[384,768]{1,0:T(8,128)(2,1)}, u32[]{:S(2)}, u32[]{:S(2)}) collective-permute-start(bf16[384,768]{1,0:T(8,128)(2,1)} %pad_maximum_fusion.3), channel_id=1, source_target_pairs={{0,4},{4,0},{8,12},{12,8},{16,20},{20,16},{24,28},{28,24},{1,5},{5... | collective-permute-start | bytes 1769480 | tf_op jit(solution)/shard_map/ppermute | solution.py:1072
  316.6 31.0 %collective-permute-start.27 = (bf16[384,768]{1,0:T(8,128)(2,1)}, bf16[384,768]{1,0:T(8,128)(2,1)}, u32[]{:S(2)}, u32[]{:S(2)}) collective-permute-start(bf16[384,768]{1,0:T(8,128)(2,1)} %broadcast_select_fusion.11), channel_id=1, source_target_pairs={{0,1},{1,0},{2,3},{3,2},{4,5},{5,4},{6,7},{7,6},{8,9},{9,8},{10,11... | collective-permute-start | bytes 1769480 | tf_op jit(solution)/shard_map/ppermute | solution.py:1063
  342.7 17.2 %collective-permute-start.25 = (bf16[1024,384]{1,0:T(8,128)(2,1)S(1)}, bf16[1024,384]{1,0:T(8,128)(2,1)S(1)}, u32[]{:S(2)}, u32[]{:S(2)}) collective-permute-start(bf16[1024,384]{1,0:T(8,128)(2,1)S(1)} %get-tuple-element.168.refs_0_), channel_id=1, source_target_pairs={{0,2},{2,0},{1,3},{3,1},{4,6},{6,4},{5,7},{7,5},{8,10},{10,8},{9,1... | collective-permute-start | bytes 2359304 | tf_op jit(solution)/shard_map/ppermute | solution.py:1060
  344.0 12.8 %collective-permute-start.29 = (bf16[240,768]{1,0:T(8,128)(2,1)S(1)}, bf16[240,768]{1,0:T(8,128)(2,1)S(1)}, u32[]{:S(2)}, u32[]{:S(2)}) collective-permute-start(bf16[240,768]{1,0:T(8,128)(2,1)S(1)} %add_convert_fusion.1), channel_id=1, source_target_pairs={{0,8},{4,12},{8,0},{12,4},{16,24},{20,28},{24,16},{28,20},{1,9},{5... | collective-permute-start | bytes 1105928 | tf_op jit(solution)/shard_map/ppermute | solution.py:1072
  349.1 9.1 %collective-permute-start.30 = (bf16[192,768]{1,0:T(8,128)(2,1)S(1)}, bf16[192,768]{1,0:T(8,128)(2,1)S(1)}, u32[]{:S(2)}, u32[]{:S(2)}) collective-permute-start(bf16[192,768]{1,0:T(8,128)(2,1)S(1)} %fusion.12), channel_id=1, source_target_pairs={{0,4},{4,0},{8,12},{12,8},{16,20},{20,16},{24,28},{28,24},{1,5},{5... | collective-permute-start | bytes 884744 | tf_op jit(solution)/shard_map/ppermute | solution.py:1072
  355.1 41.4 %collective-permute-start.50 = (bf16[768,768]{1,0:T(8,128)(2,1)}, bf16[768,768]{1,0:T(8,128)(2,1)}, u32[]{:S(2)}, u32[]{:S(2)}) collective-permute-start(bf16[768,768]{1,0:T(8,128)(2,1)} %pad_maximum_fusion.1), channel_id=1, source_target_pairs={{0,2},{2,0},{1,3},{3,1},{4,6},{6,4},{5,7},{7,5},{8,10},{10,8},{9,1... | collective-permute-start | bytes 3538952 | tf_op jit(solution)/shard_map/ppermute | solution.py:1060
  358.3 9.2 %collective-permute-start.33 = (bf16[192,768]{1,0:T(8,128)(2,1)S(1)}, bf16[192,768]{1,0:T(8,128)(2,1)S(1)}, u32[]{:S(2)}, u32[]{:S(2)}) collective-permute-start(bf16[192,768]{1,0:T(8,128)(2,1)S(1)} %fusion.14), channel_id=1, source_target_pairs={{0,8},{4,12},{8,0},{12,4},{16,24},{20,28},{24,16},{28,20},{1,9},{5... | collective-permute-start | bytes 884744 | tf_op jit(solution)/shard_map/ppermute | solution.py:1072
  359.8 9.2 %collective-permute-start.32 = (bf16[384,384]{1,0:T(8,128)(2,1)S(1)}, bf16[384,384]{1,0:T(8,128)(2,1)S(1)}, u32[]{:S(2)}, u32[]{:S(2)}) collective-permute-start(bf16[384,384]{1,0:T(8,128)(2,1)S(1)} %broadcast_select_fusion.18), channel_id=1, source_target_pairs={{0,1},{1,0},{2,3},{3,2},{4,5},{5,4},{6,7},{7,6},{8,9},{9,8},{10,11... | collective-permute-start | bytes 884744 | tf_op jit(solution)/shard_map/ppermute | solution.py:1063
  370.0 5.4 %collective-permute-start.35 = (bf16[192,384]{1,0:T(8,128)(2,1)}, bf16[192,384]{1,0:T(8,128)(2,1)S(1)}, u32[]{:S(2)}, u32[]{:S(2)}) collective-permute-start(bf16[192,384]{1,0:T(8,128)(2,1)} %fusion.15), channel_id=1, source_target_pairs={{0,4},{4,0},{8,12},{12,8},{16,20},{20,16},{24,28},{28,24},{1,5},{5... | collective-permute-start | bytes 442376 | tf_op jit(solution)/shard_map/ppermute | solution.py:1072
  370.4 17.4 %collective-permute-start.38 = (bf16[192,768]{1,0:T(8,128)(2,1)}, bf16[192,768]{1,0:T(8,128)(2,1)S(1)}, u32[]{:S(2)}, u32[]{:S(2)}) collective-permute-start(bf16[192,768]{1,0:T(8,128)(2,1)} %fusion.8), channel_id=1, source_target_pairs={{0,16},{4,20},{8,24},{12,28},{16,0},{20,4},{24,8},{28,12},{1,17},{... | collective-permute-start | bytes 884744 | tf_op jit(solution)/shard_map/ppermute | solution.py:1072
  373.7 6.6 %collective-permute-start.34 = (f32[24,768]{1,0:T(8,128)S(1)}, f32[24,768]{1,0:T(8,128)S(1)}, u32[]{:S(2)}, u32[]{:S(2)}) collective-permute-start(f32[24,768]{1,0:T(8,128)S(1)} %add.160), channel_id=1, source_target_pairs={{0,1},{1,0},{2,3},{3,2},{4,5},{5,4},{6,7},{7,6},{8,9},{9,8},{10,11... | collective-permute-start | bytes 221192 | tf_op jit(solution)/shard_map/ppermute | solution.py:1063
  376.4 7.5 %collective-permute-start.36 = (bf16[192,384]{1,0:T(8,128)(2,1)S(1)}, bf16[192,384]{1,0:T(8,128)(2,1)S(1)}, u32[]{:S(2)}, u32[]{:S(2)}) collective-permute-start(bf16[192,384]{1,0:T(8,128)(2,1)S(1)} %fusion.16), channel_id=1, source_target_pairs={{0,8},{4,12},{8,0},{12,4},{16,24},{20,28},{24,16},{28,20},{1,9},{5... | collective-permute-start | bytes 442376 | tf_op jit(solution)/shard_map/ppermute | solution.py:1072
  379.4 27.4 %collective-permute-start.42 = (bf16[1024,768]{1,0:T(8,128)(2,1)S(1)}, bf16[1024,768]{1,0:T(8,128)(2,1)S(1)}, u32[]{:S(2)}, u32[]{:S(2)}) collective-permute-start(bf16[1024,768]{1,0:T(8,128)(2,1)S(1)} %get-tuple-element.197.grad), channel_id=1, source_target_pairs={{1,2},{2,1},{5,6},{6,5},{9,10},{10,9},{13,14},{14,13},{17,18},{18,... | collective-permute-start | bytes 4718600 | tf_op jit(solution)/shard_map/ppermute | solution.py:1057
  380.3 19.6 %collective-permute-start.41 = (bf16[480,768]{1,0:T(8,128)(2,1)}, bf16[480,768]{1,0:T(8,128)(2,1)S(1)}, u32[]{:S(2)}, u32[]{:S(2)}) collective-permute-start(bf16[480,768]{1,0:T(8,128)(2,1)} %pad_maximum_fusion.2), channel_id=1, source_target_pairs={{0,4},{4,0},{8,12},{12,8},{16,20},{20,16},{24,28},{28,24},{1,5},{5... | collective-permute-start | bytes 2211848 | tf_op jit(solution)/shard_map/ppermute | solution.py:1072
  385.0 16.9 %collective-permute-start.40 = (bf16[192,384]{1,0:T(8,128)(2,1)S(1)}, bf16[192,384]{1,0:T(8,128)(2,1)S(1)}, u32[]{:S(2)}, u32[]{:S(2)}) collective-permute-start(bf16[192,384]{1,0:T(8,128)(2,1)S(1)} %fusion.13), channel_id=1, source_target_pairs={{0,16},{4,20},{8,24},{12,28},{16,0},{20,4},{24,8},{28,12},{1,17},{... | collective-permute-start | bytes 442376 | tf_op jit(solution)/shard_map/ppermute | solution.py:1072
  387.8 4.4 %collective-permute-start.37 = (f32[24,768]{1,0:T(8,128)S(1)}, f32[24,768]{1,0:T(8,128)S(1)}, u32[]{:S(2)}, u32[]{:S(2)}) collective-permute-start(f32[24,768]{1,0:T(8,128)S(1)} %add.162), channel_id=1, source_target_pairs={{0,8},{4,12},{8,0},{12,4},{16,24},{20,28},{24,16},{28,20},{1,9},{5... | collective-permute-start | bytes 221192 | tf_op jit(solution)/shard_map/ppermute | solution.py:1072
  392.2 22.4 %collective-permute-start.44 = (bf16[192,768]{1,0:T(8,128)(2,1)S(1)}, bf16[192,768]{1,0:T(8,128)(2,1)S(1)}, u32[]{:S(2)}, u32[]{:S(2)}) collective-permute-start(bf16[192,768]{1,0:T(8,128)(2,1)S(1)} %add_convert_fusion.2), channel_id=1, source_target_pairs={{0,4},{4,0},{8,12},{12,8},{16,20},{20,16},{24,28},{28,24},{1,5},{5... | collective-permute-start | bytes 884744 | tf_op jit(solution)/shard_map/ppermute | solution.py:1072
  396.5 5.4 %collective-permute-start.39 = (f32[24,768]{1,0:T(8,128)S(1)}, f32[24,768]{1,0:T(8,128)S(1)}, u32[]{:S(2)}, u32[]{:S(2)}) collective-permute-start(f32[24,768]{1,0:T(8,128)S(1)} %add.165), channel_id=1, source_target_pairs={{0,16},{4,20},{8,24},{12,28},{16,0},{20,4},{24,8},{28,12},{1,17},{... | collective-permute-start | bytes 221192 | tf_op jit(solution)/shard_map/ppermute | solution.py:1072
  401.9 11.5 %collective-permute-start.43 = (f32[24,768]{1,0:T(8,128)S(1)}, f32[24,768]{1,0:T(8,128)S(1)}, u32[]{:S(2)}, u32[]{:S(2)}) collective-permute-start(f32[24,768]{1,0:T(8,128)S(1)} %add.167), channel_id=1, source_target_pairs={{0,4},{4,0},{8,12},{12,8},{16,20},{20,16},{24,28},{28,24},{1,5},{5... | collective-permute-start | bytes 221192 | tf_op jit(solution)/shard_map/ppermute | solution.py:1072
  405.1 15.8 %collective-permute-start.48 = (bf16[960,768]{1,0:T(8,128)(2,1)}, bf16[960,768]{1,0:T(8,128)(2,1)}, u32[]{:S(2)}, u32[]{:S(2)}) collective-permute-start(bf16[960,768]{1,0:T(8,128)(2,1)} %pad_maximum_fusion), channel_id=1, source_target_pairs={{0,2},{2,0},{1,3},{3,1},{4,6},{6,4},{5,7},{7,5},{8,10},{10,8},{9,1... | collective-permute-start | bytes 4423688 | tf_op jit(solution)/shard_map/ppermute | solution.py:1060
  405.1 10.4 %collective-permute-start.46 = (bf16[192,384]{1,0:T(8,128)(2,1)S(1)}, bf16[192,384]{1,0:T(8,128)(2,1)S(1)}, u32[]{:S(2)}, u32[]{:S(2)}) collective-permute-start(bf16[192,384]{1,0:T(8,128)(2,1)S(1)} %add_convert_fusion.4), channel_id=1, source_target_pairs={{0,4},{4,0},{8,12},{12,8},{16,20},{20,16},{24,28},{28,24},{1,5},{5... | collective-permute-start | bytes 442376 | tf_op jit(solution)/shard_map/ppermute | solution.py:1072
  414.7 3.4 collective-permute-start.45
  (113 other events, 1202.0 us)

commit v5 on v4

--- a/solution.py
+++ b/solution.py
@@ -1319,8 +1319,7 @@
     up_sum = join(up_sum, after(up_z, mine_2), bit, 0)
     down_sum = join(down_sum, after(down_x, mine_2), side, 0)
     down_got = to_core(down_sum)
-    early_sum = plus(early_keep, after(early_x, mine_2))
-    early_low = low(early_sum)
+    early_low, early_keep = split(plus(early_keep, after(early_x, mine_2)))
     early_z = hop(early_low, hops[0])
     first_low, first_sums = first_grad(
         own_2,
@@ -1344,7 +1343,7 @@
         offsets_2,
     )
 
-    early_sum = plus(early_sum, after(early_z, table))
+    early_sum = plus(early_keep, after(early_z, table))
     early_low = low(early_sum)
     early_z = hop(early_low, hops[1])
     late_half = halves_of(plus(late_keep, after(late_got, early_low)))
@@ -1363,12 +1362,14 @@
     late_z = hop(late_low, hops[1])
     table_got = hop(after(table, late_low), hops[0])
     early_sum = rest(early_sum, after(early_z, late_low), hops[2:])
-    early_x = hop(early_sum, 1)
+    early_z = hop(early_sum, hops[0])
     table = table + after(table_got, early_sum)
     table_got = hop(table, hops[1])
     up_sum = join(up_sum, after(up_x, table), side, 0)
     up_got = to_core(up_sum)
-    late_sum = rest(late_sum, after(late_z, up_sum), hops[2:])
+    early_sum = join(early_sum, after(early_z, up_sum), bit, 0)
+    early_x = hop(early_sum, 1)
+    late_sum = rest(late_sum, after(late_z, early_sum), hops[2:])
     late_x = hop(late_sum, 1)
     table = table + after(table_got, late_sum)
     for step in hops[2:]:

time: 435 us -> 440 us (1.011)
  Pallas kernels: 224 us -> 188 us
  waiting for transfers between devices: 33.9 us -> 56.8 us
  starting transfers between devices: 75.3 us -> 92.7 us
    pallas_call x3, Pallas kernels: 74.1 us -> 49.5 us  [attend_back(): pl.pallas_call(functools.partial(attend_back_kernel, frames_here), grid_s...]
    ppermute x21 -> x22, starting transfers between devices: 37.1 us -> 56.1 us  [hop(): return lax.ppermute(x, 'chip', [(i, i ^ step) for i in range(chips)])]
    ppermute x7, waiting for transfers between devices: 6.56 us -> 20.5 us  [to_plane(): return lax.ppermute(x, 'mp', flip2)]
    pallas_call x2, Pallas kernels: 37.9 us -> 26.8 us  [attend(): pl.pallas_call(functools.partial(attend_kernel, frames_here, bk), grid_sp...]
    ppermute x21 -> x22, waiting for transfers between devices: 15.9 us -> 23.6 us  [hop(): return lax.ppermute(x, 'chip', [(i, i ^ step) for i in range(chips)])]
    convert_element_type x11 -> x10, other arithmetic: 11.6 us -> 10.4 us  [low(): return x.astype(BF16)]
    unnamed x222 -> x218, local copies, waits for them, and re-layouts: 23.7 us -> 23.5 us
    add x7 -> x8, other arithmetic: 12.2 us -> 12.2 us  [plus(): return a.astype(F32) + b.astype(F32)]
  transfers between devices with their start and end apart: 51 -> 52, of which waited for: 14 -> 19; matrix products, arithmetic and copies ran while one was open for 12% -> 12% of each run, Pallas kernels for 43% -> 34%
where the time goes in v5:
time: 440 us; the launch traced here: 432 us
  Pallas kernels  188 us (43%)
  starting transfers between devices  92.7 us (21%)
  waiting for transfers between devices  56.8 us (13%)
  other arithmetic  46.9 us (11%)
  local copies, waits for them, and re-layouts  44 us (10%)
    pallas_call x2, Pallas kernels, row_call(): pl.pallas_call(kernel, grid_spec=pltpu.PrefetchScalarGridSpec(num_scalar_...  72 us
    ppermute x22, starting transfers between devices, hop(): return lax.ppermute(x, 'chip', [(i, i ^ step) for i in range(chips)])  56.1 us
    pallas_call x3, Pallas kernels, attend_back(): pl.pallas_call(functools.partial(attend_back_kernel, frames_here), grid_s...  49.5 us
    pallas_call x2, Pallas kernels, attend(): pl.pallas_call(functools.partial(attend_kernel, frames_here, bk), grid_sp...  26.8 us
    ppermute x22, waiting for transfers between devices, hop(): return lax.ppermute(x, 'chip', [(i, i ^ step) for i in range(chips)])  23.6 us
    unnamed x218, local copies, waits for them, and re-layouts  23.5 us
    ppermute x7, waiting for transfers between devices, to_plane(): return lax.ppermute(x, 'mp', flip2)  20.5 us
    ppermute x18, starting transfers between devices, to_core(): return lax.ppermute(x, 'core', flip2)  19.9 us
  transfers between devices with their start and end apart: 52, of which 19 were waited for; matrix products, arithmetic and copies ran while one was open for 12% of the time, Pallas kernels for 34%

profile of v5, /device:TPU:0, one launch (start us, length us, event | category | flops | bytes accessed | tf_op | source)
XLA Modules:
  0.0 431.9 jit_solution(12384483785508858135)
XLA Ops:
  0.7 3.8 copy.31
  9.2 1.8 collective-permute-start
  11.0 2.7 copy.34.mine
  16.6 2.8 constant_dynamic-slice_fusion.2
  20.6 3.8 relay.1.weight.refs_6_.mine
  24.6 18.4 %collective-permute-start.3 = (bf16[1064,768]{1,0:T(8,128)(2,1)S(1)}, bf16[1064,768]{1,0:T(8,128)(2,1)S(1)}, u32[]{:S(2)}, u32[]{:S(2)}) collective-permute-start(bf16[1064,768]{1,0:T(8,128)(2,1)S(1)} %broadcast_select_fusion.own.tokens), channel_id=1, source_target_pairs={{0,2},{2,0},{1,3},{3,1},{4,6},{6,4},{5,7},{7,5},{8,10},{10,8},{9,1... | collective-permute-start | bytes 4902920 | tf_op jit(solution)/shard_map/ppermute | solution.py:1060
  45.6 2.9 collective-permute-start.6
  48.6 9.7 %project.1 = (bf16[2048,768]{1,0:T(8,128)(2,1)S(1)}, bf16[2048,1152]{1,0:T(8,128)(2,1)S(1)}, bf16[2048,128]{1,0:T(8,128)(2,1)S(1)}, bf16[2048,128]{1,0:T(8,128)(2,1)S(1)}) custom-call(s32[4]{0:T(128)S(1)} %get-tuple-element.198.scal, bf16[1064,768]{1,0:T(8,128)(2,1)S(1)} %collective-permute-done.3.oth, ...), custom_call_target="tpu_custom_call" | custom-call | flops 72477573120 | bytes 220200960 | tf_op jit(solution)/shard_map/project/pallas_call | solution.py:207
  60.9 13.7 %attend.2 = (bf16[1024,384]{1,0:T(8,128)(2,1)}, f32[1024,384]{1,0:T(8,128)S(1)}, f32[3,4,8,256]{3,2,1,0:T(8,128)S(1)}) custom-call(s32[4]{0:T(128)S(1)} %get-tuple-element.198.scal, bf16[2048,1152]{1,0:T(8,128)(2,1)S(1)} %get-tuple-element.111.q.qkv.k.v, bf16[2048,128]{1,0:T(8,128)(2,1)S(1)} %get-tuple-element.112.qfeat, ...), custom_call_target="tpu_custom_call" | custom-call | flops 257698037760 | bytes 251658240 | tf_op jit(solution)/shard_map/attend/pallas_call | solution.py:344
  74.6 7.9 %collective-permute-done.6.got_up = bf16[976,768]{1,0:T(8,128)(2,1)} collective-permute-done((bf16[976,768]{1,0:T(8,128)(2,1)}, bf16[976,768]{1,0:T(8,128)(2,1)}, u32[]{:S(2)}, u32[]{:S(2)}) %collective-permute-start.6) | collective-permute-done | bytes 1499168 | tf_op jit(solution)/shard_map/ppermute | solution.py:1063
  82.6 13.1 %attend.3 = (bf16[1024,384]{1,0:T(8,128)(2,1)S(1)}, f32[1024,384]{1,0:T(8,128)S(1)}, f32[3,4,8,256]{3,2,1,0:T(8,128)S(1)}) custom-call(s32[4]{0:T(128)S(1)} %get-tuple-element.154.scal, bf16[2048,1152]{1,0:T(8,128)(2,1)S(1)} %get-tuple-element.111.q.qkv.k.v, bf16[2048,128]{1,0:T(8,128)(2,1)S(1)} %get-tuple-element.112.qfeat, ...), custom_call_target="tpu_custom_call" | custom-call | flops 257698037760 | bytes 251658240 | tf_op jit(solution)/shard_map/attend/pallas_call | solution.py:344
  98.4 9.1 %collective-permute-done.7.got_down = bf16[768,768]{1,0:T(8,128)(2,1)} collective-permute-done((bf16[768,768]{1,0:T(8,128)(2,1)}, bf16[768,768]{1,0:T(8,128)(2,1)}, u32[]{:S(2)}, u32[]{:S(2)}) %collective-permute-start.7) | collective-permute-done | bytes 1179680 | tf_op jit(solution)/shard_map/ppermute | solution.py:1063
  109.1 2.4 collective-permute-done.5.mixed_oth
  112.8 39.1 %ahead.1 = (f32[1024,768]{1,0:T(8,128)}, f32[1024,768]{1,0:T(8,128)}, f32[1024,128]{1,0:T(8,128)S(1)}, bf16[1024,3072]{1,0:T(8,128)(2,1)}, bf16[1024,768]{1,0:T(...) custom-call(s32[4]{0:T(128)S(1)} %copy-done.14, ...), custom_call_target="tpu_custom_call" | custom-call | flops 314069483520 | bytes 546867200 | tf_op jit(solution)/shard_map/ahead/pallas_call | solution.py:622
  155.9 4.7 %collective-permute-done.10 = bf16[2,768,768]{2,1,0:T(8,128)(2,1)} collective-permute-done((bf16[2,768,768]{2,1,0:T(8,128)(2,1)}, bf16[2,768,768]{2,1,0:T(8,128)(2,1)}, u32[]{:S(2)}, u32[]{:S(2)}) %collective-permute-start.10) | collective-permute-done | bytes 2359328 | tf_op jit(solution)/shard_map/ppermute | solution.py:1060
  160.7 3.0 fusion.4
  163.7 2.4 collective-permute-start.11
  166.1 32.9 %behind.1 = (f32[1024,768]{1,0:T(8,128)}, bf16[1024,384]{1,0:T(8,128)(2,1)S(1)}, bf16[1024,384]{1,0:T(8,128)(2,1)S(1)}, f32[24,768]{1,0:T(8,128)S(1)}, f32[8,307...) custom-call(s32[4]{0:T(128)S(1)} %copy-done.14, ...), custom_call_target="tpu_custom_call" | custom-call | flops 338228674560 | bytes 315740160 | tf_op jit(solution)/shard_map/behind/pallas_call | solution.py:622
  199.0 2.7 bitcast_add_fusion.1
  205.2 3.9 collective-permute-done.12
  209.0 3.5 convert_add_fusion
  212.6 2.5 copy-done.62
  221.7 2.3 collective-permute-start.13
  224.1 2.3 copy-done.29
  226.4 16.6 %attend_back.3 = (bf16[1024,384]{1,0:T(8,128)(2,1)S(1)}, bf16[1024,384]{1,0:T(8,128)(2,1)S(1)}) custom-call(s32[4]{0:T(128)S(1)} %copy-done.14, bf16[2048,1152]{1,0:T(8,128)(2,1)S(1)} %copy-done.29, bf16[2048,1152]{1,0:T(8,128)(2,1)S(1)} %copy-done.29, bf16[2048,128]{1,0:T(8,128)(2,1)S(1)} %copy-done.38, bf16[2048,1152]{1,0:T(8,128)(2,1)S(1)} %copy-done.29, ...), custom_call_target="tpu_custom_call" | custom-call | flops 429496729600 | bytes 157286400 | tf_op jit(solution)/shard_map/attend_back/pallas_call | solution.py:803
  244.1 1.9 fusion.8
  246.0 10.8 %collective-permute-start.17 = (bf16[192,768]{1,0:T(8,128)(2,1)}, bf16[192,768]{1,0:T(8,128)(2,1)}, u32[]{:S(2)}, u32[]{:S(2)}) collective-permute-start(bf16[192,768]{1,0:T(8,128)(2,1)} %fusion.8), channel_id=1, source_target_pairs={{0,16},{4,20},{8,24},{12,28},{16,0},{20,4},{24,8},{28,12},{1,17},{... | collective-permute-start | bytes 884744 | tf_op jit(solution)/shard_map/ppermute | solution.py:1072
  256.8 2.6 bitcast_add_fusion
  260.8 16.4 %attend_back.4 = (bf16[1024,384]{1,0:T(8,128)(2,1)S(1)}, bf16[1024,384]{1,0:T(8,128)(2,1)S(1)}) custom-call(s32[4]{0:T(128)S(1)} %copy-done.19, bf16[2048,1152]{1,0:T(8,128)(2,1)S(1)} %bitcast.96, bf16[2048,1152]{1,0:T(8,128)(2,1)S(1)} %bitcast.96, bf16[2048,128]{1,0:T(8,128)(2,1)S(1)} %copy-done.38, bf16[2048,1152]{1,0:T(8,128)(2,1)S(1)} %bitcast.96, ...), custom_call_target="tpu_custom_call" | custom-call | flops 429496729600 | bytes 157286400 | tf_op jit(solution)/shard_map/attend_back/pallas_call | solution.py:803
  280.5 14.2 %collective-permute-start.24 = (bf16[192,768]{1,0:T(8,128)(2,1)S(1)}, bf16[192,768]{1,0:T(8,128)(2,1)S(1)}, u32[]{:S(2)}, u32[]{:S(2)}) collective-permute-start(bf16[192,768]{1,0:T(8,128)(2,1)S(1)} %add_convert_fusion.2), channel_id=1, source_target_pairs={{0,8},{4,12},{8,0},{12,4},{16,24},{20,28},{24,16},{28,20},{1,9},{5... | collective-permute-start | bytes 884744 | tf_op jit(solution)/shard_map/ppermute | solution.py:1072
  294.7 1.8 fusion.3
  298.3 10.5 %project_grad.2 = (bf16[384,768]{1,0:T(8,128)(2,1)S(1)}, bf16[384,768]{1,0:T(8,128)(2,1)S(1)}, f32[8,768]{1,0:T(8,128)S(1)}, f32[1024,768]{1,0:T(8,128)S(1)}) custom-call(s32[4]{0:T(128)S(1)} %copy-done.14, bf16[2048,768]{1,0:T(8,128)(2,1)S(1)} %copy-done.26, bf16[1024,384]{1,0:T(8,128)(2,1)S(1)} %copy-done.22, ...), custom_call_target="tpu_custom_call" | custom-call | flops 48318382080 | bytes 125829120 | tf_op jit(solution)/shard_map/project_grad/pallas_call | solution.py:885
  313.3 1.9 collective-permute-start.27
  315.3 16.6 %attend_back.5 = (bf16[1024,384]{1,0:T(8,128)(2,1)S(1)}, bf16[1024,384]{1,0:T(8,128)(2,1)S(1)}) custom-call(s32[4]{0:T(128)S(1)} %get-tuple-element.167.scal, bf16[2048,1152]{1,0:T(8,128)(2,1)S(1)} %bitcast.98, bf16[2048,1152]{1,0:T(8,128)(2,1)S(1)} %bitcast.98, bf16[2048,128]{1,0:T(8,128)(2,1)S(1)} %copy-done.39, bf16[2048,1152]{1,0:T(8,128)(2,1)S(1)} %bitcast.98, ...), custom_call_target="tpu_custom_call" | custom-call | flops 429496729600 | bytes 157286400 | tf_op jit(solution)/shard_map/attend_back/pallas_call | solution.py:803
  333.3 13.3 %collective-permute-start.29 = (bf16[240,768]{1,0:T(8,128)(2,1)S(1)}, bf16[240,768]{1,0:T(8,128)(2,1)S(1)}, u32[]{:S(2)}, u32[]{:S(2)}) collective-permute-start(bf16[240,768]{1,0:T(8,128)(2,1)S(1)} %add_convert_fusion.1), channel_id=1, source_target_pairs={{0,8},{4,12},{8,0},{12,4},{16,24},{20,28},{24,16},{28,20},{1,9},{5... | collective-permute-start | bytes 1105928 | tf_op jit(solution)/shard_map/ppermute | solution.py:1072
  348.3 3.3 project_grad.3
  359.0 5.0 %first_grad.1 = (bf16[1024,768]{1,0:T(8,128)(2,1)S(1)}, f32[16,768]{1,0:T(8,128)S(1)}) custom-call(bf16[1024,384]{1,0:T(8,128)(2,1)S(1)} %get-tuple-element.168.refs_1_.own, bf16[1024,384]{1,0:T(8,128)(2,1)S(1)} %collective-permute-done.25.got, bf16[768,1152]{1,0:T(8,128)(2,1)} %relay.1.weight.refs_6_.mine, ...), custom_call_target="tpu_custom_call" | custom-call | flops 24159191040 | bytes 188743680 | tf_op jit(solution)/shard_map/first_grad/pallas_call | solution.py:925
  365.4 2.7 collective-permute-done.32
  372.0 2.4 collective-permute-done.35
  382.3 9.4 %collective-permute-done.38 = bf16[96,768]{1,0:T(8,128)(2,1)S(1)} collective-permute-done((bf16[96,768]{1,0:T(8,128)(2,1)}, bf16[96,768]{1,0:T(8,128)(2,1)S(1)}, u32[]{:S(2)}, u32[]{:S(2)}) %collective-permute-start.38) | collective-permute-done | bytes 147488 | tf_op jit(solution)/shard_map/ppermute | solution.py:1072
  392.2 4.7 %collective-permute-done.37 = f32[24,768]{1,0:T(8,128)S(1)} collective-permute-done((f32[24,768]{1,0:T(8,128)S(1)}, f32[24,768]{1,0:T(8,128)S(1)}, u32[]{:S(2)}, u32[]{:S(2)}) %collective-permute-start.37) | collective-permute-done | bytes 73760 | tf_op jit(solution)/shard_map/ppermute | solution.py:1072
  397.0 3.3 collective-permute-start.39
  405.1 2.5 maximum_convert_fusion.1
  409.7 6.7 %last.1 = f32[980,768]{1,0:T(8,128)} custom-call(s32[4]{0:T(128)S(1)} %copy-done.15, bf16[1064,768]{1,0:T(8,128)(2,1)S(1)} %pack.1.tokens, bf16[1024,768]{1,0:T(8,128)(2,1)S(1)} %get-tuple-element.199.grad, bf16[1024,768]{1,0:T(8,128)(2,1)S(1)} %collective-permute-done.43.grad_got, f32[1024,768]{1,0:T(8,128)} %get-tuple-element.138.residual, ...), custom_call_target="tpu_custom_call" | custom-call | flops 314572800 | bytes 188743680 | tf_op jit(solution)/shard_map/last/pallas_call | solution.py:950
  418.4 1.8 collective-permute-done.47
  423.2 2.1 maximum_convert_fusion.2
  425.3 1.9 broadcast_select_fusion.2
  427.5 2.8 maximum_convert_fusion
  (394 shorter events, 81.6 us)
Async XLA Ops:
  7.4 6.4 %collective-permute-start.1 = (bf16[384,1152]{1,0:T(8,128)(2,1)}, bf16[384,1152]{1,0:T(8,128)(2,1)}, u32[]{:S(2)}, u32[]{:S(2)}) collective-permute-start(bf16[384,1152]{1,0:T(8,128)(2,1)} %copy.33), channel_id=1, source_target_pairs={{1,2},{2,1},{5,6},{6,5},{9,10},{10,9},{13,14},{14,13},{17,18},{18,... | collective-permute-start | bytes 2654216 | tf_op jit(solution)/shard_map/ppermute | solution.py:1057
  9.2 15.2 %collective-permute-start = (bf16[1064,768]{1,0:T(8,128)(2,1)S(1)}, bf16[1064,768]{1,0:T(8,128)(2,1)}, u32[]{:S(2)}, u32[]{:S(2)}) collective-permute-start(bf16[1064,768]{1,0:T(8,128)(2,1)S(1)} %pack.1.tokens), channel_id=1, source_target_pairs={{1,2},{2,1},{5,6},{6,5},{9,10},{10,9},{13,14},{14,13},{17,18},{18,... | collective-permute-start | bytes 4902920 | tf_op jit(solution)/shard_map/ppermute | solution.py:1057
  13.8 6.8 %collective-permute-start.2 = (bf16[384,1152]{1,0:T(8,128)(2,1)}, bf16[384,1152]{1,0:T(8,128)(2,1)}, u32[]{:S(2)}, u32[]{:S(2)}) collective-permute-start(bf16[384,1152]{1,0:T(8,128)(2,1)} %collective-permute-done.1.first), channel_id=1, source_target_pairs={{1,5},{2,6},{5,1},{6,2},{9,13},{10,14},{13,9},{14,10},{17,21},{18,... | collective-permute-start | bytes 2654216 | tf_op jit(solution)/shard_map/ppermute | solution.py:1106
  24.6 24.1 %collective-permute-start.3 = (bf16[1064,768]{1,0:T(8,128)(2,1)S(1)}, bf16[1064,768]{1,0:T(8,128)(2,1)S(1)}, u32[]{:S(2)}, u32[]{:S(2)}) collective-permute-start(bf16[1064,768]{1,0:T(8,128)(2,1)S(1)} %broadcast_select_fusion.own.tokens), channel_id=1, source_target_pairs={{0,2},{2,0},{1,3},{3,1},{4,6},{6,4},{5,7},{7,5},{8,10},{10,8},{9,1... | collective-permute-start | bytes 4902920 | tf_op jit(solution)/shard_map/ppermute | solution.py:1060
  45.6 36.9 %collective-permute-start.6 = (bf16[976,768]{1,0:T(8,128)(2,1)}, bf16[976,768]{1,0:T(8,128)(2,1)}, u32[]{:S(2)}, u32[]{:S(2)}) collective-permute-start(bf16[976,768]{1,0:T(8,128)(2,1)} %fusion.1), channel_id=1, source_target_pairs={{0,1},{1,0},{2,3},{3,2},{4,5},{5,4},{6,7},{7,6},{8,9},{9,8},{10,11... | collective-permute-start | bytes 4497416 | tf_op jit(solution)/shard_map/ppermute | solution.py:1063
  60.1 22.4 %collective-permute-start.4 = (bf16[768,1152]{1,0:T(8,128)(2,1)}, bf16[768,1152]{1,0:T(8,128)(2,1)}, u32[]{:S(2)}, u32[]{:S(2)}) collective-permute-start(bf16[768,1152]{1,0:T(8,128)(2,1)} %relay.1.weight.refs_6_.mine), channel_id=1, source_target_pairs={{0,2},{2,0},{1,3},{3,1},{4,6},{6,4},{5,7},{7,5},{8,10},{10,8},{9,1... | collective-permute-start | bytes 5308424 | tf_op jit(solution)/shard_map/ppermute | solution.py:1060
  60.3 47.2 %collective-permute-start.7 = (bf16[768,768]{1,0:T(8,128)(2,1)}, bf16[768,768]{1,0:T(8,128)(2,1)}, u32[]{:S(2)}, u32[]{:S(2)}) collective-permute-start(bf16[768,768]{1,0:T(8,128)(2,1)} %get-tuple-element.119), channel_id=1, source_target_pairs={{0,1},{1,0},{2,3},{3,2},{4,5},{5,4},{6,7},{7,6},{8,9},{9,8},{10,11... | collective-permute-start | bytes 3538952 | tf_op jit(solution)/shard_map/ppermute | solution.py:1063
  82.5 29.0 %collective-permute-start.8 = (bf16[976,768]{1,0:T(8,128)(2,1)}, bf16[976,768]{1,0:T(8,128)(2,1)}, u32[]{:S(2)}, u32[]{:S(2)}) collective-permute-start(bf16[976,768]{1,0:T(8,128)(2,1)} %collective-permute-done.6.got_up), channel_id=1, source_target_pairs={{0,2},{2,0},{1,3},{3,1},{4,6},{6,4},{5,7},{7,5},{8,10},{10,8},{9,1... | collective-permute-start | bytes 4497416 | tf_op jit(solution)/shard_map/ppermute | solution.py:1060
  107.5 4.2 collective-permute-start.9
  107.5 3.9 collective-permute-start.5
  155.8 4.9 %collective-permute-start.10 = (bf16[2,768,768]{2,1,0:T(8,128)(2,1)}, bf16[2,768,768]{2,1,0:T(8,128)(2,1)}, u32[]{:S(2)}, u32[]{:S(2)}) collective-permute-start(bf16[2,768,768]{2,1,0:T(8,128)(2,1)} %get-tuple-element.123), channel_id=1, source_target_pairs={{0,2},{2,0},{1,3},{3,1},{4,6},{6,4},{5,7},{7,5},{8,10},{10,8},{9,1... | collective-permute-start | bytes 7077896 | tf_op jit(solution)/shard_map/ppermute | solution.py:1060
  163.7 35.3 %collective-permute-start.11 = (bf16[768,768]{1,0:T(8,128)(2,1)}, bf16[768,768]{1,0:T(8,128)(2,1)}, u32[]{:S(2)}, u32[]{:S(2)}) collective-permute-start(bf16[768,768]{1,0:T(8,128)(2,1)} %fusion.4), channel_id=1, source_target_pairs={{0,1},{1,0},{2,3},{3,2},{4,5},{5,4},{6,7},{7,6},{8,9},{9,8},{10,11... | collective-permute-start | bytes 3538952 | tf_op jit(solution)/shard_map/ppermute | solution.py:1063
  203.2 5.8 %collective-permute-start.12 = (bf16[2,960,768]{2,1,0:T(8,128)(2,1)}, bf16[2,960,768]{2,1,0:T(8,128)(2,1)}, u32[]{:S(2)}, u32[]{:S(2)}) collective-permute-start(bf16[2,960,768]{2,1,0:T(8,128)(2,1)} %get-tuple-element.135), channel_id=1, source_target_pairs={{0,2},{2,0},{1,3},{3,1},{4,6},{6,4},{5,7},{7,5},{8,10},{10,8},{9,1... | collective-permute-start | bytes 8847368 | tf_op jit(solution)/shard_map/ppermute | solution.py:1060
  203.4 15.7 %collective-permute-start.14 = (bf16[384,768]{1,0:T(8,128)(2,1)S(1)}, bf16[384,768]{1,0:T(8,128)(2,1)S(1)}, u32[]{:S(2)}, u32[]{:S(2)}) collective-permute-start(bf16[384,768]{1,0:T(8,128)(2,1)S(1)} %fusion.6), channel_id=1, source_target_pairs={{0,4},{4,0},{8,12},{12,8},{16,20},{20,16},{24,28},{28,24},{1,5},{5... | collective-permute-start | bytes 1769480 | tf_op jit(solution)/shard_map/ppermute | solution.py:1072
  205.1 18.9 %collective-permute-start.15 = (bf16[1024,384]{1,0:T(8,128)(2,1)}, bf16[1024,384]{1,0:T(8,128)(2,1)S(1)}, u32[]{:S(2)}, u32[]{:S(2)}) collective-permute-start(bf16[1024,384]{1,0:T(8,128)(2,1)} %copy-done.20), channel_id=1, source_target_pairs={{0,2},{2,0},{1,3},{3,1},{4,6},{6,4},{5,7},{7,5},{8,10},{10,8},{9,1... | collective-permute-start | bytes 2359304 | tf_op jit(solution)/shard_map/ppermute | solution.py:1060
  216.4 40.4 %collective-permute-start.18 = (bf16[2,480,768]{2,1,0:T(8,128)(2,1)}, bf16[2,480,768]{2,1,0:T(8,128)(2,1)}, u32[]{:S(2)}, u32[]{:S(2)}) collective-permute-start(bf16[2,480,768]{2,1,0:T(8,128)(2,1)} %fusion.2), channel_id=1, source_target_pairs={{0,4},{4,0},{8,12},{12,8},{16,20},{20,16},{24,28},{28,24},{1,5},{5... | collective-permute-start | bytes 4423688 | tf_op jit(solution)/shard_map/ppermute | solution.py:1072
  220.0 24.1 %collective-permute-start.16 = (bf16[192,768]{1,0:T(8,128)(2,1)}, bf16[192,768]{1,0:T(8,128)(2,1)}, u32[]{:S(2)}, u32[]{:S(2)}) collective-permute-start(bf16[192,768]{1,0:T(8,128)(2,1)} %fusion.10), channel_id=1, source_target_pairs={{0,8},{4,12},{8,0},{12,4},{16,24},{20,28},{24,16},{28,20},{1,9},{5... | collective-permute-start | bytes 884744 | tf_op jit(solution)/shard_map/ppermute | solution.py:1072
  221.7 39.1 %collective-permute-start.13 = (f32[1024,768]{1,0:T(8,128)}, f32[1024,768]{1,0:T(8,128)}, u32[]{:S(2)}, u32[]{:S(2)}) collective-permute-start(f32[1024,768]{1,0:T(8,128)} %get-tuple-element.138.residual), channel_id=1, source_target_pairs={{1,2},{2,1},{5,6},{6,5},{9,10},{10,9},{13,14},{14,13},{17,18},{18,... | collective-permute-start | bytes 9437192 | tf_op jit(solution)/shard_map/ppermute | solution.py:1057
  243.9 16.9 %collective-permute-start.19 = (bf16[1024,384]{1,0:T(8,128)(2,1)S(1)}, bf16[1024,384]{1,0:T(8,128)(2,1)S(1)}, u32[]{:S(2)}, u32[]{:S(2)}) collective-permute-start(bf16[1024,384]{1,0:T(8,128)(2,1)S(1)} %get-tuple-element.148.refs_0_), channel_id=1, source_target_pairs={{0,2},{2,0},{1,3},{3,1},{4,6},{6,4},{5,7},{7,5},{8,10},{10,8},{9,1... | collective-permute-start | bytes 2359304 | tf_op jit(solution)/shard_map/ppermute | solution.py:1060
  246.0 33.0 %collective-permute-start.17 = (bf16[192,768]{1,0:T(8,128)(2,1)}, bf16[192,768]{1,0:T(8,128)(2,1)}, u32[]{:S(2)}, u32[]{:S(2)}) collective-permute-start(bf16[192,768]{1,0:T(8,128)(2,1)} %fusion.8), channel_id=1, source_target_pairs={{0,16},{4,20},{8,24},{12,28},{16,0},{20,4},{24,8},{28,12},{1,17},{... | collective-permute-start | bytes 884744 | tf_op jit(solution)/shard_map/ppermute | solution.py:1072
  260.4 18.6 %collective-permute-start.20 = (bf16[480,768]{1,0:T(8,128)(2,1)}, bf16[480,768]{1,0:T(8,128)(2,1)}, u32[]{:S(2)}, u32[]{:S(2)}) collective-permute-start(bf16[480,768]{1,0:T(8,128)(2,1)} %fusion.5), channel_id=1, source_target_pairs={{0,1},{1,0},{2,3},{3,2},{4,5},{5,4},{6,7},{7,6},{8,9},{9,8},{10,11... | collective-permute-start | bytes 2211848 | tf_op jit(solution)/shard_map/ppermute | solution.py:1063
  278.2 18.6 %collective-permute-start.21 = (bf16[1024,384]{1,0:T(8,128)(2,1)S(1)}, bf16[1024,384]{1,0:T(8,128)(2,1)}, u32[]{:S(2)}, u32[]{:S(2)}) collective-permute-start(bf16[1024,384]{1,0:T(8,128)(2,1)S(1)} %get-tuple-element.155.refs_1_), channel_id=1, source_target_pairs={{0,2},{2,0},{1,3},{3,1},{4,6},{6,4},{5,7},{7,5},{8,10},{10,8},{9,1... | collective-permute-start | bytes 2359304 | tf_op jit(solution)/shard_map/ppermute | solution.py:1060
  280.5 28.3 %collective-permute-start.24 = (bf16[192,768]{1,0:T(8,128)(2,1)S(1)}, bf16[192,768]{1,0:T(8,128)(2,1)S(1)}, u32[]{:S(2)}, u32[]{:S(2)}) collective-permute-start(bf16[192,768]{1,0:T(8,128)(2,1)S(1)} %add_convert_fusion.2), channel_id=1, source_target_pairs={{0,8},{4,12},{8,0},{12,4},{16,24},{20,28},{24,16},{28,20},{1,9},{5... | collective-permute-start | bytes 884744 | tf_op jit(solution)/shard_map/ppermute | solution.py:1072
  296.6 13.7 %collective-permute-start.23 = (bf16[240,768]{1,0:T(8,128)(2,1)S(1)}, bf16[240,768]{1,0:T(8,128)(2,1)S(1)}, u32[]{:S(2)}, u32[]{:S(2)}) collective-permute-start(bf16[240,768]{1,0:T(8,128)(2,1)S(1)} %fusion.9), channel_id=1, source_target_pairs={{0,8},{4,12},{8,0},{12,4},{16,24},{20,28},{24,16},{28,20},{1,9},{5... | collective-permute-start | bytes 1105928 | tf_op jit(solution)/shard_map/ppermute | solution.py:1072
  311.2 20.9 %collective-permute-start.26 = (bf16[240,768]{1,0:T(8,128)(2,1)}, bf16[240,768]{1,0:T(8,128)(2,1)}, u32[]{:S(2)}, u32[]{:S(2)}) collective-permute-start(bf16[240,768]{1,0:T(8,128)(2,1)} %fusion.7), channel_id=1, source_target_pairs={{0,16},{4,20},{8,24},{12,28},{16,0},{20,4},{24,8},{28,12},{1,17},{... | collective-permute-start | bytes 1105928 | tf_op jit(solution)/shard_map/ppermute | solution.py:1072
  312.4 39.2 %collective-permute-start.50 = (bf16[384,768]{1,0:T(8,128)(2,1)}, bf16[384,768]{1,0:T(8,128)(2,1)}, u32[]{:S(2)}, u32[]{:S(2)}) collective-permute-start(bf16[384,768]{1,0:T(8,128)(2,1)} %pad_maximum_fusion.3), channel_id=1, source_target_pairs={{0,4},{4,0},{8,12},{12,8},{16,20},{20,16},{24,28},{28,24},{1,5},{5... | collective-permute-start | bytes 1769480 | tf_op jit(solution)/shard_map/ppermute | solution.py:1072
  313.3 33.3 %collective-permute-start.27 = (bf16[384,768]{1,0:T(8,128)(2,1)}, bf16[384,768]{1,0:T(8,128)(2,1)}, u32[]{:S(2)}, u32[]{:S(2)}) collective-permute-start(bf16[384,768]{1,0:T(8,128)(2,1)} %broadcast_select_fusion.11), channel_id=1, source_target_pairs={{0,1},{1,0},{2,3},{3,2},{4,5},{5,4},{6,7},{7,6},{8,9},{9,8},{10,11... | collective-permute-start | bytes 1769480 | tf_op jit(solution)/shard_map/ppermute | solution.py:1063
  331.9 27.1 %collective-permute-start.25 = (bf16[1024,384]{1,0:T(8,128)(2,1)S(1)}, bf16[1024,384]{1,0:T(8,128)(2,1)S(1)}, u32[]{:S(2)}, u32[]{:S(2)}) collective-permute-start(bf16[1024,384]{1,0:T(8,128)(2,1)S(1)} %get-tuple-element.169.refs_0_), channel_id=1, source_target_pairs={{0,2},{2,0},{1,3},{3,1},{4,6},{6,4},{5,7},{7,5},{8,10},{10,8},{9,1... | collective-permute-start | bytes 2359304 | tf_op jit(solution)/shard_map/ppermute | solution.py:1060
  333.3 22.4 %collective-permute-start.29 = (bf16[240,768]{1,0:T(8,128)(2,1)S(1)}, bf16[240,768]{1,0:T(8,128)(2,1)S(1)}, u32[]{:S(2)}, u32[]{:S(2)}) collective-permute-start(bf16[240,768]{1,0:T(8,128)(2,1)S(1)} %add_convert_fusion.1), channel_id=1, source_target_pairs={{0,8},{4,12},{8,0},{12,4},{16,24},{20,28},{24,16},{28,20},{1,9},{5... | collective-permute-start | bytes 1105928 | tf_op jit(solution)/shard_map/ppermute | solution.py:1072
  347.9 9.1 %collective-permute-start.30 = (bf16[192,768]{1,0:T(8,128)(2,1)S(1)}, bf16[192,768]{1,0:T(8,128)(2,1)S(1)}, u32[]{:S(2)}, u32[]{:S(2)}) collective-permute-start(bf16[192,768]{1,0:T(8,128)(2,1)S(1)} %fusion.11), channel_id=1, source_target_pairs={{0,4},{4,0},{8,12},{12,8},{16,20},{20,16},{24,28},{28,24},{1,5},{5... | collective-permute-start | bytes 884744 | tf_op jit(solution)/shard_map/ppermute | solution.py:1072
  354.1 42.8 %collective-permute-start.51 = (bf16[768,768]{1,0:T(8,128)(2,1)}, bf16[768,768]{1,0:T(8,128)(2,1)}, u32[]{:S(2)}, u32[]{:S(2)}) collective-permute-start(bf16[768,768]{1,0:T(8,128)(2,1)} %pad_maximum_fusion.1), channel_id=1, source_target_pairs={{0,2},{2,0},{1,3},{3,1},{4,6},{6,4},{5,7},{7,5},{8,10},{10,8},{9,1... | collective-permute-start | bytes 3538952 | tf_op jit(solution)/shard_map/ppermute | solution.py:1060
  357.2 7.4 %collective-permute-start.33 = (bf16[96,768]{1,0:T(8,128)(2,1)S(1)}, bf16[96,768]{1,0:T(8,128)(2,1)S(1)}, u32[]{:S(2)}, u32[]{:S(2)}) collective-permute-start(bf16[96,768]{1,0:T(8,128)(2,1)S(1)} %fusion.14), channel_id=1, source_target_pairs={{0,8},{4,12},{8,0},{12,4},{16,24},{20,28},{24,16},{28,20},{1,9},{5... | collective-permute-start | bytes 442376 | tf_op jit(solution)/shard_map/ppermute | solution.py:1072
  358.9 9.1 %collective-permute-start.32 = (bf16[384,384]{1,0:T(8,128)(2,1)S(1)}, bf16[384,384]{1,0:T(8,128)(2,1)S(1)}, u32[]{:S(2)}, u32[]{:S(2)}) collective-permute-start(bf16[384,384]{1,0:T(8,128)(2,1)S(1)} %broadcast_select_fusion.18), channel_id=1, source_target_pairs={{0,1},{1,0},{2,3},{3,2},{4,5},{5,4},{6,7},{7,6},{8,9},{9,8},{10,11... | collective-permute-start | bytes 884744 | tf_op jit(solution)/shard_map/ppermute | solution.py:1063
  369.0 5.4 %collective-permute-start.35 = (bf16[192,384]{1,0:T(8,128)(2,1)}, bf16[192,384]{1,0:T(8,128)(2,1)S(1)}, u32[]{:S(2)}, u32[]{:S(2)}) collective-permute-start(bf16[192,384]{1,0:T(8,128)(2,1)} %fusion.15), channel_id=1, source_target_pairs={{0,4},{4,0},{8,12},{12,8},{16,20},{20,16},{24,28},{28,24},{1,5},{5... | collective-permute-start | bytes 442376 | tf_op jit(solution)/shard_map/ppermute | solution.py:1072
  371.6 8.2 %collective-permute-start.34 = (f32[24,768]{1,0:T(8,128)S(1)}, f32[24,768]{1,0:T(8,128)S(1)}, u32[]{:S(2)}, u32[]{:S(2)}) collective-permute-start(f32[24,768]{1,0:T(8,128)S(1)} %add.163), channel_id=1, source_target_pairs={{0,1},{1,0},{2,3},{3,2},{4,5},{5,4},{6,7},{7,6},{8,9},{9,8},{10,11... | collective-permute-start | bytes 221192 | tf_op jit(solution)/shard_map/ppermute | solution.py:1063
  375.4 5.2 %collective-permute-start.36 = (bf16[192,384]{1,0:T(8,128)(2,1)S(1)}, bf16[192,384]{1,0:T(8,128)(2,1)S(1)}, u32[]{:S(2)}, u32[]{:S(2)}) collective-permute-start(bf16[192,384]{1,0:T(8,128)(2,1)S(1)} %fusion.16), channel_id=1, source_target_pairs={{0,8},{4,12},{8,0},{12,4},{16,24},{20,28},{24,16},{28,20},{1,9},{5... | collective-permute-start | bytes 442376 | tf_op jit(solution)/shard_map/ppermute | solution.py:1072
  377.4 32.3 %collective-permute-start.43 = (bf16[1024,768]{1,0:T(8,128)(2,1)S(1)}, bf16[1024,768]{1,0:T(8,128)(2,1)S(1)}, u32[]{:S(2)}, u32[]{:S(2)}) collective-permute-start(bf16[1024,768]{1,0:T(8,128)(2,1)S(1)} %get-tuple-element.199.grad), channel_id=1, source_target_pairs={{1,2},{2,1},{5,6},{6,5},{9,10},{10,9},{13,14},{14,13},{17,18},{18,... | collective-permute-start | bytes 4718600 | tf_op jit(solution)/shard_map/ppermute | solution.py:1057
  378.2 13.5 %collective-permute-start.38 = (bf16[96,768]{1,0:T(8,128)(2,1)}, bf16[96,768]{1,0:T(8,128)(2,1)S(1)}, u32[]{:S(2)}, u32[]{:S(2)}) collective-permute-start(bf16[96,768]{1,0:T(8,128)(2,1)} %fusion.13), channel_id=1, source_target_pairs={{0,16},{4,20},{8,24},{12,28},{16,0},{20,4},{24,8},{28,12},{1,17},{... | collective-permute-start | bytes 442376 | tf_op jit(solution)/shard_map/ppermute | solution.py:1072
  379.8 22.2 %collective-permute-start.42 = (bf16[480,768]{1,0:T(8,128)(2,1)}, bf16[480,768]{1,0:T(8,128)(2,1)S(1)}, u32[]{:S(2)}, u32[]{:S(2)}) collective-permute-start(bf16[480,768]{1,0:T(8,128)(2,1)} %pad_maximum_fusion.2), channel_id=1, source_target_pairs={{0,4},{4,0},{8,12},{12,8},{16,20},{20,16},{24,28},{28,24},{1,5},{5... | collective-permute-start | bytes 2211848 | tf_op jit(solution)/shard_map/ppermute | solution.py:1072
  380.7 24.0 %collective-permute-start.40 = (bf16[192,384]{1,0:T(8,128)(2,1)S(1)}, bf16[192,384]{1,0:T(8,128)(2,1)S(1)}, u32[]{:S(2)}, u32[]{:S(2)}) collective-permute-start(bf16[192,384]{1,0:T(8,128)(2,1)S(1)} %fusion.12), channel_id=1, source_target_pairs={{0,16},{4,20},{8,24},{12,28},{16,0},{20,4},{24,8},{28,12},{1,17},{... | collective-permute-start | bytes 442376 | tf_op jit(solution)/shard_map/ppermute | solution.py:1072
  391.7 5.2 %collective-permute-start.37 = (f32[24,768]{1,0:T(8,128)S(1)}, f32[24,768]{1,0:T(8,128)S(1)}, u32[]{:S(2)}, u32[]{:S(2)}) collective-permute-start(f32[24,768]{1,0:T(8,128)S(1)} %add.165), channel_id=1, source_target_pairs={{0,8},{4,12},{8,0},{12,4},{16,24},{20,28},{24,16},{28,20},{1,9},{5... | collective-permute-start | bytes 221192 | tf_op jit(solution)/shard_map/ppermute | solution.py:1072
  396.9 7.7 %collective-permute-start.41 = (bf16[96,768]{1,0:T(8,128)(2,1)S(1)}, bf16[96,768]{1,0:T(8,128)(2,1)S(1)}, u32[]{:S(2)}, u32[]{:S(2)}) collective-permute-start(bf16[96,768]{1,0:T(8,128)(2,1)S(1)} %add_convert_fusion.4), channel_id=1, source_target_pairs={{0,8},{4,12},{8,0},{12,4},{16,24},{20,28},{24,16},{28,20},{1,9},{5... | collective-permute-start | bytes 442376 | tf_op jit(solution)/shard_map/ppermute | solution.py:1072
  397.0 7.8 %collective-permute-start.39 = (f32[24,768]{1,0:T(8,128)S(1)}, f32[24,768]{1,0:T(8,128)S(1)}, u32[]{:S(2)}, u32[]{:S(2)}) collective-permute-start(f32[24,768]{1,0:T(8,128)S(1)} %add.168), channel_id=1, source_target_pairs={{0,16},{4,20},{8,24},{12,28},{16,0},{20,4},{24,8},{28,12},{1,17},{... | collective-permute-start | bytes 221192 | tf_op jit(solution)/shard_map/ppermute | solution.py:1072
  404.8 11.6 %collective-permute-start.44 = (f32[24,768]{1,0:T(8,128)S(1)}, f32[24,768]{1,0:T(8,128)S(1)}, u32[]{:S(2)}, u32[]{:S(2)}) collective-permute-start(f32[24,768]{1,0:T(8,128)S(1)} %add.170), channel_id=1, source_target_pairs={{0,4},{4,0},{8,12},{12,8},{16,20},{20,16},{24,28},{28,24},{1,5},{5... | collective-permute-start | bytes 221192 | tf_op jit(solution)/shard_map/ppermute | solution.py:1072
  407.6 17.6 %collective-permute-start.49 = (bf16[960,768]{1,0:T(8,128)(2,1)}, bf16[960,768]{1,0:T(8,128)(2,1)}, u32[]{:S(2)}, u32[]{:S(2)}) collective-permute-start(bf16[960,768]{1,0:T(8,128)(2,1)} %pad_maximum_fusion), channel_id=1, source_target_pairs={{0,2},{2,0},{1,3},{3,1},{4,6},{6,4},{5,7},{7,5},{8,10},{10,8},{9,1... | collective-permute-start | bytes 4423688 | tf_op jit(solution)/shard_map/ppermute | solution.py:1060
  407.6 9.9 %collective-permute-start.45 = (bf16[192,768]{1,0:T(8,128)(2,1)S(1)}, bf16[192,768]{1,0:T(8,128)(2,1)S(1)}, u32[]{:S(2)}, u32[]{:S(2)}) collective-permute-start(bf16[192,768]{1,0:T(8,128)(2,1)S(1)} %pad_maximum_fusion.5), channel_id=1, source_target_pairs={{0,4},{4,0},{8,12},{12,8},{16,20},{20,16},{24,28},{28,24},{1,5},{5... | collective-permute-start | bytes 884744 | tf_op jit(solution)/shard_map/ppermute | solution.py:1072
  409.4 10.8 %collective-permute-start.47 = (bf16[192,384]{1,0:T(8,128)(2,1)S(1)}, bf16[192,384]{1,0:T(8,128)(2,1)S(1)}, u32[]{:S(2)}, u32[]{:S(2)}) collective-permute-start(bf16[192,384]{1,0:T(8,128)(2,1)S(1)} %add_convert_fusion.3), channel_id=1, source_target_pairs={{0,4},{4,0},{8,12},{12,8},{16,20},{20,16},{24,28},{28,24},{1,5},{5... | collective-permute-start | bytes 442376 | tf_op jit(solution)/shard_map/ppermute | solution.py:1072
  417.7 4.8 %collective-permute-start.46 = (bf16[384,768]{1,0:T(8,128)(2,1)S(1)}, bf16[384,768]{1,0:T(8,128)(2,1)S(1)}, u32[]{:S(2)}, u32[]{:S(2)}) collective-permute-start(bf16[384,768]{1,0:T(8,128)(2,1)S(1)} %pad_maximum_fusion.4), channel_id=1, source_target_pairs={{0,2},{2,0},{1,3},{3,1},{4,6},{6,4},{5,7},{7,5},{8,10},{10,8},{9,1... | collective-permute-start | bytes 1769480 | tf_op jit(solution)/shard_map/ppermute | solution.py:1060
  (112 other events, 1220.4 us)
